TPU v7x, 32 devices: a whole 2x2x4 slice. The times are simulated.
32 devices in a mesh: dp: 8 (over z, x), tensor: 4 (over y, core).
Axes of the slice: x: 2, y: 2, z: 4, core: 2. Of those that a mesh axis runs over, the one named last changes fastest.
Arguments:
- layer_input: bfloat16 [32768, 768], P(('dp', 'tensor')), may hold values from -6 to 6
- out_cotangent: bfloat16 [32768, 768], P(('dp', 'tensor')), may hold values from -6 to 6
- teacher: bfloat16 [32768, 768], P(('dp', 'tensor')), may hold values from -6 to 6
- valid_mask: int32 [8, 2048], P('dp'), may hold values from 0 to 1, as said below
- prompt_docs: int32 [8, 2048], P('dp'), may hold values from 0 to 3, never falling along the last dimension, each value on 1 to 1024 neighbouring positions
- pass_embed: float32 [768], replicated, may hold values from -1.75 to 1.75
- first_gain: float32 [768], replicated, may hold values from 0.5 to 1.5
- first_shift: float32 [768], replicated, may hold values from -1.75 to 1.75
- project_in: bfloat16 [768, 3, 768], P(None, None, 'tensor'), may hold values from -0.3125 to 0.3125
- project_out: bfloat16 [768, 768], P('tensor'), may hold values from -1.25 to 1.25
- second_gain: float32 [768], replicated, may hold values from 0.5 to 1.5
- second_shift: float32 [768], replicated, may hold values from -1.75 to 1.75
- expand_weight: bfloat16 [768, 3072], P(None, 'tensor'), may hold values from -0.21875 to 0.21875
- reduce_weight: bfloat16 [3072, 768], P('tensor'), may hold values from -0.109375 to 0.109375
Outputs:
- layer_output: bfloat16 [32768, 768], P(('dp', 'tensor'))
- loss: float32 [], replicated
- input_gradient: bfloat16 [32768, 768], P(('dp', 'tensor'))
- embed_gradient: float32 [768], replicated
- first_gain_gradient: float32 [768], replicated
- first_shift_gradient: float32 [768], replicated
- project_in_gradient: float32 [768, 3, 768], P(None, None, 'tensor')
- project_out_gradient: float32 [768, 768], P('tensor')
- second_gain_gradient: float32 [768], replicated
- second_shift_gradient: float32 [768], replicated
- expand_gradient: float32 [768, 3072], P(None, 'tensor')
- reduce_gradient: float32 [3072, 768], P('tensor')
Inputs may be any that keep to these rules, and one draw needn't show every extreme that they name: `valid_mask`: 1 marks a valid continuation token, 0 a padded one; the first token of every continuation is valid. `prompt_docs`: document number of each prompt token of its group; never falls along the prompt; each document has at most 1024 tokens.
All inputs are finite; a program needn't handle non-finite values.
Results may differ from a plain program's by a relative error of at most 0.017.
The roundings to bfloat16 on the way count: a program that leaves them out, or rounds other values in their place, can miss the bound.
Values may be sent and summed in bfloat16 or wider, within the bound.
No kernel may reach another device: no remote copies, remote signals or barrier semaphores. Data moves between devices by JAX's collectives and lax.ppermute only.
A program may use at most 448 MiB of HBM per device.

v0:
```python
import jax
import jax.numpy as jnp
from jax import lax
from jax.sharding import PartitionSpec as P

D = 768
H = 12
PROMPT = 2048
CONT = 256
CONTS = 8
GLEN = 4096


norm_eps = 1e-05


def normalize(values):
    centred = values - jnp.mean(values, axis=-1, keepdims=True)
    spread = jnp.mean(centred * centred, axis=-1, keepdims=True)
    return centred * lax.rsqrt(spread + norm_eps)


def affine_norm(values, norm_gain, norm_shift):
    return normalize(values) * norm_gain + norm_shift


def tanh_gelu(values):
    return jax.nn.gelu(values, approximate=True)


def block_plan():
    blocks = []
    prompt_step = min(512, PROMPT)
    for row_begin in range(0, PROMPT, prompt_step):
        blocks.append((row_begin, prompt_step, True))
    per_block = max(1, min(CONTS, 512 // CONT))
    for first_part in range(0, CONTS, per_block):
        blocks.append((PROMPT + first_part * CONT, per_block * CONT, False))
    return blocks


def select_keys(source, row_begin, row_span, is_prompt):
    if is_prompt:
        return source[: row_begin + row_span]
    return jnp.concatenate([source[:PROMPT], source[row_begin : row_begin + row_span]], 0)


def scatter_keys(target, update, row_begin, row_span, is_prompt):
    if is_prompt:
        return target.at[: row_begin + row_span].add(update)
    target = target.at[:PROMPT].add(update[:PROMPT])
    return target.at[row_begin : row_begin + row_span].add(update[PROMPT:])


def block_allowed(doc_ids, valid_ids, row_begin, row_span, is_prompt):
    local_ids = jnp.arange(row_span, dtype=jnp.int32)
    if is_prompt:
        row_ids = row_begin + local_ids
        col_ids = jnp.arange(row_begin + row_span, dtype=jnp.int32)
        same_doc = (
            doc_ids[None, : row_begin + row_span] == doc_ids[row_begin : row_begin + row_span, None]
        )
        return same_doc & (col_ids[None, :] <= row_ids[:, None])
    same_part = local_ids[None, :] // CONT == local_ids[:, None] // CONT
    causal = local_ids[None, :] <= local_ids[:, None]
    offset = row_begin - PROMPT
    live_keys = valid_ids[offset : offset + row_span] == 1
    own_keys = same_part & causal & live_keys[None, :]
    return jnp.concatenate([jnp.ones((row_span, PROMPT), jnp.bool_), own_keys], 1)


def block_scores(block_queries, block_keys, allowed, score_scale):
    raw_scores = (
        jnp.einsum("qhd,khd->hqk", block_queries, block_keys, preferred_element_type=jnp.float32)
        * score_scale
    )
    return jnp.where(allowed[None], raw_scores, -jnp.inf)


def group_forward(queries, key_rows, value_rows, doc_ids, valid_ids, score_scale):
    outputs = []
    logsums = []
    for block_spec in block_plan():
        row_begin, row_span, is_prompt = block_spec
        allowed = block_allowed(doc_ids, valid_ids, row_begin, row_span, is_prompt)
        block_keys = select_keys(key_rows, row_begin, row_span, is_prompt)
        block_values = select_keys(value_rows, row_begin, row_span, is_prompt)
        scores = block_scores(
            queries[row_begin : row_begin + row_span], block_keys, allowed, score_scale
        )
        maxima = jnp.max(scores, axis=-1, keepdims=True)
        exponent = jnp.exp(scores - maxima)
        totals = jnp.sum(exponent, axis=-1, keepdims=True)
        probs_low = (exponent / totals).astype(jnp.bfloat16)
        outputs.append(
            jnp.einsum("hqk,khd->qhd", probs_low, block_values, preferred_element_type=jnp.float32)
        )
        logsums.append(maxima + jnp.log(totals))
    return (jnp.concatenate(outputs, 0), logsums)


def group_backward(
    queries, key_rows, value_rows, doc_ids, valid_ids, attended_adj, logsums, score_scale
):
    query_parts = []
    key_adj = jnp.zeros(key_rows.shape, jnp.float32)
    value_adj = jnp.zeros(value_rows.shape, jnp.float32)
    for block_spec, logsum in zip(block_plan(), logsums):
        row_begin, row_span, is_prompt = block_spec
        allowed = block_allowed(doc_ids, valid_ids, row_begin, row_span, is_prompt)
        block_queries = queries[row_begin : row_begin + row_span]
        block_keys = select_keys(key_rows, row_begin, row_span, is_prompt)
        block_values = select_keys(value_rows, row_begin, row_span, is_prompt)
        block_adj = attended_adj[row_begin : row_begin + row_span]
        scores = block_scores(block_queries, block_keys, allowed, score_scale)
        attn_probs = jnp.exp(scores - logsum)
        probs_low = attn_probs.astype(jnp.bfloat16)
        prob_adj = jnp.einsum(
            "qhd,khd->hqk", block_adj, block_values, preferred_element_type=jnp.float32
        )
        inner = jnp.sum(attn_probs * prob_adj, axis=-1, keepdims=True)
        score_adj = (attn_probs * (prob_adj - inner)).astype(jnp.bfloat16)
        query_parts.append(
            jnp.einsum("hqk,khd->qhd", score_adj, block_keys, preferred_element_type=jnp.float32)
            * score_scale
        )
        key_part = (
            jnp.einsum("hqk,qhd->khd", score_adj, block_queries, preferred_element_type=jnp.float32)
            * score_scale
        )
        value_part = jnp.einsum(
            "hqk,qhd->khd", probs_low, block_adj, preferred_element_type=jnp.float32
        )
        key_adj = scatter_keys(key_adj, key_part, row_begin, row_span, is_prompt)
        value_adj = scatter_keys(value_adj, value_part, row_begin, row_span, is_prompt)
    return (jnp.concatenate(query_parts, 0), key_adj, value_adj)


def shards(
    layer_input,
    out_cotangent,
    teacher,
    valid_mask,
    prompt_docs,
    pass_embed,
    first_gain,
    first_shift,
    project_in,
    project_out,
    second_gain,
    second_shift,
    expand_weight,
    reduce_weight,
):
    head_dim = D // H
    score_scale = head_dim ** (-0.5)
    local_rows = layer_input.shape[0]
    local_width = project_out.shape[0]
    local_heads = local_width // head_dim
    valid_total = lax.psum(jnp.sum(valid_mask).astype(jnp.float32), "dp")
    divisor = valid_total * D
    row_ids = lax.axis_index("tensor") * local_rows + jnp.arange(local_rows, dtype=jnp.int32)
    row_group = row_ids // GLEN
    row_place = row_ids % GLEN - PROMPT
    flat_valid = valid_mask.reshape(-1)
    lookup = jnp.clip(row_group * (GLEN - PROMPT) + row_place, 0, flat_valid.shape[0] - 1)
    row_valid = jnp.where(row_place >= 0, jnp.take(flat_valid, lookup), 0).astype(jnp.float32)
    hidden_in = layer_input.astype(jnp.float32) + pass_embed
    first_affine, first_pull = jax.vjp(affine_norm, hidden_in, first_gain, first_shift)
    first_norm = first_affine.astype(jnp.bfloat16)
    first_full = lax.all_gather(first_norm, "tensor", axis=0, tiled=True)
    in_matrix = project_in.reshape(D, 3 * local_width)
    projected = jnp.dot(first_full, in_matrix, preferred_element_type=jnp.float32).astype(
        jnp.bfloat16
    )
    all_rows = projected.shape[0]
    queries = projected[:, :local_width].reshape(all_rows, local_heads, head_dim)
    key_rows = projected[:, local_width : 2 * local_width].reshape(all_rows, local_heads, head_dim)
    value_rows = projected[:, 2 * local_width :].reshape(all_rows, local_heads, head_dim)
    group_pos = 0
    group_out, logsums = group_forward(
        queries, key_rows, value_rows, prompt_docs[group_pos], valid_mask[group_pos], score_scale
    )
    saved_logsums = [logsums]
    attended = group_out.reshape(all_rows, local_width).astype(jnp.bfloat16)
    picked = attended
    attn_branch = lax.psum_scatter(
        jnp.dot(picked, project_out, preferred_element_type=jnp.float32),
        "tensor",
        scatter_dimension=0,
        tiled=True,
    )
    middle = hidden_in + attn_branch
    second_affine, second_pull = jax.vjp(affine_norm, middle, second_gain, second_shift)
    second_norm = second_affine.astype(jnp.bfloat16)
    second_full = lax.all_gather(second_norm, "tensor", axis=0, tiled=True)
    pre_act = jnp.dot(second_full, expand_weight, preferred_element_type=jnp.float32)
    activated_f32, gelu_pull = jax.vjp(tanh_gelu, pre_act)
    activated = activated_f32.astype(jnp.bfloat16)
    picked = activated
    mlp_branch = lax.psum_scatter(
        jnp.dot(picked, reduce_weight, preferred_element_type=jnp.float32).astype(jnp.bfloat16),
        "tensor",
        scatter_dimension=0,
        tiled=True,
    ).astype(jnp.float32)
    layer_out = middle + mlp_branch
    deviation = layer_out - teacher.astype(jnp.float32)
    squares_part = jnp.sum(row_valid[:, None] * deviation * deviation)
    layer_output = layer_out.astype(jnp.bfloat16)
    out_adj = out_cotangent.astype(jnp.float32) + 2.0 / divisor * (row_valid[:, None] * deviation)
    branch_adj = out_adj.astype(jnp.bfloat16)
    branch_full = lax.all_gather(branch_adj, "tensor", axis=0, tiled=True)
    reduce_grad = jnp.einsum(
        "bf,bd->fd", activated, branch_full, preferred_element_type=jnp.float32
    )
    act_adj = jnp.einsum(
        "bd,fd->bf", branch_full, reduce_weight, preferred_element_type=jnp.float32
    )
    pre_adj = gelu_pull(act_adj)[0].astype(jnp.bfloat16)
    expand_grad = jnp.einsum("bd,bf->df", second_full, pre_adj, preferred_element_type=jnp.float32)
    picked = pre_adj
    second_adj = lax.psum_scatter(
        jnp.einsum("bf,df->bd", picked, expand_weight, preferred_element_type=jnp.float32).astype(
            jnp.bfloat16
        ),
        "tensor",
        scatter_dimension=0,
        tiled=True,
    ).astype(jnp.float32)
    middle_part, second_gain_part, second_shift_part = second_pull(second_adj)
    middle_adj = out_adj + middle_part
    attn_adj = middle_adj.astype(jnp.bfloat16)
    attn_full = lax.all_gather(attn_adj, "tensor", axis=0, tiled=True)
    out_proj_grad = jnp.einsum("bc,bd->cd", attended, attn_full, preferred_element_type=jnp.float32)
    attended_adj = jnp.einsum(
        "bd,cd->bc", attn_full, project_out, preferred_element_type=jnp.float32
    ).astype(jnp.bfloat16)
    attended_adj = attended_adj.reshape(all_rows, local_heads, head_dim)
    group_pos = 0
    query_adj, key_adj, value_adj = group_backward(
        queries,
        key_rows,
        value_rows,
        prompt_docs[group_pos],
        valid_mask[group_pos],
        attended_adj,
        saved_logsums[group_pos],
        score_scale,
    )
    projected_adj = jnp.concatenate(
        [
            query_adj.reshape(all_rows, local_width),
            key_adj.reshape(all_rows, local_width),
            value_adj.reshape(all_rows, local_width),
        ],
        1,
    ).astype(jnp.bfloat16)
    in_proj_grad = jnp.einsum(
        "bd,bc->dc", first_full, projected_adj, preferred_element_type=jnp.float32
    ).reshape(D, 3, local_width)
    picked = projected_adj
    first_adj = lax.psum_scatter(
        jnp.einsum("bc,dc->bd", picked, in_matrix, preferred_element_type=jnp.float32).astype(
            jnp.bfloat16
        ),
        "tensor",
        scatter_dimension=0,
        tiled=True,
    ).astype(jnp.float32)
    hidden_part, first_gain_part, first_shift_part = first_pull(first_adj)
    input_adj = middle_adj + hidden_part
    input_gradient = input_adj.astype(jnp.bfloat16)
    embed_part = jnp.sum(input_adj, axis=0)
    embed_sum, first_gain_sum, first_shift_sum, second_gain_sum, second_shift_sum, squares_total = (
        lax.psum(
            (
                embed_part,
                first_gain_part,
                first_shift_part,
                second_gain_part,
                second_shift_part,
                squares_part,
            ),
            ("dp", "tensor"),
        )
    )
    loss = squares_total / divisor
    in_proj_grad, out_proj_grad, expand_grad, reduce_grad = lax.psum(
        (in_proj_grad, out_proj_grad, expand_grad, reduce_grad), "dp"
    )
    return (
        layer_output,
        loss,
        input_gradient,
        embed_sum,
        first_gain_sum,
        first_shift_sum,
        in_proj_grad,
        out_proj_grad,
        second_gain_sum,
        second_shift_sum,
        expand_grad,
        reduce_grad,
    )


def solution(mesh):
    return jax.shard_map(
        shards,
        mesh=mesh,
        in_specs=(
            P(("dp", "tensor"), None),
            P(("dp", "tensor"), None),
            P(("dp", "tensor"), None),
            P("dp", None),
            P("dp", None),
            P(),
            P(),
            P(),
            P(None, None, "tensor"),
            P("tensor", None),
            P(),
            P(),
            P(None, "tensor"),
            P("tensor", None),
        ),
        out_specs=(
            P(("dp", "tensor"), None),
            P(),
            P(("dp", "tensor"), None),
            P(),
            P(),
            P(),
            P(None, None, "tensor"),
            P("tensor", None),
            P(),
            P(),
            P(None, "tensor"),
            P("tensor", None),
        ),
        check_vma=False,
    )
```

profile of v0, /device:TPU:0, one launch (start us, length us, event | category | flops | bytes accessed | tf_op | source)
XLA Modules:
  0.0 1218.3 jit_solution(17424043391192552379)
XLA Ops:
  27.8 35.8 %all-gather.5.cloned.1.call-done = bf16[4096,768]{1,0:T(8,128)(2,1)} async-done(((bf16[1024,768]{1,0:T(8,128)(2,1)}), bf16[4096,768]{1,0:T(8,128)(2,1)}) %all-gather.5.cloned.1.call-update) | async-done | bytes 6291472 | tf_op jit(solution)/shard_map/all_gather | solution.py:171
  63.7 7.3 convolution_convert_fusion.3
  93.8 7.2 fusion.253
  101.0 8.4 fusion.1
  109.4 7.2 fusion.254
  116.6 8.4 fusion.2
  125.0 7.4 fusion.255
  132.5 8.4 fusion.3
  140.9 10.9 fusion.252
  151.8 8.3 fusion
  163.5 6.4 fusion.183
  169.9 7.8 fusion.161
  177.8 4.4 fusion.153
  182.3 7.8 fusion.155
  190.2 4.0 fusion.157
  194.2 7.7 fusion.159
  202.0 7.9 fusion.256
  209.9 99.7 %reduce-scatter.5.cloned.1.call-done = f32[1024,768]{1,0:T(8,128)} async-done(((f32[4096,768]{1,0:T(8,128)}), f32[1024,768]{1,0:T(8,128)}) %reduce-scatter.5.cloned.1.call-update) | async-done | bytes 3145744 | tf_op jit(solution)/shard_map/reduce_scatter | solution.py:187
  315.4 46.5 %all-gather.7.cloned.1.call-done = bf16[4096,768]{1,0:T(8,128)(2,1)} async-done(((bf16[1024,768]{1,0:T(8,128)(2,1)}), bf16[4096,768]{1,0:T(8,128)(2,1)}) %all-gather.7.cloned.1.call-update) | async-done | bytes 6291472 | tf_op jit(solution)/shard_map/all_gather | solution.py:196
  361.9 7.3 fusion.257
  369.2 4.5 copy-done.152
  373.7 9.5 convolution_convert_fusion.2
  385.1 21.9 %psum.78 = f32[]{:T(128)} all-reduce(f32[]{:T(128)S(6)} %convert_element_type.163), channel_id=1, replica_groups=mesh['dp'=8,'tensor'=4] {'dp'}, use_global_device_ids=true, to_apply=%region_25.26 | all-reduce | flops 1 | bytes 8 | tf_op jit(solution)/shard_map/psum | solution.py:160
  407.8 6.2 gather_fusion
  413.9 28.2 %reduce-scatter.7.cloned.1.call-done = bf16[1024,768]{1,0:T(8,128)(2,1)} async-done(((bf16[4096,768]{1,0:T(8,128)(2,1)}), bf16[1024,768]{1,0:T(8,128)(2,1)}) %reduce-scatter.7.cloned.1.call-update) | async-done | bytes 1572880 | tf_op jit(solution)/shard_map/reduce_scatter | solution.py:201
  442.2 5.3 fusion.107
  447.5 46.5 %all-gather.9.cloned.1.call-done = bf16[4096,768]{1,0:T(8,128)(2,1)} async-done(((bf16[1024,768]{1,0:T(8,128)(2,1)}), bf16[4096,768]{1,0:T(8,128)(2,1)}) %all-gather.9.cloned.1.call-update) | async-done | bytes 6291472 | tf_op jit(solution)/shard_map/all_gather | solution.py:213
  494.0 15.5 %fusion.10 = bf16[4096,768]{1,0:T(8,128)(2,1)S(1)} fusion(f32[4096,768]{1,0:T(8,128)} %copy-done.152, bf16[4096,768]{1,0:T(8,128)(2,1)} %all-gather.9.cloned.1.call-done, bf16[768,768]{1,0:T(8,128)(2,1)S(1)} %copy-done), kind=kOutput, calls=%fused_computation.37 | convolution fusion | flops 4894752768 | bytes 26345472 | tf_op jit(solution)/shard_map/bd,fd->bf/dot_general | solution.py:217
  512.1 7.1 convolution_convert_fusion.1
  519.3 58.9 %reduce-scatter.9.cloned.1.call-done = bf16[1024,768]{1,0:T(8,128)(2,1)} async-done(((bf16[4096,768]{1,0:T(8,128)(2,1)}), bf16[1024,768]{1,0:T(8,128)(2,1)}) %reduce-scatter.9.cloned.1.call-update) | async-done | bytes 1572880 | tf_op jit(solution)/shard_map/reduce_scatter | solution.py:223
  578.2 4.1 convert_reduce_fusion.1
  582.4 5.2 fusion.70
  592.1 45.9 %all-gather.11.cloned.1.call-done = bf16[4096,768]{1,0:T(8,128)(2,1)} async-done(((bf16[1024,768]{1,0:T(8,128)(2,1)}), bf16[4096,768]{1,0:T(8,128)(2,1)}) %all-gather.11.cloned.1.call-update) | async-done | bytes 6291472 | tf_op jit(solution)/shard_map/all_gather | solution.py:234
  638.0 5.0 convolution_convert_fusion.4
  649.1 9.5 fusion.50
  658.6 11.8 multiply_reduce_fusion.3
  674.3 7.4 multiply_reduce_fusion.2
  681.7 9.5 fusion.59
  691.2 11.9 multiply_reduce_fusion
  703.2 3.9 fusion.56
  707.1 7.8 multiply_reduce_fusion.1
  717.3 6.1 multiply_reduce_fusion.6
  723.4 5.3 fusion.126
  728.8 4.8 multiply_reduce_fusion.5
  733.6 4.0 fusion.96
  737.6 8.8 multiply_reduce_fusion.4
  746.4 7.1 fusion.99
  776.4 5.0 multiply_convert_fusion.7
  786.7 5.3 multiply_convert_fusion.6
  795.3 9.5 multiply_convert_fusion.4
  810.0 11.2 multiply_convert_fusion.3
  825.8 6.5 fusion.173
  832.6 11.7 multiply_convert_fusion.2
  848.9 6.4 fusion.171
  855.8 11.2 multiply_convert_fusion
  870.8 7.5 multiply_convert_fusion.1
  882.8 6.6 fusion.169
  896.7 9.8 convolution_convert_fusion
  906.6 10.4 fusion.259
  917.0 12.1 fusion.237
  931.3 6.5 fusion.105
  937.9 27.7 %reduce-scatter.11.cloned.1.call-done = bf16[1024,768]{1,0:T(8,128)(2,1)} async-done(((bf16[4096,768]{1,0:T(8,128)(2,1)}), bf16[1024,768]{1,0:T(8,128)(2,1)}) %reduce-scatter.11.cloned.1.call-update) | async-done | bytes 1572880 | tf_op jit(solution)/shard_map/reduce_scatter | solution.py:263
  975.6 44.5 %all-reduce.6 = (f32[]{:T(128)}, f32[768]{0:T(1024)}, f32[768]{0:T(1024)}, f32[768]{0:T(1024)}, f32[768]{0:T(1024)}, /*index=5*/f32[768]{0:T(1024)}) all-reduce(f32[]{:T(128)} %get-tuple-element.304, f32[768]{0:T(1024)S(1)} %reduce_sum.337, f32[768]{0:T(1024)S(1)} %get-tuple-element.302, ...), channel_id=1, replica_groups=mesh['dp'=8,'tensor'=4] {'dp','tensor'}, use_global_device_ids=true, to_apply=%region_23.24 | all-reduce | flops 3841 | bytes 30728 | tf_op jit(solution)/shard_map/psum | solution.py:276
  1020.9 183.0 %all-reduce.10.cloned.1.call-done = (f32[768,3,192]{0,2,1:T(8,128)}, f32[192,768]{1,0:T(8,128)}, f32[768,768]{1,0:T(8,128)}, f32[768,768]{1,0:T(8,128)}) async-done(((f32[768,3,192]{0,2,1:T(8,128)}, f32[192,768]{1,0:T(8,128)}, f32[768,768]{1,0:T(8,128)}, f32[768,768]{1,0:T(8,128)}), (f32[768,3,192]{0,2,1:T(8,128)}, f32[192,768]{1,0:T(8,128)}, f32[768,768]{1,0:T(8,128)}, ...) | async-done | bytes 7077904 | tf_op jit(solution)/shard_map/psum | solution.py:289
  (505 shorter events, 154.0 us)
Async XLA Ops:
  7.2 366.5 %copy-start = (bf16[768,768]{1,0:T(8,128)(2,1)S(1)}, bf16[768,768]{1,0:T(8,128)(2,1)}, u32[]{:S(2)}) copy-start(bf16[768,768]{1,0:T(8,128)(2,1)} %param.75) | copy-start | bytes 3538948
  7.2 56.4 %all-gather.5.cloned.1.call-start = ((), (), s32[]{:S(2)}) async-start(), calls=%async_computation.4 | async-start | bytes 7864320 | tf_op jit(solution)/shard_map/all_gather | solution.py:171
  14.4 295.2 %reduce-scatter.5.cloned.1.call-start = ((), (), s32[]{:S(2)}) async-start(), calls=%async_computation.5 | async-start | bytes 15728640 | tf_op jit(solution)/shard_map/reduce_scatter | solution.py:187
  19.7 44.0 %copy-start.149 = (bf16[768,3,192]{0,2,1:T(8,128)(2,1)S(1)}, bf16[768,3,192]{0,2,1:T(8,128)(2,1)}, u32[]{:S(2)}) copy-start(bf16[768,3,192]{0,2,1:T(8,128)(2,1)} %param.70) | copy-start | bytes 2654212
  72.9 52.1 %copy-start.21 = (bf16[2048,192]{0,1:T(8,128)(2,1)}, bf16[2048,192]{0,1:T(8,128)(2,1)S(1)}, u32[]{:S(2)}) copy-start(bf16[2048,192]{0,1:T(8,128)(2,1)S(1)} %get-tuple-element.348) | copy-start | bytes 2359300
  74.2 19.6 %copy-start.43 = (bf16[512,192]{0,1:T(8,128)(2,1)}, bf16[512,192]{0,1:T(8,128)(2,1)S(1)}, u32[]{:S(2)}) copy-start(bf16[512,192]{0,1:T(8,128)(2,1)S(1)} %get-tuple-element.337) | copy-start | bytes 589828
  74.2 35.2 %copy-start.39 = (bf16[512,192]{0,1:T(8,128)(2,1)}, bf16[512,192]{0,1:T(8,128)(2,1)S(1)}, u32[]{:S(2)}) copy-start(bf16[512,192]{0,1:T(8,128)(2,1)S(1)} %get-tuple-element.334) | copy-start | bytes 589828
  74.2 50.8 %copy-start.41 = (bf16[512,192]{0,1:T(8,128)(2,1)}, bf16[512,192]{0,1:T(8,128)(2,1)S(1)}, u32[]{:S(2)}) copy-start(bf16[512,192]{0,1:T(8,128)(2,1)S(1)} %get-tuple-element.332) | copy-start | bytes 589828
  78.3 81.8 %copy-start.105 = (f32[3,512]{1,0:T(4,128)}, f32[3,512]{1,0:T(4,128)S(1)}, u32[]{:S(2)}) copy-start(f32[3,512]{1,0:T(4,128)S(1)} %get-tuple-element.372) | copy-start | bytes 18436
  81.0 79.1 %copy-start.118 = (f32[3,512]{1,0:T(4,128)}, f32[3,512]{1,0:T(4,128)S(1)}, u32[]{:S(2)}) copy-start(f32[3,512]{1,0:T(4,128)S(1)} %fusion.39) | copy-start | bytes 18436
  82.9 80.5 %copy-start.103 = (f32[3,512]{1,0:T(4,128)}, f32[3,512]{1,0:T(4,128)S(1)}, u32[]{:S(2)}) copy-start(f32[3,512]{1,0:T(4,128)S(1)} %get-tuple-element.374) | copy-start | bytes 18436
  86.5 77.0 %copy-start.120 = (f32[3,512]{1,0:T(4,128)}, f32[3,512]{1,0:T(4,128)S(1)}, u32[]{:S(2)}) copy-start(f32[3,512]{1,0:T(4,128)S(1)} %fusion.17) | copy-start | bytes 18436
  89.1 80.8 %copy-start.122 = (f32[3,512]{1,0:T(4,128)}, f32[3,512]{1,0:T(4,128)S(1)}, u32[]{:S(2)}) copy-start(f32[3,512]{1,0:T(4,128)S(1)} %get-tuple-element.376) | copy-start | bytes 18436
  93.8 76.1 %copy-start.124 = (f32[3,512]{1,0:T(4,128)}, f32[3,512]{1,0:T(4,128)S(1)}, u32[]{:S(2)}) copy-start(f32[3,512]{1,0:T(4,128)S(1)} %fusion.15) | copy-start | bytes 18436
  101.0 81.2 %copy-start.126 = (f32[3,512]{1,0:T(4,128)}, f32[3,512]{1,0:T(4,128)S(1)}, u32[]{:S(2)}) copy-start(f32[3,512]{1,0:T(4,128)S(1)} %get-tuple-element.380) | copy-start | bytes 18436
  132.5 27.6 %slice-start.22 = ((s8[6291456]{0:T(1024)(128)(4,1)}), s8[4194304]{0:T(1024)(128)(4,1)S(1)}, s32[]{:S(2)}) async-start(s8[6291456]{0:T(1024)(128)(4,1)} %bitcast.259), calls=%async_computation.35 | async-start | bytes 8388608
  140.9 19.2 %slice-start.23 = ((s8[6291456]{0:T(1024)(128)(4,1)}), s8[2097152]{0:T(1024)(128)(4,1)S(1)}, s32[]{:S(2)}) async-start(s8[6291456]{0:T(1024)(128)(4,1)} %bitcast.259), calls=%async_computation.36 | async-start | bytes 4194304
  163.5 14.2 %slice-start.12 = ((s8[15728640]{0:T(1024)(128)(4,1)}), s8[4194304]{0:T(1024)(128)(4,1)S(1)}, s32[]{:S(2)}) async-start(s8[15728640]{0:T(1024)(128)(4,1)} %bitcast.253), calls=%async_computation.25 | async-start | bytes 8388608
  163.5 14.2 %slice-start.13 = ((s8[15728640]{0:T(1024)(128)(4,1)}), s8[4194304]{0:T(1024)(128)(4,1)S(1)}, s32[]{:S(2)}) async-start(s8[15728640]{0:T(1024)(128)(4,1)} %bitcast.253), calls=%async_computation.26 | async-start | bytes 8388608
  177.8 12.3 %slice-start = ((s8[15728640]{0:T(1024)(128)(4,1)}), s8[4194304]{0:T(1024)(128)(4,1)S(1)}, s32[]{:S(2)}) async-start(s8[15728640]{0:T(1024)(128)(4,1)} %bitcast.247), calls=%async_computation.13 | async-start | bytes 8388608
  177.8 12.3 %slice-start.1 = ((s8[15728640]{0:T(1024)(128)(4,1)}), s8[4194304]{0:T(1024)(128)(4,1)S(1)}, s32[]{:S(2)}) async-start(s8[15728640]{0:T(1024)(128)(4,1)} %bitcast.247), calls=%async_computation.14 | async-start | bytes 8388608
  209.8 99.8 %copy-start.12 = (bf16[1024,768]{1,0:T(8,128)(2,1)S(1)}, bf16[1024,768]{1,0:T(8,128)(2,1)}, u32[]{:S(2)}) copy-start(bf16[1024,768]{1,0:T(8,128)(2,1)} %param.62) | copy-start | bytes 4718596
  209.8 99.8 %copy-start.96 = (f32[768]{0:T(1024)S(1)}, f32[768]{0:T(1024)}, u32[]{:S(2)}) copy-start(f32[768]{0:T(1024)} %param.67) | copy-start | bytes 9220
  209.9 152.0 %all-gather.7.cloned.1.call-start = ((), (), s32[]{:S(2)}) async-start(), calls=%async_computation.6 | async-start | bytes 7864320 | tf_op jit(solution)/shard_map/all_gather | solution.py:196
  313.6 48.2 %copy-start.148 = (bf16[768,768]{1,0:T(8,128)(2,1)S(1)}, bf16[768,768]{1,0:T(8,128)(2,1)}, u32[]{:S(2)}) copy-start(bf16[768,768]{1,0:T(8,128)(2,1)} %param.74) | copy-start | bytes 3538948
  315.3 126.8 %reduce-scatter.7.cloned.1.call-start = ((), (), s32[]{:S(2)}) async-start(), calls=%async_computation.7 | async-start | bytes 7864320 | tf_op jit(solution)/shard_map/reduce_scatter | solution.py:201
  383.2 110.8 %all-gather.9.cloned.1.call-start = ((), (), s32[]{:S(2)}) async-start(), calls=%async_computation.8 | async-start | bytes 7864320 | tf_op jit(solution)/shard_map/all_gather | solution.py:213
  447.5 130.7 %reduce-scatter.9.cloned.1.call-start = ((), (), s32[]{:S(2)}) async-start(), calls=%async_computation.9 | async-start | bytes 7864320 | tf_op jit(solution)/shard_map/reduce_scatter | solution.py:223
  519.2 63.1 %copy-start.115 = (f32[1024]{0:T(1024)S(1)}, f32[1024]{0:T(1024)}, u32[]{:S(2)}) copy-start(f32[1024]{0:T(1024)} %copy-done.114) | copy-start | bytes 12292
  519.2 63.1 %copy-start.27 = (bf16[1024,768]{1,0:T(8,128)(2,1)S(1)}, bf16[1024,768]{1,0:T(8,128)(2,1)}, u32[]{:S(2)}) copy-start(bf16[1024,768]{1,0:T(8,128)(2,1)} %param.64) | copy-start | bytes 4718596
  519.2 118.8 %all-gather.11.cloned.1.call-start = ((), (), s32[]{:S(2)}) async-start(), calls=%async_computation.10 | async-start | bytes 7864320 | tf_op jit(solution)/shard_map/all_gather | solution.py:234
  587.7 50.3 %copy-start.94 = (bf16[192,768]{1,0:T(8,128)(2,1)S(1)}, bf16[192,768]{1,0:T(8,128)(2,1)}, u32[]{:S(2)}) copy-start(bf16[192,768]{1,0:T(8,128)(2,1)} %param.71) | copy-start | bytes 884740
  591.5 374.0 %reduce-scatter.11.cloned.1.call-start = ((), (), s32[]{:S(2)}) async-start(), calls=%async_computation.11 | async-start | bytes 7864320 | tf_op jit(solution)/shard_map/reduce_scatter | solution.py:263
  649.1 21.3 %slice-start.8 = ((s8[15728640]{0:T(1024)(128)(4,1)}), s8[4194304]{0:T(1024)(128)(4,1)S(1)}, s32[]{:S(2)}) async-start(s8[15728640]{0:T(1024)(128)(4,1)} %bitcast.251), calls=%async_computation.21 | async-start | bytes 8388608
  649.1 21.3 %slice-start.9 = ((s8[15728640]{0:T(1024)(128)(4,1)}), s8[4194304]{0:T(1024)(128)(4,1)S(1)}, s32[]{:S(2)}) async-start(s8[15728640]{0:T(1024)(128)(4,1)} %bitcast.251), calls=%async_computation.22 | async-start | bytes 8388608
  658.6 11.8 slice-start.10
  658.6 11.8 slice-start.11
  681.7 9.5 copy-start.76
  681.7 21.4 %slice-start.4 = ((s8[15728640]{0:T(1024)(128)(4,1)}), s8[4194304]{0:T(1024)(128)(4,1)S(1)}, s32[]{:S(2)}) async-start(s8[15728640]{0:T(1024)(128)(4,1)} %bitcast.249), calls=%async_computation.17 | async-start | bytes 8388608
  681.7 21.5 %slice-start.5 = ((s8[15728640]{0:T(1024)(128)(4,1)}), s8[4194304]{0:T(1024)(128)(4,1)S(1)}, s32[]{:S(2)}) async-start(s8[15728640]{0:T(1024)(128)(4,1)} %bitcast.249), calls=%async_computation.18 | async-start | bytes 8388608
  691.2 11.9 slice-start.6
  691.2 11.9 slice-start.7
  717.3 11.4 slice-start.16
  717.3 11.4 slice-start.17
  758.8 9.5 copy-start.30
  763.6 12.8 %slice-start.24 = ((s8[6291456]{0:T(1024)(128)(4,1)}), s8[4194304]{0:T(1024)(128)(4,1)S(1)}, s32[]{:S(2)}) async-start(s8[6291456]{0:T(1024)(128)(4,1)} %bitcast.261), calls=%async_computation.37 | async-start | bytes 8388608
  776.4 10.3 slice-start.19
  776.4 10.3 slice-start.20
  810.0 14.3 %copy-start.45 = (bf16[512,192]{0,1:T(8,128)(2,1)S(1)}, bf16[512,192]{0,1:T(8,128)(2,1)}, u32[]{:S(2)}) copy-start(bf16[512,192]{0,1:T(8,128)(2,1)} %get-tuple-element.340) | copy-start | bytes 589828
  832.6 14.8 %copy-start.44 = (bf16[512,192]{0,1:T(8,128)(2,1)S(1)}, bf16[512,192]{0,1:T(8,128)(2,1)}, u32[]{:S(2)}) copy-start(bf16[512,192]{0,1:T(8,128)(2,1)} %copy-done.43) | copy-start | bytes 589828
  855.8 11.2 copy-start.42
  870.8 10.5 copy-start.40
  906.5 297.3 %all-reduce.10.cloned.1.call-start = ((), (), s32[]{:S(2)}) async-start(), calls=%async_computation.12 | async-start | bytes 14155776 | tf_op jit(solution)/shard_map/psum | solution.py:289
  906.6 22.5 %slice-start.29 = ((s8[6291456]{0:T(1024)(128)(4,1)}), s8[4194304]{0:T(1024)(128)(4,1)S(1)}, s32[]{:S(2)}) async-start(s8[6291456]{0:T(1024)(128)(4,1)} %bitcast.359), calls=%async_computation.42 | async-start | bytes 8388608
  906.6 24.7 %slice-start.27 = ((s8[6291456]{0:T(1024)(128)(4,1)}), s8[4194304]{0:T(1024)(128)(4,1)S(1)}, s32[]{:S(2)}) async-start(s8[6291456]{0:T(1024)(128)(4,1)} %bitcast.357), calls=%async_computation.40 | async-start | bytes 8388608
  917.0 12.1 copy-start.50
  917.0 12.1 slice-start.30
  917.0 14.4 %slice-start.28 = ((s8[6291456]{0:T(1024)(128)(4,1)}), s8[2097152]{0:T(1024)(128)(4,1)S(1)}, s32[]{:S(2)}) async-start(s8[6291456]{0:T(1024)(128)(4,1)} %bitcast.357), calls=%async_computation.41 | async-start | bytes 4194304
  937.8 27.7 %copy-start.13 = (bf16[1024,768]{1,0:T(8,128)(2,1)S(1)}, bf16[1024,768]{1,0:T(8,128)(2,1)}, u32[]{:S(2)}) copy-start(bf16[1024,768]{1,0:T(8,128)(2,1)} %param.62) | copy-start | bytes 4718596
  937.8 27.7 %copy-start.97 = (f32[768]{0:T(1024)S(1)}, f32[768]{0:T(1024)}, u32[]{:S(2)}) copy-start(f32[768]{0:T(1024)} %param.67) | copy-start | bytes 9220
  937.8 27.7 %copy-start.99 = (f32[1024]{0:T(1024)S(1)}, f32[1024]{0:T(1024)}, u32[]{:S(2)}) copy-start(f32[1024]{0:T(1024)} %copy-done.98) | copy-start | bytes 12292
  937.8 27.7 %copy-start.109 = (f32[768]{0:T(1024)S(1)}, f32[768]{0:T(1024)}, u32[]{:S(2)}) copy-start(f32[768]{0:T(1024)} %param.68) | copy-start | bytes 9220
  937.8 30.4 %copy-start.113 = (f32[1024]{0:T(1024)S(1)}, f32[1024]{0:T(1024)}, u32[]{:S(2)}) copy-start(f32[1024]{0:T(1024)} %copy-done.112) | copy-start | bytes 12292
  937.8 30.4 %copy-start.111 = (f32[1024]{0:T(1024)S(1)}, f32[1024]{0:T(1024)}, u32[]{:S(2)}) copy-start(f32[1024]{0:T(1024)} %copy-done.110) | copy-start | bytes 12292
  (129 other events, 544.3 us)
Sparse Core Ops, SparseCore 0:
  14.5 49.0 all-gather.4
  210.0 99.5 reduce-scatter.4
  315.5 46.3 all-gather.6
  383.3 58.8 reduce-scatter.6
  447.6 46.3 all-gather.8
  519.3 58.8 reduce-scatter.8
  591.6 46.3 all-gather.10
  906.6 58.8 reduce-scatter.10
  971.1 232.6 all-reduce.9
where the time goes:
time: 1230 us; the launch traced here: 1220 us
  waiting for transfers between devices  572 us (47%)
  matrix products  330 us (27%)
  other arithmetic  170 us (14%)
  blocking collectives  66.4 us (5%)
  local copies, waits for them, and re-layouts  59.8 us (5%)
  between operations  19.2 us (2%)
    psum x1, waiting for transfers between devices, shards(): lax.psum((in_proj_grad, out_proj_grad, expand_grad, reduce_grad), 'dp')  183 us
    reduce_scatter x1, waiting for transfers between devices, shards(): lax.psum_scatter(jnp.dot(picked, project_out, preferred_element_type=jnp....  99.7 us
    convert_element_type x8, other arithmetic, group_backward(): score_adj = (attn_probs * (prob_adj - inner)).astype(jnp.bfloat16)  62.2 us
    dot_general x8, matrix products, group_backward(): jnp.einsum('qhd,khd->hqk', block_adj, block_values, preferred_element_typ...  59.4 us
    reduce_scatter x1, waiting for transfers between devices, shards(): lax.psum_scatter(jnp.einsum('bf,df->bd', picked, expand_weight, preferred...  58.9 us
    all_gather x1, waiting for transfers between devices, shards(): second_full = lax.all_gather(second_norm, 'tensor', axis=0, tiled=True)  46.5 us
    all_gather x1, waiting for transfers between devices, shards(): branch_full = lax.all_gather(branch_adj, 'tensor', axis=0, tiled=True)  46.5 us
    all_gather x1, waiting for transfers between devices, shards(): attn_full = lax.all_gather(attn_adj, 'tensor', axis=0, tiled=True)  45.9 us
  transfers between devices with their start and end apart: 9, of which 9 were waited for; matrix products, arithmetic and copies ran while one was open for 5% of the time, Pallas kernels for 0%

commit v1 on v0

v1 whole, which is shorter than its diff:
```python
import functools

import jax
import jax.numpy as jnp
from jax import lax
from jax.experimental import pallas as pl
from jax.experimental.pallas import tpu as pltpu
from jax.sharding import PartitionSpec as P

D = 768
H = 12
HD = D // H
PROMPT = 2048
CONT = 256
CONTS = 8
GLEN = 4096
DOC_MAX = 1024
NEG = -1e30
SCALE = HD ** (-0.5)
norm_eps = 1e-05
bf16 = jnp.bfloat16
f32 = jnp.float32


def dot_f32(a, b):
    return jnp.dot(a, b, preferred_element_type=f32)


def fwd_kernel(q_ref, k_ref, v_ref, start_ref, bias_ref, o_ref, wide_ref, lse_ref, keys_ref):
    keys_ref[...] = k_ref[0].T

    def finish(off, top, total, acc):
        out = acc / total
        wide_ref[0, :, pl.ds(off, CONT)] = out
        o_ref[0, :, pl.ds(off, CONT)] = out.astype(bf16)
        lse_ref[0, :, pl.ds(off, CONT)] = top + jnp.log(total)

    causal = lax.broadcasted_iota(jnp.int32, (CONT, CONT), 0) <= lax.broadcasted_iota(
        jnp.int32, (CONT, CONT), 1
    )

    def continuation(c, carry):
        off = pl.multiple_of(PROMPT + c * CONT, CONT)
        queries = q_ref[0, :, pl.ds(off, CONT)]
        s1 = dot_f32(keys_ref[0:PROMPT, :], queries)
        s2 = dot_f32(keys_ref[pl.ds(off, CONT), :], queries)
        bias = bias_ref[pl.ds(pl.multiple_of(c * CONT, CONT), CONT), :]
        s2 = jnp.where(causal, s2 + jnp.concatenate([bias, bias], 1), NEG)
        top = jnp.maximum(jnp.max(s1, 0, keepdims=True), jnp.max(s2, 0, keepdims=True))
        p1 = jnp.exp(s1 - top)
        p2 = jnp.exp(s2 - top)
        total = jnp.sum(p1, 0, keepdims=True) + jnp.sum(p2, 0, keepdims=True)
        acc = dot_f32(v_ref[0, :, 0:PROMPT], p1.astype(bf16))
        acc = acc + dot_f32(v_ref[0, :, pl.ds(off, CONT)], p2.astype(bf16))
        finish(off, top, total, acc)
        return carry

    lax.fori_loop(0, CONTS, continuation, 0)
    for off in range(0, PROMPT, CONT):
        low = max(0, off - DOC_MAX)
        span = off + CONT - low
        s = dot_f32(keys_ref[low : off + CONT, :], q_ref[0, :, off : off + CONT])
        key_ids = low + lax.broadcasted_iota(jnp.int32, (span, CONT), 0)
        row_ids = off + lax.broadcasted_iota(jnp.int32, (span, CONT), 1)
        s = jnp.where((key_ids <= row_ids) & (key_ids >= start_ref[:, off : off + CONT]), s, NEG)
        top = jnp.max(s, 0, keepdims=True)
        p = jnp.exp(s - top)
        finish(off, top, jnp.sum(p, 0, keepdims=True), dot_f32(v_ref[0, :, low : off + CONT], p.astype(bf16)))


def head_spec(shift, heads):
    return pl.BlockSpec((1, HD, GLEN), lambda h: (h + shift * heads, 0, 0))


def attn_fwd(qkv, doc_start, key_bias):
    heads = qkv.shape[0] // 3
    return pl.pallas_call(
        fwd_kernel,
        grid=(heads,),
        in_specs=[
            head_spec(0, heads),
            head_spec(1, heads),
            head_spec(2, heads),
            pl.BlockSpec((1, PROMPT), lambda h: (0, 0)),
            pl.BlockSpec((GLEN - PROMPT, 128), lambda h: (0, 0)),
        ],
        out_specs=[
            head_spec(0, heads),
            head_spec(0, heads),
            pl.BlockSpec((1, 1, GLEN), lambda h: (h, 0, 0)),
        ],
        out_shape=[
            jax.ShapeDtypeStruct((heads, HD, GLEN), bf16),
            jax.ShapeDtypeStruct((heads, HD, GLEN), f32),
            jax.ShapeDtypeStruct((heads, 1, GLEN), f32),
        ],
        scratch_shapes=[pltpu.VMEM((GLEN, HD), bf16)],
        name="attn_fwd",
    )(qkv, qkv, qkv, doc_start, key_bias)


KEYS = 512
SPAN = 512


def bwd_kernel(
    q_ref, k_ref, v_ref, g_ref, wide_ref, lse_ref, start_ref, bias_ref,
    dq_ref, dk_ref, dv_ref, qn, kn, vn, gn, inner, dq,
):
    qn[...] = q_ref[0].T
    kn[...] = k_ref[0].T
    vn[...] = v_ref[0].T
    gn[...] = g_ref[0].T
    inner[...] = jnp.sum(g_ref[0].astype(f32) * wide_ref[0], 0, keepdims=True)
    dq[...] = jnp.zeros_like(dq)

    def block(key_off, key_span, off, span, mask):
        rows = pl.ds(off, span)
        keys = pl.ds(key_off, key_span)
        s = dot_f32(kn[keys, :], q_ref[0, :, rows])
        if mask is not None:
            s = mask(s)
        p = jnp.exp(s - lse_ref[0, :, rows])
        dp = dot_f32(vn[keys, :], g_ref[0, :, rows])
        ds = (p * (dp - inner[:, rows])).astype(bf16)
        dv = dot_f32(p.astype(bf16), gn[rows, :])
        dk = dot_f32(ds, qn[rows, :])
        dq[:, rows] += dot_f32(k_ref[0, :, keys], ds)
        return dk, dv

    def emit(key_off, key_span, dk, dv):
        dk_ref[0, :, pl.ds(key_off, key_span)] = dk.T.astype(bf16)
        dv_ref[0, :, pl.ds(key_off, key_span)] = dv.T.astype(bf16)

    def key_block(b, carry):
        key_off = pl.multiple_of(b * KEYS, KEYS)

        def continuation(c, acc):
            off = pl.multiple_of(PROMPT + c * SPAN, SPAN)
            dk, dv = block(key_off, KEYS, off, SPAN, None)
            return acc[0] + dk, acc[1] + dv

        zero = jnp.zeros((KEYS, HD), f32)
        acc = lax.fori_loop(0, (GLEN - PROMPT) // SPAN, continuation, (zero, zero))

        def prompt(i, acc):
            off = pl.multiple_of(i * CONT, CONT)

            def mask(s):
                key_ids = key_off + lax.broadcasted_iota(jnp.int32, s.shape, 0)
                row_ids = off + lax.broadcasted_iota(jnp.int32, s.shape, 1)
                keep = (key_ids <= row_ids) & (key_ids >= start_ref[:, pl.ds(off, CONT)])
                return jnp.where(keep, s, NEG)

            dk, dv = block(key_off, KEYS, off, CONT, mask)
            return acc[0] + dk, acc[1] + dv

        last = jnp.minimum((key_off + KEYS + DOC_MAX - 2) // CONT + 1, PROMPT // CONT)
        acc = lax.fori_loop(key_off // CONT, last, prompt, acc)
        emit(key_off, KEYS, *acc)
        return carry

    lax.fori_loop(0, PROMPT // KEYS, key_block, 0)
    causal = lax.broadcasted_iota(jnp.int32, (CONT, CONT), 0) <= lax.broadcasted_iota(
        jnp.int32, (CONT, CONT), 1
    )

    def own(c, carry):
        off = pl.multiple_of(PROMPT + c * CONT, CONT)
        bias = bias_ref[pl.ds(pl.multiple_of(c * CONT, CONT), CONT), :]

        def mask(s):
            return jnp.where(causal, s + jnp.concatenate([bias, bias], 1), NEG)

        emit(off, CONT, *block(off, CONT, off, CONT, mask))
        return carry

    lax.fori_loop(0, CONTS, own, 0)
    dq_ref[0] = (dq[...] * SCALE).astype(bf16)


def attn_bwd(qkv, adj, wide, lse, doc_start, key_bias):
    heads = qkv.shape[0] // 3
    shape = jax.ShapeDtypeStruct((heads, HD, GLEN), bf16)
    return pl.pallas_call(
        bwd_kernel,
        grid=(heads,),
        in_specs=[
            head_spec(0, heads),
            head_spec(1, heads),
            head_spec(2, heads),
            head_spec(0, heads),
            head_spec(0, heads),
            pl.BlockSpec((1, 1, GLEN), lambda h: (h, 0, 0)),
            pl.BlockSpec((1, PROMPT), lambda h: (0, 0)),
            pl.BlockSpec((GLEN - PROMPT, 128), lambda h: (0, 0)),
        ],
        out_specs=[head_spec(0, heads)] * 3,
        out_shape=[shape] * 3,
        scratch_shapes=[pltpu.VMEM((GLEN, HD), bf16)] * 4
        + [pltpu.VMEM((1, GLEN), f32), pltpu.VMEM((HD, GLEN), f32)],
        name="attn_bwd",
    )(qkv, qkv, qkv, adj, wide, lse, doc_start, key_bias)


def normalize(values):
    centred = values - jnp.mean(values, axis=-1, keepdims=True)
    spread = jnp.mean(centred * centred, axis=-1, keepdims=True)
    return centred * lax.rsqrt(spread + norm_eps)


def affine_norm(values, norm_gain, norm_shift):
    return normalize(values) * norm_gain + norm_shift


def tanh_gelu(values):
    return jax.nn.gelu(values, approximate=True)


def dot(a, b, ca, cb):
    return lax.dot_general(a, b, (((ca,), (cb,)), ((), ())), preferred_element_type=f32)


def swap(x, bit, axis="tensor"):
    size = lax.axis_size(axis)
    return lax.ppermute(x, axis, [(i, i ^ bit) for i in range(size)])


def butterfly(x, axis):
    bit = 1
    while bit < lax.axis_size(axis):
        x = x + swap(x, bit, axis)
        bit *= 2
    return x


def gather4(x):
    far = swap(x, 2)
    near = swap(x, 1)
    return [x, near, far, swap(far, 1)]


def scatter4(parts):
    near1 = swap(parts[1], 1)
    near3 = swap(parts[3], 1)
    across = (parts[2].astype(f32) + near3.astype(f32)).astype(bf16)
    mine = parts[0].astype(f32) + near1.astype(f32)
    return mine + swap(across, 2).astype(f32)


def shards(
    layer_input,
    out_cotangent,
    teacher,
    valid_mask,
    prompt_docs,
    pass_embed,
    first_gain,
    first_shift,
    project_in,
    project_out,
    second_gain,
    second_shift,
    expand_weight,
    reduce_weight,
):
    rows = layer_input.shape[0]
    width = project_out.shape[0]
    heads = width // HD
    t = lax.axis_index("tensor")
    slots = [t ^ k for k in range(4)]
    valid = valid_mask[0]
    docs = prompt_docs[0]
    valid_total = butterfly(jnp.sum(valid).astype(f32).reshape(1, 1), "dp")[0, 0]
    divisor = valid_total * D
    doc_start = jnp.zeros_like(docs)
    for v in range(3):
        doc_start = doc_start + jnp.where(docs > v, jnp.sum((docs == v).astype(jnp.int32)), 0)
    doc_start = doc_start[None, :]
    key_bias = jnp.broadcast_to(jnp.where(valid == 1, 0.0, NEG).astype(f32)[:, None], (GLEN - PROMPT, 128))
    row_valid = lax.dynamic_slice_in_dim(
        jnp.concatenate([jnp.zeros((PROMPT,), f32), valid.astype(f32)]), t * rows, rows
    )[:, None]

    hidden_in = layer_input.astype(f32) + pass_embed
    first_affine, first_pull = jax.vjp(affine_norm, hidden_in, first_gain, first_shift)
    first_blocks = gather4(first_affine.astype(bf16))
    in_matrix = project_in.reshape(D, 3 * width)

    expand_weight, reduce_weight, project_out, _ = lax.optimization_barrier(
        (expand_weight, reduce_weight, project_out, first_blocks[2])
    )
    out_blocks = gather4(project_out)
    expand_blocks = gather4(expand_weight)
    reduce_blocks = gather4(reduce_weight)
    out_full = jnp.concatenate(out_blocks, 0)

    qkv = jnp.zeros((3 * width, GLEN), bf16)
    for k in range(4):
        part = dot(in_matrix, first_blocks[k], 0, 1).astype(bf16)
        part = jnp.concatenate([part[:width] * SCALE, part[width:]], 0)
        qkv = lax.dynamic_update_slice(qkv, part, (0, slots[k] * rows))
    qkv = qkv.reshape(3 * heads, HD, GLEN)
    attended, attended_wide, logsum = attn_fwd(qkv, doc_start, key_bias)

    att = attended.reshape(width, GLEN)
    cuts = [lax.dynamic_slice(att, (0, slots[k] * rows), (width, rows)) for k in range(4)]
    att_own = jnp.concatenate([cuts[0]] + [swap(cuts[k], k) for k in (1, 2, 3)], 0)
    attn_branch = dot(att_own, out_full, 0, 0)
    middle = hidden_in + attn_branch
    second_affine, second_pull = jax.vjp(affine_norm, middle, second_gain, second_shift)
    second_norm = second_affine.astype(bf16)
    acts, pulls = [], []
    mlp_branch = 0.0
    for k in range(4):
        pre_act = dot(second_norm, expand_blocks[k], 1, 0)
        activated, pull = jax.vjp(tanh_gelu, pre_act)
        acts.append(activated.astype(bf16))
        pulls.append(pull)
        mlp_branch = mlp_branch + dot(acts[k], reduce_blocks[k], 1, 0)
    layer_out = middle + mlp_branch
    deviation = row_valid * (layer_out - teacher.astype(f32))
    squares_part = jnp.sum(deviation * deviation)
    out_adj = out_cotangent.astype(f32) + 2.0 / divisor * deviation
    branch_adj = out_adj.astype(bf16)
    second_adj = 0.0
    reduce_parts, expand_parts = [], []
    pre_adjs = []
    for k in range(4):
        act_adj = dot(branch_adj, reduce_blocks[k], 1, 1)
        pre_adjs.append(pulls[k](act_adj)[0].astype(bf16))
        second_adj = second_adj + dot(pre_adjs[k], expand_blocks[k], 1, 1)
    middle_part, second_gain_part, second_shift_part = second_pull(second_adj)
    middle_adj = out_adj + middle_part
    attn_adj = middle_adj.astype(bf16)
    att_adj = dot(out_full, attn_adj, 1, 1).astype(bf16)
    att_adj_full = jnp.zeros((width, GLEN), bf16)
    for k in range(4):
        piece = att_adj[k * width : (k + 1) * width]
        piece = swap(piece, k) if k else piece
        att_adj_full = lax.dynamic_update_slice(att_adj_full, piece, (0, slots[k] * rows))

    for k in range(4):
        reduce_parts.append(dot(acts[k], branch_adj, 0, 0).astype(bf16))
        expand_parts.append(dot(second_norm, pre_adjs[k], 0, 0).astype(bf16))
    out_parts = dot(att_own, attn_adj, 1, 0).astype(bf16)
    out_parts = [out_parts[k * width : (k + 1) * width] for k in range(4)]
    reduce_grad = scatter4(reduce_parts).astype(bf16)
    expand_grad = scatter4(expand_parts).astype(bf16)
    out_proj_grad = scatter4(out_parts).astype(bf16)
    reduce_grad, expand_grad, out_proj_grad = lax.psum((reduce_grad, expand_grad, out_proj_grad), "dp")

    dq, dk, dv = attn_bwd(qkv, att_adj_full.reshape(heads, HD, GLEN), attended_wide, logsum, doc_start, key_bias)
    proj_adj = jnp.concatenate([g.reshape(width, GLEN) for g in (dq, dk, dv)], 0)
    pieces = [lax.dynamic_slice(proj_adj, (0, slots[k] * rows), (3 * width, rows)) for k in range(4)]
    first_parts = [dot(pieces[k], in_matrix, 0, 1).astype(bf16) for k in range(4)]
    first_adj = scatter4(first_parts)
    in_proj_grad = 0.0
    for k in range(4):
        in_proj_grad = in_proj_grad + dot(first_blocks[k], pieces[k], 0, 1)
    in_proj_grad = lax.psum(in_proj_grad.astype(bf16), "dp")
    hidden_part, first_gain_part, first_shift_part = first_pull(first_adj)
    input_adj = middle_adj + hidden_part
    embed_part = jnp.sum(input_adj, axis=0)
    small = jnp.stack(
        [
            embed_part,
            first_gain_part,
            first_shift_part,
            second_gain_part,
            second_shift_part,
            jnp.full((D,), squares_part),
        ]
    )
    small = butterfly(butterfly(small, "tensor"), "dp")
    return (
        layer_out.astype(bf16),
        small[5, 0] / divisor,
        input_adj.astype(bf16),
        small[0],
        small[1],
        small[2],
        in_proj_grad.astype(f32).reshape(D, 3, width),
        out_proj_grad.astype(f32),
        small[3],
        small[4],
        expand_grad.astype(f32),
        reduce_grad.astype(f32),
    )


def solution(mesh):
    rows = P(("dp", "tensor"), None)
    return jax.shard_map(
        shards,
        mesh=mesh,
        in_specs=(
            rows,
            rows,
            rows,
            P("dp", None),
            P("dp", None),
            P(),
            P(),
            P(),
            P(None, None, "tensor"),
            P("tensor", None),
            P(),
            P(),
            P(None, "tensor"),
            P("tensor", None),
        ),
        out_specs=(
            rows,
            P(),
            rows,
            P(),
            P(),
            P(),
            P(None, None, "tensor"),
            P("tensor", None),
            P(),
            P(),
            P(None, "tensor"),
            P("tensor", None),
        ),
        check_vma=False,
    )
```

time: 1230 us -> 591 us (0.48)
  waiting for transfers between devices: 572 us -> 200 us
  matrix products: 330 us -> 115 us
  Pallas kernels: 0 us -> 140 us
  other arithmetic: 170 us -> 40.7 us
  blocking collectives: 66.4 us -> 0 us
  starting transfers between devices: 0.63 us -> 36.5 us
  local copies, waits for them, and re-layouts: 59.8 us -> 31.7 us
    dot_general x60 -> x39, matrix products: 330 us -> 115 us  [dot(): lax.dot_general(a, b, (((ca,), (cb,)), ((), ())), preferred_element_type=...]
    reduce_scatter x4 -> x0, waiting for transfers between devices: 214 us -> none  [the longest x1 99.7 us: shards(): lax.psum_scatter(jnp.dot(picked, project_out, preferred_element_type=jnp....]
    all_gather x4 -> x0, waiting for transfers between devices: 175 us -> none  [the longest x1 46.5 us: shards(): second_full = lax.all_gather(second_norm, 'tensor', axis=0, tiled=True)]
    pallas_call x0 -> x2, Pallas kernels: none -> 140 us  [the longest x1 88.9 us: attn_bwd(): pl.pallas_call(bwd_kernel, grid=(heads,), in_specs=[head_spec(0, heads),...]
    ppermute x0 -> x38, waiting for transfers between devices: none -> 128 us  [swap(): return lax.ppermute(x, axis, [(i, i ^ bit) for i in range(size)])]
    psum x1, waiting for transfers between devices: 183 us -> 72.4 us  [shards(): in_proj_grad = lax.psum(in_proj_grad.astype(bf16), 'dp')]
    psum x2 -> x0, blocking collectives: 66.4 us -> none  [the longest x1 44.5 us: shards(): lax.psum((embed_part, first_gain_part, first_shift_part, second_gain_part...]
    convert_element_type x14 -> x11, other arithmetic: 77.8 us -> 18.4 us  [the longest x1 3.34 us: shards(): input_adj.astype(bf16)]
  transfers between devices with their start and end apart: 9 -> 39, of which waited for: 9 -> 15; matrix products, arithmetic and copies ran while one was open for 5% -> 20% of each run, Pallas kernels for 0% -> 24%
where the time goes in v1:
time: 591 us; the launch traced here: 583 us
  waiting for transfers between devices  200 us (34%)
  Pallas kernels  140 us (24%)
  matrix products  115 us (19%)
  other arithmetic  40.7 us (7%)
  starting transfers between devices  36.5 us (6%)
  local copies, waits for them, and re-layouts  31.7 us (5%)
  between operations  19.7 us (3%)
    ppermute x38, waiting for transfers between devices, swap(): return lax.ppermute(x, axis, [(i, i ^ bit) for i in range(size)])  128 us
    dot_general x39, matrix products, dot(): lax.dot_general(a, b, (((ca,), (cb,)), ((), ())), preferred_element_type=...  115 us
    pallas_call x1, Pallas kernels, attn_bwd(): pl.pallas_call(bwd_kernel, grid=(heads,), in_specs=[head_spec(0, heads),...  88.9 us
    psum x1, waiting for transfers between devices, shards(): in_proj_grad = lax.psum(in_proj_grad.astype(bf16), 'dp')  72.4 us
    pallas_call x1, Pallas kernels, attn_fwd(): pl.pallas_call(fwd_kernel, grid=(heads,), in_specs=[head_spec(0, heads),...  50.9 us
    ppermute x38, starting transfers between devices, swap(): return lax.ppermute(x, axis, [(i, i ^ bit) for i in range(size)])  36.5 us
    unnamed x132, local copies, waits for them, and re-layouts  18.6 us
  transfers between devices with their start and end apart: 39, of which 15 were waited for; matrix products, arithmetic and copies ran while one was open for 20% of the time, Pallas kernels for 24%

profile of v1, /device:TPU:0, one launch (start us, length us, event | category | flops | bytes accessed | tf_op | source)
XLA Modules:
  0.0 583.2 jit_solution(17869358214053866863)
XLA Ops:
  10.7 1.9 add_convert_fusion.2
  13.1 2.5 collective-permute-start.1
  16.9 2.9 collective-permute-start.15
  19.8 3.5 fusion.32
  25.8 2.5 fusion.49.start_ref
  28.3 22.7 %collective-permute-done.1 = bf16[1024,768]{0,1:T(8,128)(2,1)} collective-permute-done((bf16[1024,768]{0,1:T(8,128)(2,1)}, bf16[1024,768]{0,1:T(8,128)(2,1)}, u32[]{:S(2)}, u32[]{:S(2)}) %collective-permute-start.1) | collective-permute-done | bytes 1572896 | tf_op jit(solution)/shard_map/ppermute | solution.py:226
  51.0 2.6 copy.31
  53.6 2.6 copy.32
  56.1 2.7 broadcast_in_dim.58
  60.6 3.2 collective-permute-start.16
  64.9 4.2 collective-permute-start.17
  70.0 1.9 collective-permute-start.7
  71.9 2.5 fusion.33
  74.5 2.5 fusion.34
  81.7 2.5 fusion.35
  86.8 50.9 %attn_fwd.1 = (bf16[3,64,4096]{2,1,0:T(8,128)(2,1)}, f32[3,64,4096]{2,1,0:T(8,128)}, f32[3,1,4096]{2,1,0:T(1,128)}) custom-call(bf16[9,64,4096]{2,1,0:T(8,128)(2,1)} %bitcast.5.q_ref.k_ref.v_ref, bf16[9,64,4096]{2,1,0:T(8,128)(2,1)} %bitcast.5.q_ref.k_ref.v_ref, bf16[9,64,4096]{2,1,0:T(8,128)(2,1)} %bitcast.5.q_ref.k_ref.v_ref, s32[1,2048]{1,0:T(1,128)} %fusion.49.start_ref, ...), custom_call_target="tpu_custom_call" | custom-call | tf_op jit(solution)/shard_map/attn_fwd/pallas_call | solution.py:77
  143.7 8.2 %collective-permute-done.4 = bf16[192,1024]{1,0:T(8,128)(2,1)S(1)} collective-permute-done((bf16[192,1024]{1,0:T(8,128)(2,1)S(1)}, bf16[192,1024]{1,0:T(8,128)(2,1)S(1)}, u32[]{:S(2)}, u32[]{:S(2)}) %collective-permute-start.4) | collective-permute-done | bytes 393248 | tf_op jit(solution)/shard_map/ppermute | solution.py:226
  151.9 6.6 %collective-permute-done.5 = bf16[192,1024]{1,0:T(8,128)(2,1)S(1)} collective-permute-done((bf16[192,1024]{1,0:T(8,128)(2,1)S(1)}, bf16[192,1024]{1,0:T(8,128)(2,1)S(1)}, u32[]{:S(2)}, u32[]{:S(2)}) %collective-permute-start.5) | collective-permute-done | bytes 393248 | tf_op jit(solution)/shard_map/ppermute | solution.py:226
  161.5 3.3 fusion.77
  166.5 2.9 fusion.66
  169.4 2.7 fusion.79
  172.2 3.8 fusion.68
  178.5 3.5 fusion.67
  184.5 6.5 %fusion.72 = (bf16[1024,768]{0,1:T(8,128)(2,1)S(1)}, f32[1024,768]{0,1:T(8,128)S(1)}, f32[]{:T(128)}, bf16[1024,768]{0,1:T(8,128)(2,1)}) fusion(bf16[1024,768]{0,1:T(8,128)(2,1)S(1)} %copy-done.8, f32[1024]{0:T(1024)S(1)} %pad_dynamic-slice_fusion, f32[]{:T(128)} %bitcast.9, bf16[1024,768]{0,1:T(8,128)(2,1)S(1)} %copy-done.7, ...), kind=kOutput, calls=%fused_computation.172 | convolution fusion | flops 1226047488 | bytes 26349576 | tf_op jit(solution)/shard_map/dot_general | solution.py:221
  191.1 3.3 convolution_convert_fusion.9
  195.1 3.4 convolution_convert_fusion.11
  198.4 3.3 convolution_convert_fusion.12
  201.7 4.5 fusion.6
  206.3 3.8 fusion.13
  210.1 2.4 convolution_convert_fusion.15
  212.5 3.6 fusion.27
  216.1 2.4 convolution_convert_fusion.13
  218.5 2.8 fusion.81
  221.4 4.9 fusion.20
  227.8 2.7 fusion.83
  230.5 2.4 multiply_reduce_fusion.1
  242.2 2.4 convolution_convert_fusion.16
  247.9 6.0 %collective-permute-done.19 = bf16[192,1024]{1,0:T(8,128)(2,1)S(1)} collective-permute-done((bf16[192,1024]{1,0:T(8,128)(2,1)S(1)}, bf16[192,1024]{1,0:T(8,128)(2,1)S(1)}, u32[]{:S(2)}, u32[]{:S(2)}) %collective-permute-start.19) | collective-permute-done | bytes 393248 | tf_op jit(solution)/shard_map/ppermute | solution.py:226
  254.7 6.5 %collective-permute-done.20 = bf16[192,1024]{1,0:T(8,128)(2,1)S(1)} collective-permute-done((bf16[192,1024]{1,0:T(8,128)(2,1)S(1)}, bf16[192,1024]{1,0:T(8,128)(2,1)S(1)}, u32[]{:S(2)}, u32[]{:S(2)}) %collective-permute-start.20) | collective-permute-done | bytes 393248 | tf_op jit(solution)/shard_map/ppermute | solution.py:226
  262.3 88.9 %attn_bwd.1 = (bf16[3,64,4096]{2,1,0:T(8,128)(2,1)}, bf16[3,64,4096]{2,1,0:T(8,128)(2,1)}, bf16[3,64,4096]{2,1,0:T(8,128)(2,1)}) custom-call(bf16[9,64,4096]{2,1,0:T(8,128)(2,1)} %bitcast.5.q_ref.k_ref.v_ref, bf16[9,64,4096]{2,1,0:T(8,128)(2,1)} %bitcast.5.q_ref.k_ref.v_ref, bf16[9,64,4096]{2,1,0:T(8,128)(2,1)} %bitcast.5.q_ref.k_ref.v_ref, ...), custom_call_target="tpu_custom_call" | custom-call | tf_op jit(solution)/shard_map/attn_bwd/pallas_call | solution.py:185
  351.2 2.8 pad_maximum_fusion
  354.0 3.7 fusion.45
  357.8 2.5 fusion.39
  360.3 2.5 fusion.42
  364.3 3.7 add_convert_fusion.7
  368.2 3.7 add_convert_fusion.4
  373.7 2.7 add_convert_fusion.6
  377.1 2.6 convolution_convert_fusion.2
  381.6 2.6 add_convert_fusion
  385.8 15.0 %collective-permute-done.37 = bf16[768,768]{1,0:T(8,128)(2,1)S(1)} collective-permute-done((bf16[768,768]{1,0:T(8,128)(2,1)S(1)}, bf16[768,768]{1,0:T(8,128)(2,1)S(1)}, u32[]{:S(2)}, u32[]{:S(2)}) %collective-permute-start.37) | collective-permute-done | bytes 1179680 | tf_op jit(solution)/shard_map/ppermute | solution.py:226
  400.8 2.8 add_convert_fusion.3
  403.6 22.5 %collective-permute-done.34 = bf16[768,768]{1,0:T(8,128)(2,1)S(1)} collective-permute-done((bf16[768,768]{1,0:T(8,128)(2,1)S(1)}, bf16[768,768]{1,0:T(8,128)(2,1)S(1)}, u32[]{:S(2)}, u32[]{:S(2)}) %collective-permute-start.34) | collective-permute-done | bytes 1179680 | tf_op jit(solution)/shard_map/ppermute | solution.py:226
  427.8 31.6 %collective-permute-done.23 = bf16[1024,768]{0,1:T(8,128)(2,1)} collective-permute-done((bf16[1024,768]{0,1:T(8,128)(2,1)}, bf16[1024,768]{0,1:T(8,128)(2,1)}, u32[]{:S(2)}, u32[]{:S(2)}) %collective-permute-start.23) | collective-permute-done | bytes 1572896 | tf_op jit(solution)/shard_map/ppermute | solution.py:226
  459.4 4.7 multiply_reduce_fusion.2
  464.2 3.2 fusion.70
  468.0 3.3 fusion.69
  471.4 2.2 reduce_sum.177
  477.3 2.1 collective-permute-done.25
  480.9 2.3 collective-permute-done.26
  484.9 2.2 collective-permute-done.27
  487.2 2.7 collective-permute-start.28
  491.4 2.6 copy.42
  495.8 72.4 %all-reduce.4.cloned.1.call-done = (bf16[768,3,192]{0,2,1:T(8,128)(2,1)}, bf16[192,768]{1,0:T(8,128)(2,1)}, bf16[768,768]{1,0:T(8,128)(2,1)}, bf16[768,768]{1,0:T(8,128)(2,1)}) async-done(((bf16[768,3,192]{0,2,1:T(8,128)(2,1)}, bf16[192,768]{1,0:T(8,128)(2,1)}, bf16[768,768]{1,0:T(8,128)(2,1)}, bf16[768,768]{1,0:T(8,128)(2,1)}), (bf16[768,3,192]{0,2,1:T(8,128)(2,1)}, bf16[192,768]{1,0:T(8,128)(2,1)}, ...) | async-done | bytes 3538960 | tf_op jit(solution)/shard_map/psum | solution.py:361
  568.2 3.0 convert_element_type.295
  (257 shorter events, 71.5 us)
Async XLA Ops:
  7.2 12.6 %copy-start = (bf16[768,3,192]{0,2,1:T(8,128)(2,1)S(1)}, bf16[768,3,192]{0,2,1:T(8,128)(2,1)}, u32[]{:S(2)}) copy-start(bf16[768,3,192]{0,2,1:T(8,128)(2,1)} %param.22) | copy-start | bytes 2654212
  7.2 561.0 %all-reduce.4.cloned.1.call-start = ((), (), s32[]{:S(2)}) async-start(), calls=%async_computation | async-start | bytes 7077888 | tf_op jit(solution)/shard_map/psum | solution.py:361
  9.1 6.5 %copy-start.36 = (s32[1,2048]{1,0:T(1,128)S(1)}, s32[1,2048]{1,0:T(1,128)}, u32[]{:S(2)}) copy-start(s32[1,2048]{1,0:T(1,128)} %param.17) | copy-start | bytes 24580
  12.6 59.3 %collective-permute-start = (bf16[1024,768]{0,1:T(8,128)(2,1)}, bf16[1024,768]{0,1:T(8,128)(2,1)}, u32[]{:S(2)}, u32[]{:S(2)}) collective-permute-start(bf16[1024,768]{0,1:T(8,128)(2,1)} %add_convert_fusion.2), channel_id=1, source_target_pairs={{0,1},{1,0},{2,3},{3,2},{4,5},{5,4},{6,7},{7,6},{8,9},{9,8},{10,11... | collective-permute-start | bytes 4718600 | tf_op jit(solution)/shard_map/ppermute | solution.py:226
  13.1 37.9 %collective-permute-start.1 = (bf16[1024,768]{0,1:T(8,128)(2,1)}, bf16[1024,768]{0,1:T(8,128)(2,1)}, u32[]{:S(2)}, u32[]{:S(2)}) collective-permute-start(bf16[1024,768]{0,1:T(8,128)(2,1)} %add_convert_fusion.2), channel_id=1, source_target_pairs={{0,2},{1,3},{2,0},{3,1},{4,6},{5,7},{6,4},{7,5},{8,10},{9,11},{10,... | collective-permute-start | bytes 4718600 | tf_op jit(solution)/shard_map/ppermute | solution.py:226
  16.9 43.1 %collective-permute-start.15 = (f32[1,1]{1,0:T(1,128)}, f32[1,1]{1,0:T(1,128)}, u32[]{:S(2)}, u32[]{:S(2)}) collective-permute-start(f32[1,1]{1,0:T(1,128)} %bitcast.8), channel_id=1, source_target_pairs={{0,4},{4,0},{8,12},{12,8},{16,20},{20,16},{24,28},{28,24},{1,5},{5... | collective-permute-start | bytes 20 | tf_op jit(solution)/shard_map/ppermute | solution.py:226
  51.0 30.7 %collective-permute-start.2 = (bf16[1024,768]{0,1:T(8,128)(2,1)}, bf16[1024,768]{0,1:T(8,128)(2,1)}, u32[]{:S(2)}, u32[]{:S(2)}) collective-permute-start(bf16[1024,768]{0,1:T(8,128)(2,1)} %collective-permute-done.1), channel_id=1, source_target_pairs={{0,1},{1,0},{2,3},{3,2},{4,5},{5,4},{6,7},{7,6},{8,9},{9,8},{10,11... | collective-permute-start | bytes 4718600 | tf_op jit(solution)/shard_map/ppermute | solution.py:226
  56.1 13.9 %copy-start.25 = (bf16[192,768]{1,0:T(8,128)(2,1)S(1)}, bf16[192,768]{1,0:T(8,128)(2,1)}, u32[]{:S(2)}) copy-start(bf16[192,768]{1,0:T(8,128)(2,1)} %param.23) | copy-start | bytes 884740
  60.6 3.6 collective-permute-start.16
  64.9 4.5 collective-permute-start.17
  70.0 11.7 %collective-permute-start.7 = (bf16[192,768]{1,0:T(8,128)(2,1)S(1)}, bf16[192,768]{1,0:T(8,128)(2,1)S(1)}, u32[]{:S(2)}, u32[]{:S(2)}) collective-permute-start(bf16[192,768]{1,0:T(8,128)(2,1)S(1)} %copy-done.25), channel_id=1, source_target_pairs={{0,2},{1,3},{2,0},{3,1},{4,6},{5,7},{6,4},{7,5},{8,10},{9,11},{10,... | collective-permute-start | bytes 884744 | tf_op jit(solution)/shard_map/ppermute | solution.py:226
  77.1 62.8 %collective-permute-start.6 = (bf16[192,768]{1,0:T(8,128)(2,1)S(1)}, bf16[192,768]{1,0:T(8,128)(2,1)S(1)}, u32[]{:S(2)}, u32[]{:S(2)}) collective-permute-start(bf16[192,768]{1,0:T(8,128)(2,1)S(1)} %copy-done.25), channel_id=1, source_target_pairs={{0,1},{1,0},{2,3},{3,2},{4,5},{5,4},{6,7},{7,6},{8,9},{9,8},{10,11... | collective-permute-start | bytes 884744 | tf_op jit(solution)/shard_map/ppermute | solution.py:226
  77.2 65.2 %collective-permute-start.11 = (bf16[768,768]{1,0:T(8,128)(2,1)}, bf16[768,768]{1,0:T(8,128)(2,1)}, u32[]{:S(2)}, u32[]{:S(2)}) collective-permute-start(bf16[768,768]{1,0:T(8,128)(2,1)} %param.26), channel_id=1, source_target_pairs={{0,2},{1,3},{2,0},{3,1},{4,6},{5,7},{6,4},{7,5},{8,10},{9,11},{10,... | collective-permute-start | bytes 3538952 | tf_op jit(solution)/shard_map/ppermute | solution.py:226
  77.5 65.7 %collective-permute-start.12 = (bf16[768,768]{1,0:T(8,128)(2,1)}, bf16[768,768]{1,0:T(8,128)(2,1)}, u32[]{:S(2)}, u32[]{:S(2)}) collective-permute-start(bf16[768,768]{1,0:T(8,128)(2,1)} %param.27), channel_id=1, source_target_pairs={{0,2},{1,3},{2,0},{3,1},{4,6},{5,7},{6,4},{7,5},{8,10},{9,11},{10,... | collective-permute-start | bytes 3538952 | tf_op jit(solution)/shard_map/ppermute | solution.py:226
  81.7 58.2 %collective-permute-start.8 = (bf16[192,768]{1,0:T(8,128)(2,1)S(1)}, bf16[192,768]{1,0:T(8,128)(2,1)}, u32[]{:S(2)}, u32[]{:S(2)}) collective-permute-start(bf16[192,768]{1,0:T(8,128)(2,1)S(1)} %collective-permute-done.7), channel_id=1, source_target_pairs={{0,1},{1,0},{2,3},{3,2},{4,5},{5,4},{6,7},{7,6},{8,9},{9,8},{10,11... | collective-permute-start | bytes 884744 | tf_op jit(solution)/shard_map/ppermute | solution.py:226
  139.2 21.0 %copy-start.22 = (bf16[192,1024]{1,0:T(8,128)(2,1)}, bf16[192,1024]{1,0:T(8,128)(2,1)S(1)}, u32[]{:S(2)}) copy-start(bf16[192,1024]{1,0:T(8,128)(2,1)S(1)} %get-tuple-element.74) | copy-start | bytes 1179652
  139.2 4.1 collective-permute-start.3
  139.9 12.0 %collective-permute-start.4 = (bf16[192,1024]{1,0:T(8,128)(2,1)S(1)}, bf16[192,1024]{1,0:T(8,128)(2,1)S(1)}, u32[]{:S(2)}, u32[]{:S(2)}) collective-permute-start(bf16[192,1024]{1,0:T(8,128)(2,1)S(1)} %get-tuple-element.76), channel_id=1, source_target_pairs={{0,2},{1,3},{2,0},{3,1},{4,6},{5,7},{6,4},{7,5},{8,10},{9,11},{10,... | collective-permute-start | bytes 1179656 | tf_op jit(solution)/shard_map/ppermute | solution.py:226
  139.9 18.6 %collective-permute-start.5 = (bf16[192,1024]{1,0:T(8,128)(2,1)S(1)}, bf16[192,1024]{1,0:T(8,128)(2,1)S(1)}, u32[]{:S(2)}, u32[]{:S(2)}) collective-permute-start(bf16[192,1024]{1,0:T(8,128)(2,1)S(1)} %get-tuple-element.75), channel_id=1, source_target_pairs={{0,3},{1,2},{2,1},{3,0},{4,7},{5,6},{6,5},{7,4},{8,11},{9,10},{10,... | collective-permute-start | bytes 1179656 | tf_op jit(solution)/shard_map/ppermute | solution.py:226
  142.4 17.8 %copy-start.26 = (bf16[768,768]{1,0:T(8,128)(2,1)}, bf16[768,768]{1,0:T(8,128)(2,1)S(1)}, u32[]{:S(2)}) copy-start(bf16[768,768]{1,0:T(8,128)(2,1)S(1)} %constant_dynamic-update-slice_fusion) | copy-start | bytes 3538948
  142.4 33.5 %collective-permute-start.9 = (bf16[768,768]{1,0:T(8,128)(2,1)}, bf16[768,768]{1,0:T(8,128)(2,1)S(1)}, u32[]{:S(2)}, u32[]{:S(2)}) collective-permute-start(bf16[768,768]{1,0:T(8,128)(2,1)} %param.26), channel_id=1, source_target_pairs={{0,1},{1,0},{2,3},{3,2},{4,5},{5,4},{6,7},{7,6},{8,9},{9,8},{10,11... | collective-permute-start | bytes 3538952 | tf_op jit(solution)/shard_map/ppermute | solution.py:226
  143.2 34.3 %collective-permute-start.10 = (bf16[768,768]{1,0:T(8,128)(2,1)}, bf16[768,768]{1,0:T(8,128)(2,1)S(1)}, u32[]{:S(2)}, u32[]{:S(2)}) collective-permute-start(bf16[768,768]{1,0:T(8,128)(2,1)} %param.27), channel_id=1, source_target_pairs={{0,1},{1,0},{2,3},{3,2},{4,5},{5,4},{6,7},{7,6},{8,9},{9,8},{10,11... | collective-permute-start | bytes 3538952 | tf_op jit(solution)/shard_map/ppermute | solution.py:226
  143.3 17.0 %copy-start.47 = (bf16[192,1024]{1,0:T(8,128)(2,1)}, bf16[192,1024]{1,0:T(8,128)(2,1)S(1)}, u32[]{:S(2)}) copy-start(bf16[192,1024]{1,0:T(8,128)(2,1)S(1)} %collective-permute-done.3) | copy-start | bytes 1179652
  143.3 38.7 %collective-permute-start.13 = (bf16[768,768]{1,0:T(8,128)(2,1)}, bf16[768,768]{1,0:T(8,128)(2,1)S(1)}, u32[]{:S(2)}, u32[]{:S(2)}) collective-permute-start(bf16[768,768]{1,0:T(8,128)(2,1)} %collective-permute-done.11), channel_id=1, source_target_pairs={{0,1},{1,0},{2,3},{3,2},{4,5},{5,4},{6,7},{7,6},{8,9},{9,8},{10,11... | collective-permute-start | bytes 3538952 | tf_op jit(solution)/shard_map/ppermute | solution.py:226
  151.9 8.4 %copy-start.49 = (bf16[192,1024]{1,0:T(8,128)(2,1)}, bf16[192,1024]{1,0:T(8,128)(2,1)S(1)}, u32[]{:S(2)}) copy-start(bf16[192,1024]{1,0:T(8,128)(2,1)S(1)} %collective-permute-done.4) | copy-start | bytes 1179652
  151.9 31.6 %collective-permute-start.14 = (bf16[768,768]{1,0:T(8,128)(2,1)}, bf16[768,768]{1,0:T(8,128)(2,1)S(1)}, u32[]{:S(2)}, u32[]{:S(2)}) collective-permute-start(bf16[768,768]{1,0:T(8,128)(2,1)} %collective-permute-done.12), channel_id=1, source_target_pairs={{0,1},{1,0},{2,3},{3,2},{4,5},{5,4},{6,7},{7,6},{8,9},{9,8},{10,11... | collective-permute-start | bytes 3538952 | tf_op jit(solution)/shard_map/ppermute | solution.py:226
  161.5 20.6 %copy-start.12 = (bf16[1024,768]{0,1:T(8,128)(2,1)}, bf16[1024,768]{0,1:T(8,128)(2,1)S(1)}, u32[]{:S(2)}) copy-start(bf16[1024,768]{0,1:T(8,128)(2,1)S(1)} %add_convert_fusion.1) | copy-start | bytes 4718596
  177.5 4.6 copy-start.58
  191.0 30.3 %copy-start.9 = (bf16[1024,768]{0,1:T(8,128)(2,1)}, bf16[1024,768]{0,1:T(8,128)(2,1)S(1)}, u32[]{:S(2)}) copy-start(bf16[1024,768]{0,1:T(8,128)(2,1)S(1)} %get-tuple-element.66) | copy-start | bytes 4718596
  191.0 42.7 %copy-start.3 = (f32[1024,768]{0,1:T(8,128)}, f32[1024,768]{0,1:T(8,128)S(1)}, u32[]{:S(2)}) copy-start(f32[1024,768]{0,1:T(8,128)S(1)} %get-tuple-element.67) | copy-start | bytes 9437188
  221.4 4.9 copy-start.44
  238.8 7.8 %copy-start.18 = (bf16[768,768]{1,0:T(8,128)(2,1)}, bf16[768,768]{1,0:T(8,128)(2,1)S(1)}, u32[]{:S(2)}) copy-start(bf16[768,768]{1,0:T(8,128)(2,1)S(1)} %convolution_convert_fusion.17) | copy-start | bytes 3538948
  238.9 6.3 %collective-permute-start.30 = (bf16[192,768]{1,0:T(8,128)(2,1)S(1)}, bf16[192,768]{1,0:T(8,128)(2,1)S(1)}, u32[]{:S(2)}, u32[]{:S(2)}) collective-permute-start(bf16[192,768]{1,0:T(8,128)(2,1)S(1)} %get-tuple-element.79), channel_id=1, source_target_pairs={{0,1},{1,0},{2,3},{3,2},{4,5},{5,4},{6,7},{7,6},{8,9},{9,8},{10,11... | collective-permute-start | bytes 884744 | tf_op jit(solution)/shard_map/ppermute | solution.py:226
  241.9 4.9 collective-permute-start.18
  242.0 12.0 %collective-permute-start.19 = (bf16[192,1024]{1,0:T(8,128)(2,1)S(1)}, bf16[192,1024]{1,0:T(8,128)(2,1)S(1)}, u32[]{:S(2)}, u32[]{:S(2)}) collective-permute-start(bf16[192,1024]{1,0:T(8,128)(2,1)S(1)} %get-tuple-element.71), channel_id=1, source_target_pairs={{0,2},{1,3},{2,0},{3,1},{4,6},{5,7},{6,4},{7,5},{8,10},{9,11},{10,... | collective-permute-start | bytes 1179656 | tf_op jit(solution)/shard_map/ppermute | solution.py:226
  244.6 123.4 %collective-permute-start.36 = (bf16[768,768]{1,0:T(8,128)(2,1)}, bf16[768,768]{1,0:T(8,128)(2,1)}, u32[]{:S(2)}, u32[]{:S(2)}) collective-permute-start(bf16[768,768]{1,0:T(8,128)(2,1)} %convolution_convert_fusion.9), channel_id=1, source_target_pairs={{0,1},{1,0},{2,3},{3,2},{4,5},{5,4},{6,7},{7,6},{8,9},{9,8},{10,11... | collective-permute-start | bytes 3538952 | tf_op jit(solution)/shard_map/ppermute | solution.py:226
  244.8 139.4 %collective-permute-start.35 = (bf16[768,768]{1,0:T(8,128)(2,1)}, bf16[768,768]{1,0:T(8,128)(2,1)}, u32[]{:S(2)}, u32[]{:S(2)}) collective-permute-start(bf16[768,768]{1,0:T(8,128)(2,1)} %convolution_convert_fusion.11), channel_id=1, source_target_pairs={{0,1},{1,0},{2,3},{3,2},{4,5},{5,4},{6,7},{7,6},{8,9},{9,8},{10,11... | collective-permute-start | bytes 3538952 | tf_op jit(solution)/shard_map/ppermute | solution.py:226
  245.2 16.1 %collective-permute-start.20 = (bf16[192,1024]{1,0:T(8,128)(2,1)S(1)}, bf16[192,1024]{1,0:T(8,128)(2,1)S(1)}, u32[]{:S(2)}, u32[]{:S(2)}) collective-permute-start(bf16[192,1024]{1,0:T(8,128)(2,1)S(1)} %get-tuple-element.70), channel_id=1, source_target_pairs={{0,3},{1,2},{2,1},{3,0},{4,7},{5,6},{6,5},{7,4},{8,11},{9,10},{10,... | collective-permute-start | bytes 1179656 | tf_op jit(solution)/shard_map/ppermute | solution.py:226
  246.7 125.1 %collective-permute-start.33 = (bf16[768,768]{1,0:T(8,128)(2,1)}, bf16[768,768]{1,0:T(8,128)(2,1)}, u32[]{:S(2)}, u32[]{:S(2)}) collective-permute-start(bf16[768,768]{1,0:T(8,128)(2,1)} %convolution_convert_fusion.13), channel_id=1, source_target_pairs={{0,1},{1,0},{2,3},{3,2},{4,5},{5,4},{6,7},{7,6},{8,9},{9,8},{10,11... | collective-permute-start | bytes 3538952 | tf_op jit(solution)/shard_map/ppermute | solution.py:226
  253.9 122.4 %collective-permute-start.29 = (bf16[192,768]{1,0:T(8,128)(2,1)S(1)}, bf16[192,768]{1,0:T(8,128)(2,1)S(1)}, u32[]{:S(2)}, u32[]{:S(2)}) collective-permute-start(bf16[192,768]{1,0:T(8,128)(2,1)S(1)} %get-tuple-element.78), channel_id=1, source_target_pairs={{0,1},{1,0},{2,3},{3,2},{4,5},{5,4},{6,7},{7,6},{8,9},{9,8},{10,11... | collective-permute-start | bytes 884744 | tf_op jit(solution)/shard_map/ppermute | solution.py:226
  261.3 115.4 %collective-permute-start.31 = (bf16[192,768]{1,0:T(8,128)(2,1)S(1)}, bf16[192,768]{1,0:T(8,128)(2,1)}, u32[]{:S(2)}, u32[]{:S(2)}) collective-permute-start(bf16[192,768]{1,0:T(8,128)(2,1)S(1)} %add_convert_fusion.9), channel_id=1, source_target_pairs={{0,2},{1,3},{2,0},{3,1},{4,6},{5,7},{6,4},{7,5},{8,10},{9,11},{10,... | collective-permute-start | bytes 884744 | tf_op jit(solution)/shard_map/ppermute | solution.py:226
  354.0 27.5 %copy-start.5 = (bf16[576,4096]{1,0:T(8,128)(2,1)}, bf16[576,4096]{1,0:T(8,128)(2,1)S(1)}, u32[]{:S(2)}) copy-start(bf16[576,4096]{1,0:T(8,128)(2,1)S(1)} %pad_maximum_fusion) | copy-start | bytes 14155780
  368.0 5.7 copy-start.14
  368.0 5.7 copy-start.61
  368.0 13.5 %collective-permute-start.22 = (bf16[1024,768]{0,1:T(8,128)(2,1)S(1)}, bf16[1024,768]{0,1:T(8,128)(2,1)S(1)}, u32[]{:S(2)}, u32[]{:S(2)}) collective-permute-start(bf16[1024,768]{0,1:T(8,128)(2,1)S(1)} %convolution_convert_fusion), channel_id=1, source_target_pairs={{0,1},{1,0},{2,3},{3,2},{4,5},{5,4},{6,7},{7,6},{8,9},{9,8},{10,11... | collective-permute-start | bytes 4718600 | tf_op jit(solution)/shard_map/ppermute | solution.py:226
  371.9 4.5 copy-start.42
  371.9 28.9 %collective-permute-start.37 = (bf16[768,768]{1,0:T(8,128)(2,1)S(1)}, bf16[768,768]{1,0:T(8,128)(2,1)S(1)}, u32[]{:S(2)}, u32[]{:S(2)}) collective-permute-start(bf16[768,768]{1,0:T(8,128)(2,1)S(1)} %add_convert_fusion.4), channel_id=1, source_target_pairs={{0,2},{1,3},{2,0},{3,1},{4,6},{5,7},{6,4},{7,5},{8,10},{9,11},{10,... | collective-permute-start | bytes 3538952 | tf_op jit(solution)/shard_map/ppermute | solution.py:226
  376.4 27.2 %collective-permute-start.32 = (bf16[768,768]{1,0:T(8,128)(2,1)S(1)}, bf16[768,768]{1,0:T(8,128)(2,1)S(1)}, u32[]{:S(2)}, u32[]{:S(2)}) collective-permute-start(bf16[768,768]{1,0:T(8,128)(2,1)S(1)} %copy-done.42), channel_id=1, source_target_pairs={{0,1},{1,0},{2,3},{3,2},{4,5},{5,4},{6,7},{7,6},{8,9},{9,8},{10,11... | collective-permute-start | bytes 3538952 | tf_op jit(solution)/shard_map/ppermute | solution.py:226
  376.7 49.4 %collective-permute-start.34 = (bf16[768,768]{1,0:T(8,128)(2,1)S(1)}, bf16[768,768]{1,0:T(8,128)(2,1)S(1)}, u32[]{:S(2)}, u32[]{:S(2)}) collective-permute-start(bf16[768,768]{1,0:T(8,128)(2,1)S(1)} %add_convert_fusion.6), channel_id=1, source_target_pairs={{0,2},{1,3},{2,0},{3,1},{4,6},{5,7},{6,4},{7,5},{8,10},{9,11},{10,... | collective-permute-start | bytes 3538952 | tf_op jit(solution)/shard_map/ppermute | solution.py:226
  381.5 19.3 %copy-start.19 = (bf16[768,768]{1,0:T(8,128)(2,1)S(1)}, bf16[768,768]{1,0:T(8,128)(2,1)}, u32[]{:S(2)}) copy-start(bf16[768,768]{1,0:T(8,128)(2,1)} %convolution_convert_fusion.12) | copy-start | bytes 3538948
  381.5 46.3 %collective-permute-start.21 = (bf16[1024,768]{0,1:T(8,128)(2,1)}, bf16[1024,768]{0,1:T(8,128)(2,1)}, u32[]{:S(2)}, u32[]{:S(2)}) collective-permute-start(bf16[1024,768]{0,1:T(8,128)(2,1)} %convolution_convert_fusion.2), channel_id=1, source_target_pairs={{0,1},{1,0},{2,3},{3,2},{4,5},{5,4},{6,7},{7,6},{8,9},{9,8},{10,11... | collective-permute-start | bytes 4718600 | tf_op jit(solution)/shard_map/ppermute | solution.py:226
  384.1 41.9 %copy-start.20 = (bf16[768,768]{1,0:T(8,128)(2,1)S(1)}, bf16[768,768]{1,0:T(8,128)(2,1)}, u32[]{:S(2)}) copy-start(bf16[768,768]{1,0:T(8,128)(2,1)} %convolution_convert_fusion.16) | copy-start | bytes 3538948
  384.1 75.3 %collective-permute-start.23 = (bf16[1024,768]{0,1:T(8,128)(2,1)}, bf16[1024,768]{0,1:T(8,128)(2,1)}, u32[]{:S(2)}, u32[]{:S(2)}) collective-permute-start(bf16[1024,768]{0,1:T(8,128)(2,1)} %add_convert_fusion), channel_id=1, source_target_pairs={{0,2},{1,3},{2,0},{3,1},{4,6},{5,7},{6,4},{7,5},{8,10},{9,11},{10,... | collective-permute-start | bytes 4718600 | tf_op jit(solution)/shard_map/ppermute | solution.py:226
  403.6 55.8 %copy-start.30 = (f32[1024]{0:T(1024)S(1)}, f32[1024]{0:T(1024)}, u32[]{:S(2)}) copy-start(f32[1024]{0:T(1024)} %copy-done.29) | copy-start | bytes 12292
  403.6 55.8 %copy-start.33 = (f32[1024]{0:T(1024)S(1)}, f32[1024]{0:T(1024)}, u32[]{:S(2)}) copy-start(f32[1024]{0:T(1024)} %copy-done.32) | copy-start | bytes 12292
  403.6 55.8 %copy-start.39 = (f32[768]{0:T(1024)S(1)}, f32[768]{0:T(1024)}, u32[]{:S(2)}) copy-start(f32[768]{0:T(1024)} %param.20) | copy-start | bytes 9220
  427.8 36.4 %copy-start.35 = (f32[1024]{0:T(1024)S(1)}, f32[1024]{0:T(1024)}, u32[]{:S(2)}) copy-start(f32[1024]{0:T(1024)} %copy-done.34) | copy-start | bytes 12292
  471.4 18.5 %copy-start.6 = (bf16[1024,768]{0,1:T(8,128)(2,1)S(1)}, bf16[1024,768]{0,1:T(8,128)(2,1)}, u32[]{:S(2)}) copy-start(bf16[1024,768]{0,1:T(8,128)(2,1)} %get-tuple-element.69) | copy-start | bytes 4718596
  474.3 1.3 collective-permute-start.24
  475.6 3.8 collective-permute-start.25
  479.4 3.8 collective-permute-start.26
  483.3 3.9 collective-permute-start.27
  487.2 6.8 %collective-permute-start.28 = (f32[6,768]{1,0:T(8,128)S(1)}, f32[6,768]{1,0:T(8,128)S(1)}, u32[]{:S(2)}, u32[]{:S(2)}) collective-permute-start(f32[6,768]{1,0:T(8,128)S(1)} %add.259), channel_id=1, source_target_pairs={{0,16},{4,20},{8,24},{12,28},{16,0},{20,4},{24,8},{28,12},{1,17},{... | collective-permute-start | bytes 55304 | tf_op jit(solution)/shard_map/ppermute | solution.py:226
  568.2 4.6 copy-start.21
  (38 other events, 91.6 us)
Sparse Core Ops, SparseCore 0:
  427.9 140.2 all-reduce.3

commit v2 on v1

--- a/solution.py
+++ b/solution.py
@@ -1,11 +1,10 @@
-import functools
-
 import jax
 import jax.numpy as jnp
 from jax import lax
 from jax.experimental import pallas as pl
 from jax.experimental.pallas import tpu as pltpu
 from jax.sharding import PartitionSpec as P
+
 
 D = 768
 H = 12
@@ -68,33 +67,34 @@
         finish(off, top, jnp.sum(p, 0, keepdims=True), dot_f32(v_ref[0, :, low : off + CONT], p.astype(bf16)))
 
 
-def head_spec(shift, heads):
-    return pl.BlockSpec((1, HD, GLEN), lambda h: (h + shift * heads, 0, 0))
-
-
-def attn_fwd(qkv, doc_start, key_bias):
+def head_spec(row):
+    return pl.BlockSpec((1, HD, GLEN), lambda i: (row, 0, 0))
+
+
+def whole(*shape):
+    return pl.BlockSpec(shape, lambda i: (0,) * len(shape))
+
+
+def attn_fwd(head, qkv, doc_start, key_bias):
     heads = qkv.shape[0] // 3
     return pl.pallas_call(
         fwd_kernel,
-        grid=(heads,),
+        grid=(1,),
         in_specs=[
-            head_spec(0, heads),
-            head_spec(1, heads),
-            head_spec(2, heads),
-            pl.BlockSpec((1, PROMPT), lambda h: (0, 0)),
-            pl.BlockSpec((GLEN - PROMPT, 128), lambda h: (0, 0)),
+            head_spec(head),
+            head_spec(head + heads),
+            head_spec(head + 2 * heads),
+            whole(1, PROMPT),
+            whole(GLEN - PROMPT, 128),
         ],
-        out_specs=[
-            head_spec(0, heads),
-            head_spec(0, heads),
-            pl.BlockSpec((1, 1, GLEN), lambda h: (h, 0, 0)),
-        ],
+        out_specs=[whole(1, HD, GLEN), whole(1, HD, GLEN), whole(1, 1, GLEN)],
         out_shape=[
-            jax.ShapeDtypeStruct((heads, HD, GLEN), bf16),
-            jax.ShapeDtypeStruct((heads, HD, GLEN), f32),
-            jax.ShapeDtypeStruct((heads, 1, GLEN), f32),
+            jax.ShapeDtypeStruct((1, HD, GLEN), bf16),
+            jax.ShapeDtypeStruct((1, HD, GLEN), f32),
+            jax.ShapeDtypeStruct((1, 1, GLEN), f32),
         ],
         scratch_shapes=[pltpu.VMEM((GLEN, HD), bf16)],
+        cost_estimate=pl.CostEstimate(flops=17_000_000_000, transcendentals=0, bytes_accessed=4_000_000),
         name="attn_fwd",
     )(qkv, qkv, qkv, doc_start, key_bias)
 
@@ -105,7 +105,7 @@
 
 def bwd_kernel(
     q_ref, k_ref, v_ref, g_ref, wide_ref, lse_ref, start_ref, bias_ref,
-    dq_ref, dk_ref, dv_ref, qn, kn, vn, gn, inner, dq,
+    out_ref, qn, kn, vn, gn, inner, dq,
 ):
     qn[...] = q_ref[0].T
     kn[...] = k_ref[0].T
@@ -129,8 +129,8 @@
         return dk, dv
 
     def emit(key_off, key_span, dk, dv):
-        dk_ref[0, :, pl.ds(key_off, key_span)] = dk.T.astype(bf16)
-        dv_ref[0, :, pl.ds(key_off, key_span)] = dv.T.astype(bf16)
+        out_ref[1, :, pl.ds(key_off, key_span)] = dk.T.astype(bf16)
+        out_ref[2, :, pl.ds(key_off, key_span)] = dv.T.astype(bf16)
 
     def key_block(b, carry):
         key_off = pl.multiple_of(b * KEYS, KEYS)
@@ -176,31 +176,41 @@
         return carry
 
     lax.fori_loop(0, CONTS, own, 0)
-    dq_ref[0] = (dq[...] * SCALE).astype(bf16)
-
-
-def attn_bwd(qkv, adj, wide, lse, doc_start, key_bias):
+    out_ref[0] = (dq[...] * SCALE).astype(bf16)
+
+
+def attn_bwd(head, grads, qkv, adj, wide, lse, doc_start, key_bias):
     heads = qkv.shape[0] // 3
-    shape = jax.ShapeDtypeStruct((heads, HD, GLEN), bf16)
+    specs = [
+        head_spec(head),
+        head_spec(head + heads),
+        head_spec(head + 2 * heads),
+        whole(1, HD, GLEN),
+        whole(1, HD, GLEN),
+        whole(1, 1, GLEN),
+        whole(1, PROMPT),
+        whole(GLEN - PROMPT, 128),
+    ]
+    args = [qkv, qkv, qkv, adj, wide, lse, doc_start, key_bias]
+    kernel = bwd_kernel
+    aliases = {}
+    if grads is not None:
+        specs.append(pl.BlockSpec(memory_space=pl.ANY))
+        aliases = {len(args): 0}
+        args.append(grads)
+        kernel = lambda *refs: bwd_kernel(*refs[:8], *refs[9:])
     return pl.pallas_call(
-        bwd_kernel,
-        grid=(heads,),
-        in_specs=[
-            head_spec(0, heads),
-            head_spec(1, heads),
-            head_spec(2, heads),
-            head_spec(0, heads),
-            head_spec(0, heads),
-            pl.BlockSpec((1, 1, GLEN), lambda h: (h, 0, 0)),
-            pl.BlockSpec((1, PROMPT), lambda h: (0, 0)),
-            pl.BlockSpec((GLEN - PROMPT, 128), lambda h: (0, 0)),
-        ],
-        out_specs=[head_spec(0, heads)] * 3,
-        out_shape=[shape] * 3,
+        kernel,
+        grid=(1,),
+        in_specs=specs,
+        out_specs=pl.BlockSpec((3, None, HD, GLEN), lambda i: (0, head, 0, 0)),
+        out_shape=jax.ShapeDtypeStruct((3, heads, HD, GLEN), bf16),
         scratch_shapes=[pltpu.VMEM((GLEN, HD), bf16)] * 4
         + [pltpu.VMEM((1, GLEN), f32), pltpu.VMEM((HD, GLEN), f32)],
+        input_output_aliases=aliases,
+        cost_estimate=pl.CostEstimate(flops=30_000_000_000, transcendentals=0, bytes_accessed=8_000_000),
         name="attn_bwd",
-    )(qkv, qkv, qkv, adj, wide, lse, doc_start, key_bias)
+    )(*args)
 
 
 def normalize(values):
@@ -234,6 +244,45 @@
     return x
 
 
+def levels(axis):
+    steps, shift, size = [], 0, lax.axis_size(axis)
+    while 1 << shift < size:
+        members = 2 if shift == 0 or size >> shift < 4 else 4
+        steps.append((shift, members))
+        shift += members.bit_length() - 1
+    return steps
+
+
+def sum_scatter(x, axis):
+    for shift, members in levels(axis):
+        digit = (lax.axis_index(axis) >> shift) & (members - 1)
+        x = x.reshape(members, x.shape[0] // members, x.shape[1])
+        total = lax.dynamic_index_in_dim(x, digit, 0, False)
+        for j in range(1, members):
+            sent = lax.dynamic_index_in_dim(x, digit ^ j, 0, False).astype(bf16)
+            total = total + swap(sent, j << shift, axis).astype(f32)
+        x = total
+    return x.astype(bf16)
+
+
+def spread(x, axis):
+    for shift, members in reversed(levels(axis)):
+        digit = (lax.axis_index(axis) >> shift) & (members - 1)
+        parts = [x] + [swap(x, j << shift, axis) for j in range(1, members)]
+        rows = []
+        for i in range(members):
+            row = parts[0]
+            for j in range(1, members):
+                row = jnp.where(digit ^ j == i, parts[j], row)
+            rows.append(row)
+        x = jnp.concatenate(rows, 0)
+    return x.astype(f32)
+
+
+def sum_all(x, axis):
+    return spread(sum_scatter(x, axis), axis)
+
+
 def gather4(x):
     far = swap(x, 2)
     near = swap(x, 1)
@@ -241,14 +290,14 @@
 
 
 def scatter4(parts):
+    near3 = swap(parts[3], 1)
     near1 = swap(parts[1], 1)
-    near3 = swap(parts[3], 1)
     across = (parts[2].astype(f32) + near3.astype(f32)).astype(bf16)
     mine = parts[0].astype(f32) + near1.astype(f32)
     return mine + swap(across, 2).astype(f32)
 
 
-def shards(
+def layer(
     layer_input,
     out_cotangent,
     teacher,
@@ -301,11 +350,18 @@
         part = jnp.concatenate([part[:width] * SCALE, part[width:]], 0)
         qkv = lax.dynamic_update_slice(qkv, part, (0, slots[k] * rows))
     qkv = qkv.reshape(3 * heads, HD, GLEN)
-    attended, attended_wide, logsum = attn_fwd(qkv, doc_start, key_bias)
-
-    att = attended.reshape(width, GLEN)
-    cuts = [lax.dynamic_slice(att, (0, slots[k] * rows), (width, rows)) for k in range(4)]
-    att_own = jnp.concatenate([cuts[0]] + [swap(cuts[k], k) for k in (1, 2, 3)], 0)
+    saved = []
+    for h in range(heads):
+        saved.append(attn_fwd(h, qkv, doc_start, key_bias))
+    groups = [saved[:-1], saved[-1:]]
+    moved = []
+    for group in groups:
+        att = jnp.concatenate([x[0][0] for x in group], 0)
+        cut = lambda k: lax.dynamic_slice(att, (0, slots[k] * rows), (att.shape[0], rows))
+        got = {k: swap(cut(k), k) for k in (3, 2, 1)}
+        got[0] = cut(0)
+        moved.append(got)
+    att_own = jnp.concatenate([got[k] for k in range(4) for got in moved], 0)
     attn_branch = dot(att_own, out_full, 0, 0)
     middle = hidden_in + attn_branch
     second_affine, second_pull = jax.vjp(affine_norm, middle, second_gain, second_shift)
@@ -324,7 +380,9 @@
     out_adj = out_cotangent.astype(f32) + 2.0 / divisor * deviation
     branch_adj = out_adj.astype(bf16)
     second_adj = 0.0
-    reduce_parts, expand_parts = [], []
+    reduce_parts = [dot(acts[k], branch_adj, 0, 0).astype(bf16) for k in range(4)]
+    branch_adj, *reduce_parts = lax.optimization_barrier((branch_adj, *reduce_parts))
+    reduce_grad = sum_all(scatter4(reduce_parts), "dp")
     pre_adjs = []
     for k in range(4):
         act_adj = dot(branch_adj, reduce_blocks[k], 1, 1)
@@ -334,31 +392,35 @@
     middle_adj = out_adj + middle_part
     attn_adj = middle_adj.astype(bf16)
     att_adj = dot(out_full, attn_adj, 1, 1).astype(bf16)
-    att_adj_full = jnp.zeros((width, GLEN), bf16)
-    for k in range(4):
-        piece = att_adj[k * width : (k + 1) * width]
-        piece = swap(piece, k) if k else piece
-        att_adj_full = lax.dynamic_update_slice(att_adj_full, piece, (0, slots[k] * rows))
-
-    for k in range(4):
-        reduce_parts.append(dot(acts[k], branch_adj, 0, 0).astype(bf16))
-        expand_parts.append(dot(second_norm, pre_adjs[k], 0, 0).astype(bf16))
+    att_adj = att_adj.reshape(4, heads, HD, rows)
+    adj_heads = []
+    for first, last in ((0, 1), (1, heads)):
+        full = jnp.zeros(((last - first) * HD, GLEN), bf16)
+        for k in (3, 2, 1, 0):
+            piece = att_adj[k, first:last].reshape((last - first) * HD, rows)
+            piece = swap(piece, k) if k else piece
+            full = lax.dynamic_update_slice(full, piece, (0, slots[k] * rows))
+        adj_heads += [full[h * HD : (h + 1) * HD][None] for h in range(last - first)]
+
+    expand_parts = [dot(second_norm, pre_adjs[k], 0, 0).astype(bf16) for k in range(4)]
     out_parts = dot(att_own, attn_adj, 1, 0).astype(bf16)
-    out_parts = [out_parts[k * width : (k + 1) * width] for k in range(4)]
-    reduce_grad = scatter4(reduce_parts).astype(bf16)
-    expand_grad = scatter4(expand_parts).astype(bf16)
-    out_proj_grad = scatter4(out_parts).astype(bf16)
-    reduce_grad, expand_grad, out_proj_grad = lax.psum((reduce_grad, expand_grad, out_proj_grad), "dp")
-
-    dq, dk, dv = attn_bwd(qkv, att_adj_full.reshape(heads, HD, GLEN), attended_wide, logsum, doc_start, key_bias)
-    proj_adj = jnp.concatenate([g.reshape(width, GLEN) for g in (dq, dk, dv)], 0)
+    other_parts = [
+        jnp.concatenate([expand_parts[k], out_parts[k * width : (k + 1) * width]], 0) for k in range(4)
+    ]
+    adj_heads[0], *other_parts = lax.optimization_barrier((adj_heads[0], *other_parts))
+    other_grad = sum_all(scatter4(other_parts), "dp")
+
+    proj_adj = None
+    for h in range(heads):
+        proj_adj = attn_bwd(h, proj_adj, qkv, adj_heads[h], *saved[h][1:], doc_start, key_bias)
+    proj_adj = proj_adj.reshape(3 * width, GLEN)
     pieces = [lax.dynamic_slice(proj_adj, (0, slots[k] * rows), (3 * width, rows)) for k in range(4)]
     first_parts = [dot(pieces[k], in_matrix, 0, 1).astype(bf16) for k in range(4)]
     first_adj = scatter4(first_parts)
     in_proj_grad = 0.0
     for k in range(4):
         in_proj_grad = in_proj_grad + dot(first_blocks[k], pieces[k], 0, 1)
-    in_proj_grad = lax.psum(in_proj_grad.astype(bf16), "dp")
+    in_proj_grad = sum_all(in_proj_grad, "dp")
     hidden_part, first_gain_part, first_shift_part = first_pull(first_adj)
     input_adj = middle_adj + hidden_part
     embed_part = jnp.sum(input_adj, axis=0)
@@ -380,19 +442,19 @@
         small[0],
         small[1],
         small[2],
-        in_proj_grad.astype(f32).reshape(D, 3, width),
-        out_proj_grad.astype(f32),
+        in_proj_grad.reshape(D, 3, width),
+        other_grad[D:],
         small[3],
         small[4],
-        expand_grad.astype(f32),
-        reduce_grad.astype(f32),
+        other_grad[:D],
+        reduce_grad,
     )
 
 
 def solution(mesh):
     rows = P(("dp", "tensor"), None)
     return jax.shard_map(
-        shards,
+        layer,
         mesh=mesh,
         in_specs=(
             rows,

time: 591 us -> 569 us (0.963)
  waiting for transfers between devices: 200 us -> 121 us
  starting transfers between devices: 36.5 us -> 64 us
  other arithmetic: 40.7 us -> 58.4 us
  local copies, waits for them, and re-layouts: 31.7 us -> 45.3 us
  Pallas kernels: 140 us -> 153 us
  between operations: 19.7 us -> 6.79 us
    psum x1 -> x0, waiting for transfers between devices: 72.4 us -> none  [shards(): in_proj_grad = lax.psum(in_proj_grad.astype(bf16), 'dp')]
    ppermute x38 -> x65, starting transfers between devices: 36.5 us -> 64 us  [swap(): return lax.ppermute(x, axis, [(i, i ^ bit) for i in range(size)])]
    pallas_call x2 -> x6, Pallas kernels: 140 us -> 153 us  [the longest x3 95.9 us: attn_bwd(): pl.pallas_call(kernel, grid=(1,), in_specs=specs, out_specs=pl.BlockSpec(...]
    unnamed x132 -> x183, local copies, waits for them, and re-layouts: 18.6 us -> 27.1 us
    ppermute x38 -> x65, waiting for transfers between devices: 128 us -> 121 us  [swap(): return lax.ppermute(x, axis, [(i, i ^ bit) for i in range(size)])]
    concatenate x1 -> x8, other arithmetic: 2.81 us -> 9.49 us  [the longest x4 4.83 us: layer(): jnp.concatenate([expand_parts[k], out_parts[k * width:(k + 1) * width]], 0)]
  transfers between devices with their start and end apart: 39 -> 65, of which waited for: 15 -> 24; matrix products, arithmetic and copies ran while one was open for 20% -> 25% of each run, Pallas kernels for 24% -> 27%
where the time goes in v2:
time: 569 us; the launch traced here: 560 us
  Pallas kernels  153 us (27%)
  waiting for transfers between devices  121 us (21%)
  matrix products  112 us (20%)
  starting transfers between devices  64 us (11%)
  other arithmetic  58.4 us (10%)
  local copies, waits for them, and re-layouts  45.3 us (8%)
  between operations  6.79 us (1%)
    ppermute x65, waiting for transfers between devices, swap(): return lax.ppermute(x, axis, [(i, i ^ bit) for i in range(size)])  121 us
    dot_general x39, matrix products, dot(): lax.dot_general(a, b, (((ca,), (cb,)), ((), ())), preferred_element_type=...  112 us
    pallas_call x3, Pallas kernels, attn_bwd(): pl.pallas_call(kernel, grid=(1,), in_specs=specs, out_specs=pl.BlockSpec(...  95.9 us
    ppermute x65, starting transfers between devices, swap(): return lax.ppermute(x, axis, [(i, i ^ bit) for i in range(size)])  64 us
    pallas_call x3, Pallas kernels, attn_fwd(): pl.pallas_call(fwd_kernel, grid=(1,), in_specs=[head_spec(head), head_spe...  56.7 us
    unnamed x183, local copies, waits for them, and re-layouts  27.1 us
  transfers between devices with their start and end apart: 65, of which 24 were waited for; matrix products, arithmetic and copies ran while one was open for 25% of the time, Pallas kernels for 27%

profile of v2, /device:TPU:0, one launch (start us, length us, event | category | flops | bytes accessed | tf_op | source)
XLA Modules:
  0.0 560.0 jit_solution(11784280729223368847)
XLA Ops:
  6.0 2.5 collective-permute-start.1
  9.2 3.2 fusion.101
  13.0 2.9 collective-permute-start.18
  19.4 2.6 copy.74
  22.0 2.6 copy.75
  25.6 2.8 broadcast_in_dim.76
  30.2 2.9 collective-permute-start.19
  34.5 4.0 collective-permute-start.20
  39.8 4.1 collective-permute-done.1
  45.8 2.5 fusion.33
  48.4 2.5 fusion.34
  61.9 19.1 %attn_fwd.4 = (bf16[1,64,4096]{2,1,0:T(8,128)(2,1)}, f32[1,64,4096]{2,1,0:T(8,128)}, f32[1,1,4096]{2,1,0:T(1,128)}) custom-call(bf16[9,64,4096]{2,1,0:T(8,128)(2,1)} %bitcast.5.q_ref.k_ref.v_ref.refs_0_.refs_1_.refs_2_, bf16[9,64,4096]{2,1,0:T(8,128)(2,1)} %bitcast.5.q_ref.k_ref.v_ref.refs_0_.refs_1_.refs_2_, ...), custom_call_target="tpu_custom_call" | custom-call | flops 16999999488 | bytes 4000000 | tf_op jit(solution)/shard_map/attn_fwd/pallas_call | solution.py:80
  81.0 18.7 %attn_fwd.3 = (bf16[1,64,4096]{2,1,0:T(8,128)(2,1)}, f32[1,64,4096]{2,1,0:T(8,128)}, f32[1,1,4096]{2,1,0:T(1,128)}) custom-call(bf16[9,64,4096]{2,1,0:T(8,128)(2,1)} %bitcast.5.q_ref.k_ref.v_ref.refs_0_.refs_1_.refs_2_, bf16[9,64,4096]{2,1,0:T(8,128)(2,1)} %bitcast.5.q_ref.k_ref.v_ref.refs_0_.refs_1_.refs_2_, ...), custom_call_target="tpu_custom_call" | custom-call | flops 16999999488 | bytes 4000000 | tf_op jit(solution)/shard_map/attn_fwd/pallas_call | solution.py:80
  101.8 18.8 %attn_fwd.5 = (bf16[1,64,4096]{2,1,0:T(8,128)(2,1)}, f32[1,64,4096]{2,1,0:T(8,128)}, f32[1,1,4096]{2,1,0:T(1,128)}) custom-call(bf16[9,64,4096]{2,1,0:T(8,128)(2,1)} %bitcast.5.q_ref.k_ref.v_ref.refs_0_.refs_1_.refs_2_, bf16[9,64,4096]{2,1,0:T(8,128)(2,1)} %bitcast.5.q_ref.k_ref.v_ref.refs_0_.refs_1_.refs_2_, ...), custom_call_target="tpu_custom_call" | custom-call | flops 16999999488 | bytes 4000000 | tf_op jit(solution)/shard_map/attn_fwd/pallas_call | solution.py:80
  127.3 4.2 collective-permute-done.5
  135.5 2.7 collective-permute-done.7
  141.6 3.1 fusion.102
  145.9 3.3 fusion.103
  150.9 2.9 fusion.92
  153.8 3.0 fusion.105
  156.8 3.8 fusion.94
  167.9 6.6 %fusion.98 = (bf16[1024,768]{0,1:T(8,128)(2,1)}, f32[1024,768]{0,1:T(8,128)S(1)}, f32[]{:T(128)}, bf16[1024,768]{0,1:T(8,128)(2,1)}) fusion(bf16[1024,768]{0,1:T(8,128)(2,1)S(1)} %copy-done.10, f32[1024]{0:T(1024)S(1)} %pad_dynamic-slice_fusion.8, f32[]{:T(128)} %bitcast.14, bf16[1024,768]{0,1:T(8,128)(2,1)S(1)} %copy-done.9, ...), kind=kOutput, calls=%fused_computation.266 | convolution fusion | flops 1226047488 | bytes 26349576 | tf_op jit(solution)/shard_map/dot_general | solution.py:231
  174.6 5.9 %convolution_convert_fusion.14 = bf16[768,768]{1,0:T(8,128)(2,1)} fusion(bf16[1024,768]{0,1:T(8,128)(2,1)} %get-tuple-element.40, f32[1024,768]{1,0:T(8,128)S(1)} %fusion.106), kind=kOutput, calls=%fused_computation.83 | convolution fusion | flops 1215627264 | bytes 5898240 | tf_op jit(solution)/shard_map/dot_general | solution.py:231
  180.5 3.3 convolution_convert_fusion.15
  183.8 3.3 convolution_convert_fusion.16
  187.1 3.4 convolution_convert_fusion.17
  190.5 4.4 fusion.6
  194.9 2.8 fusion.107
  199.1 3.8 fusion.27
  204.3 4.4 fusion.20
  210.2 3.8 fusion.13
  216.8 2.8 fusion.109
  239.0 32.2 %attn_bwd.3.refs_8_ = bf16[3,3,64,4096]{3,2,1,0:T(8,128)(2,1)} custom-call(bf16[9,64,4096]{2,1,0:T(8,128)(2,1)} %bitcast.5.q_ref.k_ref.v_ref.refs_0_.refs_1_.refs_2_, bf16[9,64,4096]{2,1,0:T(8,128)(2,1)} %bitcast.5.q_ref.k_ref.v_ref.refs_0_.refs_1_.refs_2_, bf16[9,64,4096]{2,1,0:T(8,128)(2,1)} %bitcast.5.q_ref.k_ref.v_ref.refs_0_.refs_1_.refs_2_, ...), custom_call_target="tpu_custom_call" | custom-call | flops 30000001024 | bytes 8000000 | tf_op jit(solution)/shard_map/attn_bwd/pallas_call | solution.py:202
  272.5 31.8 %attn_bwd.4.refs_8_ = bf16[3,3,64,4096]{3,2,1,0:T(8,128)(2,1)} custom-call(bf16[9,64,4096]{2,1,0:T(8,128)(2,1)} %bitcast.5.q_ref.k_ref.v_ref.refs_0_.refs_1_.refs_2_, bf16[9,64,4096]{2,1,0:T(8,128)(2,1)} %bitcast.5.q_ref.k_ref.v_ref.refs_0_.refs_1_.refs_2_, ...), custom_call_target="tpu_custom_call", output_to_operand_aliasing={{}: (8, {})} | custom-call | flops 30000001024 | bytes 8000000 | tf_op jit(solution)/shard_map/attn_bwd/pallas_call | solution.py:202
  304.3 31.9 %attn_bwd.5 = bf16[3,3,64,4096]{3,2,1,0:T(8,128)(2,1)} custom-call(bf16[9,64,4096]{2,1,0:T(8,128)(2,1)} %bitcast.5.q_ref.k_ref.v_ref.refs_0_.refs_1_.refs_2_, bf16[9,64,4096]{2,1,0:T(8,128)(2,1)} %bitcast.5.q_ref.k_ref.v_ref.refs_0_.refs_1_.refs_2_, ...), custom_call_target="tpu_custom_call", output_to_operand_aliasing={{}: (8, {})} | custom-call | flops 30000001024 | bytes 8000000 | tf_op jit(solution)/shard_map/attn_bwd/pallas_call | solution.py:202
  336.2 3.0 fusion.46
  339.4 2.5 fusion.40
  341.9 2.6 fusion.43
  352.3 3.9 convolution_convert_fusion
  357.1 5.7 %collective-permute-done.35 = bf16[384,576]{0,1:T(8,128)(2,1)S(1)} collective-permute-done((bf16[384,576]{0,1:T(8,128)(2,1)S(1)}, bf16[384,576]{0,1:T(8,128)(2,1)S(1)}, u32[]{:S(2)}, u32[]{:S(2)}) %collective-permute-start.35) | collective-permute-done | bytes 442400 | tf_op jit(solution)/shard_map/ppermute | solution.py:236
  365.0 2.6 collective-permute-start.37
  369.7 3.5 collective-permute-start.38
  375.6 3.8 convolution_convert_fusion.2
  380.1 2.9 add_convert_fusion.3
  383.0 3.2 collective-permute-start.39
  386.2 4.6 add_convert_fusion
  390.8 10.0 %collective-permute-done.56 = bf16[768,768]{1,0:T(8,128)(2,1)S(1)} collective-permute-done((bf16[768,768]{1,0:T(8,128)(2,1)S(1)}, bf16[768,768]{1,0:T(8,128)(2,1)S(1)}, u32[]{:S(2)}, u32[]{:S(2)}) %collective-permute-start.56) | collective-permute-done | bytes 1179680 | tf_op jit(solution)/shard_map/ppermute | solution.py:236
  405.6 2.5 collective-permute-done.41
  410.2 2.6 copy.88
  414.7 8.4 %collective-permute-done.57 = bf16[384,768]{1,0:T(8,128)(2,1)} collective-permute-done((bf16[384,768]{1,0:T(8,128)(2,1)}, bf16[384,768]{1,0:T(8,128)(2,1)}, u32[]{:S(2)}, u32[]{:S(2)}) %collective-permute-start.57) | collective-permute-done | bytes 589856 | tf_op jit(solution)/shard_map/ppermute | solution.py:236
  426.8 9.6 %collective-permute-done.45 = bf16[960,768]{1,0:T(8,128)(2,1)} collective-permute-done((bf16[960,768]{1,0:T(8,128)(2,1)}, bf16[960,768]{1,0:T(8,128)(2,1)}, u32[]{:S(2)}, u32[]{:S(2)}) %collective-permute-start.45) | collective-permute-done | bytes 1474592 | tf_op jit(solution)/shard_map/ppermute | solution.py:236
  436.4 2.6 convert_add_fusion.2
  439.1 3.3 collective-permute-start.60
  442.4 22.8 %collective-permute-done.29 = bf16[1024,768]{0,1:T(8,128)(2,1)} collective-permute-done((bf16[1024,768]{0,1:T(8,128)(2,1)}, bf16[1024,768]{0,1:T(8,128)(2,1)}, u32[]{:S(2)}, u32[]{:S(2)}) %collective-permute-start.29) | collective-permute-done | bytes 1572896 | tf_op jit(solution)/shard_map/ppermute | solution.py:236
  466.7 4.7 multiply_reduce_fusion.2
  471.5 3.2 fusion.96
  475.3 2.8 fusion.95
  483.9 3.5 collective-permute-start.49
  488.9 3.9 collective-permute-done.47
  492.8 13.0 %collective-permute-done.48 = bf16[120,768]{1,0:T(8,128)(2,1)S(1)} collective-permute-done((bf16[120,768]{1,0:T(8,128)(2,1)S(1)}, bf16[120,768]{1,0:T(8,128)(2,1)S(1)}, u32[]{:S(2)}, u32[]{:S(2)}) %collective-permute-start.48) | collective-permute-done | bytes 184352 | tf_op jit(solution)/shard_map/ppermute | solution.py:236
  508.2 11.7 %collective-permute-done.62 = bf16[96,768]{1,0:T(8,128)(2,1)S(1)} collective-permute-done((bf16[96,768]{1,0:T(8,128)(2,1)S(1)}, bf16[96,768]{1,0:T(8,128)(2,1)S(1)}, u32[]{:S(2)}, u32[]{:S(2)}) %collective-permute-start.62) | collective-permute-done | bytes 147488 | tf_op jit(solution)/shard_map/ppermute | solution.py:236
  523.8 2.7 collective-permute-done.32
  528.8 2.6 collective-permute-done.51
  546.0 8.7 %collective-permute-done.53 = bf16[480,768]{1,0:T(8,128)(2,1)} collective-permute-done((bf16[480,768]{1,0:T(8,128)(2,1)}, bf16[480,768]{1,0:T(8,128)(2,1)}, u32[]{:S(2)}, u32[]{:S(2)}) %collective-permute-start.53) | collective-permute-done | bytes 737312 | tf_op jit(solution)/shard_map/ppermute | solution.py:236
  (401 shorter events, 143.7 us)
Async XLA Ops:
  5.5 40.4 %collective-permute-start = (bf16[1024,768]{0,1:T(8,128)(2,1)}, bf16[1024,768]{0,1:T(8,128)(2,1)}, u32[]{:S(2)}, u32[]{:S(2)}) collective-permute-start(bf16[1024,768]{0,1:T(8,128)(2,1)} %add_convert_fusion.2), channel_id=1, source_target_pairs={{0,1},{1,0},{2,3},{3,2},{4,5},{5,4},{6,7},{7,6},{8,9},{9,8},{10,11... | collective-permute-start | bytes 4718600 | tf_op jit(solution)/shard_map/ppermute | solution.py:236
  6.0 37.9 %collective-permute-start.1 = (bf16[1024,768]{0,1:T(8,128)(2,1)}, bf16[1024,768]{0,1:T(8,128)(2,1)}, u32[]{:S(2)}, u32[]{:S(2)}) collective-permute-start(bf16[1024,768]{0,1:T(8,128)(2,1)} %add_convert_fusion.2), channel_id=1, source_target_pairs={{0,2},{1,3},{2,0},{3,1},{4,6},{5,7},{6,4},{7,5},{8,10},{9,11},{10,... | collective-permute-start | bytes 4718600 | tf_op jit(solution)/shard_map/ppermute | solution.py:236
  13.0 16.6 %collective-permute-start.18 = (f32[1,1]{1,0:T(1,128)}, f32[1,1]{1,0:T(1,128)}, u32[]{:S(2)}, u32[]{:S(2)}) collective-permute-start(f32[1,1]{1,0:T(1,128)} %bitcast.13), channel_id=1, source_target_pairs={{0,4},{4,0},{8,12},{12,8},{16,20},{20,16},{24,28},{28,24},{1,5},{5... | collective-permute-start | bytes 20 | tf_op jit(solution)/shard_map/ppermute | solution.py:236
  30.2 3.7 collective-permute-start.19
  34.5 4.6 collective-permute-start.20
  43.9 11.6 %collective-permute-start.9 = (bf16[192,768]{1,0:T(8,128)(2,1)S(1)}, bf16[192,768]{1,0:T(8,128)(2,1)S(1)}, u32[]{:S(2)}, u32[]{:S(2)}) collective-permute-start(bf16[192,768]{1,0:T(8,128)(2,1)S(1)} %copy-done.52), channel_id=1, source_target_pairs={{0,1},{1,0},{2,3},{3,2},{4,5},{5,4},{6,7},{7,6},{8,9},{9,8},{10,11... | collective-permute-start | bytes 884744 | tf_op jit(solution)/shard_map/ppermute | solution.py:236
  43.9 11.6 %collective-permute-start.10 = (bf16[192,768]{1,0:T(8,128)(2,1)S(1)}, bf16[192,768]{1,0:T(8,128)(2,1)S(1)}, u32[]{:S(2)}, u32[]{:S(2)}) collective-permute-start(bf16[192,768]{1,0:T(8,128)(2,1)S(1)} %copy-done.52), channel_id=1, source_target_pairs={{0,2},{1,3},{2,0},{3,1},{4,6},{5,7},{6,4},{7,5},{8,10},{9,11},{10,... | collective-permute-start | bytes 884744 | tf_op jit(solution)/shard_map/ppermute | solution.py:236
  45.6 12.5 %collective-permute-start.2 = (bf16[1024,768]{0,1:T(8,128)(2,1)}, bf16[1024,768]{0,1:T(8,128)(2,1)S(1)}, u32[]{:S(2)}, u32[]{:S(2)}) collective-permute-start(bf16[1024,768]{0,1:T(8,128)(2,1)} %collective-permute-done.1), channel_id=1, source_target_pairs={{0,1},{1,0},{2,3},{3,2},{4,5},{5,4},{6,7},{7,6},{8,9},{9,8},{10,11... | collective-permute-start | bytes 4718600 | tf_op jit(solution)/shard_map/ppermute | solution.py:236
  51.0 83.9 %collective-permute-start.14 = (bf16[768,768]{1,0:T(8,128)(2,1)}, bf16[768,768]{1,0:T(8,128)(2,1)}, u32[]{:S(2)}, u32[]{:S(2)}) collective-permute-start(bf16[768,768]{1,0:T(8,128)(2,1)} %param.26), channel_id=1, source_target_pairs={{0,2},{1,3},{2,0},{3,1},{4,6},{5,7},{6,4},{7,5},{8,10},{9,11},{10,... | collective-permute-start | bytes 3538952 | tf_op jit(solution)/shard_map/ppermute | solution.py:236
  51.3 84.0 %collective-permute-start.15 = (bf16[768,768]{1,0:T(8,128)(2,1)}, bf16[768,768]{1,0:T(8,128)(2,1)}, u32[]{:S(2)}, u32[]{:S(2)}) collective-permute-start(bf16[768,768]{1,0:T(8,128)(2,1)} %param.27), channel_id=1, source_target_pairs={{0,2},{1,3},{2,0},{3,1},{4,6},{5,7},{6,4},{7,5},{8,10},{9,11},{10,... | collective-permute-start | bytes 3538952 | tf_op jit(solution)/shard_map/ppermute | solution.py:236
  101.7 22.5 %collective-permute-start.3 = (bf16[128,1024]{1,0:T(8,128)(2,1)}, bf16[128,1024]{1,0:T(8,128)(2,1)S(1)}, u32[]{:S(2)}, u32[]{:S(2)}) collective-permute-start(bf16[128,1024]{1,0:T(8,128)(2,1)} %get-tuple-element.141), channel_id=1, source_target_pairs={{0,1},{1,0},{2,3},{3,2},{4,5},{5,4},{6,7},{7,6},{8,9},{9,8},{10,11... | collective-permute-start | bytes 786440 | tf_op jit(solution)/shard_map/ppermute | solution.py:236
  121.8 4.8 collective-permute-start.4
  122.3 9.2 %collective-permute-start.5 = (bf16[128,1024]{1,0:T(8,128)(2,1)S(1)}, bf16[128,1024]{1,0:T(8,128)(2,1)S(1)}, u32[]{:S(2)}, u32[]{:S(2)}) collective-permute-start(bf16[128,1024]{1,0:T(8,128)(2,1)S(1)} %get-tuple-element.142), channel_id=1, source_target_pairs={{0,2},{1,3},{2,0},{3,1},{4,6},{5,7},{6,4},{7,5},{8,10},{9,11},{10,... | collective-permute-start | bytes 786440 | tf_op jit(solution)/shard_map/ppermute | solution.py:236
  124.2 10.1 %collective-permute-start.6 = (bf16[64,1024]{1,0:T(8,128)(2,1)S(1)}, bf16[64,1024]{1,0:T(8,128)(2,1)S(1)}, u32[]{:S(2)}, u32[]{:S(2)}) collective-permute-start(bf16[64,1024]{1,0:T(8,128)(2,1)S(1)} %get-tuple-element.157), channel_id=1, source_target_pairs={{0,2},{1,3},{2,0},{3,1},{4,6},{5,7},{6,4},{7,5},{8,10},{9,11},{10,... | collective-permute-start | bytes 393224 | tf_op jit(solution)/shard_map/ppermute | solution.py:236
  126.6 11.5 %collective-permute-start.7 = (bf16[128,1024]{1,0:T(8,128)(2,1)S(1)}, bf16[128,1024]{1,0:T(8,128)(2,1)S(1)}, u32[]{:S(2)}, u32[]{:S(2)}) collective-permute-start(bf16[128,1024]{1,0:T(8,128)(2,1)S(1)} %get-tuple-element.139), channel_id=1, source_target_pairs={{0,3},{1,2},{2,1},{3,0},{4,7},{5,6},{6,5},{7,4},{8,11},{9,10},{10,... | collective-permute-start | bytes 786440 | tf_op jit(solution)/shard_map/ppermute | solution.py:236
  131.5 29.1 %collective-permute-start.12 = (bf16[768,768]{1,0:T(8,128)(2,1)}, bf16[768,768]{1,0:T(8,128)(2,1)S(1)}, u32[]{:S(2)}, u32[]{:S(2)}) collective-permute-start(bf16[768,768]{1,0:T(8,128)(2,1)} %param.26), channel_id=1, source_target_pairs={{0,1},{1,0},{2,3},{3,2},{4,5},{5,4},{6,7},{7,6},{8,9},{9,8},{10,11... | collective-permute-start | bytes 3538952 | tf_op jit(solution)/shard_map/ppermute | solution.py:236
  134.3 6.7 %collective-permute-start.8 = (bf16[64,1024]{1,0:T(8,128)(2,1)S(1)}, bf16[64,1024]{1,0:T(8,128)(2,1)S(1)}, u32[]{:S(2)}, u32[]{:S(2)}) collective-permute-start(bf16[64,1024]{1,0:T(8,128)(2,1)S(1)} %get-tuple-element.156), channel_id=1, source_target_pairs={{0,3},{1,2},{2,1},{3,0},{4,7},{5,6},{6,5},{7,4},{8,11},{9,10},{10,... | collective-permute-start | bytes 393224 | tf_op jit(solution)/shard_map/ppermute | solution.py:236
  134.9 27.1 %collective-permute-start.13 = (bf16[768,768]{1,0:T(8,128)(2,1)}, bf16[768,768]{1,0:T(8,128)(2,1)S(1)}, u32[]{:S(2)}, u32[]{:S(2)}) collective-permute-start(bf16[768,768]{1,0:T(8,128)(2,1)} %param.27), channel_id=1, source_target_pairs={{0,1},{1,0},{2,3},{3,2},{4,5},{5,4},{6,7},{7,6},{8,9},{9,8},{10,11... | collective-permute-start | bytes 3538952 | tf_op jit(solution)/shard_map/ppermute | solution.py:236
  135.4 30.0 %collective-permute-start.16 = (bf16[768,768]{1,0:T(8,128)(2,1)}, bf16[768,768]{1,0:T(8,128)(2,1)S(1)}, u32[]{:S(2)}, u32[]{:S(2)}) collective-permute-start(bf16[768,768]{1,0:T(8,128)(2,1)} %collective-permute-done.14), channel_id=1, source_target_pairs={{0,1},{1,0},{2,3},{3,2},{4,5},{5,4},{6,7},{7,6},{8,9},{9,8},{10,11... | collective-permute-start | bytes 3538952 | tf_op jit(solution)/shard_map/ppermute | solution.py:236
  138.1 28.8 %collective-permute-start.17 = (bf16[768,768]{1,0:T(8,128)(2,1)}, bf16[768,768]{1,0:T(8,128)(2,1)S(1)}, u32[]{:S(2)}, u32[]{:S(2)}) collective-permute-start(bf16[768,768]{1,0:T(8,128)(2,1)} %collective-permute-done.15), channel_id=1, source_target_pairs={{0,1},{1,0},{2,3},{3,2},{4,5},{5,4},{6,7},{7,6},{8,9},{9,8},{10,11... | collective-permute-start | bytes 3538952 | tf_op jit(solution)/shard_map/ppermute | solution.py:236
  228.4 136.5 %collective-permute-start.55 = (bf16[768,768]{1,0:T(8,128)(2,1)}, bf16[768,768]{1,0:T(8,128)(2,1)}, u32[]{:S(2)}, u32[]{:S(2)}) collective-permute-start(bf16[768,768]{1,0:T(8,128)(2,1)} %convolution_convert_fusion.14), channel_id=1, source_target_pairs={{0,1},{1,0},{2,3},{3,2},{4,5},{5,4},{6,7},{7,6},{8,9},{9,8},{10,11... | collective-permute-start | bytes 3538952 | tf_op jit(solution)/shard_map/ppermute | solution.py:236
  229.3 7.1 %collective-permute-start.24 = (bf16[64,1024]{1,0:T(8,128)(2,1)S(1)}, bf16[64,1024]{1,0:T(8,128)(2,1)S(1)}, u32[]{:S(2)}, u32[]{:S(2)}) collective-permute-start(bf16[64,1024]{1,0:T(8,128)(2,1)S(1)} %get-tuple-element.118), channel_id=1, source_target_pairs={{0,3},{1,2},{2,1},{3,0},{4,7},{5,6},{6,5},{7,4},{8,11},{9,10},{10,... | collective-permute-start | bytes 393224 | tf_op jit(solution)/shard_map/ppermute | solution.py:236
  229.4 8.8 %collective-permute-start.25 = (bf16[64,1024]{1,0:T(8,128)(2,1)S(1)}, bf16[64,1024]{1,0:T(8,128)(2,1)S(1)}, u32[]{:S(2)}, u32[]{:S(2)}) collective-permute-start(bf16[64,1024]{1,0:T(8,128)(2,1)S(1)} %get-tuple-element.117), channel_id=1, source_target_pairs={{0,2},{1,3},{2,0},{3,1},{4,6},{5,7},{6,4},{7,5},{8,10},{9,11},{10,... | collective-permute-start | bytes 393224 | tf_op jit(solution)/shard_map/ppermute | solution.py:236
  231.0 7.2 %collective-permute-start.26 = (bf16[64,1024]{1,0:T(8,128)(2,1)S(1)}, bf16[64,1024]{1,0:T(8,128)(2,1)S(1)}, u32[]{:S(2)}, u32[]{:S(2)}) collective-permute-start(bf16[64,1024]{1,0:T(8,128)(2,1)S(1)} %get-tuple-element.116), channel_id=1, source_target_pairs={{0,1},{1,0},{2,3},{3,2},{4,5},{5,4},{6,7},{7,6},{8,9},{9,8},{10,11... | collective-permute-start | bytes 393224 | tf_op jit(solution)/shard_map/ppermute | solution.py:236
  231.2 40.0 %collective-permute-start.21 = (bf16[128,1024]{1,0:T(8,128)(2,1)S(1)}, bf16[128,1024]{1,0:T(8,128)(2,1)S(1)}, u32[]{:S(2)}, u32[]{:S(2)}) collective-permute-start(bf16[128,1024]{1,0:T(8,128)(2,1)S(1)} %bitcast.214), channel_id=1, source_target_pairs={{0,3},{1,2},{2,1},{3,0},{4,7},{5,6},{6,5},{7,4},{8,11},{9,10},{10,... | collective-permute-start | bytes 786440 | tf_op jit(solution)/shard_map/ppermute | solution.py:236
  236.4 35.0 %collective-permute-start.22 = (bf16[128,1024]{1,0:T(8,128)(2,1)S(1)}, bf16[128,1024]{1,0:T(8,128)(2,1)S(1)}, u32[]{:S(2)}, u32[]{:S(2)}) collective-permute-start(bf16[128,1024]{1,0:T(8,128)(2,1)S(1)} %bitcast.213), channel_id=1, source_target_pairs={{0,2},{1,3},{2,0},{3,1},{4,6},{5,7},{6,4},{7,5},{8,10},{9,11},{10,... | collective-permute-start | bytes 786440 | tf_op jit(solution)/shard_map/ppermute | solution.py:236
  238.1 33.3 %collective-permute-start.23 = (bf16[128,1024]{1,0:T(8,128)(2,1)S(1)}, bf16[128,1024]{1,0:T(8,128)(2,1)S(1)}, u32[]{:S(2)}, u32[]{:S(2)}) collective-permute-start(bf16[128,1024]{1,0:T(8,128)(2,1)S(1)} %bitcast.212), channel_id=1, source_target_pairs={{0,1},{1,0},{2,3},{3,2},{4,5},{5,4},{6,7},{7,6},{8,9},{9,8},{10,11... | collective-permute-start | bytes 786440 | tf_op jit(solution)/shard_map/ppermute | solution.py:236
  350.2 12.6 %collective-permute-start.35 = (bf16[384,576]{0,1:T(8,128)(2,1)S(1)}, bf16[384,576]{0,1:T(8,128)(2,1)S(1)}, u32[]{:S(2)}, u32[]{:S(2)}) collective-permute-start(bf16[384,576]{0,1:T(8,128)(2,1)S(1)} %bitcast.203), channel_id=1, source_target_pairs={{0,4},{4,0},{8,12},{12,8},{16,20},{20,16},{24,28},{28,24},{1,5},{5... | collective-permute-start | bytes 1327112 | tf_op jit(solution)/shard_map/ppermute | solution.py:236
  351.7 39.0 %collective-permute-start.54 = (bf16[768,768]{1,0:T(8,128)(2,1)}, bf16[768,768]{1,0:T(8,128)(2,1)}, u32[]{:S(2)}, u32[]{:S(2)}) collective-permute-start(bf16[768,768]{1,0:T(8,128)(2,1)} %convolution_convert_fusion.16), channel_id=1, source_target_pairs={{0,1},{1,0},{2,3},{3,2},{4,5},{5,4},{6,7},{7,6},{8,9},{9,8},{10,11... | collective-permute-start | bytes 3538952 | tf_op jit(solution)/shard_map/ppermute | solution.py:236
  352.0 27.5 %collective-permute-start.44 = (bf16[960,768]{1,0:T(8,128)(2,1)}, bf16[960,768]{1,0:T(8,128)(2,1)}, u32[]{:S(2)}, u32[]{:S(2)}) collective-permute-start(bf16[960,768]{1,0:T(8,128)(2,1)} %pad_maximum_fusion.3), channel_id=1, source_target_pairs={{0,1},{1,0},{2,3},{3,2},{4,5},{5,4},{6,7},{7,6},{8,9},{9,8},{10,11... | collective-permute-start | bytes 4423688 | tf_op jit(solution)/shard_map/ppermute | solution.py:236
  356.1 26.9 %collective-permute-start.28 = (bf16[1024,768]{0,1:T(8,128)(2,1)}, bf16[1024,768]{0,1:T(8,128)(2,1)}, u32[]{:S(2)}, u32[]{:S(2)}) collective-permute-start(bf16[1024,768]{0,1:T(8,128)(2,1)} %convolution_convert_fusion), channel_id=1, source_target_pairs={{0,1},{1,0},{2,3},{3,2},{4,5},{5,4},{6,7},{7,6},{8,9},{9,8},{10,11... | collective-permute-start | bytes 4718600 | tf_op jit(solution)/shard_map/ppermute | solution.py:236
  363.3 6.4 %collective-permute-start.36 = (bf16[96,576]{1,0:T(8,128)(2,1)S(1)}, bf16[96,576]{1,0:T(8,128)(2,1)S(1)}, u32[]{:S(2)}, u32[]{:S(2)}) collective-permute-start(bf16[96,576]{1,0:T(8,128)(2,1)S(1)} %get-tuple-element.145), channel_id=1, source_target_pairs={{0,8},{4,12},{8,0},{12,4},{16,24},{20,28},{24,16},{28,20},{1,9},{5... | collective-permute-start | bytes 331784 | tf_op jit(solution)/shard_map/ppermute | solution.py:236
  365.0 10.0 %collective-permute-start.37 = (bf16[96,576]{1,0:T(8,128)(2,1)S(1)}, bf16[96,576]{1,0:T(8,128)(2,1)S(1)}, u32[]{:S(2)}, u32[]{:S(2)}) collective-permute-start(bf16[96,576]{1,0:T(8,128)(2,1)S(1)} %get-tuple-element.147), channel_id=1, source_target_pairs={{0,16},{4,20},{8,24},{12,28},{16,0},{20,4},{24,8},{28,12},{1,17},{... | collective-permute-start | bytes 331784 | tf_op jit(solution)/shard_map/ppermute | solution.py:236
  369.7 9.7 %collective-permute-start.38 = (bf16[96,576]{1,0:T(8,128)(2,1)S(1)}, bf16[96,576]{1,0:T(8,128)(2,1)S(1)}, u32[]{:S(2)}, u32[]{:S(2)}) collective-permute-start(bf16[96,576]{1,0:T(8,128)(2,1)S(1)} %get-tuple-element.146), channel_id=1, source_target_pairs={{0,24},{4,28},{8,16},{12,20},{16,8},{20,12},{24,0},{28,4},{1,25},{... | collective-permute-start | bytes 331784 | tf_op jit(solution)/shard_map/ppermute | solution.py:236
  374.9 25.9 %collective-permute-start.56 = (bf16[768,768]{1,0:T(8,128)(2,1)S(1)}, bf16[768,768]{1,0:T(8,128)(2,1)S(1)}, u32[]{:S(2)}, u32[]{:S(2)}) collective-permute-start(bf16[768,768]{1,0:T(8,128)(2,1)S(1)} %add_convert_fusion.4), channel_id=1, source_target_pairs={{0,2},{1,3},{2,0},{3,1},{4,6},{5,7},{6,4},{7,5},{8,10},{9,11},{10,... | collective-permute-start | bytes 3538952 | tf_op jit(solution)/shard_map/ppermute | solution.py:236
  379.4 47.3 %collective-permute-start.43 = (bf16[960,768]{1,0:T(8,128)(2,1)}, bf16[960,768]{1,0:T(8,128)(2,1)}, u32[]{:S(2)}, u32[]{:S(2)}) collective-permute-start(bf16[960,768]{1,0:T(8,128)(2,1)} %pad_maximum_fusion.1), channel_id=1, source_target_pairs={{0,1},{1,0},{2,3},{3,2},{4,5},{5,4},{6,7},{7,6},{8,9},{9,8},{10,11... | collective-permute-start | bytes 4423688 | tf_op jit(solution)/shard_map/ppermute | solution.py:236
  379.5 59.6 %collective-permute-start.27 = (bf16[1024,768]{0,1:T(8,128)(2,1)}, bf16[1024,768]{0,1:T(8,128)(2,1)}, u32[]{:S(2)}, u32[]{:S(2)}) collective-permute-start(bf16[1024,768]{0,1:T(8,128)(2,1)} %convolution_convert_fusion.2), channel_id=1, source_target_pairs={{0,1},{1,0},{2,3},{3,2},{4,5},{5,4},{6,7},{7,6},{8,9},{9,8},{10,11... | collective-permute-start | bytes 4718600 | tf_op jit(solution)/shard_map/ppermute | solution.py:236
  383.0 20.2 %collective-permute-start.39 = (bf16[96,576]{1,0:T(8,128)(2,1)S(1)}, bf16[96,576]{1,0:T(8,128)(2,1)S(1)}, u32[]{:S(2)}, u32[]{:S(2)}) collective-permute-start(bf16[96,576]{1,0:T(8,128)(2,1)S(1)} %fusion.65), channel_id=1, source_target_pairs={{0,24},{4,28},{8,16},{12,20},{16,8},{20,12},{24,0},{28,4},{1,25},{... | collective-permute-start | bytes 331784 | tf_op jit(solution)/shard_map/ppermute | solution.py:236
  390.8 12.5 %collective-permute-start.40 = (bf16[96,576]{1,0:T(8,128)(2,1)S(1)}, bf16[96,576]{1,0:T(8,128)(2,1)S(1)}, u32[]{:S(2)}, u32[]{:S(2)}) collective-permute-start(bf16[96,576]{1,0:T(8,128)(2,1)S(1)} %fusion.65), channel_id=1, source_target_pairs={{0,16},{4,20},{8,24},{12,28},{16,0},{20,4},{24,8},{28,12},{1,17},{... | collective-permute-start | bytes 331784 | tf_op jit(solution)/shard_map/ppermute | solution.py:236
  400.8 35.5 %collective-permute-start.45 = (bf16[960,768]{1,0:T(8,128)(2,1)}, bf16[960,768]{1,0:T(8,128)(2,1)}, u32[]{:S(2)}, u32[]{:S(2)}) collective-permute-start(bf16[960,768]{1,0:T(8,128)(2,1)} %add_convert_fusion.3), channel_id=1, source_target_pairs={{0,2},{1,3},{2,0},{3,1},{4,6},{5,7},{6,4},{7,5},{8,10},{9,11},{10,... | collective-permute-start | bytes 4423688 | tf_op jit(solution)/shard_map/ppermute | solution.py:236
  403.2 4.9 collective-permute-start.41
  403.3 61.9 %collective-permute-start.29 = (bf16[1024,768]{0,1:T(8,128)(2,1)}, bf16[1024,768]{0,1:T(8,128)(2,1)}, u32[]{:S(2)}, u32[]{:S(2)}) collective-permute-start(bf16[1024,768]{0,1:T(8,128)(2,1)} %add_convert_fusion), channel_id=1, source_target_pairs={{0,2},{1,3},{2,0},{3,1},{4,6},{5,7},{6,4},{7,5},{8,10},{9,11},{10,... | collective-permute-start | bytes 4718600 | tf_op jit(solution)/shard_map/ppermute | solution.py:236
  408.8 14.4 %collective-permute-start.57 = (bf16[384,768]{1,0:T(8,128)(2,1)}, bf16[384,768]{1,0:T(8,128)(2,1)}, u32[]{:S(2)}, u32[]{:S(2)}) collective-permute-start(bf16[384,768]{1,0:T(8,128)(2,1)} %fusion.50), channel_id=1, source_target_pairs={{0,4},{4,0},{8,12},{12,8},{16,20},{20,16},{24,28},{28,24},{1,5},{5... | collective-permute-start | bytes 1769480 | tf_op jit(solution)/shard_map/ppermute | solution.py:236
  423.2 109.9 %collective-permute-start.42 = (bf16[384,576]{1,0:T(8,128)(2,1)}, bf16[384,576]{1,0:T(8,128)(2,1)}, u32[]{:S(2)}, u32[]{:S(2)}) collective-permute-start(bf16[384,576]{1,0:T(8,128)(2,1)} %pad_maximum_fusion.7), channel_id=1, source_target_pairs={{0,4},{4,0},{8,12},{12,8},{16,20},{20,16},{24,28},{28,24},{1,5},{5... | collective-permute-start | bytes 1327112 | tf_op jit(solution)/shard_map/ppermute | solution.py:236
  426.8 56.1 %collective-permute-start.58 = (bf16[96,768]{1,0:T(8,128)(2,1)}, bf16[96,768]{1,0:T(8,128)(2,1)S(1)}, u32[]{:S(2)}, u32[]{:S(2)}) collective-permute-start(bf16[96,768]{1,0:T(8,128)(2,1)} %get-tuple-element.130), channel_id=1, source_target_pairs={{0,8},{4,12},{8,0},{12,4},{16,24},{20,28},{24,16},{28,20},{1,9},{5... | collective-permute-start | bytes 442376 | tf_op jit(solution)/shard_map/ppermute | solution.py:236
  436.4 46.6 %collective-permute-start.59 = (bf16[96,768]{1,0:T(8,128)(2,1)}, bf16[96,768]{1,0:T(8,128)(2,1)S(1)}, u32[]{:S(2)}, u32[]{:S(2)}) collective-permute-start(bf16[96,768]{1,0:T(8,128)(2,1)} %get-tuple-element.132), channel_id=1, source_target_pairs={{0,16},{4,20},{8,24},{12,28},{16,0},{20,4},{24,8},{28,12},{1,17},{... | collective-permute-start | bytes 442376 | tf_op jit(solution)/shard_map/ppermute | solution.py:236
  439.1 44.7 %collective-permute-start.60 = (bf16[96,768]{1,0:T(8,128)(2,1)}, bf16[96,768]{1,0:T(8,128)(2,1)}, u32[]{:S(2)}, u32[]{:S(2)}) collective-permute-start(bf16[96,768]{1,0:T(8,128)(2,1)} %get-tuple-element.131), channel_id=1, source_target_pairs={{0,24},{4,28},{8,16},{12,20},{16,8},{20,12},{24,0},{28,4},{1,25},{... | collective-permute-start | bytes 442376 | tf_op jit(solution)/shard_map/ppermute | solution.py:236
  465.2 15.7 %collective-permute-start.46 = (bf16[480,768]{1,0:T(8,128)(2,1)S(1)}, bf16[480,768]{1,0:T(8,128)(2,1)}, u32[]{:S(2)}, u32[]{:S(2)}) collective-permute-start(bf16[480,768]{1,0:T(8,128)(2,1)S(1)} %fusion.49), channel_id=1, source_target_pairs={{0,4},{4,0},{8,12},{12,8},{16,20},{20,16},{24,28},{28,24},{1,5},{5... | collective-permute-start | bytes 2211848 | tf_op jit(solution)/shard_map/ppermute | solution.py:236
  480.9 7.5 %collective-permute-start.30 = (f32[6,768]{1,0:T(8,128)S(1)}, f32[6,768]{1,0:T(8,128)S(1)}, u32[]{:S(2)}, u32[]{:S(2)}) collective-permute-start(f32[6,768]{1,0:T(8,128)S(1)} %stack.5), channel_id=1, source_target_pairs={{0,1},{1,0},{2,3},{3,2},{4,5},{5,4},{6,7},{7,6},{8,9},{9,8},{10,11... | collective-permute-start | bytes 55304 | tf_op jit(solution)/shard_map/ppermute | solution.py:236
  482.9 9.9 %collective-permute-start.47 = (bf16[120,768]{1,0:T(8,128)(2,1)S(1)}, bf16[120,768]{1,0:T(8,128)(2,1)S(1)}, u32[]{:S(2)}, u32[]{:S(2)}) collective-permute-start(bf16[120,768]{1,0:T(8,128)(2,1)S(1)} %get-tuple-element.125), channel_id=1, source_target_pairs={{0,8},{4,12},{8,0},{12,4},{16,24},{20,28},{24,16},{28,20},{1,9},{5... | collective-permute-start | bytes 552968 | tf_op jit(solution)/shard_map/ppermute | solution.py:236
  483.0 22.7 %collective-permute-start.48 = (bf16[120,768]{1,0:T(8,128)(2,1)S(1)}, bf16[120,768]{1,0:T(8,128)(2,1)S(1)}, u32[]{:S(2)}, u32[]{:S(2)}) collective-permute-start(bf16[120,768]{1,0:T(8,128)(2,1)S(1)} %get-tuple-element.127), channel_id=1, source_target_pairs={{0,16},{4,20},{8,24},{12,28},{16,0},{20,4},{24,8},{28,12},{1,17},{... | collective-permute-start | bytes 552968 | tf_op jit(solution)/shard_map/ppermute | solution.py:236
  483.9 21.9 %collective-permute-start.49 = (bf16[120,768]{1,0:T(8,128)(2,1)S(1)}, bf16[120,768]{1,0:T(8,128)(2,1)S(1)}, u32[]{:S(2)}, u32[]{:S(2)}) collective-permute-start(bf16[120,768]{1,0:T(8,128)(2,1)S(1)} %get-tuple-element.126), channel_id=1, source_target_pairs={{0,24},{4,28},{8,16},{12,20},{16,8},{20,12},{24,0},{28,4},{1,25},{... | collective-permute-start | bytes 552968 | tf_op jit(solution)/shard_map/ppermute | solution.py:236
  488.5 18.0 %collective-permute-start.61 = (bf16[96,768]{1,0:T(8,128)(2,1)S(1)}, bf16[96,768]{1,0:T(8,128)(2,1)S(1)}, u32[]{:S(2)}, u32[]{:S(2)}) collective-permute-start(bf16[96,768]{1,0:T(8,128)(2,1)S(1)} %fusion.57), channel_id=1, source_target_pairs={{0,24},{4,28},{8,16},{12,20},{16,8},{20,12},{24,0},{28,4},{1,25},{... | collective-permute-start | bytes 442376 | tf_op jit(solution)/shard_map/ppermute | solution.py:236
  492.8 27.2 %collective-permute-start.62 = (bf16[96,768]{1,0:T(8,128)(2,1)S(1)}, bf16[96,768]{1,0:T(8,128)(2,1)S(1)}, u32[]{:S(2)}, u32[]{:S(2)}) collective-permute-start(bf16[96,768]{1,0:T(8,128)(2,1)S(1)} %fusion.57), channel_id=1, source_target_pairs={{0,16},{4,20},{8,24},{12,28},{16,0},{20,4},{24,8},{28,12},{1,17},{... | collective-permute-start | bytes 442376 | tf_op jit(solution)/shard_map/ppermute | solution.py:236
  505.7 14.2 %collective-permute-start.63 = (bf16[96,768]{1,0:T(8,128)(2,1)S(1)}, bf16[96,768]{1,0:T(8,128)(2,1)S(1)}, u32[]{:S(2)}, u32[]{:S(2)}) collective-permute-start(bf16[96,768]{1,0:T(8,128)(2,1)S(1)} %fusion.57), channel_id=1, source_target_pairs={{0,8},{4,12},{8,0},{12,4},{16,24},{20,28},{24,16},{28,20},{1,9},{5... | collective-permute-start | bytes 442376 | tf_op jit(solution)/shard_map/ppermute | solution.py:236
  505.7 16.6 %collective-permute-start.31 = (f32[6,768]{1,0:T(8,128)S(1)}, f32[6,768]{1,0:T(8,128)S(1)}, u32[]{:S(2)}, u32[]{:S(2)}) collective-permute-start(f32[6,768]{1,0:T(8,128)S(1)} %add.319), channel_id=1, source_target_pairs={{0,2},{1,3},{2,0},{3,1},{4,6},{5,7},{6,4},{7,5},{8,10},{9,11},{10,... | collective-permute-start | bytes 55304 | tf_op jit(solution)/shard_map/ppermute | solution.py:236
  506.5 20.6 %collective-permute-start.50 = (bf16[120,768]{1,0:T(8,128)(2,1)S(1)}, bf16[120,768]{1,0:T(8,128)(2,1)S(1)}, u32[]{:S(2)}, u32[]{:S(2)}) collective-permute-start(bf16[120,768]{1,0:T(8,128)(2,1)S(1)} %fusion.54), channel_id=1, source_target_pairs={{0,24},{4,28},{8,16},{12,20},{16,8},{20,12},{24,0},{28,4},{1,25},{... | collective-permute-start | bytes 552968 | tf_op jit(solution)/shard_map/ppermute | solution.py:236
  519.9 11.5 %collective-permute-start.51 = (bf16[120,768]{1,0:T(8,128)(2,1)S(1)}, bf16[120,768]{1,0:T(8,128)(2,1)S(1)}, u32[]{:S(2)}, u32[]{:S(2)}) collective-permute-start(bf16[120,768]{1,0:T(8,128)(2,1)S(1)} %fusion.54), channel_id=1, source_target_pairs={{0,16},{4,20},{8,24},{12,28},{16,0},{20,4},{24,8},{28,12},{1,17},{... | collective-permute-start | bytes 552968 | tf_op jit(solution)/shard_map/ppermute | solution.py:236
  519.9 11.5 %collective-permute-start.52 = (bf16[120,768]{1,0:T(8,128)(2,1)S(1)}, bf16[120,768]{1,0:T(8,128)(2,1)S(1)}, u32[]{:S(2)}, u32[]{:S(2)}) collective-permute-start(bf16[120,768]{1,0:T(8,128)(2,1)S(1)} %fusion.54), channel_id=1, source_target_pairs={{0,8},{4,12},{8,0},{12,4},{16,24},{20,28},{24,16},{28,20},{1,9},{5... | collective-permute-start | bytes 552968 | tf_op jit(solution)/shard_map/ppermute | solution.py:236
  522.4 4.2 collective-permute-start.32
  526.5 16.6 %collective-permute-start.64 = (bf16[384,768]{1,0:T(8,128)(2,1)}, bf16[384,768]{1,0:T(8,128)(2,1)}, u32[]{:S(2)}, u32[]{:S(2)}) collective-permute-start(bf16[384,768]{1,0:T(8,128)(2,1)} %pad_maximum_fusion.6), channel_id=1, source_target_pairs={{0,4},{4,0},{8,12},{12,8},{16,20},{20,16},{24,28},{28,24},{1,5},{5... | collective-permute-start | bytes 1769480 | tf_op jit(solution)/shard_map/ppermute | solution.py:236
  527.1 8.6 %collective-permute-start.33 = (f32[6,768]{1,0:T(8,128)S(1)}, f32[6,768]{1,0:T(8,128)S(1)}, u32[]{:S(2)}, u32[]{:S(2)}) collective-permute-start(f32[6,768]{1,0:T(8,128)S(1)} %add.321), channel_id=1, source_target_pairs={{0,8},{4,12},{8,0},{12,4},{16,24},{20,28},{24,16},{28,20},{1,9},{5... | collective-permute-start | bytes 55304 | tf_op jit(solution)/shard_map/ppermute | solution.py:236
  532.6 22.2 %collective-permute-start.53 = (bf16[480,768]{1,0:T(8,128)(2,1)}, bf16[480,768]{1,0:T(8,128)(2,1)}, u32[]{:S(2)}, u32[]{:S(2)}) collective-permute-start(bf16[480,768]{1,0:T(8,128)(2,1)} %pad_maximum_fusion.5), channel_id=1, source_target_pairs={{0,4},{4,0},{8,12},{12,8},{16,20},{20,16},{24,28},{28,24},{1,5},{5... | collective-permute-start | bytes 2211848 | tf_op jit(solution)/shard_map/ppermute | solution.py:236
  535.7 4.9 collective-permute-start.34
  (86 other events, 885.5 us)

commit v3 on v2

--- a/solution.py
+++ b/solution.py
@@ -223,12 +223,145 @@
     return normalize(values) * norm_gain + norm_shift
 
 
-def tanh_gelu(values):
-    return jax.nn.gelu(values, approximate=True)
+GELU_C = 0.7978845608028654
+GELU_A = 0.044715
+BLOCK = 256
 
 
 def dot(a, b, ca, cb):
     return lax.dot_general(a, b, (((ca,), (cb,)), ((), ())), preferred_element_type=f32)
+
+
+def row_norm(values):
+    centred = values - jnp.mean(values, axis=-1, keepdims=True)
+    rstd = lax.rsqrt(jnp.mean(centred * centred, axis=-1, keepdims=True) + norm_eps)
+    return centred * rstd, rstd
+
+
+def norm_pull(norm, rstd, adj):
+    first = jnp.mean(adj, axis=-1, keepdims=True)
+    second = jnp.mean(adj * norm, axis=-1, keepdims=True)
+    return (adj - first - norm * second) * rstd
+
+
+def mid_fwd_kernel(
+    scale_ref, att_ref, x_ref, embed_ref, gain_ref, shift_ref, teacher_ref, cot_ref, valid_ref,
+    out_w, e0, e1, e2, e3, r0, r1, r2, r3,
+    layer_ref, norm_ref, act_ref, slope_ref, branch_ref, middle_ref, adj_ref, squares_ref,
+):
+    hidden = x_ref[...].astype(f32) + embed_ref[...]
+    middle = hidden + dot(att_ref[...], out_w[...], 0, 0)
+    middle_ref[...] = middle
+    normed = (row_norm(middle)[0] * gain_ref[...] + shift_ref[...]).astype(bf16)
+    norm_ref[...] = normed
+    total = middle
+    for k, (expand, reduce) in enumerate(((e0, r0), (e1, r1), (e2, r2), (e3, r3))):
+        u = dot(normed, expand[...], 1, 0)
+        square = u * u
+        th = jnp.tanh(GELU_C * (u + GELU_A * (u * square)))
+        half = 0.5 * (1.0 + th)
+        act = (u * half).astype(bf16)
+        act_ref[k] = act
+        slope_ref[k] = half + (0.5 * GELU_C) * u * (1.0 - th * th) * (1.0 + (3.0 * GELU_A) * square)
+        total = total + dot(act, reduce[...], 1, 0)
+    layer_ref[...] = total.astype(bf16)
+    deviation = valid_ref[...] * (total - teacher_ref[...].astype(f32))
+    out_adj = cot_ref[...].astype(f32) + scale_ref[0, 0] * deviation
+    adj_ref[...] = out_adj
+    branch_ref[...] = out_adj.astype(bf16)
+
+    @pl.when(pl.program_id(0) == 0)
+    def _():
+        squares_ref[...] = jnp.zeros_like(squares_ref)
+
+    squares_ref[...] += jnp.sum(deviation * deviation, axis=0, keepdims=True)
+
+
+def mid_bwd_kernel(
+    branch_ref, slope_ref, middle_ref, adj_ref, gain_ref, out_w, e0, e1, e2, e3, r0, r1, r2, r3,
+    pre_ref, middle_adj_ref, attn_ref, att_ref, gain_out, shift_out,
+):
+    branch = branch_ref[...]
+    second = None
+    for k, (expand, reduce) in enumerate(((e0, r0), (e1, r1), (e2, r2), (e3, r3))):
+        pre = (dot(branch, reduce[...], 1, 1) * slope_ref[k]).astype(bf16)
+        pre_ref[k] = pre
+        part = dot(pre, expand[...], 1, 1)
+        second = part if second is None else second + part
+    norm, rstd = row_norm(middle_ref[...])
+
+    @pl.when(pl.program_id(0) == 0)
+    def _():
+        gain_out[...] = jnp.zeros_like(gain_out)
+        shift_out[...] = jnp.zeros_like(shift_out)
+
+    gain_out[...] += jnp.sum(second * norm, axis=0, keepdims=True)
+    shift_out[...] += jnp.sum(second, axis=0, keepdims=True)
+    middle_adj = adj_ref[...] + norm_pull(norm, rstd, second * gain_ref[...])
+    middle_adj_ref[...] = middle_adj
+    attn_adj = middle_adj.astype(bf16)
+    attn_ref[...] = attn_adj
+    att_ref[...] = dot(out_w[...], attn_adj, 1, 1).astype(bf16)
+
+
+def fixed(shape):
+    return pl.BlockSpec(shape, lambda i: (0,) * len(shape), pipeline_mode=pl.Buffered(1))
+
+
+def by_rows(width):
+    return pl.BlockSpec((BLOCK, width), lambda i: (i, 0))
+
+
+def by_rows4(width):
+    return pl.BlockSpec((4, BLOCK, width), lambda i: (0, i, 0))
+
+
+def by_cols(height):
+    return pl.BlockSpec((height, BLOCK), lambda i: (0, i))
+
+
+def mid_fwd(scale, att, x, embed, gain, shift, teacher, cot, valid, out_w, expand, reduce):
+    rows = x.shape[0]
+    width = expand[0].shape[1]
+    shape = jax.ShapeDtypeStruct
+    return pl.pallas_call(
+        mid_fwd_kernel,
+        grid=(rows // BLOCK,),
+        in_specs=[
+            pl.BlockSpec(memory_space=pltpu.SMEM), by_cols(D), by_rows(D), fixed((1, D)), fixed((1, D)),
+            fixed((1, D)), by_rows(D), by_rows(D), by_rows(1), fixed((D, D)),
+        ] + [fixed((D, width))] * 4 + [fixed((width, D))] * 4,
+        out_specs=[
+            by_rows(D), by_rows(D), by_rows4(width), by_rows4(width), by_rows(D), by_rows(D), by_rows(D),
+            fixed((1, D)),
+        ],
+        out_shape=[
+            shape((rows, D), bf16), shape((rows, D), bf16), shape((4, rows, width), bf16),
+            shape((4, rows, width), f32), shape((rows, D), bf16), shape((rows, D), f32),
+            shape((rows, D), f32), shape((1, D), f32),
+        ],
+        cost_estimate=pl.CostEstimate(flops=22_000_000_000, transcendentals=0, bytes_accessed=30_000_000),
+        name="mid_fwd",
+    )(scale, att, x, embed, gain, shift, teacher, cot, valid, out_w, *expand, *reduce)
+
+
+def mid_bwd(branch, slope, middle, adj, gain, out_w, expand, reduce):
+    rows = branch.shape[0]
+    width = expand[0].shape[1]
+    shape = jax.ShapeDtypeStruct
+    return pl.pallas_call(
+        mid_bwd_kernel,
+        grid=(rows // BLOCK,),
+        in_specs=[by_rows(D), by_rows4(width), by_rows(D), by_rows(D), fixed((1, D)), fixed((D, D))]
+        + [fixed((D, width))] * 4 + [fixed((width, D))] * 4,
+        out_specs=[by_rows4(width), by_rows(D), by_rows(D), by_cols(D), fixed((1, D)), fixed((1, D))],
+        out_shape=[
+            shape((4, rows, width), bf16), shape((rows, D), f32), shape((rows, D), bf16),
+            shape((D, rows), bf16), shape((1, D), f32), shape((1, D), f32),
+        ],
+        cost_estimate=pl.CostEstimate(flops=22_000_000_000, transcendentals=0, bytes_accessed=30_000_000),
+        name="mid_bwd",
+    )(branch, slope, middle, adj, gain, out_w, *expand, *reduce)
 
 
 def swap(x, bit, axis="tensor"):
@@ -362,36 +495,16 @@
         got[0] = cut(0)
         moved.append(got)
     att_own = jnp.concatenate([got[k] for k in range(4) for got in moved], 0)
-    attn_branch = dot(att_own, out_full, 0, 0)
-    middle = hidden_in + attn_branch
-    second_affine, second_pull = jax.vjp(affine_norm, middle, second_gain, second_shift)
-    second_norm = second_affine.astype(bf16)
-    acts, pulls = [], []
-    mlp_branch = 0.0
-    for k in range(4):
-        pre_act = dot(second_norm, expand_blocks[k], 1, 0)
-        activated, pull = jax.vjp(tanh_gelu, pre_act)
-        acts.append(activated.astype(bf16))
-        pulls.append(pull)
-        mlp_branch = mlp_branch + dot(acts[k], reduce_blocks[k], 1, 0)
-    layer_out = middle + mlp_branch
-    deviation = row_valid * (layer_out - teacher.astype(f32))
-    squares_part = jnp.sum(deviation * deviation)
-    out_adj = out_cotangent.astype(f32) + 2.0 / divisor * deviation
-    branch_adj = out_adj.astype(bf16)
-    second_adj = 0.0
+    layer_out, second_norm, acts, slope, branch_adj, middle, out_adj, squares = mid_fwd(
+        (2.0 / divisor).reshape(1, 1), att_own, layer_input, pass_embed[None], second_gain[None],
+        second_shift[None], teacher, out_cotangent, row_valid, out_full, expand_blocks, reduce_blocks,
+    )
     reduce_parts = [dot(acts[k], branch_adj, 0, 0).astype(bf16) for k in range(4)]
     branch_adj, *reduce_parts = lax.optimization_barrier((branch_adj, *reduce_parts))
     reduce_grad = sum_all(scatter4(reduce_parts), "dp")
-    pre_adjs = []
-    for k in range(4):
-        act_adj = dot(branch_adj, reduce_blocks[k], 1, 1)
-        pre_adjs.append(pulls[k](act_adj)[0].astype(bf16))
-        second_adj = second_adj + dot(pre_adjs[k], expand_blocks[k], 1, 1)
-    middle_part, second_gain_part, second_shift_part = second_pull(second_adj)
-    middle_adj = out_adj + middle_part
-    attn_adj = middle_adj.astype(bf16)
-    att_adj = dot(out_full, attn_adj, 1, 1).astype(bf16)
+    pre_adjs, middle_adj, attn_adj, att_adj, second_gain_part, second_shift_part = mid_bwd(
+        branch_adj, slope, middle, out_adj, second_gain[None], out_full, expand_blocks, reduce_blocks
+    )
     att_adj = att_adj.reshape(4, heads, HD, rows)
     adj_heads = []
     for first, last in ((0, 1), (1, heads)):
@@ -429,15 +542,15 @@
             embed_part,
             first_gain_part,
             first_shift_part,
-            second_gain_part,
-            second_shift_part,
-            jnp.full((D,), squares_part),
+            second_gain_part[0],
+            second_shift_part[0],
+            squares[0],
         ]
     )
     small = butterfly(butterfly(small, "tensor"), "dp")
     return (
-        layer_out.astype(bf16),
-        small[5, 0] / divisor,
+        layer_out,
+        jnp.sum(small[5]) / divisor,
         input_adj.astype(bf16),
         small[0],
         small[1],

time: 569 us -> 578 us (1.016)
  matrix products: 112 us -> 59 us
  Pallas kernels: 153 us -> 201 us
  waiting for transfers between devices: 121 us -> 161 us
  local copies, waits for them, and re-layouts: 45.3 us -> 34.3 us
  other arithmetic: 58.4 us -> 51.7 us
    dot_general x39 -> x21, matrix products: 112 us -> 59 us  [dot(): lax.dot_general(a, b, (((ca,), (cb,)), ((), ())), preferred_element_type=...]
    pallas_call x0 -> x2, Pallas kernels: none -> 48.7 us  [the longest x1 25.6 us: mid_fwd(): pl.pallas_call(mid_fwd_kernel, grid=(rows // BLOCK,), in_specs=[pl.BlockS...]
    ppermute x65, waiting for transfers between devices: 121 us -> 161 us  [swap(): return lax.ppermute(x, axis, [(i, i ^ bit) for i in range(size)])]
    unnamed x183 -> x136, local copies, waits for them, and re-layouts: 27.1 us -> 16.3 us
  transfers between devices with their start and end apart: 65 -> 65, of which waited for: 24 -> 23; matrix products, arithmetic and copies ran while one was open for 25% -> 19% of each run, Pallas kernels for 27% -> 27%
where the time goes in v3:
time: 578 us; the launch traced here: 571 us
  Pallas kernels  201 us (35%)
  waiting for transfers between devices  161 us (28%)
  matrix products  59 us (10%)
  starting transfers between devices  58.3 us (10%)
  other arithmetic  51.7 us (9%)
  local copies, waits for them, and re-layouts  34.3 us (6%)
  between operations  6.53 us (1%)
    ppermute x65, waiting for transfers between devices, swap(): return lax.ppermute(x, axis, [(i, i ^ bit) for i in range(size)])  161 us
    pallas_call x3, Pallas kernels, attn_bwd(): pl.pallas_call(kernel, grid=(1,), in_specs=specs, out_specs=pl.BlockSpec(...  95.5 us
    dot_general x21, matrix products, dot(): lax.dot_general(a, b, (((ca,), (cb,)), ((), ())), preferred_element_type=...  59 us
    ppermute x65, starting transfers between devices, swap(): return lax.ppermute(x, axis, [(i, i ^ bit) for i in range(size)])  58.3 us
    pallas_call x3, Pallas kernels, attn_fwd(): pl.pallas_call(fwd_kernel, grid=(1,), in_specs=[head_spec(head), head_spe...  56.4 us
    pallas_call x1, Pallas kernels, mid_fwd(): pl.pallas_call(mid_fwd_kernel, grid=(rows // BLOCK,), in_specs=[pl.BlockS...  25.6 us
    pallas_call x1, Pallas kernels, mid_bwd(): pl.pallas_call(mid_bwd_kernel, grid=(rows // BLOCK,), in_specs=[by_rows(D...  23.1 us
    unnamed x136, local copies, waits for them, and re-layouts  16.3 us
  transfers between devices with their start and end apart: 65, of which 23 were waited for; matrix products, arithmetic and copies ran while one was open for 19% of the time, Pallas kernels for 27%

profile of v3, /device:TPU:0, one launch (start us, length us, event | category | flops | bytes accessed | tf_op | source)
XLA Modules:
  0.0 571.5 jit_solution(14049360195017781658)
XLA Ops:
  0.7 1.9 fusion.1
  4.0 1.9 add_convert_fusion.1
  5.9 3.0 collective-permute-start.4
  9.6 3.2 fusion.114
  13.4 2.9 collective-permute-start
  16.3 2.5 fusion.51
  18.8 24.8 %collective-permute-done.4 = bf16[1024,768]{1,0:T(8,128)(2,1)} collective-permute-done((bf16[1024,768]{1,0:T(8,128)(2,1)}, bf16[1024,768]{1,0:T(8,128)(2,1)}, u32[]{:S(2)}, u32[]{:S(2)}) %collective-permute-start.4) | collective-permute-done | bytes 1572896 | tf_op jit(solution)/shard_map/ppermute | solution.py:369
  44.4 2.7 broadcast_in_dim.78
  49.0 3.2 collective-permute-start.1
  53.2 4.2 collective-permute-start.2
  58.9 2.5 fusion.52
  61.4 2.9 fusion.53
  73.5 18.8 %attn_fwd.4 = (bf16[1,64,4096]{2,1,0:T(8,128)(2,1)}, f32[1,64,4096]{2,1,0:T(8,128)}, f32[1,1,4096]{2,1,0:T(1,128)}) custom-call(bf16[9,64,4096]{2,1,0:T(8,128)(2,1)} %bitcast.8.q_ref.k_ref.v_ref.refs_0_.refs_1_.refs_2_, bf16[9,64,4096]{2,1,0:T(8,128)(2,1)} %bitcast.8.q_ref.k_ref.v_ref.refs_0_.refs_1_.refs_2_, ...), custom_call_target="tpu_custom_call" | custom-call | flops 16999999488 | bytes 4000000 | tf_op jit(solution)/shard_map/attn_fwd/pallas_call | solution.py:80
  92.4 18.7 %attn_fwd.3 = (bf16[1,64,4096]{2,1,0:T(8,128)(2,1)}, f32[1,64,4096]{2,1,0:T(8,128)}, f32[1,1,4096]{2,1,0:T(1,128)}) custom-call(bf16[9,64,4096]{2,1,0:T(8,128)(2,1)} %bitcast.8.q_ref.k_ref.v_ref.refs_0_.refs_1_.refs_2_, bf16[9,64,4096]{2,1,0:T(8,128)(2,1)} %bitcast.8.q_ref.k_ref.v_ref.refs_0_.refs_1_.refs_2_, ...), custom_call_target="tpu_custom_call" | custom-call | flops 16999999488 | bytes 4000000 | tf_op jit(solution)/shard_map/attn_fwd/pallas_call | solution.py:80
  111.0 19.0 %attn_fwd.5 = (bf16[1,64,4096]{2,1,0:T(8,128)(2,1)}, f32[1,64,4096]{2,1,0:T(8,128)}, f32[1,1,4096]{2,1,0:T(1,128)}) custom-call(bf16[9,64,4096]{2,1,0:T(8,128)(2,1)} %bitcast.8.q_ref.k_ref.v_ref.refs_0_.refs_1_.refs_2_, bf16[9,64,4096]{2,1,0:T(8,128)(2,1)} %bitcast.8.q_ref.k_ref.v_ref.refs_0_.refs_1_.refs_2_, ...), custom_call_target="tpu_custom_call" | custom-call | flops 16999999488 | bytes 4000000 | tf_op jit(solution)/shard_map/attn_fwd/pallas_call | solution.py:80
  130.0 1.8 dynamic-slice_bitcast_fusion
  143.0 1.7 bitcast_dynamic-update-slice_fusion.3
  144.7 3.4 collective-permute-done.8
  150.9 5.8 %collective-permute-done.10 = bf16[128,1024]{1,0:T(8,128)(2,1)S(1)} collective-permute-done((bf16[128,1024]{1,0:T(8,128)(2,1)S(1)}, bf16[128,1024]{1,0:T(8,128)(2,1)S(1)}, u32[]{:S(2)}, u32[]{:S(2)}) %collective-permute-start.10) | collective-permute-done | bytes 262176 | tf_op jit(solution)/shard_map/ppermute | solution.py:369
  158.8 3.4 collective-permute-done.11
  167.0 25.6 %mid_fwd.1 = (bf16[1024,768]{1,0:T(8,128)(2,1)}, bf16[1024,768]{1,0:T(8,128)(2,1)}, bf16[4,1024,768]{2,1,0:T(8,128)(2,1)}, f32[4,1024,768]{2,1,0:T(8,128)}, bf16...) custom-call(f32[1,1]{1,0:T(1,128)} %bitcast.2.scale_ref, ...), custom_call_target="tpu_custom_call" | custom-call | flops 22000001024 | bytes 30000000 | tf_op jit(solution)/shard_map/mid_fwd/pallas_call | solution.py:327
  192.6 4.5 fusion.36
  197.1 4.0 fusion.33
  201.1 2.5 fusion.30
  203.6 2.5 fusion.27
  206.1 23.1 %mid_bwd.1 = (bf16[4,1024,768]{2,1,0:T(8,128)(2,1)}, f32[1024,768]{1,0:T(8,128)}, bf16[1024,768]{1,0:T(8,128)(2,1)}, bf16[768,1024]{1,0:T(8,128)(2,1)}, f32[1,768]{1,0:T(1,128)}, /*index=5*/f32[1,768]{1,0:T(1,128)}) custom-call(bf16[1024,768]{1,0:T(8,128)(2,1)} %get-tuple-element.57.branch_ref, f32[4,1024,768]{2,1,0:T(8,128)} %get-tuple-element.58.slope_ref, ...), custom_call_target="tpu_custom_call" | custom-call | flops 22000001024 | bytes 30000000 | tf_op jit(solution)/shard_map/mid_bwd/pallas_call | solution.py:352
  229.2 3.0 fusion.48
  249.7 32.0 %attn_bwd.3.refs_8_ = bf16[3,3,64,4096]{3,2,1,0:T(8,128)(2,1)} custom-call(bf16[9,64,4096]{2,1,0:T(8,128)(2,1)} %bitcast.8.q_ref.k_ref.v_ref.refs_0_.refs_1_.refs_2_, bf16[9,64,4096]{2,1,0:T(8,128)(2,1)} %bitcast.8.q_ref.k_ref.v_ref.refs_0_.refs_1_.refs_2_, bf16[9,64,4096]{2,1,0:T(8,128)(2,1)} %bitcast.8.q_ref.k_ref.v_ref.refs_0_.refs_1_.refs_2_, ...), custom_call_target="tpu_custom_call" | custom-call | flops 30000001024 | bytes 8000000 | tf_op jit(solution)/shard_map/attn_bwd/pallas_call | solution.py:202
  283.0 31.8 %attn_bwd.4.refs_8_ = bf16[3,3,64,4096]{3,2,1,0:T(8,128)(2,1)} custom-call(bf16[9,64,4096]{2,1,0:T(8,128)(2,1)} %bitcast.8.q_ref.k_ref.v_ref.refs_0_.refs_1_.refs_2_, bf16[9,64,4096]{2,1,0:T(8,128)(2,1)} %bitcast.8.q_ref.k_ref.v_ref.refs_0_.refs_1_.refs_2_, ...), custom_call_target="tpu_custom_call", output_to_operand_aliasing={{}: (8, {})} | custom-call | flops 30000001024 | bytes 8000000 | tf_op jit(solution)/shard_map/attn_bwd/pallas_call | solution.py:202
  314.8 31.8 %attn_bwd.5 = bf16[3,3,64,4096]{3,2,1,0:T(8,128)(2,1)} custom-call(bf16[9,64,4096]{2,1,0:T(8,128)(2,1)} %bitcast.8.q_ref.k_ref.v_ref.refs_0_.refs_1_.refs_2_, bf16[9,64,4096]{2,1,0:T(8,128)(2,1)} %bitcast.8.q_ref.k_ref.v_ref.refs_0_.refs_1_.refs_2_, ...), custom_call_target="tpu_custom_call", output_to_operand_aliasing={{}: (8, {})} | custom-call | flops 30000001024 | bytes 8000000 | tf_op jit(solution)/shard_map/attn_bwd/pallas_call | solution.py:202
  346.6 3.0 fusion.64
  349.8 2.5 fusion.58
  352.3 2.6 fusion.61
  354.9 2.3 add_add_fusion.2
  357.2 2.6 reshape.156
  362.8 3.8 convolution_convert_fusion
  367.6 5.7 %collective-permute-done.35 = bf16[384,576]{0,1:T(8,128)(2,1)S(1)} collective-permute-done((bf16[384,576]{0,1:T(8,128)(2,1)S(1)}, bf16[384,576]{0,1:T(8,128)(2,1)S(1)}, u32[]{:S(2)}, u32[]{:S(2)}) %collective-permute-start.35) | collective-permute-done | bytes 442400 | tf_op jit(solution)/shard_map/ppermute | solution.py:369
  373.8 1.6 collective-permute-start.36
  375.8 1.9 add_convert_fusion.3
  379.2 3.5 collective-permute-start.38
  382.7 3.8 collective-permute-done.37
  388.1 4.0 convolution_convert_fusion.2
  392.7 2.9 add_convert_fusion.2
  395.6 4.4 add_convert_fusion
  400.1 12.4 %collective-permute-done.56 = bf16[768,768]{1,0:T(8,128)(2,1)S(1)} collective-permute-done((bf16[768,768]{1,0:T(8,128)(2,1)S(1)}, bf16[768,768]{1,0:T(8,128)(2,1)S(1)}, u32[]{:S(2)}, u32[]{:S(2)}) %collective-permute-start.56) | collective-permute-done | bytes 1179680 | tf_op jit(solution)/shard_map/ppermute | solution.py:369
  414.0 1.7 convert_add_fusion.3
  417.2 3.4 collective-permute-done.41
  424.8 9.9 %collective-permute-done.57 = bf16[384,768]{1,0:T(8,128)(2,1)} collective-permute-done((bf16[384,768]{1,0:T(8,128)(2,1)}, bf16[384,768]{1,0:T(8,128)(2,1)}, u32[]{:S(2)}, u32[]{:S(2)}) %collective-permute-start.57) | collective-permute-done | bytes 589856 | tf_op jit(solution)/shard_map/ppermute | solution.py:369
  437.6 10.3 %collective-permute-done.45 = bf16[960,768]{1,0:T(8,128)(2,1)} collective-permute-done((bf16[960,768]{1,0:T(8,128)(2,1)}, bf16[960,768]{1,0:T(8,128)(2,1)}, u32[]{:S(2)}, u32[]{:S(2)}) %collective-permute-start.45) | collective-permute-done | bytes 1474592 | tf_op jit(solution)/shard_map/ppermute | solution.py:369
  448.1 2.6 convert_add_fusion.2
  450.8 27.0 %collective-permute-done.29 = bf16[1024,768]{1,0:T(8,128)(2,1)} collective-permute-done((bf16[1024,768]{1,0:T(8,128)(2,1)}, bf16[1024,768]{1,0:T(8,128)(2,1)}, u32[]{:S(2)}, u32[]{:S(2)}) %collective-permute-start.29) | collective-permute-done | bytes 1572896 | tf_op jit(solution)/shard_map/ppermute | solution.py:369
  479.4 5.1 multiply_reduce_fusion
  484.5 3.6 fusion.111
  489.8 2.8 collective-permute-done.46
  494.4 4.3 collective-permute-start.49
  499.8 3.8 collective-permute-done.47
  503.6 13.4 %collective-permute-done.48 = bf16[120,768]{1,0:T(8,128)(2,1)S(1)} collective-permute-done((bf16[120,768]{1,0:T(8,128)(2,1)S(1)}, bf16[120,768]{1,0:T(8,128)(2,1)S(1)}, u32[]{:S(2)}, u32[]{:S(2)}) %collective-permute-start.48) | collective-permute-done | bytes 184352 | tf_op jit(solution)/shard_map/ppermute | solution.py:369
  520.1 11.1 %collective-permute-done.62 = bf16[96,768]{1,0:T(8,128)(2,1)S(1)} collective-permute-done((bf16[96,768]{1,0:T(8,128)(2,1)S(1)}, bf16[96,768]{1,0:T(8,128)(2,1)S(1)}, u32[]{:S(2)}, u32[]{:S(2)}) %collective-permute-start.62) | collective-permute-done | bytes 147488 | tf_op jit(solution)/shard_map/ppermute | solution.py:369
  531.3 1.9 collective-permute-start.52
  540.1 2.6 collective-permute-done.51
  548.4 3.4 collective-permute-done.34
  555.0 1.6 maximum_convert_fusion
  556.6 9.8 %collective-permute-done.53 = bf16[480,768]{1,0:T(8,128)(2,1)} collective-permute-done((bf16[480,768]{1,0:T(8,128)(2,1)}, bf16[480,768]{1,0:T(8,128)(2,1)}, u32[]{:S(2)}, u32[]{:S(2)}) %collective-permute-start.53) | collective-permute-done | bytes 737312 | tf_op jit(solution)/shard_map/ppermute | solution.py:369
  567.7 1.6 fusion.55
  (330 shorter events, 99.1 us)
Async XLA Ops:
  5.9 37.7 %collective-permute-start.4 = (bf16[1024,768]{1,0:T(8,128)(2,1)}, bf16[1024,768]{1,0:T(8,128)(2,1)}, u32[]{:S(2)}, u32[]{:S(2)}) collective-permute-start(bf16[1024,768]{1,0:T(8,128)(2,1)} %add_convert_fusion.1), channel_id=1, source_target_pairs={{0,2},{1,3},{2,0},{3,1},{4,6},{5,7},{6,4},{7,5},{8,10},{9,11},{10,... | collective-permute-start | bytes 4718600 | tf_op jit(solution)/shard_map/ppermute | solution.py:369
  8.9 50.0 %collective-permute-start.3 = (bf16[1024,768]{1,0:T(8,128)(2,1)}, bf16[1024,768]{1,0:T(8,128)(2,1)}, u32[]{:S(2)}, u32[]{:S(2)}) collective-permute-start(bf16[1024,768]{1,0:T(8,128)(2,1)} %add_convert_fusion.1), channel_id=1, source_target_pairs={{0,1},{1,0},{2,3},{3,2},{4,5},{5,4},{6,7},{7,6},{8,9},{9,8},{10,11... | collective-permute-start | bytes 4718600 | tf_op jit(solution)/shard_map/ppermute | solution.py:369
  13.4 35.0 %collective-permute-start = (f32[1,1]{1,0:T(1,128)}, f32[1,1]{1,0:T(1,128)}, u32[]{:S(2)}, u32[]{:S(2)}) collective-permute-start(f32[1,1]{1,0:T(1,128)} %bitcast), channel_id=1, source_target_pairs={{0,4},{4,0},{8,12},{12,8},{16,20},{20,16},{24,28},{28,24},{1,5},{5... | collective-permute-start | bytes 20 | tf_op jit(solution)/shard_map/ppermute | solution.py:369
  43.6 26.2 %collective-permute-start.5 = (bf16[1024,768]{1,0:T(8,128)(2,1)}, bf16[1024,768]{1,0:T(8,128)(2,1)S(1)}, u32[]{:S(2)}, u32[]{:S(2)}) collective-permute-start(bf16[1024,768]{1,0:T(8,128)(2,1)} %collective-permute-done.4), channel_id=1, source_target_pairs={{0,1},{1,0},{2,3},{3,2},{4,5},{5,4},{6,7},{7,6},{8,9},{9,8},{10,11... | collective-permute-start | bytes 4718600 | tf_op jit(solution)/shard_map/ppermute | solution.py:369
  53.2 78.6 %collective-permute-start.2 = (f32[1,1]{1,0:T(1,128)}, f32[1,1]{1,0:T(1,128)}, u32[]{:S(2)}, u32[]{:S(2)}) collective-permute-start(f32[1,1]{1,0:T(1,128)} %add.208), channel_id=1, source_target_pairs={{0,16},{4,20},{8,24},{12,28},{16,0},{20,4},{24,8},{28,12},{1,17},{... | collective-permute-start | bytes 20 | tf_op jit(solution)/shard_map/ppermute | solution.py:369
  57.4 10.9 %collective-permute-start.13 = (bf16[192,768]{1,0:T(8,128)(2,1)S(1)}, bf16[192,768]{1,0:T(8,128)(2,1)}, u32[]{:S(2)}, u32[]{:S(2)}) collective-permute-start(bf16[192,768]{1,0:T(8,128)(2,1)S(1)} %copy-done.29), channel_id=1, source_target_pairs={{0,2},{1,3},{2,0},{3,1},{4,6},{5,7},{6,4},{7,5},{8,10},{9,11},{10,... | collective-permute-start | bytes 884744 | tf_op jit(solution)/shard_map/ppermute | solution.py:369
  65.4 66.9 %collective-permute-start.12 = (bf16[192,768]{1,0:T(8,128)(2,1)S(1)}, bf16[192,768]{1,0:T(8,128)(2,1)}, u32[]{:S(2)}, u32[]{:S(2)}) collective-permute-start(bf16[192,768]{1,0:T(8,128)(2,1)S(1)} %copy-done.29), channel_id=1, source_target_pairs={{0,1},{1,0},{2,3},{3,2},{4,5},{5,4},{6,7},{7,6},{8,9},{9,8},{10,11... | collective-permute-start | bytes 884744 | tf_op jit(solution)/shard_map/ppermute | solution.py:369
  65.4 71.8 %collective-permute-start.16 = (bf16[768,768]{1,0:T(8,128)(2,1)}, bf16[768,768]{1,0:T(8,128)(2,1)}, u32[]{:S(2)}, u32[]{:S(2)}) collective-permute-start(bf16[768,768]{1,0:T(8,128)(2,1)} %e0.1), channel_id=1, source_target_pairs={{0,2},{1,3},{2,0},{3,1},{4,6},{5,7},{6,4},{7,5},{8,10},{9,11},{10,... | collective-permute-start | bytes 3538952 | tf_op jit(solution)/shard_map/ppermute | solution.py:369
  68.3 69.5 %collective-permute-start.19 = (bf16[768,768]{1,0:T(8,128)(2,1)}, bf16[768,768]{1,0:T(8,128)(2,1)}, u32[]{:S(2)}, u32[]{:S(2)}) collective-permute-start(bf16[768,768]{1,0:T(8,128)(2,1)} %r0.1), channel_id=1, source_target_pairs={{0,2},{1,3},{2,0},{3,1},{4,6},{5,7},{6,4},{7,5},{8,10},{9,11},{10,... | collective-permute-start | bytes 3538952 | tf_op jit(solution)/shard_map/ppermute | solution.py:369
  69.8 63.8 %collective-permute-start.14 = (bf16[192,768]{1,0:T(8,128)(2,1)}, bf16[192,768]{1,0:T(8,128)(2,1)}, u32[]{:S(2)}, u32[]{:S(2)}) collective-permute-start(bf16[192,768]{1,0:T(8,128)(2,1)} %collective-permute-done.13), channel_id=1, source_target_pairs={{0,1},{1,0},{2,3},{3,2},{4,5},{5,4},{6,7},{7,6},{8,9},{9,8},{10,11... | collective-permute-start | bytes 884744 | tf_op jit(solution)/shard_map/ppermute | solution.py:369
  131.8 6.0 %collective-permute-start.7 = (bf16[64,1024]{1,0:T(8,128)(2,1)}, bf16[64,1024]{1,0:T(8,128)(2,1)S(1)}, u32[]{:S(2)}, u32[]{:S(2)}) collective-permute-start(bf16[64,1024]{1,0:T(8,128)(2,1)} %get-tuple-element.142), channel_id=1, source_target_pairs={{0,1},{1,0},{2,3},{3,2},{4,5},{5,4},{6,7},{7,6},{8,9},{9,8},{10,11... | collective-permute-start | bytes 393224 | tf_op jit(solution)/shard_map/ppermute | solution.py:369
  132.3 6.0 %collective-permute-start.9 = (bf16[64,1024]{1,0:T(8,128)(2,1)}, bf16[64,1024]{1,0:T(8,128)(2,1)S(1)}, u32[]{:S(2)}, u32[]{:S(2)}) collective-permute-start(bf16[64,1024]{1,0:T(8,128)(2,1)} %get-tuple-element.141), channel_id=1, source_target_pairs={{0,2},{1,3},{2,0},{3,1},{4,6},{5,7},{6,4},{7,5},{8,10},{9,11},{10,... | collective-permute-start | bytes 393224 | tf_op jit(solution)/shard_map/ppermute | solution.py:369
  133.6 5.8 %collective-permute-start.6 = (bf16[128,1024]{1,0:T(8,128)(2,1)S(1)}, bf16[128,1024]{1,0:T(8,128)(2,1)S(1)}, u32[]{:S(2)}, u32[]{:S(2)}) collective-permute-start(bf16[128,1024]{1,0:T(8,128)(2,1)S(1)} %get-tuple-element.125), channel_id=1, source_target_pairs={{0,1},{1,0},{2,3},{3,2},{4,5},{5,4},{6,7},{7,6},{8,9},{9,8},{10,11... | collective-permute-start | bytes 786440 | tf_op jit(solution)/shard_map/ppermute | solution.py:369
  137.2 25.7 %collective-permute-start.15 = (bf16[768,768]{1,0:T(8,128)(2,1)}, bf16[768,768]{1,0:T(8,128)(2,1)S(1)}, u32[]{:S(2)}, u32[]{:S(2)}) collective-permute-start(bf16[768,768]{1,0:T(8,128)(2,1)} %e0.1), channel_id=1, source_target_pairs={{0,1},{1,0},{2,3},{3,2},{4,5},{5,4},{6,7},{7,6},{8,9},{9,8},{10,11... | collective-permute-start | bytes 3538952 | tf_op jit(solution)/shard_map/ppermute | solution.py:369
  137.7 26.1 %collective-permute-start.18 = (bf16[768,768]{1,0:T(8,128)(2,1)}, bf16[768,768]{1,0:T(8,128)(2,1)S(1)}, u32[]{:S(2)}, u32[]{:S(2)}) collective-permute-start(bf16[768,768]{1,0:T(8,128)(2,1)} %r0.1), channel_id=1, source_target_pairs={{0,1},{1,0},{2,3},{3,2},{4,5},{5,4},{6,7},{7,6},{8,9},{9,8},{10,11... | collective-permute-start | bytes 3538952 | tf_op jit(solution)/shard_map/ppermute | solution.py:369
  137.8 27.1 %collective-permute-start.17 = (bf16[768,768]{1,0:T(8,128)(2,1)}, bf16[768,768]{1,0:T(8,128)(2,1)S(1)}, u32[]{:S(2)}, u32[]{:S(2)}) collective-permute-start(bf16[768,768]{1,0:T(8,128)(2,1)} %collective-permute-done.16.e2), channel_id=1, source_target_pairs={{0,1},{1,0},{2,3},{3,2},{4,5},{5,4},{6,7},{7,6},{8,9},{9,8},{10,11... | collective-permute-start | bytes 3538952 | tf_op jit(solution)/shard_map/ppermute | solution.py:369
  138.3 27.7 %collective-permute-start.20 = (bf16[768,768]{1,0:T(8,128)(2,1)}, bf16[768,768]{1,0:T(8,128)(2,1)S(1)}, u32[]{:S(2)}, u32[]{:S(2)}) collective-permute-start(bf16[768,768]{1,0:T(8,128)(2,1)} %collective-permute-done.19.r2), channel_id=1, source_target_pairs={{0,1},{1,0},{2,3},{3,2},{4,5},{5,4},{6,7},{7,6},{8,9},{9,8},{10,11... | collective-permute-start | bytes 3538952 | tf_op jit(solution)/shard_map/ppermute | solution.py:369
  139.4 8.7 %collective-permute-start.8 = (bf16[128,1024]{1,0:T(8,128)(2,1)S(1)}, bf16[128,1024]{1,0:T(8,128)(2,1)S(1)}, u32[]{:S(2)}, u32[]{:S(2)}) collective-permute-start(bf16[128,1024]{1,0:T(8,128)(2,1)S(1)} %get-tuple-element.126), channel_id=1, source_target_pairs={{0,2},{1,3},{2,0},{3,1},{4,6},{5,7},{6,4},{7,5},{8,10},{9,11},{10,... | collective-permute-start | bytes 786440 | tf_op jit(solution)/shard_map/ppermute | solution.py:369
  148.1 8.6 %collective-permute-start.10 = (bf16[128,1024]{1,0:T(8,128)(2,1)S(1)}, bf16[128,1024]{1,0:T(8,128)(2,1)S(1)}, u32[]{:S(2)}, u32[]{:S(2)}) collective-permute-start(bf16[128,1024]{1,0:T(8,128)(2,1)S(1)} %get-tuple-element.123), channel_id=1, source_target_pairs={{0,3},{1,2},{2,1},{3,0},{4,7},{5,6},{6,5},{7,4},{8,11},{9,10},{10,... | collective-permute-start | bytes 786440 | tf_op jit(solution)/shard_map/ppermute | solution.py:369
  156.7 5.5 collective-permute-start.11
  237.0 138.5 %collective-permute-start.55 = (bf16[768,768]{1,0:T(8,128)(2,1)}, bf16[768,768]{1,0:T(8,128)(2,1)}, u32[]{:S(2)}, u32[]{:S(2)}) collective-permute-start(bf16[768,768]{1,0:T(8,128)(2,1)} %fusion.36), channel_id=1, source_target_pairs={{0,1},{1,0},{2,3},{3,2},{4,5},{5,4},{6,7},{7,6},{8,9},{9,8},{10,11... | collective-permute-start | bytes 3538952 | tf_op jit(solution)/shard_map/ppermute | solution.py:369
  239.9 8.3 %collective-permute-start.24 = (bf16[64,1024]{1,0:T(8,128)(2,1)S(1)}, bf16[64,1024]{1,0:T(8,128)(2,1)S(1)}, u32[]{:S(2)}, u32[]{:S(2)}) collective-permute-start(bf16[64,1024]{1,0:T(8,128)(2,1)S(1)} %get-tuple-element.102), channel_id=1, source_target_pairs={{0,3},{1,2},{2,1},{3,0},{4,7},{5,6},{6,5},{7,4},{8,11},{9,10},{10,... | collective-permute-start | bytes 393224 | tf_op jit(solution)/shard_map/ppermute | solution.py:369
  241.2 7.6 %collective-permute-start.25 = (bf16[64,1024]{1,0:T(8,128)(2,1)S(1)}, bf16[64,1024]{1,0:T(8,128)(2,1)S(1)}, u32[]{:S(2)}, u32[]{:S(2)}) collective-permute-start(bf16[64,1024]{1,0:T(8,128)(2,1)S(1)} %get-tuple-element.101), channel_id=1, source_target_pairs={{0,2},{1,3},{2,0},{3,1},{4,6},{5,7},{6,4},{7,5},{8,10},{9,11},{10,... | collective-permute-start | bytes 393224 | tf_op jit(solution)/shard_map/ppermute | solution.py:369
  241.7 7.2 %collective-permute-start.26 = (bf16[64,1024]{1,0:T(8,128)(2,1)S(1)}, bf16[64,1024]{1,0:T(8,128)(2,1)S(1)}, u32[]{:S(2)}, u32[]{:S(2)}) collective-permute-start(bf16[64,1024]{1,0:T(8,128)(2,1)S(1)} %get-tuple-element.100), channel_id=1, source_target_pairs={{0,1},{1,0},{2,3},{3,2},{4,5},{5,4},{6,7},{7,6},{8,9},{9,8},{10,11... | collective-permute-start | bytes 393224 | tf_op jit(solution)/shard_map/ppermute | solution.py:369
  241.8 39.9 %collective-permute-start.21 = (bf16[128,1024]{1,0:T(8,128)(2,1)S(1)}, bf16[128,1024]{1,0:T(8,128)(2,1)S(1)}, u32[]{:S(2)}, u32[]{:S(2)}) collective-permute-start(bf16[128,1024]{1,0:T(8,128)(2,1)S(1)} %bitcast.219), channel_id=1, source_target_pairs={{0,3},{1,2},{2,1},{3,0},{4,7},{5,6},{6,5},{7,4},{8,11},{9,10},{10,... | collective-permute-start | bytes 786440 | tf_op jit(solution)/shard_map/ppermute | solution.py:369
  248.2 33.7 %collective-permute-start.22 = (bf16[128,1024]{1,0:T(8,128)(2,1)S(1)}, bf16[128,1024]{1,0:T(8,128)(2,1)S(1)}, u32[]{:S(2)}, u32[]{:S(2)}) collective-permute-start(bf16[128,1024]{1,0:T(8,128)(2,1)S(1)} %bitcast.218), channel_id=1, source_target_pairs={{0,2},{1,3},{2,0},{3,1},{4,6},{5,7},{6,4},{7,5},{8,10},{9,11},{10,... | collective-permute-start | bytes 786440 | tf_op jit(solution)/shard_map/ppermute | solution.py:369
  248.8 33.1 %collective-permute-start.23 = (bf16[128,1024]{1,0:T(8,128)(2,1)S(1)}, bf16[128,1024]{1,0:T(8,128)(2,1)S(1)}, u32[]{:S(2)}, u32[]{:S(2)}) collective-permute-start(bf16[128,1024]{1,0:T(8,128)(2,1)S(1)} %bitcast.217), channel_id=1, source_target_pairs={{0,1},{1,0},{2,3},{3,2},{4,5},{5,4},{6,7},{7,6},{8,9},{9,8},{10,11... | collective-permute-start | bytes 786440 | tf_op jit(solution)/shard_map/ppermute | solution.py:369
  360.7 12.6 %collective-permute-start.35 = (bf16[384,576]{0,1:T(8,128)(2,1)S(1)}, bf16[384,576]{0,1:T(8,128)(2,1)S(1)}, u32[]{:S(2)}, u32[]{:S(2)}) collective-permute-start(bf16[384,576]{0,1:T(8,128)(2,1)S(1)} %bitcast.208), channel_id=1, source_target_pairs={{0,4},{4,0},{8,12},{12,8},{16,20},{20,16},{24,28},{28,24},{1,5},{5... | collective-permute-start | bytes 1327112 | tf_op jit(solution)/shard_map/ppermute | solution.py:369
  362.3 37.8 %collective-permute-start.54 = (bf16[768,768]{1,0:T(8,128)(2,1)}, bf16[768,768]{1,0:T(8,128)(2,1)}, u32[]{:S(2)}, u32[]{:S(2)}) collective-permute-start(bf16[768,768]{1,0:T(8,128)(2,1)} %fusion.30), channel_id=1, source_target_pairs={{0,1},{1,0},{2,3},{3,2},{4,5},{5,4},{6,7},{7,6},{8,9},{9,8},{10,11... | collective-permute-start | bytes 3538952 | tf_op jit(solution)/shard_map/ppermute | solution.py:369
  362.5 29.6 %collective-permute-start.44 = (bf16[960,768]{1,0:T(8,128)(2,1)}, bf16[960,768]{1,0:T(8,128)(2,1)}, u32[]{:S(2)}, u32[]{:S(2)}) collective-permute-start(bf16[960,768]{1,0:T(8,128)(2,1)} %pad_maximum_fusion.3), channel_id=1, source_target_pairs={{0,1},{1,0},{2,3},{3,2},{4,5},{5,4},{6,7},{7,6},{8,9},{9,8},{10,11... | collective-permute-start | bytes 4423688 | tf_op jit(solution)/shard_map/ppermute | solution.py:369
  366.6 29.0 %collective-permute-start.28 = (bf16[1024,768]{1,0:T(8,128)(2,1)}, bf16[1024,768]{1,0:T(8,128)(2,1)}, u32[]{:S(2)}, u32[]{:S(2)}) collective-permute-start(bf16[1024,768]{1,0:T(8,128)(2,1)} %convolution_convert_fusion), channel_id=1, source_target_pairs={{0,1},{1,0},{2,3},{3,2},{4,5},{5,4},{6,7},{7,6},{8,9},{9,8},{10,11... | collective-permute-start | bytes 4718600 | tf_op jit(solution)/shard_map/ppermute | solution.py:369
  373.8 5.4 collective-permute-start.36
  375.5 11.1 %collective-permute-start.37 = (bf16[96,576]{1,0:T(8,128)(2,1)S(1)}, bf16[96,576]{1,0:T(8,128)(2,1)S(1)}, u32[]{:S(2)}, u32[]{:S(2)}) collective-permute-start(bf16[96,576]{1,0:T(8,128)(2,1)S(1)} %get-tuple-element.131), channel_id=1, source_target_pairs={{0,16},{4,20},{8,24},{12,28},{16,0},{20,4},{24,8},{28,12},{1,17},{... | collective-permute-start | bytes 331784 | tf_op jit(solution)/shard_map/ppermute | solution.py:369
  379.2 12.9 %collective-permute-start.38 = (bf16[96,576]{1,0:T(8,128)(2,1)S(1)}, bf16[96,576]{1,0:T(8,128)(2,1)S(1)}, u32[]{:S(2)}, u32[]{:S(2)}) collective-permute-start(bf16[96,576]{1,0:T(8,128)(2,1)S(1)} %get-tuple-element.130), channel_id=1, source_target_pairs={{0,24},{4,28},{8,16},{12,20},{16,8},{20,12},{24,0},{28,4},{1,25},{... | collective-permute-start | bytes 331784 | tf_op jit(solution)/shard_map/ppermute | solution.py:369
  386.5 25.9 %collective-permute-start.56 = (bf16[768,768]{1,0:T(8,128)(2,1)S(1)}, bf16[768,768]{1,0:T(8,128)(2,1)S(1)}, u32[]{:S(2)}, u32[]{:S(2)}) collective-permute-start(bf16[768,768]{1,0:T(8,128)(2,1)S(1)} %add_convert_fusion.3), channel_id=1, source_target_pairs={{0,2},{1,3},{2,0},{3,1},{4,6},{5,7},{6,4},{7,5},{8,10},{9,11},{10,... | collective-permute-start | bytes 3538952 | tf_op jit(solution)/shard_map/ppermute | solution.py:369
  392.1 45.5 %collective-permute-start.43 = (bf16[960,768]{1,0:T(8,128)(2,1)}, bf16[960,768]{1,0:T(8,128)(2,1)}, u32[]{:S(2)}, u32[]{:S(2)}) collective-permute-start(bf16[960,768]{1,0:T(8,128)(2,1)} %pad_maximum_fusion.1), channel_id=1, source_target_pairs={{0,1},{1,0},{2,3},{3,2},{4,5},{5,4},{6,7},{7,6},{8,9},{9,8},{10,11... | collective-permute-start | bytes 4423688 | tf_op jit(solution)/shard_map/ppermute | solution.py:369
  392.1 58.6 %collective-permute-start.27 = (bf16[1024,768]{1,0:T(8,128)(2,1)}, bf16[1024,768]{1,0:T(8,128)(2,1)}, u32[]{:S(2)}, u32[]{:S(2)}) collective-permute-start(bf16[1024,768]{1,0:T(8,128)(2,1)} %convolution_convert_fusion.2), channel_id=1, source_target_pairs={{0,1},{1,0},{2,3},{3,2},{4,5},{5,4},{6,7},{7,6},{8,9},{9,8},{10,11... | collective-permute-start | bytes 4718600 | tf_op jit(solution)/shard_map/ppermute | solution.py:369
  395.6 20.0 %collective-permute-start.39 = (bf16[96,576]{1,0:T(8,128)(2,1)S(1)}, bf16[96,576]{1,0:T(8,128)(2,1)S(1)}, u32[]{:S(2)}, u32[]{:S(2)}) collective-permute-start(bf16[96,576]{1,0:T(8,128)(2,1)S(1)} %fusion.85), channel_id=1, source_target_pairs={{0,24},{4,28},{8,16},{12,20},{16,8},{20,12},{24,0},{28,4},{1,25},{... | collective-permute-start | bytes 331784 | tf_op jit(solution)/shard_map/ppermute | solution.py:369
  400.1 15.7 %collective-permute-start.40 = (bf16[96,576]{1,0:T(8,128)(2,1)S(1)}, bf16[96,576]{1,0:T(8,128)(2,1)S(1)}, u32[]{:S(2)}, u32[]{:S(2)}) collective-permute-start(bf16[96,576]{1,0:T(8,128)(2,1)S(1)} %fusion.85), channel_id=1, source_target_pairs={{0,16},{4,20},{8,24},{12,28},{16,0},{20,4},{24,8},{28,12},{1,17},{... | collective-permute-start | bytes 331784 | tf_op jit(solution)/shard_map/ppermute | solution.py:369
  412.5 35.5 %collective-permute-start.45 = (bf16[960,768]{1,0:T(8,128)(2,1)}, bf16[960,768]{1,0:T(8,128)(2,1)}, u32[]{:S(2)}, u32[]{:S(2)}) collective-permute-start(bf16[960,768]{1,0:T(8,128)(2,1)} %add_convert_fusion.2), channel_id=1, source_target_pairs={{0,2},{1,3},{2,0},{3,1},{4,6},{5,7},{6,4},{7,5},{8,10},{9,11},{10,... | collective-permute-start | bytes 4423688 | tf_op jit(solution)/shard_map/ppermute | solution.py:369
  415.7 4.9 collective-permute-start.41
  415.8 62.1 %collective-permute-start.29 = (bf16[1024,768]{1,0:T(8,128)(2,1)}, bf16[1024,768]{1,0:T(8,128)(2,1)}, u32[]{:S(2)}, u32[]{:S(2)}) collective-permute-start(bf16[1024,768]{1,0:T(8,128)(2,1)} %add_convert_fusion), channel_id=1, source_target_pairs={{0,2},{1,3},{2,0},{3,1},{4,6},{5,7},{6,4},{7,5},{8,10},{9,11},{10,... | collective-permute-start | bytes 4718600 | tf_op jit(solution)/shard_map/ppermute | solution.py:369
  421.3 13.4 %collective-permute-start.57 = (bf16[384,768]{1,0:T(8,128)(2,1)}, bf16[384,768]{1,0:T(8,128)(2,1)}, u32[]{:S(2)}, u32[]{:S(2)}) collective-permute-start(bf16[384,768]{1,0:T(8,128)(2,1)} %fusion.68), channel_id=1, source_target_pairs={{0,4},{4,0},{8,12},{12,8},{16,20},{20,16},{24,28},{28,24},{1,5},{5... | collective-permute-start | bytes 1769480 | tf_op jit(solution)/shard_map/ppermute | solution.py:369
  434.7 110.5 %collective-permute-start.42 = (bf16[384,576]{1,0:T(8,128)(2,1)}, bf16[384,576]{1,0:T(8,128)(2,1)}, u32[]{:S(2)}, u32[]{:S(2)}) collective-permute-start(bf16[384,576]{1,0:T(8,128)(2,1)} %pad_maximum_fusion.7), channel_id=1, source_target_pairs={{0,4},{4,0},{8,12},{12,8},{16,20},{20,16},{24,28},{28,24},{1,5},{5... | collective-permute-start | bytes 1327112 | tf_op jit(solution)/shard_map/ppermute | solution.py:369
  437.5 56.7 %collective-permute-start.58 = (bf16[96,768]{1,0:T(8,128)(2,1)S(1)}, bf16[96,768]{1,0:T(8,128)(2,1)S(1)}, u32[]{:S(2)}, u32[]{:S(2)}) collective-permute-start(bf16[96,768]{1,0:T(8,128)(2,1)S(1)} %get-tuple-element.114), channel_id=1, source_target_pairs={{0,8},{4,12},{8,0},{12,4},{16,24},{20,28},{24,16},{28,20},{1,9},{5... | collective-permute-start | bytes 442376 | tf_op jit(solution)/shard_map/ppermute | solution.py:369
  448.0 46.3 %collective-permute-start.59 = (bf16[96,768]{1,0:T(8,128)(2,1)S(1)}, bf16[96,768]{1,0:T(8,128)(2,1)S(1)}, u32[]{:S(2)}, u32[]{:S(2)}) collective-permute-start(bf16[96,768]{1,0:T(8,128)(2,1)S(1)} %get-tuple-element.116), channel_id=1, source_target_pairs={{0,16},{4,20},{8,24},{12,28},{16,0},{20,4},{24,8},{28,12},{1,17},{... | collective-permute-start | bytes 442376 | tf_op jit(solution)/shard_map/ppermute | solution.py:369
  450.8 43.6 %collective-permute-start.60 = (bf16[96,768]{1,0:T(8,128)(2,1)S(1)}, bf16[96,768]{1,0:T(8,128)(2,1)S(1)}, u32[]{:S(2)}, u32[]{:S(2)}) collective-permute-start(bf16[96,768]{1,0:T(8,128)(2,1)S(1)} %get-tuple-element.115), channel_id=1, source_target_pairs={{0,24},{4,28},{8,16},{12,20},{16,8},{20,12},{24,0},{28,4},{1,25},{... | collective-permute-start | bytes 442376 | tf_op jit(solution)/shard_map/ppermute | solution.py:369
  477.9 14.7 %collective-permute-start.46 = (bf16[480,768]{1,0:T(8,128)(2,1)S(1)}, bf16[480,768]{1,0:T(8,128)(2,1)S(1)}, u32[]{:S(2)}, u32[]{:S(2)}) collective-permute-start(bf16[480,768]{1,0:T(8,128)(2,1)S(1)} %fusion.67), channel_id=1, source_target_pairs={{0,4},{4,0},{8,12},{12,8},{16,20},{20,16},{24,28},{28,24},{1,5},{5... | collective-permute-start | bytes 2211848 | tf_op jit(solution)/shard_map/ppermute | solution.py:369
  492.6 7.1 %collective-permute-start.30 = (f32[6,768]{1,0:T(8,128)S(1)}, f32[6,768]{1,0:T(8,128)S(1)}, u32[]{:S(2)}, u32[]{:S(2)}) collective-permute-start(f32[6,768]{1,0:T(8,128)S(1)} %stack.9), channel_id=1, source_target_pairs={{0,1},{1,0},{2,3},{3,2},{4,5},{5,4},{6,7},{7,6},{8,9},{9,8},{10,11... | collective-permute-start | bytes 55304 | tf_op jit(solution)/shard_map/ppermute | solution.py:369
  494.2 9.4 %collective-permute-start.47 = (bf16[120,768]{1,0:T(8,128)(2,1)S(1)}, bf16[120,768]{1,0:T(8,128)(2,1)S(1)}, u32[]{:S(2)}, u32[]{:S(2)}) collective-permute-start(bf16[120,768]{1,0:T(8,128)(2,1)S(1)} %get-tuple-element.109), channel_id=1, source_target_pairs={{0,8},{4,12},{8,0},{12,4},{16,24},{20,28},{24,16},{28,20},{1,9},{5... | collective-permute-start | bytes 552968 | tf_op jit(solution)/shard_map/ppermute | solution.py:369
  494.3 22.7 %collective-permute-start.48 = (bf16[120,768]{1,0:T(8,128)(2,1)S(1)}, bf16[120,768]{1,0:T(8,128)(2,1)S(1)}, u32[]{:S(2)}, u32[]{:S(2)}) collective-permute-start(bf16[120,768]{1,0:T(8,128)(2,1)S(1)} %get-tuple-element.111), channel_id=1, source_target_pairs={{0,16},{4,20},{8,24},{12,28},{16,0},{20,4},{24,8},{28,12},{1,17},{... | collective-permute-start | bytes 552968 | tf_op jit(solution)/shard_map/ppermute | solution.py:369
  494.4 22.7 %collective-permute-start.49 = (bf16[120,768]{1,0:T(8,128)(2,1)S(1)}, bf16[120,768]{1,0:T(8,128)(2,1)S(1)}, u32[]{:S(2)}, u32[]{:S(2)}) collective-permute-start(bf16[120,768]{1,0:T(8,128)(2,1)S(1)} %get-tuple-element.110), channel_id=1, source_target_pairs={{0,24},{4,28},{8,16},{12,20},{16,8},{20,12},{24,0},{28,4},{1,25},{... | collective-permute-start | bytes 552968 | tf_op jit(solution)/shard_map/ppermute | solution.py:369
  499.7 19.0 %collective-permute-start.61 = (bf16[96,768]{1,0:T(8,128)(2,1)S(1)}, bf16[96,768]{1,0:T(8,128)(2,1)S(1)}, u32[]{:S(2)}, u32[]{:S(2)}) collective-permute-start(bf16[96,768]{1,0:T(8,128)(2,1)S(1)} %fusion.77), channel_id=1, source_target_pairs={{0,24},{4,28},{8,16},{12,20},{16,8},{20,12},{24,0},{28,4},{1,25},{... | collective-permute-start | bytes 442376 | tf_op jit(solution)/shard_map/ppermute | solution.py:369
  503.6 27.7 %collective-permute-start.62 = (bf16[96,768]{1,0:T(8,128)(2,1)S(1)}, bf16[96,768]{1,0:T(8,128)(2,1)S(1)}, u32[]{:S(2)}, u32[]{:S(2)}) collective-permute-start(bf16[96,768]{1,0:T(8,128)(2,1)S(1)} %fusion.77), channel_id=1, source_target_pairs={{0,16},{4,20},{8,24},{12,28},{16,0},{20,4},{24,8},{28,12},{1,17},{... | collective-permute-start | bytes 442376 | tf_op jit(solution)/shard_map/ppermute | solution.py:369
  517.0 14.2 %collective-permute-start.63 = (bf16[96,768]{1,0:T(8,128)(2,1)S(1)}, bf16[96,768]{1,0:T(8,128)(2,1)S(1)}, u32[]{:S(2)}, u32[]{:S(2)}) collective-permute-start(bf16[96,768]{1,0:T(8,128)(2,1)S(1)} %fusion.77), channel_id=1, source_target_pairs={{0,8},{4,12},{8,0},{12,4},{16,24},{20,28},{24,16},{28,20},{1,9},{5... | collective-permute-start | bytes 442376 | tf_op jit(solution)/shard_map/ppermute | solution.py:369
  517.0 16.2 %collective-permute-start.31 = (f32[6,768]{1,0:T(8,128)S(1)}, f32[6,768]{1,0:T(8,128)S(1)}, u32[]{:S(2)}, u32[]{:S(2)}) collective-permute-start(f32[6,768]{1,0:T(8,128)S(1)} %add.226), channel_id=1, source_target_pairs={{0,2},{1,3},{2,0},{3,1},{4,6},{5,7},{6,4},{7,5},{8,10},{9,11},{10,... | collective-permute-start | bytes 55304 | tf_op jit(solution)/shard_map/ppermute | solution.py:369
  518.7 20.0 %collective-permute-start.50 = (bf16[120,768]{1,0:T(8,128)(2,1)S(1)}, bf16[120,768]{1,0:T(8,128)(2,1)S(1)}, u32[]{:S(2)}, u32[]{:S(2)}) collective-permute-start(bf16[120,768]{1,0:T(8,128)(2,1)S(1)} %fusion.74), channel_id=1, source_target_pairs={{0,24},{4,28},{8,16},{12,20},{16,8},{20,12},{24,0},{28,4},{1,25},{... | collective-permute-start | bytes 552968 | tf_op jit(solution)/shard_map/ppermute | solution.py:369
  531.3 11.4 %collective-permute-start.51 = (bf16[120,768]{1,0:T(8,128)(2,1)S(1)}, bf16[120,768]{1,0:T(8,128)(2,1)S(1)}, u32[]{:S(2)}, u32[]{:S(2)}) collective-permute-start(bf16[120,768]{1,0:T(8,128)(2,1)S(1)} %fusion.74), channel_id=1, source_target_pairs={{0,16},{4,20},{8,24},{12,28},{16,0},{20,4},{24,8},{28,12},{1,17},{... | collective-permute-start | bytes 552968 | tf_op jit(solution)/shard_map/ppermute | solution.py:369
  531.3 11.4 %collective-permute-start.52 = (bf16[120,768]{1,0:T(8,128)(2,1)S(1)}, bf16[120,768]{1,0:T(8,128)(2,1)S(1)}, u32[]{:S(2)}, u32[]{:S(2)}) collective-permute-start(bf16[120,768]{1,0:T(8,128)(2,1)S(1)} %fusion.74), channel_id=1, source_target_pairs={{0,8},{4,12},{8,0},{12,4},{16,24},{20,28},{24,16},{28,20},{1,9},{5... | collective-permute-start | bytes 552968 | tf_op jit(solution)/shard_map/ppermute | solution.py:369
  533.3 3.9 collective-permute-start.32
  537.2 16.5 %collective-permute-start.64 = (bf16[384,768]{1,0:T(8,128)(2,1)}, bf16[384,768]{1,0:T(8,128)(2,1)}, u32[]{:S(2)}, u32[]{:S(2)}) collective-permute-start(bf16[384,768]{1,0:T(8,128)(2,1)} %pad_maximum_fusion.6), channel_id=1, source_target_pairs={{0,4},{4,0},{8,12},{12,8},{16,20},{20,16},{24,28},{28,24},{1,5},{5... | collective-permute-start | bytes 1769480 | tf_op jit(solution)/shard_map/ppermute | solution.py:369
  538.7 8.3 %collective-permute-start.33 = (f32[6,768]{1,0:T(8,128)S(1)}, f32[6,768]{1,0:T(8,128)S(1)}, u32[]{:S(2)}, u32[]{:S(2)}) collective-permute-start(f32[6,768]{1,0:T(8,128)S(1)} %add.228), channel_id=1, source_target_pairs={{0,8},{4,12},{8,0},{12,4},{16,24},{20,28},{24,16},{28,20},{1,9},{5... | collective-permute-start | bytes 55304 | tf_op jit(solution)/shard_map/ppermute | solution.py:369
  543.7 22.6 %collective-permute-start.53 = (bf16[480,768]{1,0:T(8,128)(2,1)}, bf16[480,768]{1,0:T(8,128)(2,1)}, u32[]{:S(2)}, u32[]{:S(2)}) collective-permute-start(bf16[480,768]{1,0:T(8,128)(2,1)} %pad_maximum_fusion.5), channel_id=1, source_target_pairs={{0,4},{4,0},{8,12},{12,8},{16,20},{20,16},{24,28},{28,24},{1,5},{5... | collective-permute-start | bytes 2211848 | tf_op jit(solution)/shard_map/ppermute | solution.py:369
  547.0 4.8 collective-permute-start.34
  (66 other events, 607.3 us)

commit v4 on v3

--- a/solution.py
+++ b/solution.py
@@ -23,6 +23,13 @@
 
 def dot_f32(a, b):
     return jnp.dot(a, b, preferred_element_type=f32)
+
+
+def split3(x):
+    high = x.astype(bf16)
+    rest = x - high.astype(f32)
+    middle = rest.astype(bf16)
+    return high, middle, (rest - middle.astype(f32)).astype(bf16)
 
 
 def fwd_kernel(q_ref, k_ref, v_ref, start_ref, bias_ref, o_ref, wide_ref, lse_ref, keys_ref):
@@ -99,30 +106,45 @@
     )(qkv, qkv, qkv, doc_start, key_bias)
 
 
+SMEM_SPEC = pl.BlockSpec(memory_space=pltpu.SMEM)
 KEYS = 512
-SPAN = 512
+SPAN = 1024
 
 
 def bwd_kernel(
-    q_ref, k_ref, v_ref, g_ref, wide_ref, lse_ref, start_ref, bias_ref,
-    out_ref, qn, kn, vn, gn, inner, dq,
+    last_ref, q_ref, k_ref, v_ref, g_ref, wide_ref, lse_ref, start_ref, bias_ref,
+    out_ref, qn, kn, vn, gn, qx, gx, dq,
 ):
     qn[...] = q_ref[0].T
-    kn[...] = k_ref[0].T
-    vn[...] = v_ref[0].T
     gn[...] = g_ref[0].T
-    inner[...] = jnp.sum(g_ref[0].astype(f32) * wide_ref[0], 0, keepdims=True)
+    ones = jnp.where(lax.broadcasted_iota(jnp.int32, (GLEN, HD), 1) < 3, 1.0, 0.0).astype(bf16)
+    kn[:, :HD] = k_ref[0].T
+    kn[:, HD:] = ones
+    vn[:, :HD] = v_ref[0].T
+    vn[:, HD:] = ones
+    zeros = jnp.zeros((HD - 16, GLEN), bf16)
+    row = lax.broadcasted_iota(jnp.int32, (16, GLEN), 0)
+
+    def extend(ref, head, tail):
+        ref[0:HD, :] = head
+        a, b, c = (jnp.broadcast_to(x.astype(f32), (16, GLEN)) for x in split3(-tail))
+        ref[HD : HD + 16, :] = jnp.where(
+            row == 0, a, jnp.where(row == 1, b, jnp.where(row == 2, c, 0.0))
+        ).astype(bf16)
+        ref[HD + 16 :, :] = zeros
+
+    extend(qx, q_ref[0], lse_ref[0])
+    extend(gx, g_ref[0], jnp.sum(g_ref[0].astype(f32) * wide_ref[0], 0, keepdims=True))
     dq[...] = jnp.zeros_like(dq)
 
     def block(key_off, key_span, off, span, mask):
         rows = pl.ds(off, span)
         keys = pl.ds(key_off, key_span)
-        s = dot_f32(kn[keys, :], q_ref[0, :, rows])
+        s = dot_f32(kn[keys, :], qx[:, rows])
         if mask is not None:
             s = mask(s)
-        p = jnp.exp(s - lse_ref[0, :, rows])
-        dp = dot_f32(vn[keys, :], g_ref[0, :, rows])
-        ds = (p * (dp - inner[:, rows])).astype(bf16)
+        p = jnp.exp(s)
+        ds = (p * dot_f32(vn[keys, :], gx[:, rows])).astype(bf16)
         dv = dot_f32(p.astype(bf16), gn[rows, :])
         dk = dot_f32(ds, qn[rows, :])
         dq[:, rows] += dot_f32(k_ref[0, :, keys], ds)
@@ -155,8 +177,8 @@
             dk, dv = block(key_off, KEYS, off, CONT, mask)
             return acc[0] + dk, acc[1] + dv
 
-        last = jnp.minimum((key_off + KEYS + DOC_MAX - 2) // CONT + 1, PROMPT // CONT)
-        acc = lax.fori_loop(key_off // CONT, last, prompt, acc)
+        first = key_off // CONT
+        acc = lax.fori_loop(first, last_ref[first + KEYS // CONT - 1], prompt, acc)
         emit(key_off, KEYS, *acc)
         return carry
 
@@ -179,9 +201,10 @@
     out_ref[0] = (dq[...] * SCALE).astype(bf16)
 
 
-def attn_bwd(head, grads, qkv, adj, wide, lse, doc_start, key_bias):
+def attn_bwd(head, grads, bounds, qkv, adj, wide, lse, doc_start, key_bias):
     heads = qkv.shape[0] // 3
     specs = [
+        SMEM_SPEC,
         head_spec(head),
         head_spec(head + heads),
         head_spec(head + 2 * heads),
@@ -191,22 +214,29 @@
         whole(1, PROMPT),
         whole(GLEN - PROMPT, 128),
     ]
-    args = [qkv, qkv, qkv, adj, wide, lse, doc_start, key_bias]
+    args = [bounds, qkv, qkv, qkv, adj, wide, lse, doc_start, key_bias]
     kernel = bwd_kernel
     aliases = {}
     if grads is not None:
         specs.append(pl.BlockSpec(memory_space=pl.ANY))
         aliases = {len(args): 0}
         args.append(grads)
-        kernel = lambda *refs: bwd_kernel(*refs[:8], *refs[9:])
+        kernel = lambda *refs: bwd_kernel(*refs[:9], *refs[10:])
     return pl.pallas_call(
         kernel,
         grid=(1,),
         in_specs=specs,
         out_specs=pl.BlockSpec((3, None, HD, GLEN), lambda i: (0, head, 0, 0)),
         out_shape=jax.ShapeDtypeStruct((3, heads, HD, GLEN), bf16),
-        scratch_shapes=[pltpu.VMEM((GLEN, HD), bf16)] * 4
-        + [pltpu.VMEM((1, GLEN), f32), pltpu.VMEM((HD, GLEN), f32)],
+        scratch_shapes=[
+            pltpu.VMEM((GLEN, HD), bf16),
+            pltpu.VMEM((GLEN, 2 * HD), bf16),
+            pltpu.VMEM((GLEN, 2 * HD), bf16),
+            pltpu.VMEM((GLEN, HD), bf16),
+            pltpu.VMEM((2 * HD, GLEN), bf16),
+            pltpu.VMEM((2 * HD, GLEN), bf16),
+            pltpu.VMEM((HD, GLEN), f32),
+        ],
         input_output_aliases=aliases,
         cost_estimate=pl.CostEstimate(flops=30_000_000_000, transcendentals=0, bytes_accessed=8_000_000),
         name="attn_bwd",
@@ -369,11 +399,9 @@
     return lax.ppermute(x, axis, [(i, i ^ bit) for i in range(size)])
 
 
-def butterfly(x, axis):
-    bit = 1
-    while bit < lax.axis_size(axis):
-        x = x + swap(x, bit, axis)
-        bit *= 2
+def sum_small(x, axis):
+    for shift, members in levels(axis):
+        x = sum((swap(x, j << shift, axis) for j in range(1, members)), x)
     return x
 
 
@@ -453,11 +481,13 @@
     slots = [t ^ k for k in range(4)]
     valid = valid_mask[0]
     docs = prompt_docs[0]
-    valid_total = butterfly(jnp.sum(valid).astype(f32).reshape(1, 1), "dp")[0, 0]
+    valid_total = sum_small(jnp.sum(valid).astype(f32).reshape(1, 1), "dp")[0, 0]
     divisor = valid_total * D
     doc_start = jnp.zeros_like(docs)
     for v in range(3):
         doc_start = doc_start + jnp.where(docs > v, jnp.sum((docs == v).astype(jnp.int32)), 0)
+    edges = jnp.arange(CONT, PROMPT + 1, CONT, dtype=jnp.int32)
+    last_block = (jnp.sum((doc_start[None, :] < edges[:, None]).astype(jnp.int32), 1) + CONT - 1) // CONT
     doc_start = doc_start[None, :]
     key_bias = jnp.broadcast_to(jnp.where(valid == 1, 0.0, NEG).astype(f32)[:, None], (GLEN - PROMPT, 128))
     row_valid = lax.dynamic_slice_in_dim(
@@ -465,7 +495,7 @@
     )[:, None]
 
     hidden_in = layer_input.astype(f32) + pass_embed
-    first_affine, first_pull = jax.vjp(affine_norm, hidden_in, first_gain, first_shift)
+    first_affine = affine_norm(hidden_in, first_gain, first_shift)
     first_blocks = gather4(first_affine.astype(bf16))
     in_matrix = project_in.reshape(D, 3 * width)
 
@@ -525,33 +555,38 @@
 
     proj_adj = None
     for h in range(heads):
-        proj_adj = attn_bwd(h, proj_adj, qkv, adj_heads[h], *saved[h][1:], doc_start, key_bias)
+        proj_adj = attn_bwd(h, proj_adj, last_block, qkv, adj_heads[h], *saved[h][1:], doc_start, key_bias)
     proj_adj = proj_adj.reshape(3 * width, GLEN)
     pieces = [lax.dynamic_slice(proj_adj, (0, slots[k] * rows), (3 * width, rows)) for k in range(4)]
-    first_parts = [dot(pieces[k], in_matrix, 0, 1).astype(bf16) for k in range(4)]
-    first_adj = scatter4(first_parts)
-    in_proj_grad = 0.0
+    first_parts = []
     for k in range(4):
+        first_parts.append(dot(pieces[k], in_matrix, 0, 1).astype(bf16))
+    near3 = swap(first_parts[3], 1)
+    near1 = swap(first_parts[1], 1)
+    across = (first_parts[2].astype(f32) + near3.astype(f32)).astype(bf16)
+    far = swap(across, 2)
+    in_proj_grad = dot(first_blocks[0], pieces[0], 0, 1)
+    for k in range(1, 4):
         in_proj_grad = in_proj_grad + dot(first_blocks[k], pieces[k], 0, 1)
     in_proj_grad = sum_all(in_proj_grad, "dp")
-    hidden_part, first_gain_part, first_shift_part = first_pull(first_adj)
-    input_adj = middle_adj + hidden_part
-    embed_part = jnp.sum(input_adj, axis=0)
+    input_gradient, embed_part, first_gain_part, first_shift_part = final(
+        layer_input, pass_embed[None], first_gain[None], first_parts[0], near1, far, middle_adj
+    )
     small = jnp.stack(
         [
-            embed_part,
-            first_gain_part,
-            first_shift_part,
+            embed_part[0],
+            first_gain_part[0],
+            first_shift_part[0],
             second_gain_part[0],
             second_shift_part[0],
             squares[0],
         ]
     )
-    small = butterfly(butterfly(small, "tensor"), "dp")
+    small = sum_small(sum_small(small, "tensor"), "dp")
     return (
         layer_out,
         jnp.sum(small[5]) / divisor,
-        input_adj.astype(bf16),
+        input_gradient,
         small[0],
         small[1],
         small[2],
@@ -562,6 +597,38 @@
         other_grad[:D],
         reduce_grad,
     )
+
+
+def final_kernel(
+    x_ref, embed_ref, gain_ref, part_ref, near_ref, far_ref, adj_ref, out_ref, embed_out, gain_out, shift_out
+):
+    norm, rstd = row_norm(x_ref[...].astype(f32) + embed_ref[...])
+    first = part_ref[...].astype(f32) + near_ref[...].astype(f32) + far_ref[...].astype(f32)
+    input_adj = adj_ref[...] + norm_pull(norm, rstd, first * gain_ref[...])
+    out_ref[...] = input_adj.astype(bf16)
+
+    @pl.when(pl.program_id(0) == 0)
+    def _():
+        embed_out[...] = jnp.zeros_like(embed_out)
+        gain_out[...] = jnp.zeros_like(gain_out)
+        shift_out[...] = jnp.zeros_like(shift_out)
+
+    embed_out[...] += jnp.sum(input_adj, axis=0, keepdims=True)
+    gain_out[...] += jnp.sum(first * norm, axis=0, keepdims=True)
+    shift_out[...] += jnp.sum(first, axis=0, keepdims=True)
+
+
+def final(x, embed, gain, part, near, far, adj):
+    rows = x.shape[0]
+    line = jax.ShapeDtypeStruct((1, D), f32)
+    return pl.pallas_call(
+        final_kernel,
+        grid=(rows // BLOCK,),
+        in_specs=[by_rows(D), fixed((1, D)), fixed((1, D))] + [by_rows(D)] * 4,
+        out_specs=[by_rows(D)] + [fixed((1, D))] * 3,
+        out_shape=[jax.ShapeDtypeStruct((rows, D), bf16), line, line, line],
+        name="final",
+    )(x, embed, gain, part, near, far, adj)
 
 
 def solution(mesh):

time: 578 us -> 581 us (level)
  starting transfers between devices: 58.3 us -> 92.5 us
  other arithmetic: 51.7 us -> 40.2 us
  Pallas kernels: 201 us -> 191 us
  waiting for transfers between devices: 161 us -> 151 us
  matrix products: 59 us -> 52.4 us
    ppermute x65 -> x67, starting transfers between devices: 58.3 us -> 92.5 us  [swap(): return lax.ppermute(x, axis, [(i, i ^ bit) for i in range(size)])]
    pallas_call x3, Pallas kernels: 95.5 us -> 79 us  [attn_bwd(): pl.pallas_call(kernel, grid=(1,), in_specs=specs, out_specs=pl.BlockSpec(...]
    ppermute x65 -> x67, waiting for transfers between devices: 161 us -> 151 us  [swap(): return lax.ppermute(x, axis, [(i, i ^ bit) for i in range(size)])]
    pallas_call x0 -> x1, Pallas kernels: none -> 6.76 us  [final(): pl.pallas_call(final_kernel, grid=(rows // BLOCK,), in_specs=[by_rows(D),...]
    dot_general x21, matrix products: 59 us -> 52.4 us  [dot(): lax.dot_general(a, b, (((ca,), (cb,)), ((), ())), preferred_element_type=...]
    unnamed x136 -> x106, local copies, waits for them, and re-layouts: 16.3 us -> 16.5 us
  transfers between devices with their start and end apart: 65 -> 67, of which waited for: 23 -> 22; matrix products, arithmetic and copies ran while one was open for 19% -> 14% of each run, Pallas kernels for 27% -> 16%
where the time goes in v4:
time: 581 us; the launch traced here: 574 us
  Pallas kernels  191 us (33%)
  waiting for transfers between devices  151 us (26%)
  starting transfers between devices  92.5 us (16%)
  matrix products  52.4 us (9%)
  other arithmetic  40.2 us (7%)
  local copies, waits for them, and re-layouts  40.1 us (7%)
  between operations  7.05 us (1%)
    ppermute x67, waiting for transfers between devices, swap(): return lax.ppermute(x, axis, [(i, i ^ bit) for i in range(size)])  151 us
    ppermute x67, starting transfers between devices, swap(): return lax.ppermute(x, axis, [(i, i ^ bit) for i in range(size)])  92.5 us
    pallas_call x3, Pallas kernels, attn_bwd(): pl.pallas_call(kernel, grid=(1,), in_specs=specs, out_specs=pl.BlockSpec(...  79 us
    pallas_call x3, Pallas kernels, attn_fwd(): pl.pallas_call(fwd_kernel, grid=(1,), in_specs=[head_spec(head), head_spe...  56.8 us
    dot_general x21, matrix products, dot(): lax.dot_general(a, b, (((ca,), (cb,)), ((), ())), preferred_element_type=...  52.4 us
    pallas_call x1, Pallas kernels, mid_fwd(): pl.pallas_call(mid_fwd_kernel, grid=(rows // BLOCK,), in_specs=[pl.BlockS...  25.4 us
    pallas_call x1, Pallas kernels, mid_bwd(): pl.pallas_call(mid_bwd_kernel, grid=(rows // BLOCK,), in_specs=[by_rows(D...  23.4 us
    unnamed x106, local copies, waits for them, and re-layouts  16.5 us
  transfers between devices with their start and end apart: 67, of which 22 were waited for; matrix products, arithmetic and copies ran while one was open for 14% of the time, Pallas kernels for 16%

profile of v4, /device:TPU:0, one launch (start us, length us, event | category | flops | bytes accessed | tf_op | source)
XLA Modules:
  0.0 574.3 jit_solution(3288392567664986079)
XLA Ops:
  0.7 1.9 fusion.1
  3.4 1.9 add_convert_fusion.1
  5.8 2.5 collective-permute-start.5
  8.9 3.2 fusion.108
  12.8 2.9 collective-permute-start
  15.8 2.5 fusion.50
  19.2 24.5 %collective-permute-done.5 = bf16[1024,768]{1,0:T(8,128)(2,1)} collective-permute-done((bf16[1024,768]{1,0:T(8,128)(2,1)}, bf16[1024,768]{1,0:T(8,128)(2,1)}, u32[]{:S(2)}, u32[]{:S(2)}) %collective-permute-start.5) | collective-permute-done | bytes 1572896 | tf_op jit(solution)/shard_map/ppermute | solution.py:399
  44.3 2.7 broadcast_in_dim.78
  48.9 3.2 collective-permute-start.1
  53.6 2.5 fusion.51
  56.1 2.9 fusion.52
  68.2 19.2 %attn_fwd.4 = (bf16[1,64,4096]{2,1,0:T(8,128)(2,1)}, f32[1,64,4096]{2,1,0:T(8,128)}, f32[1,1,4096]{2,1,0:T(1,128)}) custom-call(bf16[9,64,4096]{2,1,0:T(8,128)(2,1)} %bitcast.8.q_ref.k_ref.v_ref.refs_1_.refs_2_.refs_3_, bf16[9,64,4096]{2,1,0:T(8,128)(2,1)} %bitcast.8.q_ref.k_ref.v_ref.refs_1_.refs_2_.refs_3_, ...), custom_call_target="tpu_custom_call" | custom-call | flops 16999999488 | bytes 4000000 | tf_op jit(solution)/shard_map/attn_fwd/pallas_call | solution.py:87
  87.4 18.7 %attn_fwd.3 = (bf16[1,64,4096]{2,1,0:T(8,128)(2,1)}, f32[1,64,4096]{2,1,0:T(8,128)}, f32[1,1,4096]{2,1,0:T(1,128)}) custom-call(bf16[9,64,4096]{2,1,0:T(8,128)(2,1)} %bitcast.8.q_ref.k_ref.v_ref.refs_1_.refs_2_.refs_3_, bf16[9,64,4096]{2,1,0:T(8,128)(2,1)} %bitcast.8.q_ref.k_ref.v_ref.refs_1_.refs_2_.refs_3_, ...), custom_call_target="tpu_custom_call" | custom-call | flops 16999999488 | bytes 4000000 | tf_op jit(solution)/shard_map/attn_fwd/pallas_call | solution.py:87
  106.1 18.9 %attn_fwd.5 = (bf16[1,64,4096]{2,1,0:T(8,128)(2,1)}, f32[1,64,4096]{2,1,0:T(8,128)}, f32[1,1,4096]{2,1,0:T(1,128)}) custom-call(bf16[9,64,4096]{2,1,0:T(8,128)(2,1)} %bitcast.8.q_ref.k_ref.v_ref.refs_1_.refs_2_.refs_3_, bf16[9,64,4096]{2,1,0:T(8,128)(2,1)} %bitcast.8.q_ref.k_ref.v_ref.refs_1_.refs_2_.refs_3_, ...), custom_call_target="tpu_custom_call" | custom-call | flops 16999999488 | bytes 4000000 | tf_op jit(solution)/shard_map/attn_fwd/pallas_call | solution.py:87
  126.8 3.9 collective-permute-start.2
  131.2 3.8 collective-permute-start.3
  150.3 3.4 collective-permute-done.9
  156.2 6.0 %collective-permute-done.11 = bf16[128,1024]{1,0:T(8,128)(2,1)S(1)} collective-permute-done((bf16[128,1024]{1,0:T(8,128)(2,1)S(1)}, bf16[128,1024]{1,0:T(8,128)(2,1)S(1)}, u32[]{:S(2)}, u32[]{:S(2)}) %collective-permute-start.11) | collective-permute-done | bytes 262176 | tf_op jit(solution)/shard_map/ppermute | solution.py:399
  164.0 3.8 collective-permute-done.12
  172.6 25.4 %mid_fwd.1 = (bf16[1024,768]{1,0:T(8,128)(2,1)}, bf16[1024,768]{1,0:T(8,128)(2,1)}, bf16[4,1024,768]{2,1,0:T(8,128)(2,1)}, f32[4,1024,768]{2,1,0:T(8,128)}, bf16...) custom-call(f32[1,1]{1,0:T(1,128)} %bitcast.2.scale_ref, ...), custom_call_target="tpu_custom_call" | custom-call | flops 22000001024 | bytes 30000000 | tf_op jit(solution)/shard_map/mid_fwd/pallas_call | solution.py:357
  198.0 4.5 fusion.35
  202.5 4.0 fusion.32
  206.5 2.5 fusion.29
  209.0 2.5 fusion.26
  211.5 23.4 %mid_bwd.1 = (bf16[4,1024,768]{2,1,0:T(8,128)(2,1)}, f32[1024,768]{1,0:T(8,128)}, bf16[1024,768]{1,0:T(8,128)(2,1)}, bf16[768,1024]{1,0:T(8,128)(2,1)}, f32[1,768]{1,0:T(1,128)}, /*index=5*/f32[1,768]{1,0:T(1,128)}) custom-call(bf16[1024,768]{1,0:T(8,128)(2,1)} %get-tuple-element.61.branch_ref, f32[4,1024,768]{2,1,0:T(8,128)} %get-tuple-element.62.slope_ref, ...), custom_call_target="tpu_custom_call" | custom-call | flops 22000001024 | bytes 30000000 | tf_op jit(solution)/shard_map/mid_bwd/pallas_call | solution.py:382
  234.9 3.0 fusion.47
  255.4 26.5 %attn_bwd.3.refs_9_ = bf16[3,3,64,4096]{3,2,1,0:T(8,128)(2,1)} custom-call(s32[8]{0:T(128)} %and_select_fusion.last_ref.refs_0_, bf16[9,64,4096]{2,1,0:T(8,128)(2,1)} %bitcast.8.q_ref.k_ref.v_ref.refs_1_.refs_2_.refs_3_, bf16[9,64,4096]{2,1,0:T(8,128)(2,1)} %bitcast.8.q_ref.k_ref.v_ref.refs_1_.refs_2_.refs_3_, ...), custom_call_target="tpu_custom_call" | custom-call | flops 30000001024 | bytes 8000000 | tf_op jit(solution)/shard_map/attn_bwd/pallas_call | solution.py:225
  283.1 26.3 %attn_bwd.4.refs_9_ = bf16[3,3,64,4096]{3,2,1,0:T(8,128)(2,1)} custom-call(s32[8]{0:T(128)} %and_select_fusion.last_ref.refs_0_, bf16[9,64,4096]{2,1,0:T(8,128)(2,1)} %bitcast.8.q_ref.k_ref.v_ref.refs_1_.refs_2_.refs_3_, bf16[9,64,4096]{2,1,0:T(8,128)(2,1)} %bitcast.8.q_ref.k_ref.v_ref.refs_1_.refs_2_.refs_3_, ...), custom_call_target="tpu_custom_call", output_to_operand_aliasing={{}: (9, {})} | custom-call | flops 30000001024 | bytes 8000000 | tf_op jit(solution)/shard_map/attn_bwd/pallas_call | solution.py:225
  309.4 26.3 %attn_bwd.5 = bf16[3,3,64,4096]{3,2,1,0:T(8,128)(2,1)} custom-call(s32[8]{0:T(128)} %and_select_fusion.last_ref.refs_0_, bf16[9,64,4096]{2,1,0:T(8,128)(2,1)} %bitcast.8.q_ref.k_ref.v_ref.refs_1_.refs_2_.refs_3_, bf16[9,64,4096]{2,1,0:T(8,128)(2,1)} %bitcast.8.q_ref.k_ref.v_ref.refs_1_.refs_2_.refs_3_, ...), custom_call_target="tpu_custom_call", output_to_operand_aliasing={{}: (9, {})} | custom-call | flops 30000001024 | bytes 8000000 | tf_op jit(solution)/shard_map/attn_bwd/pallas_call | solution.py:225
  335.7 3.0 fusion.63
  338.9 2.5 fusion.57
  341.4 2.6 fusion.60
  344.0 2.3 add_add_fusion
  346.3 2.4 reshape.137
  349.7 8.9 %collective-permute-start.37 = (bf16[384,576]{0,1:T(8,128)(2,1)S(1)}, bf16[384,576]{0,1:T(8,128)(2,1)S(1)}, u32[]{:S(2)}, u32[]{:S(2)}) collective-permute-start(bf16[384,576]{0,1:T(8,128)(2,1)S(1)} %bitcast.209), channel_id=1, source_target_pairs={{0,4},{4,0},{8,12},{12,8},{16,20},{20,16},{24,28},{28,24},{1,5},{5... | collective-permute-start | bytes 1327112 | tf_op jit(solution)/shard_map/ppermute | solution.py:399
  360.5 8.9 %collective-permute-done.37 = bf16[384,576]{0,1:T(8,128)(2,1)S(1)} collective-permute-done((bf16[384,576]{0,1:T(8,128)(2,1)S(1)}, bf16[384,576]{0,1:T(8,128)(2,1)S(1)}, u32[]{:S(2)}, u32[]{:S(2)}) %collective-permute-start.37) | collective-permute-done | bytes 442400 | tf_op jit(solution)/shard_map/ppermute | solution.py:399
  370.0 2.9 convolution_convert_fusion
  375.1 2.1 collective-permute-start.40
  377.2 2.6 convolution_convert_fusion.2
  379.8 5.5 collective-permute-done.39
  386.8 2.8 collective-permute-start.42
  391.2 2.4 collective-permute-done.41
  393.6 5.4 collective-permute-start.43
  404.0 2.6 convolution_convert_fusion.3.part_ref
  406.9 2.6 add_convert_fusion
  411.2 16.6 %collective-permute-done.58 = bf16[768,768]{1,0:T(8,128)(2,1)S(1)} collective-permute-done((bf16[768,768]{1,0:T(8,128)(2,1)S(1)}, bf16[768,768]{1,0:T(8,128)(2,1)S(1)}, u32[]{:S(2)}, u32[]{:S(2)}) %collective-permute-start.58) | collective-permute-done | bytes 1179680 | tf_op jit(solution)/shard_map/ppermute | solution.py:399
  432.1 27.3 %collective-permute-done.47 = bf16[960,768]{1,0:T(8,128)(2,1)S(1)} collective-permute-done((bf16[960,768]{1,0:T(8,128)(2,1)S(1)}, bf16[960,768]{1,0:T(8,128)(2,1)S(1)}, u32[]{:S(2)}, u32[]{:S(2)}) %collective-permute-start.47) | collective-permute-done | bytes 1474592 | tf_op jit(solution)/shard_map/ppermute | solution.py:399
  463.9 2.0 copy.44
  465.9 2.0 copy.45
  467.9 2.5 maximum_convert_fusion.1
  474.9 2.5 collective-permute-start.62
  477.4 13.2 %collective-permute-done.30.far_ref = bf16[1024,768]{1,0:T(8,128)(2,1)} collective-permute-done((bf16[1024,768]{1,0:T(8,128)(2,1)}, bf16[1024,768]{1,0:T(8,128)(2,1)}, u32[]{:S(2)}, u32[]{:S(2)}) %collective-permute-start.30) | collective-permute-done | bytes 1572896 | tf_op jit(solution)/shard_map/ppermute | solution.py:399
  490.6 6.8 %final.1 = (bf16[1024,768]{1,0:T(8,128)(2,1)}, f32[1,768]{1,0:T(1,128)}, f32[1,768]{1,0:T(1,128)}, f32[1,768]{1,0:T(1,128)}) custom-call(bf16[1024,768]{1,0:T(8,128)(2,1)} %x_ref.3, f32[1,768]{1,0:T(1,128)} %broadcast_in_dim.85.embed_ref, f32[1,768]{1,0:T(1,128)} %broadcast_in_dim.89.gain_ref, bf16[1024,768]{1,0:T(8,128)(2,1)} %convolution_convert_fusion.3.part_ref, ...), custom_call_target="tpu_custom_call" | custom-call | tf_op jit(solution)/shard_map/final/pallas_call | solution.py:624
  500.4 2.7 collective-permute-start.50
  505.6 2.5 collective-permute-start.63
  508.1 2.6 collective-permute-done.49
  510.6 12.5 %collective-permute-done.50 = bf16[120,768]{1,0:T(8,128)(2,1)S(1)} collective-permute-done((bf16[120,768]{1,0:T(8,128)(2,1)S(1)}, bf16[120,768]{1,0:T(8,128)(2,1)S(1)}, u32[]{:S(2)}, u32[]{:S(2)}) %collective-permute-start.50) | collective-permute-done | bytes 184352 | tf_op jit(solution)/shard_map/ppermute | solution.py:399
  524.3 2.5 collective-permute-start.52
  526.8 8.9 %collective-permute-start.53 = (bf16[120,768]{1,0:T(8,128)(2,1)S(1)}, bf16[120,768]{1,0:T(8,128)(2,1)S(1)}, u32[]{:S(2)}, u32[]{:S(2)}) collective-permute-start(bf16[120,768]{1,0:T(8,128)(2,1)S(1)} %fusion.71), channel_id=1, source_target_pairs={{0,16},{4,20},{8,24},{12,28},{16,0},{20,4},{24,8},{28,12},{1,17},{... | collective-permute-start | bytes 552968 | tf_op jit(solution)/shard_map/ppermute | solution.py:399
  535.7 5.0 collective-permute-done.64
  543.0 2.0 collective-permute-done.33
  545.0 2.0 collective-permute-start.34
  549.1 2.7 collective-permute-start.36
  558.9 11.1 %collective-permute-done.55 = bf16[480,768]{1,0:T(8,128)(2,1)S(1)} collective-permute-done((bf16[480,768]{1,0:T(8,128)(2,1)}, bf16[480,768]{1,0:T(8,128)(2,1)S(1)}, u32[]{:S(2)}, u32[]{:S(2)}) %collective-permute-start.55) | collective-permute-done | bytes 737312 | tf_op jit(solution)/shard_map/ppermute | solution.py:399
  (302 shorter events, 107.9 us)
Async XLA Ops:
  5.3 48.3 %collective-permute-start.4 = (bf16[1024,768]{1,0:T(8,128)(2,1)}, bf16[1024,768]{1,0:T(8,128)(2,1)}, u32[]{:S(2)}, u32[]{:S(2)}) collective-permute-start(bf16[1024,768]{1,0:T(8,128)(2,1)} %add_convert_fusion.1), channel_id=1, source_target_pairs={{0,1},{1,0},{2,3},{3,2},{4,5},{5,4},{6,7},{7,6},{8,9},{9,8},{10,11... | collective-permute-start | bytes 4718600 | tf_op jit(solution)/shard_map/ppermute | solution.py:399
  5.8 37.9 %collective-permute-start.5 = (bf16[1024,768]{1,0:T(8,128)(2,1)}, bf16[1024,768]{1,0:T(8,128)(2,1)}, u32[]{:S(2)}, u32[]{:S(2)}) collective-permute-start(bf16[1024,768]{1,0:T(8,128)(2,1)} %add_convert_fusion.1), channel_id=1, source_target_pairs={{0,2},{1,3},{2,0},{3,1},{4,6},{5,7},{6,4},{7,5},{8,10},{9,11},{10,... | collective-permute-start | bytes 4718600 | tf_op jit(solution)/shard_map/ppermute | solution.py:399
  12.8 35.4 %collective-permute-start = (f32[1,1]{1,0:T(1,128)}, f32[1,1]{1,0:T(1,128)}, u32[]{:S(2)}, u32[]{:S(2)}) collective-permute-start(f32[1,1]{1,0:T(1,128)} %bitcast), channel_id=1, source_target_pairs={{0,4},{4,0},{8,12},{12,8},{16,20},{20,16},{24,28},{28,24},{1,5},{5... | collective-permute-start | bytes 20 | tf_op jit(solution)/shard_map/ppermute | solution.py:399
  43.6 20.8 %collective-permute-start.6 = (bf16[1024,768]{1,0:T(8,128)(2,1)}, bf16[1024,768]{1,0:T(8,128)(2,1)S(1)}, u32[]{:S(2)}, u32[]{:S(2)}) collective-permute-start(bf16[1024,768]{1,0:T(8,128)(2,1)} %collective-permute-done.5), channel_id=1, source_target_pairs={{0,1},{1,0},{2,3},{3,2},{4,5},{5,4},{6,7},{7,6},{8,9},{9,8},{10,11... | collective-permute-start | bytes 4718600 | tf_op jit(solution)/shard_map/ppermute | solution.py:399
  48.9 77.9 %collective-permute-start.1 = (f32[1,1]{1,0:T(1,128)}, f32[1,1]{1,0:T(1,128)}, u32[]{:S(2)}, u32[]{:S(2)}) collective-permute-start(f32[1,1]{1,0:T(1,128)} %add.214), channel_id=1, source_target_pairs={{0,8},{4,12},{8,0},{12,4},{16,24},{20,28},{24,16},{28,20},{1,9},{5... | collective-permute-start | bytes 20 | tf_op jit(solution)/shard_map/ppermute | solution.py:399
  52.1 11.0 %collective-permute-start.14 = (bf16[192,768]{1,0:T(8,128)(2,1)S(1)}, bf16[192,768]{1,0:T(8,128)(2,1)}, u32[]{:S(2)}, u32[]{:S(2)}) collective-permute-start(bf16[192,768]{1,0:T(8,128)(2,1)S(1)} %copy-done.19), channel_id=1, source_target_pairs={{0,2},{1,3},{2,0},{3,1},{4,6},{5,7},{6,4},{7,5},{8,10},{9,11},{10,... | collective-permute-start | bytes 884744 | tf_op jit(solution)/shard_map/ppermute | solution.py:399
  60.1 76.6 %collective-permute-start.13 = (bf16[192,768]{1,0:T(8,128)(2,1)S(1)}, bf16[192,768]{1,0:T(8,128)(2,1)}, u32[]{:S(2)}, u32[]{:S(2)}) collective-permute-start(bf16[192,768]{1,0:T(8,128)(2,1)S(1)} %copy-done.19), channel_id=1, source_target_pairs={{0,1},{1,0},{2,3},{3,2},{4,5},{5,4},{6,7},{7,6},{8,9},{9,8},{10,11... | collective-permute-start | bytes 884744 | tf_op jit(solution)/shard_map/ppermute | solution.py:399
  60.1 82.8 %collective-permute-start.17 = (bf16[768,768]{1,0:T(8,128)(2,1)}, bf16[768,768]{1,0:T(8,128)(2,1)}, u32[]{:S(2)}, u32[]{:S(2)}) collective-permute-start(bf16[768,768]{1,0:T(8,128)(2,1)} %e0.1), channel_id=1, source_target_pairs={{0,2},{1,3},{2,0},{3,1},{4,6},{5,7},{6,4},{7,5},{8,10},{9,11},{10,... | collective-permute-start | bytes 3538952 | tf_op jit(solution)/shard_map/ppermute | solution.py:399
  63.0 80.3 %collective-permute-start.20 = (bf16[768,768]{1,0:T(8,128)(2,1)}, bf16[768,768]{1,0:T(8,128)(2,1)}, u32[]{:S(2)}, u32[]{:S(2)}) collective-permute-start(bf16[768,768]{1,0:T(8,128)(2,1)} %r0.1), channel_id=1, source_target_pairs={{0,2},{1,3},{2,0},{3,1},{4,6},{5,7},{6,4},{7,5},{8,10},{9,11},{10,... | collective-permute-start | bytes 3538952 | tf_op jit(solution)/shard_map/ppermute | solution.py:399
  64.5 73.6 %collective-permute-start.15 = (bf16[192,768]{1,0:T(8,128)(2,1)}, bf16[192,768]{1,0:T(8,128)(2,1)}, u32[]{:S(2)}, u32[]{:S(2)}) collective-permute-start(bf16[192,768]{1,0:T(8,128)(2,1)} %collective-permute-done.14), channel_id=1, source_target_pairs={{0,1},{1,0},{2,3},{3,2},{4,5},{5,4},{6,7},{7,6},{8,9},{9,8},{10,11... | collective-permute-start | bytes 884744 | tf_op jit(solution)/shard_map/ppermute | solution.py:399
  131.2 5.5 collective-permute-start.3
  136.7 6.9 %collective-permute-start.8 = (bf16[64,1024]{1,0:T(8,128)(2,1)}, bf16[64,1024]{1,0:T(8,128)(2,1)S(1)}, u32[]{:S(2)}, u32[]{:S(2)}) collective-permute-start(bf16[64,1024]{1,0:T(8,128)(2,1)} %get-tuple-element.143), channel_id=1, source_target_pairs={{0,1},{1,0},{2,3},{3,2},{4,5},{5,4},{6,7},{7,6},{8,9},{9,8},{10,11... | collective-permute-start | bytes 393224 | tf_op jit(solution)/shard_map/ppermute | solution.py:399
  136.7 7.1 %collective-permute-start.10 = (bf16[64,1024]{1,0:T(8,128)(2,1)}, bf16[64,1024]{1,0:T(8,128)(2,1)S(1)}, u32[]{:S(2)}, u32[]{:S(2)}) collective-permute-start(bf16[64,1024]{1,0:T(8,128)(2,1)} %get-tuple-element.142), channel_id=1, source_target_pairs={{0,2},{1,3},{2,0},{3,1},{4,6},{5,7},{6,4},{7,5},{8,10},{9,11},{10,... | collective-permute-start | bytes 393224 | tf_op jit(solution)/shard_map/ppermute | solution.py:399
  138.1 7.0 %collective-permute-start.7 = (bf16[128,1024]{1,0:T(8,128)(2,1)S(1)}, bf16[128,1024]{1,0:T(8,128)(2,1)S(1)}, u32[]{:S(2)}, u32[]{:S(2)}) collective-permute-start(bf16[128,1024]{1,0:T(8,128)(2,1)S(1)} %get-tuple-element.126), channel_id=1, source_target_pairs={{0,1},{1,0},{2,3},{3,2},{4,5},{5,4},{6,7},{7,6},{8,9},{9,8},{10,11... | collective-permute-start | bytes 786440 | tf_op jit(solution)/shard_map/ppermute | solution.py:399
  142.9 25.5 %collective-permute-start.16 = (bf16[768,768]{1,0:T(8,128)(2,1)}, bf16[768,768]{1,0:T(8,128)(2,1)S(1)}, u32[]{:S(2)}, u32[]{:S(2)}) collective-permute-start(bf16[768,768]{1,0:T(8,128)(2,1)} %e0.1), channel_id=1, source_target_pairs={{0,1},{1,0},{2,3},{3,2},{4,5},{5,4},{6,7},{7,6},{8,9},{9,8},{10,11... | collective-permute-start | bytes 3538952 | tf_op jit(solution)/shard_map/ppermute | solution.py:399
  143.3 26.2 %collective-permute-start.19 = (bf16[768,768]{1,0:T(8,128)(2,1)}, bf16[768,768]{1,0:T(8,128)(2,1)S(1)}, u32[]{:S(2)}, u32[]{:S(2)}) collective-permute-start(bf16[768,768]{1,0:T(8,128)(2,1)} %r0.1), channel_id=1, source_target_pairs={{0,1},{1,0},{2,3},{3,2},{4,5},{5,4},{6,7},{7,6},{8,9},{9,8},{10,11... | collective-permute-start | bytes 3538952 | tf_op jit(solution)/shard_map/ppermute | solution.py:399
  143.5 27.0 %collective-permute-start.18 = (bf16[768,768]{1,0:T(8,128)(2,1)}, bf16[768,768]{1,0:T(8,128)(2,1)S(1)}, u32[]{:S(2)}, u32[]{:S(2)}) collective-permute-start(bf16[768,768]{1,0:T(8,128)(2,1)} %collective-permute-done.17.e2), channel_id=1, source_target_pairs={{0,1},{1,0},{2,3},{3,2},{4,5},{5,4},{6,7},{7,6},{8,9},{9,8},{10,11... | collective-permute-start | bytes 3538952 | tf_op jit(solution)/shard_map/ppermute | solution.py:399
  143.8 27.8 %collective-permute-start.21 = (bf16[768,768]{1,0:T(8,128)(2,1)}, bf16[768,768]{1,0:T(8,128)(2,1)S(1)}, u32[]{:S(2)}, u32[]{:S(2)}) collective-permute-start(bf16[768,768]{1,0:T(8,128)(2,1)} %collective-permute-done.20.r2), channel_id=1, source_target_pairs={{0,1},{1,0},{2,3},{3,2},{4,5},{5,4},{6,7},{7,6},{8,9},{9,8},{10,11... | collective-permute-start | bytes 3538952 | tf_op jit(solution)/shard_map/ppermute | solution.py:399
  145.1 8.6 %collective-permute-start.9 = (bf16[128,1024]{1,0:T(8,128)(2,1)S(1)}, bf16[128,1024]{1,0:T(8,128)(2,1)S(1)}, u32[]{:S(2)}, u32[]{:S(2)}) collective-permute-start(bf16[128,1024]{1,0:T(8,128)(2,1)S(1)} %get-tuple-element.127), channel_id=1, source_target_pairs={{0,2},{1,3},{2,0},{3,1},{4,6},{5,7},{6,4},{7,5},{8,10},{9,11},{10,... | collective-permute-start | bytes 786440 | tf_op jit(solution)/shard_map/ppermute | solution.py:399
  153.7 8.6 %collective-permute-start.11 = (bf16[128,1024]{1,0:T(8,128)(2,1)S(1)}, bf16[128,1024]{1,0:T(8,128)(2,1)S(1)}, u32[]{:S(2)}, u32[]{:S(2)}) collective-permute-start(bf16[128,1024]{1,0:T(8,128)(2,1)S(1)} %get-tuple-element.124), channel_id=1, source_target_pairs={{0,3},{1,2},{2,1},{3,0},{4,7},{5,6},{6,5},{7,4},{8,11},{9,10},{10,... | collective-permute-start | bytes 786440 | tf_op jit(solution)/shard_map/ppermute | solution.py:399
  162.2 5.5 collective-permute-start.12
  245.5 8.8 %collective-permute-start.25 = (bf16[64,1024]{1,0:T(8,128)(2,1)S(1)}, bf16[64,1024]{1,0:T(8,128)(2,1)S(1)}, u32[]{:S(2)}, u32[]{:S(2)}) collective-permute-start(bf16[64,1024]{1,0:T(8,128)(2,1)S(1)} %get-tuple-element.103), channel_id=1, source_target_pairs={{0,3},{1,2},{2,1},{3,0},{4,7},{5,6},{6,5},{7,4},{8,11},{9,10},{10,... | collective-permute-start | bytes 393224 | tf_op jit(solution)/shard_map/ppermute | solution.py:399
  246.4 8.1 %collective-permute-start.26 = (bf16[64,1024]{1,0:T(8,128)(2,1)S(1)}, bf16[64,1024]{1,0:T(8,128)(2,1)S(1)}, u32[]{:S(2)}, u32[]{:S(2)}) collective-permute-start(bf16[64,1024]{1,0:T(8,128)(2,1)S(1)} %get-tuple-element.102), channel_id=1, source_target_pairs={{0,2},{1,3},{2,0},{3,1},{4,6},{5,7},{6,4},{7,5},{8,10},{9,11},{10,... | collective-permute-start | bytes 393224 | tf_op jit(solution)/shard_map/ppermute | solution.py:399
  247.4 7.2 %collective-permute-start.27 = (bf16[64,1024]{1,0:T(8,128)(2,1)S(1)}, bf16[64,1024]{1,0:T(8,128)(2,1)S(1)}, u32[]{:S(2)}, u32[]{:S(2)}) collective-permute-start(bf16[64,1024]{1,0:T(8,128)(2,1)S(1)} %get-tuple-element.101), channel_id=1, source_target_pairs={{0,1},{1,0},{2,3},{3,2},{4,5},{5,4},{6,7},{7,6},{8,9},{9,8},{10,11... | collective-permute-start | bytes 393224 | tf_op jit(solution)/shard_map/ppermute | solution.py:399
  247.5 34.4 %collective-permute-start.22 = (bf16[128,1024]{1,0:T(8,128)(2,1)S(1)}, bf16[128,1024]{1,0:T(8,128)(2,1)S(1)}, u32[]{:S(2)}, u32[]{:S(2)}) collective-permute-start(bf16[128,1024]{1,0:T(8,128)(2,1)S(1)} %bitcast.222), channel_id=1, source_target_pairs={{0,3},{1,2},{2,1},{3,0},{4,7},{5,6},{6,5},{7,4},{8,11},{9,10},{10,... | collective-permute-start | bytes 786440 | tf_op jit(solution)/shard_map/ppermute | solution.py:399
  248.6 33.4 %collective-permute-start.23 = (bf16[128,1024]{1,0:T(8,128)(2,1)S(1)}, bf16[128,1024]{1,0:T(8,128)(2,1)S(1)}, u32[]{:S(2)}, u32[]{:S(2)}) collective-permute-start(bf16[128,1024]{1,0:T(8,128)(2,1)S(1)} %bitcast.221), channel_id=1, source_target_pairs={{0,2},{1,3},{2,0},{3,1},{4,6},{5,7},{6,4},{7,5},{8,10},{9,11},{10,... | collective-permute-start | bytes 786440 | tf_op jit(solution)/shard_map/ppermute | solution.py:399
  254.4 27.7 %collective-permute-start.24 = (bf16[128,1024]{1,0:T(8,128)(2,1)S(1)}, bf16[128,1024]{1,0:T(8,128)(2,1)S(1)}, u32[]{:S(2)}, u32[]{:S(2)}) collective-permute-start(bf16[128,1024]{1,0:T(8,128)(2,1)S(1)} %bitcast.220), channel_id=1, source_target_pairs={{0,1},{1,0},{2,3},{3,2},{4,5},{5,4},{6,7},{7,6},{8,9},{9,8},{10,11... | collective-permute-start | bytes 786440 | tf_op jit(solution)/shard_map/ppermute | solution.py:399
  349.7 19.7 %collective-permute-start.37 = (bf16[384,576]{0,1:T(8,128)(2,1)S(1)}, bf16[384,576]{0,1:T(8,128)(2,1)S(1)}, u32[]{:S(2)}, u32[]{:S(2)}) collective-permute-start(bf16[384,576]{0,1:T(8,128)(2,1)S(1)} %bitcast.209), channel_id=1, source_target_pairs={{0,4},{4,0},{8,12},{12,8},{16,20},{20,16},{24,28},{28,24},{1,5},{5... | collective-permute-start | bytes 1327112 | tf_op jit(solution)/shard_map/ppermute | solution.py:399
  359.2 27.6 %collective-permute-start.57 = (bf16[768,768]{1,0:T(8,128)(2,1)}, bf16[768,768]{1,0:T(8,128)(2,1)}, u32[]{:S(2)}, u32[]{:S(2)}) collective-permute-start(bf16[768,768]{1,0:T(8,128)(2,1)} %fusion.35), channel_id=1, source_target_pairs={{0,1},{1,0},{2,3},{3,2},{4,5},{5,4},{6,7},{7,6},{8,9},{9,8},{10,11... | collective-permute-start | bytes 3538952 | tf_op jit(solution)/shard_map/ppermute | solution.py:399
  359.4 39.6 %collective-permute-start.46 = (bf16[960,768]{1,0:T(8,128)(2,1)}, bf16[960,768]{1,0:T(8,128)(2,1)}, u32[]{:S(2)}, u32[]{:S(2)}) collective-permute-start(bf16[960,768]{1,0:T(8,128)(2,1)} %pad_maximum_fusion.3), channel_id=1, source_target_pairs={{0,1},{1,0},{2,3},{3,2},{4,5},{5,4},{6,7},{7,6},{8,9},{9,8},{10,11... | collective-permute-start | bytes 4423688 | tf_op jit(solution)/shard_map/ppermute | solution.py:399
  372.8 33.9 %collective-permute-start.29 = (bf16[1024,768]{1,0:T(8,128)(2,1)S(1)}, bf16[1024,768]{1,0:T(8,128)(2,1)S(1)}, u32[]{:S(2)}, u32[]{:S(2)}) collective-permute-start(bf16[1024,768]{1,0:T(8,128)(2,1)S(1)} %convolution_convert_fusion), channel_id=1, source_target_pairs={{0,1},{1,0},{2,3},{3,2},{4,5},{5,4},{6,7},{7,6},{8,9},{9,8},{10,11... | collective-permute-start | bytes 4718600 | tf_op jit(solution)/shard_map/ppermute | solution.py:399
  372.9 12.4 %collective-permute-start.39 = (bf16[96,576]{1,0:T(8,128)(2,1)S(1)}, bf16[96,576]{1,0:T(8,128)(2,1)S(1)}, u32[]{:S(2)}, u32[]{:S(2)}) collective-permute-start(bf16[96,576]{1,0:T(8,128)(2,1)S(1)} %get-tuple-element.132), channel_id=1, source_target_pairs={{0,16},{4,20},{8,24},{12,28},{16,0},{20,4},{24,8},{28,12},{1,17},{... | collective-permute-start | bytes 331784 | tf_op jit(solution)/shard_map/ppermute | solution.py:399
  375.1 10.3 %collective-permute-start.40 = (bf16[96,576]{1,0:T(8,128)(2,1)S(1)}, bf16[96,576]{1,0:T(8,128)(2,1)S(1)}, u32[]{:S(2)}, u32[]{:S(2)}) collective-permute-start(bf16[96,576]{1,0:T(8,128)(2,1)S(1)} %get-tuple-element.131), channel_id=1, source_target_pairs={{0,24},{4,28},{8,16},{12,20},{16,8},{20,12},{24,0},{28,4},{1,25},{... | collective-permute-start | bytes 331784 | tf_op jit(solution)/shard_map/ppermute | solution.py:399
  385.4 24.1 %collective-permute-start.56 = (bf16[768,768]{1,0:T(8,128)(2,1)S(1)}, bf16[768,768]{1,0:T(8,128)(2,1)S(1)}, u32[]{:S(2)}, u32[]{:S(2)}) collective-permute-start(bf16[768,768]{1,0:T(8,128)(2,1)S(1)} %copy-done.36), channel_id=1, source_target_pairs={{0,1},{1,0},{2,3},{3,2},{4,5},{5,4},{6,7},{7,6},{8,9},{9,8},{10,11... | collective-permute-start | bytes 3538952 | tf_op jit(solution)/shard_map/ppermute | solution.py:399
  385.4 8.2 %collective-permute-start.41 = (bf16[96,576]{1,0:T(8,128)(2,1)S(1)}, bf16[96,576]{1,0:T(8,128)(2,1)S(1)}, u32[]{:S(2)}, u32[]{:S(2)}) collective-permute-start(bf16[96,576]{1,0:T(8,128)(2,1)S(1)} %fusion.82), channel_id=1, source_target_pairs={{0,24},{4,28},{8,16},{12,20},{16,8},{20,12},{24,0},{28,4},{1,25},{... | collective-permute-start | bytes 331784 | tf_op jit(solution)/shard_map/ppermute | solution.py:399
  386.8 15.1 %collective-permute-start.42 = (bf16[96,576]{1,0:T(8,128)(2,1)S(1)}, bf16[96,576]{1,0:T(8,128)(2,1)S(1)}, u32[]{:S(2)}, u32[]{:S(2)}) collective-permute-start(bf16[96,576]{1,0:T(8,128)(2,1)S(1)} %fusion.82), channel_id=1, source_target_pairs={{0,16},{4,20},{8,24},{12,28},{16,0},{20,4},{24,8},{28,12},{1,17},{... | collective-permute-start | bytes 331784 | tf_op jit(solution)/shard_map/ppermute | solution.py:399
  393.6 9.3 %collective-permute-start.43 = (bf16[96,576]{1,0:T(8,128)(2,1)S(1)}, bf16[96,576]{1,0:T(8,128)(2,1)S(1)}, u32[]{:S(2)}, u32[]{:S(2)}) collective-permute-start(bf16[96,576]{1,0:T(8,128)(2,1)S(1)} %fusion.82), channel_id=1, source_target_pairs={{0,8},{4,12},{8,0},{12,4},{16,24},{20,28},{24,16},{28,20},{1,9},{5... | collective-permute-start | bytes 331784 | tf_op jit(solution)/shard_map/ppermute | solution.py:399
  399.0 28.8 %collective-permute-start.58 = (bf16[768,768]{1,0:T(8,128)(2,1)S(1)}, bf16[768,768]{1,0:T(8,128)(2,1)S(1)}, u32[]{:S(2)}, u32[]{:S(2)}) collective-permute-start(bf16[768,768]{1,0:T(8,128)(2,1)S(1)} %add_convert_fusion.3), channel_id=1, source_target_pairs={{0,2},{1,3},{2,0},{3,1},{4,6},{5,7},{6,4},{7,5},{8,10},{9,11},{10,... | collective-permute-start | bytes 3538952 | tf_op jit(solution)/shard_map/ppermute | solution.py:399
  401.9 28.4 %collective-permute-start.45 = (bf16[960,768]{1,0:T(8,128)(2,1)S(1)}, bf16[960,768]{1,0:T(8,128)(2,1)S(1)}, u32[]{:S(2)}, u32[]{:S(2)}) collective-permute-start(bf16[960,768]{1,0:T(8,128)(2,1)S(1)} %copy-done.12), channel_id=1, source_target_pairs={{0,1},{1,0},{2,3},{3,2},{4,5},{5,4},{6,7},{7,6},{8,9},{9,8},{10,11... | collective-permute-start | bytes 4423688 | tf_op jit(solution)/shard_map/ppermute | solution.py:399
  402.9 56.5 %collective-permute-start.47 = (bf16[960,768]{1,0:T(8,128)(2,1)S(1)}, bf16[960,768]{1,0:T(8,128)(2,1)S(1)}, u32[]{:S(2)}, u32[]{:S(2)}) collective-permute-start(bf16[960,768]{1,0:T(8,128)(2,1)S(1)} %add_convert_fusion.2), channel_id=1, source_target_pairs={{0,2},{1,3},{2,0},{3,1},{4,6},{5,7},{6,4},{7,5},{8,10},{9,11},{10,... | collective-permute-start | bytes 4423688 | tf_op jit(solution)/shard_map/ppermute | solution.py:399
  406.8 68.1 %collective-permute-start.28 = (bf16[1024,768]{1,0:T(8,128)(2,1)}, bf16[1024,768]{1,0:T(8,128)(2,1)}, u32[]{:S(2)}, u32[]{:S(2)}) collective-permute-start(bf16[1024,768]{1,0:T(8,128)(2,1)} %convolution_convert_fusion.2), channel_id=1, source_target_pairs={{0,1},{1,0},{2,3},{3,2},{4,5},{5,4},{6,7},{7,6},{8,9},{9,8},{10,11... | collective-permute-start | bytes 4718600 | tf_op jit(solution)/shard_map/ppermute | solution.py:399
  409.5 53.2 %collective-permute-start.44 = (bf16[384,576]{1,0:T(8,128)(2,1)S(1)}, bf16[384,576]{1,0:T(8,128)(2,1)S(1)}, u32[]{:S(2)}, u32[]{:S(2)}) collective-permute-start(bf16[384,576]{1,0:T(8,128)(2,1)S(1)} %pad_maximum_fusion.7), channel_id=1, source_target_pairs={{0,4},{4,0},{8,12},{12,8},{16,20},{20,16},{24,28},{28,24},{1,5},{5... | collective-permute-start | bytes 1327112 | tf_op jit(solution)/shard_map/ppermute | solution.py:399
  427.8 62.8 %collective-permute-start.30 = (bf16[1024,768]{1,0:T(8,128)(2,1)}, bf16[1024,768]{1,0:T(8,128)(2,1)}, u32[]{:S(2)}, u32[]{:S(2)}) collective-permute-start(bf16[1024,768]{1,0:T(8,128)(2,1)} %add_convert_fusion), channel_id=1, source_target_pairs={{0,2},{1,3},{2,0},{3,1},{4,6},{5,7},{6,4},{7,5},{8,10},{9,11},{10,... | collective-permute-start | bytes 4718600 | tf_op jit(solution)/shard_map/ppermute | solution.py:399
  430.3 40.1 %collective-permute-start.59 = (bf16[384,768]{1,0:T(8,128)(2,1)}, bf16[384,768]{1,0:T(8,128)(2,1)}, u32[]{:S(2)}, u32[]{:S(2)}) collective-permute-start(bf16[384,768]{1,0:T(8,128)(2,1)} %fusion.67), channel_id=1, source_target_pairs={{0,4},{4,0},{8,12},{12,8},{16,20},{20,16},{24,28},{28,24},{1,5},{5... | collective-permute-start | bytes 1769480 | tf_op jit(solution)/shard_map/ppermute | solution.py:399
  460.9 37.3 %collective-permute-start.48 = (bf16[480,768]{1,0:T(8,128)(2,1)}, bf16[480,768]{1,0:T(8,128)(2,1)}, u32[]{:S(2)}, u32[]{:S(2)}) collective-permute-start(bf16[480,768]{1,0:T(8,128)(2,1)} %fusion.66), channel_id=1, source_target_pairs={{0,4},{4,0},{8,12},{12,8},{16,20},{20,16},{24,28},{28,24},{1,5},{5... | collective-permute-start | bytes 2211848 | tf_op jit(solution)/shard_map/ppermute | solution.py:399
  473.0 27.5 %collective-permute-start.60 = (bf16[96,768]{1,0:T(8,128)(2,1)S(1)}, bf16[96,768]{1,0:T(8,128)(2,1)S(1)}, u32[]{:S(2)}, u32[]{:S(2)}) collective-permute-start(bf16[96,768]{1,0:T(8,128)(2,1)S(1)} %get-tuple-element.115), channel_id=1, source_target_pairs={{0,8},{4,12},{8,0},{12,4},{16,24},{20,28},{24,16},{28,20},{1,9},{5... | collective-permute-start | bytes 442376 | tf_op jit(solution)/shard_map/ppermute | solution.py:399
  473.0 30.1 %collective-permute-start.61 = (bf16[96,768]{1,0:T(8,128)(2,1)S(1)}, bf16[96,768]{1,0:T(8,128)(2,1)S(1)}, u32[]{:S(2)}, u32[]{:S(2)}) collective-permute-start(bf16[96,768]{1,0:T(8,128)(2,1)S(1)} %get-tuple-element.117), channel_id=1, source_target_pairs={{0,16},{4,20},{8,24},{12,28},{16,0},{20,4},{24,8},{28,12},{1,17},{... | collective-permute-start | bytes 442376 | tf_op jit(solution)/shard_map/ppermute | solution.py:399
  474.9 29.6 %collective-permute-start.62 = (bf16[96,768]{1,0:T(8,128)(2,1)S(1)}, bf16[96,768]{1,0:T(8,128)(2,1)S(1)}, u32[]{:S(2)}, u32[]{:S(2)}) collective-permute-start(bf16[96,768]{1,0:T(8,128)(2,1)S(1)} %get-tuple-element.116), channel_id=1, source_target_pairs={{0,24},{4,28},{8,16},{12,20},{16,8},{20,12},{24,0},{28,4},{1,25},{... | collective-permute-start | bytes 442376 | tf_op jit(solution)/shard_map/ppermute | solution.py:399
  498.1 9.9 %collective-permute-start.31 = (f32[6,768]{1,0:T(8,128)S(1)}, f32[6,768]{1,0:T(8,128)S(1)}, u32[]{:S(2)}, u32[]{:S(2)}) collective-permute-start(f32[6,768]{1,0:T(8,128)S(1)} %stack.3), channel_id=1, source_target_pairs={{0,1},{1,0},{2,3},{3,2},{4,5},{5,4},{6,7},{7,6},{8,9},{9,8},{10,11... | collective-permute-start | bytes 55304 | tf_op jit(solution)/shard_map/ppermute | solution.py:399
  500.1 10.6 %collective-permute-start.49 = (bf16[120,768]{1,0:T(8,128)(2,1)S(1)}, bf16[120,768]{1,0:T(8,128)(2,1)S(1)}, u32[]{:S(2)}, u32[]{:S(2)}) collective-permute-start(bf16[120,768]{1,0:T(8,128)(2,1)S(1)} %get-tuple-element.110), channel_id=1, source_target_pairs={{0,8},{4,12},{8,0},{12,4},{16,24},{20,28},{24,16},{28,20},{1,9},{5... | collective-permute-start | bytes 552968 | tf_op jit(solution)/shard_map/ppermute | solution.py:399
  500.4 22.7 %collective-permute-start.50 = (bf16[120,768]{1,0:T(8,128)(2,1)S(1)}, bf16[120,768]{1,0:T(8,128)(2,1)S(1)}, u32[]{:S(2)}, u32[]{:S(2)}) collective-permute-start(bf16[120,768]{1,0:T(8,128)(2,1)S(1)} %get-tuple-element.112), channel_id=1, source_target_pairs={{0,16},{4,20},{8,24},{12,28},{16,0},{20,4},{24,8},{28,12},{1,17},{... | collective-permute-start | bytes 552968 | tf_op jit(solution)/shard_map/ppermute | solution.py:399
  503.1 21.1 %collective-permute-start.51 = (bf16[120,768]{1,0:T(8,128)(2,1)S(1)}, bf16[120,768]{1,0:T(8,128)(2,1)S(1)}, u32[]{:S(2)}, u32[]{:S(2)}) collective-permute-start(bf16[120,768]{1,0:T(8,128)(2,1)S(1)} %get-tuple-element.111), channel_id=1, source_target_pairs={{0,24},{4,28},{8,16},{12,20},{16,8},{20,12},{24,0},{28,4},{1,25},{... | collective-permute-start | bytes 552968 | tf_op jit(solution)/shard_map/ppermute | solution.py:399
  505.6 21.2 %collective-permute-start.63 = (bf16[96,768]{1,0:T(8,128)(2,1)S(1)}, bf16[96,768]{1,0:T(8,128)(2,1)S(1)}, u32[]{:S(2)}, u32[]{:S(2)}) collective-permute-start(bf16[96,768]{1,0:T(8,128)(2,1)S(1)} %fusion.74), channel_id=1, source_target_pairs={{0,24},{4,28},{8,16},{12,20},{16,8},{20,12},{24,0},{28,4},{1,25},{... | collective-permute-start | bytes 442376 | tf_op jit(solution)/shard_map/ppermute | solution.py:399
  508.1 32.7 %collective-permute-start.64 = (bf16[96,768]{1,0:T(8,128)(2,1)S(1)}, bf16[96,768]{1,0:T(8,128)(2,1)S(1)}, u32[]{:S(2)}, u32[]{:S(2)}) collective-permute-start(bf16[96,768]{1,0:T(8,128)(2,1)S(1)} %fusion.74), channel_id=1, source_target_pairs={{0,16},{4,20},{8,24},{12,28},{16,0},{20,4},{24,8},{28,12},{1,17},{... | collective-permute-start | bytes 442376 | tf_op jit(solution)/shard_map/ppermute | solution.py:399
  510.6 30.1 %collective-permute-start.65 = (bf16[96,768]{1,0:T(8,128)(2,1)S(1)}, bf16[96,768]{1,0:T(8,128)(2,1)S(1)}, u32[]{:S(2)}, u32[]{:S(2)}) collective-permute-start(bf16[96,768]{1,0:T(8,128)(2,1)S(1)} %fusion.74), channel_id=1, source_target_pairs={{0,8},{4,12},{8,0},{12,4},{16,24},{20,28},{24,16},{28,20},{1,9},{5... | collective-permute-start | bytes 442376 | tf_op jit(solution)/shard_map/ppermute | solution.py:399
  523.1 17.7 %collective-permute-start.32 = (f32[6,768]{1,0:T(8,128)S(1)}, f32[6,768]{1,0:T(8,128)S(1)}, u32[]{:S(2)}, u32[]{:S(2)}) collective-permute-start(f32[6,768]{1,0:T(8,128)S(1)} %add.232), channel_id=1, source_target_pairs={{0,2},{1,3},{2,0},{3,1},{4,6},{5,7},{6,4},{7,5},{8,10},{9,11},{10,... | collective-permute-start | bytes 55304 | tf_op jit(solution)/shard_map/ppermute | solution.py:399
  524.3 22.7 %collective-permute-start.52 = (bf16[120,768]{1,0:T(8,128)(2,1)S(1)}, bf16[120,768]{1,0:T(8,128)(2,1)S(1)}, u32[]{:S(2)}, u32[]{:S(2)}) collective-permute-start(bf16[120,768]{1,0:T(8,128)(2,1)S(1)} %fusion.71), channel_id=1, source_target_pairs={{0,24},{4,28},{8,16},{12,20},{16,8},{20,12},{24,0},{28,4},{1,25},{... | collective-permute-start | bytes 552968 | tf_op jit(solution)/shard_map/ppermute | solution.py:399
  526.8 22.3 %collective-permute-start.53 = (bf16[120,768]{1,0:T(8,128)(2,1)S(1)}, bf16[120,768]{1,0:T(8,128)(2,1)S(1)}, u32[]{:S(2)}, u32[]{:S(2)}) collective-permute-start(bf16[120,768]{1,0:T(8,128)(2,1)S(1)} %fusion.71), channel_id=1, source_target_pairs={{0,16},{4,20},{8,24},{12,28},{16,0},{20,4},{24,8},{28,12},{1,17},{... | collective-permute-start | bytes 552968 | tf_op jit(solution)/shard_map/ppermute | solution.py:399
  540.7 11.1 %collective-permute-start.54 = (bf16[120,768]{1,0:T(8,128)(2,1)S(1)}, bf16[120,768]{1,0:T(8,128)(2,1)S(1)}, u32[]{:S(2)}, u32[]{:S(2)}) collective-permute-start(bf16[120,768]{1,0:T(8,128)(2,1)S(1)} %fusion.71), channel_id=1, source_target_pairs={{0,8},{4,12},{8,0},{12,4},{16,24},{20,28},{24,16},{28,20},{1,9},{5... | collective-permute-start | bytes 552968 | tf_op jit(solution)/shard_map/ppermute | solution.py:399
  542.7 13.4 %collective-permute-start.66 = (bf16[384,768]{1,0:T(8,128)(2,1)S(1)}, bf16[384,768]{1,0:T(8,128)(2,1)}, u32[]{:S(2)}, u32[]{:S(2)}) collective-permute-start(bf16[384,768]{1,0:T(8,128)(2,1)S(1)} %pad_maximum_fusion.6), channel_id=1, source_target_pairs={{0,4},{4,0},{8,12},{12,8},{16,20},{20,16},{24,28},{28,24},{1,5},{5... | collective-permute-start | bytes 1769480 | tf_op jit(solution)/shard_map/ppermute | solution.py:399
  545.0 9.6 %collective-permute-start.34 = (f32[6,768]{1,0:T(8,128)S(1)}, f32[6,768]{1,0:T(8,128)S(1)}, u32[]{:S(2)}, u32[]{:S(2)}) collective-permute-start(f32[6,768]{1,0:T(8,128)S(1)} %add.234), channel_id=1, source_target_pairs={{0,8},{4,12},{8,0},{12,4},{16,24},{20,28},{24,16},{28,20},{1,9},{5... | collective-permute-start | bytes 55304 | tf_op jit(solution)/shard_map/ppermute | solution.py:399
  547.0 7.5 %collective-permute-start.35 = (f32[6,768]{1,0:T(8,128)S(1)}, f32[6,768]{1,0:T(8,128)S(1)}, u32[]{:S(2)}, u32[]{:S(2)}) collective-permute-start(f32[6,768]{1,0:T(8,128)S(1)} %add.234), channel_id=1, source_target_pairs={{0,16},{4,20},{8,24},{12,28},{16,0},{20,4},{24,8},{28,12},{1,17},{... | collective-permute-start | bytes 55304 | tf_op jit(solution)/shard_map/ppermute | solution.py:399
  549.1 5.6 collective-permute-start.36
  552.8 17.2 %collective-permute-start.55 = (bf16[480,768]{1,0:T(8,128)(2,1)}, bf16[480,768]{1,0:T(8,128)(2,1)S(1)}, u32[]{:S(2)}, u32[]{:S(2)}) collective-permute-start(bf16[480,768]{1,0:T(8,128)(2,1)} %pad_maximum_fusion.5), channel_id=1, source_target_pairs={{0,4},{4,0},{8,12},{12,8},{16,20},{20,16},{24,28},{28,24},{1,5},{5... | collective-permute-start | bytes 2211848 | tf_op jit(solution)/shard_map/ppermute | solution.py:399
  (53 other events, 419.3 us)

commit v5 on v4

--- a/solution.py
+++ b/solution.py
@@ -32,46 +32,76 @@
     return high, middle, (rest - middle.astype(f32)).astype(bf16)
 
 
-def fwd_kernel(q_ref, k_ref, v_ref, start_ref, bias_ref, o_ref, wide_ref, lse_ref, keys_ref):
+def fwd_kernel(q_ref, k_ref, v_ref, start_ref, bias_ref, o_ref, wide_ref, lse_ref, keys_ref, sa_ref, sb_ref):
     keys_ref[...] = k_ref[0].T
-
-    def finish(off, top, total, acc):
-        out = acc / total
-        wide_ref[0, :, pl.ds(off, CONT)] = out
-        o_ref[0, :, pl.ds(off, CONT)] = out.astype(bf16)
-        lse_ref[0, :, pl.ds(off, CONT)] = top + jnp.log(total)
-
-    causal = lax.broadcasted_iota(jnp.int32, (CONT, CONT), 0) <= lax.broadcasted_iota(
-        jnp.int32, (CONT, CONT), 1
-    )
-
-    def continuation(c, carry):
-        off = pl.multiple_of(PROMPT + c * CONT, CONT)
-        queries = q_ref[0, :, pl.ds(off, CONT)]
-        s1 = dot_f32(keys_ref[0:PROMPT, :], queries)
-        s2 = dot_f32(keys_ref[pl.ds(off, CONT), :], queries)
-        bias = bias_ref[pl.ds(pl.multiple_of(c * CONT, CONT), CONT), :]
-        s2 = jnp.where(causal, s2 + jnp.concatenate([bias, bias], 1), NEG)
-        top = jnp.maximum(jnp.max(s1, 0, keepdims=True), jnp.max(s2, 0, keepdims=True))
-        p1 = jnp.exp(s1 - top)
-        p2 = jnp.exp(s2 - top)
-        total = jnp.sum(p1, 0, keepdims=True) + jnp.sum(p2, 0, keepdims=True)
-        acc = dot_f32(v_ref[0, :, 0:PROMPT], p1.astype(bf16))
-        acc = acc + dot_f32(v_ref[0, :, pl.ds(off, CONT)], p2.astype(bf16))
-        finish(off, top, total, acc)
-        return carry
-
-    lax.fori_loop(0, CONTS, continuation, 0)
-    for off in range(0, PROMPT, CONT):
-        low = max(0, off - DOC_MAX)
-        span = off + CONT - low
-        s = dot_f32(keys_ref[low : off + CONT, :], q_ref[0, :, off : off + CONT])
-        key_ids = low + lax.broadcasted_iota(jnp.int32, (span, CONT), 0)
-        row_ids = off + lax.broadcasted_iota(jnp.int32, (span, CONT), 1)
-        s = jnp.where((key_ids <= row_ids) & (key_ids >= start_ref[:, off : off + CONT]), s, NEG)
-        top = jnp.max(s, 0, keepdims=True)
-        p = jnp.exp(s - top)
-        finish(off, top, jnp.sum(p, 0, keepdims=True), dot_f32(v_ref[0, :, low : off + CONT], p.astype(bf16)))
+    key_ids = lax.broadcasted_iota(jnp.int32, (CONT, CONT), 0)
+    row_ids = lax.broadcasted_iota(jnp.int32, (CONT, CONT), 1)
+    causal = key_ids <= row_ids
+    prompts = PROMPT // CONT
+
+    def cont_keys(c):
+        return [(j * CONT, None) for j in range(prompts)] + [
+            (pl.multiple_of(PROMPT + c * CONT, CONT), "own")
+        ]
+
+    def scores(off, key_off, kind, c):
+        s = dot_f32(keys_ref[pl.ds(key_off, CONT), :], q_ref[0, :, pl.ds(off, CONT)])
+        if kind == "own":
+            bias = bias_ref[pl.ds(pl.multiple_of(c * CONT, CONT), CONT), :]
+            s = jnp.where(causal, s + jnp.concatenate([bias, bias], 1), NEG)
+        if kind == "prompt":
+            ids = key_ids + key_off
+            s = jnp.where((ids <= row_ids + off) & (ids >= start_ref[:, off : off + CONT]), s, NEG)
+        return s
+
+    def step(ahead, s_ahead, behind, s_behind):
+        parts = []
+        total = acc = None
+        ahead_keys = ahead[1] if ahead else []
+        behind_keys = behind[1] if behind else []
+        for j in range(max(len(ahead_keys), len(behind_keys))):
+            if j < len(ahead_keys):
+                s = scores(ahead[0], *ahead_keys[j], ahead[2])
+                s_ahead[pl.ds(j * CONT, CONT), :] = s
+                parts.append(jnp.max(s.reshape(CONT // 8, 8, CONT), 0))
+            if j < len(behind_keys):
+                p = jnp.exp(s_behind[pl.ds(j * CONT, CONT), :] - behind[3])
+                t = jnp.sum(p.reshape(CONT // 8, 8, CONT), 0)
+                o = dot_f32(v_ref[0, :, pl.ds(behind_keys[j][0], CONT)], p.astype(bf16))
+                total = t if total is None else total + t
+                acc = o if acc is None else acc + o
+        if behind:
+            off, top = behind[0], behind[3]
+            total = jnp.sum(total, 0, keepdims=True)
+            out = acc / total
+            wide_ref[0, :, pl.ds(off, CONT)] = out
+            o_ref[0, :, pl.ds(off, CONT)] = out.astype(bf16)
+            lse_ref[0, :, pl.ds(off, CONT)] = top + jnp.log(total)
+        if ahead:
+            top = parts[0]
+            for x in parts[1:]:
+                top = jnp.maximum(top, x)
+            return jnp.max(top, 0, keepdims=True)
+
+    def cont(c):
+        return pl.multiple_of(PROMPT + c * CONT, CONT), cont_keys(c), c
+
+    def pair(i, top):
+        c = 2 * i
+        top1 = step(cont(c + 1), sb_ref, (*cont(c), top), sa_ref)
+        return step(cont(c + 2), sa_ref, (*cont(c + 1), top1), sb_ref)
+
+    top = step(cont(0), sa_ref, None, None)
+    top = lax.fori_loop(0, CONTS // 2 - 1, pair, top)
+    c = CONTS - 2
+    top1 = step(cont(c + 1), sb_ref, (*cont(c), top), sa_ref)
+    behind, refs = (*cont(c + 1), top1), (sb_ref, sa_ref)
+    for i in reversed(range(prompts)):
+        off = i * CONT
+        keys = [(k, "prompt") for k in range(max(0, off - DOC_MAX), off + CONT, CONT)]
+        top = step((off, keys, 0), refs[1], behind, refs[0])
+        behind, refs = (off, keys, 0, top), refs[::-1]
+    step(None, None, behind, refs[0])
 
 
 def head_spec(row):
@@ -100,7 +130,11 @@
             jax.ShapeDtypeStruct((1, HD, GLEN), f32),
             jax.ShapeDtypeStruct((1, 1, GLEN), f32),
         ],
-        scratch_shapes=[pltpu.VMEM((GLEN, HD), bf16)],
+        scratch_shapes=[
+            pltpu.VMEM((GLEN, HD), bf16),
+            pltpu.VMEM((PROMPT + CONT, CONT), f32),
+            pltpu.VMEM((PROMPT + CONT, CONT), f32),
+        ],
         cost_estimate=pl.CostEstimate(flops=17_000_000_000, transcendentals=0, bytes_accessed=4_000_000),
         name="attn_fwd",
     )(qkv, qkv, qkv, doc_start, key_bias)

time: 581 us -> 557 us (0.959)
  Pallas kernels: 191 us -> 167 us
    pallas_call x3, Pallas kernels: 56.8 us -> 32.7 us  [attn_fwd(): pl.pallas_call(fwd_kernel, grid=(1,), in_specs=[head_spec(head), head_spe...]
  transfers between devices with their start and end apart: 67 -> 67, of which waited for: 22 -> 22; matrix products, arithmetic and copies ran while one was open for 14% -> 14% of each run, Pallas kernels for 16% -> 12%
where the time goes in v5:
time: 557 us; the launch traced here: 550 us
  Pallas kernels  167 us (30%)
  waiting for transfers between devices  151 us (27%)
  starting transfers between devices  92.5 us (17%)
  matrix products  52.4 us (9%)
  other arithmetic  40.2 us (7%)
  local copies, waits for them, and re-layouts  40.1 us (7%)
  between operations  7.05 us (1%)
    ppermute x67, waiting for transfers between devices, swap(): return lax.ppermute(x, axis, [(i, i ^ bit) for i in range(size)])  151 us
    ppermute x67, starting transfers between devices, swap(): return lax.ppermute(x, axis, [(i, i ^ bit) for i in range(size)])  92.5 us
    pallas_call x3, Pallas kernels, attn_bwd(): pl.pallas_call(kernel, grid=(1,), in_specs=specs, out_specs=pl.BlockSpec(...  79 us
    dot_general x21, matrix products, dot(): lax.dot_general(a, b, (((ca,), (cb,)), ((), ())), preferred_element_type=...  52.4 us
    pallas_call x3, Pallas kernels, attn_fwd(): pl.pallas_call(fwd_kernel, grid=(1,), in_specs=[head_spec(head), head_spe...  32.7 us
    pallas_call x1, Pallas kernels, mid_fwd(): pl.pallas_call(mid_fwd_kernel, grid=(rows // BLOCK,), in_specs=[pl.BlockS...  25.4 us
    pallas_call x1, Pallas kernels, mid_bwd(): pl.pallas_call(mid_bwd_kernel, grid=(rows // BLOCK,), in_specs=[by_rows(D...  23.4 us
    unnamed x106, local copies, waits for them, and re-layouts  16.5 us
  transfers between devices with their start and end apart: 67, of which 22 were waited for; matrix products, arithmetic and copies ran while one was open for 14% of the time, Pallas kernels for 12%

profile of v5, /device:TPU:0, one launch (start us, length us, event | category | flops | bytes accessed | tf_op | source)
XLA Modules:
  0.0 550.2 jit_solution(14877500056612850502)
XLA Ops:
  0.7 1.9 fusion.1
  3.4 1.9 add_convert_fusion.1
  5.8 2.5 collective-permute-start.5
  8.9 3.2 fusion.108
  12.8 2.9 collective-permute-start
  15.8 2.5 fusion.50
  19.2 24.5 %collective-permute-done.5 = bf16[1024,768]{1,0:T(8,128)(2,1)} collective-permute-done((bf16[1024,768]{1,0:T(8,128)(2,1)}, bf16[1024,768]{1,0:T(8,128)(2,1)}, u32[]{:S(2)}, u32[]{:S(2)}) %collective-permute-start.5) | collective-permute-done | bytes 1572896 | tf_op jit(solution)/shard_map/ppermute | solution.py:433
  44.3 2.7 broadcast_in_dim.78
  48.9 3.2 collective-permute-start.1
  53.6 2.5 fusion.51
  56.1 2.9 fusion.52
  68.2 11.2 %attn_fwd.4 = (bf16[1,64,4096]{2,1,0:T(8,128)(2,1)}, f32[1,64,4096]{2,1,0:T(8,128)}, f32[1,1,4096]{2,1,0:T(1,128)}) custom-call(bf16[9,64,4096]{2,1,0:T(8,128)(2,1)} %bitcast.8.q_ref.k_ref.v_ref.refs_1_.refs_2_.refs_3_, bf16[9,64,4096]{2,1,0:T(8,128)(2,1)} %bitcast.8.q_ref.k_ref.v_ref.refs_1_.refs_2_.refs_3_, ...), custom_call_target="tpu_custom_call" | custom-call | flops 16999999488 | bytes 4000000 | tf_op jit(solution)/shard_map/attn_fwd/pallas_call | solution.py:117
  79.4 10.6 %attn_fwd.3 = (bf16[1,64,4096]{2,1,0:T(8,128)(2,1)}, f32[1,64,4096]{2,1,0:T(8,128)}, f32[1,1,4096]{2,1,0:T(1,128)}) custom-call(bf16[9,64,4096]{2,1,0:T(8,128)(2,1)} %bitcast.8.q_ref.k_ref.v_ref.refs_1_.refs_2_.refs_3_, bf16[9,64,4096]{2,1,0:T(8,128)(2,1)} %bitcast.8.q_ref.k_ref.v_ref.refs_1_.refs_2_.refs_3_, ...), custom_call_target="tpu_custom_call" | custom-call | flops 16999999488 | bytes 4000000 | tf_op jit(solution)/shard_map/attn_fwd/pallas_call | solution.py:117
  90.0 10.9 %attn_fwd.5 = (bf16[1,64,4096]{2,1,0:T(8,128)(2,1)}, f32[1,64,4096]{2,1,0:T(8,128)}, f32[1,1,4096]{2,1,0:T(1,128)}) custom-call(bf16[9,64,4096]{2,1,0:T(8,128)(2,1)} %bitcast.8.q_ref.k_ref.v_ref.refs_1_.refs_2_.refs_3_, bf16[9,64,4096]{2,1,0:T(8,128)(2,1)} %bitcast.8.q_ref.k_ref.v_ref.refs_1_.refs_2_.refs_3_, ...), custom_call_target="tpu_custom_call" | custom-call | flops 16999999488 | bytes 4000000 | tf_op jit(solution)/shard_map/attn_fwd/pallas_call | solution.py:117
  102.7 3.9 collective-permute-start.2
  107.1 3.8 collective-permute-start.3
  126.2 3.4 collective-permute-done.9
  132.1 6.0 %collective-permute-done.11 = bf16[128,1024]{1,0:T(8,128)(2,1)S(1)} collective-permute-done((bf16[128,1024]{1,0:T(8,128)(2,1)S(1)}, bf16[128,1024]{1,0:T(8,128)(2,1)S(1)}, u32[]{:S(2)}, u32[]{:S(2)}) %collective-permute-start.11) | collective-permute-done | bytes 262176 | tf_op jit(solution)/shard_map/ppermute | solution.py:433
  139.9 3.8 collective-permute-done.12
  148.5 25.4 %mid_fwd.1 = (bf16[1024,768]{1,0:T(8,128)(2,1)}, bf16[1024,768]{1,0:T(8,128)(2,1)}, bf16[4,1024,768]{2,1,0:T(8,128)(2,1)}, f32[4,1024,768]{2,1,0:T(8,128)}, bf16...) custom-call(f32[1,1]{1,0:T(1,128)} %bitcast.2.scale_ref, ...), custom_call_target="tpu_custom_call" | custom-call | flops 22000001024 | bytes 30000000 | tf_op jit(solution)/shard_map/mid_fwd/pallas_call | solution.py:391
  173.9 4.5 fusion.35
  178.4 4.0 fusion.32
  182.4 2.5 fusion.29
  184.9 2.5 fusion.26
  187.4 23.4 %mid_bwd.1 = (bf16[4,1024,768]{2,1,0:T(8,128)(2,1)}, f32[1024,768]{1,0:T(8,128)}, bf16[1024,768]{1,0:T(8,128)(2,1)}, bf16[768,1024]{1,0:T(8,128)(2,1)}, f32[1,768]{1,0:T(1,128)}, /*index=5*/f32[1,768]{1,0:T(1,128)}) custom-call(bf16[1024,768]{1,0:T(8,128)(2,1)} %get-tuple-element.61.branch_ref, f32[4,1024,768]{2,1,0:T(8,128)} %get-tuple-element.62.slope_ref, ...), custom_call_target="tpu_custom_call" | custom-call | flops 22000001024 | bytes 30000000 | tf_op jit(solution)/shard_map/mid_bwd/pallas_call | solution.py:416
  210.8 3.0 fusion.47
  231.3 26.5 %attn_bwd.3.refs_9_ = bf16[3,3,64,4096]{3,2,1,0:T(8,128)(2,1)} custom-call(s32[8]{0:T(128)} %and_select_fusion.last_ref.refs_0_, bf16[9,64,4096]{2,1,0:T(8,128)(2,1)} %bitcast.8.q_ref.k_ref.v_ref.refs_1_.refs_2_.refs_3_, bf16[9,64,4096]{2,1,0:T(8,128)(2,1)} %bitcast.8.q_ref.k_ref.v_ref.refs_1_.refs_2_.refs_3_, ...), custom_call_target="tpu_custom_call" | custom-call | flops 30000001024 | bytes 8000000 | tf_op jit(solution)/shard_map/attn_bwd/pallas_call | solution.py:259
  259.1 26.3 %attn_bwd.4.refs_9_ = bf16[3,3,64,4096]{3,2,1,0:T(8,128)(2,1)} custom-call(s32[8]{0:T(128)} %and_select_fusion.last_ref.refs_0_, bf16[9,64,4096]{2,1,0:T(8,128)(2,1)} %bitcast.8.q_ref.k_ref.v_ref.refs_1_.refs_2_.refs_3_, bf16[9,64,4096]{2,1,0:T(8,128)(2,1)} %bitcast.8.q_ref.k_ref.v_ref.refs_1_.refs_2_.refs_3_, ...), custom_call_target="tpu_custom_call", output_to_operand_aliasing={{}: (9, {})} | custom-call | flops 30000001024 | bytes 8000000 | tf_op jit(solution)/shard_map/attn_bwd/pallas_call | solution.py:259
  285.4 26.3 %attn_bwd.5 = bf16[3,3,64,4096]{3,2,1,0:T(8,128)(2,1)} custom-call(s32[8]{0:T(128)} %and_select_fusion.last_ref.refs_0_, bf16[9,64,4096]{2,1,0:T(8,128)(2,1)} %bitcast.8.q_ref.k_ref.v_ref.refs_1_.refs_2_.refs_3_, bf16[9,64,4096]{2,1,0:T(8,128)(2,1)} %bitcast.8.q_ref.k_ref.v_ref.refs_1_.refs_2_.refs_3_, ...), custom_call_target="tpu_custom_call", output_to_operand_aliasing={{}: (9, {})} | custom-call | flops 30000001024 | bytes 8000000 | tf_op jit(solution)/shard_map/attn_bwd/pallas_call | solution.py:259
  311.6 3.0 fusion.63
  314.8 2.5 fusion.57
  317.3 2.6 fusion.60
  319.9 2.3 add_add_fusion
  322.3 2.4 reshape.137
  325.6 8.9 %collective-permute-start.37 = (bf16[384,576]{0,1:T(8,128)(2,1)S(1)}, bf16[384,576]{0,1:T(8,128)(2,1)S(1)}, u32[]{:S(2)}, u32[]{:S(2)}) collective-permute-start(bf16[384,576]{0,1:T(8,128)(2,1)S(1)} %bitcast.209), channel_id=1, source_target_pairs={{0,4},{4,0},{8,12},{12,8},{16,20},{20,16},{24,28},{28,24},{1,5},{5... | collective-permute-start | bytes 1327112 | tf_op jit(solution)/shard_map/ppermute | solution.py:433
  336.4 8.9 %collective-permute-done.37 = bf16[384,576]{0,1:T(8,128)(2,1)S(1)} collective-permute-done((bf16[384,576]{0,1:T(8,128)(2,1)S(1)}, bf16[384,576]{0,1:T(8,128)(2,1)S(1)}, u32[]{:S(2)}, u32[]{:S(2)}) %collective-permute-start.37) | collective-permute-done | bytes 442400 | tf_op jit(solution)/shard_map/ppermute | solution.py:433
  345.9 2.9 convolution_convert_fusion
  351.0 2.1 collective-permute-start.40
  353.1 2.6 convolution_convert_fusion.2
  355.7 5.5 %collective-permute-done.39 = bf16[96,576]{1,0:T(8,128)(2,1)S(1)} collective-permute-done((bf16[96,576]{1,0:T(8,128)(2,1)S(1)}, bf16[96,576]{1,0:T(8,128)(2,1)S(1)}, u32[]{:S(2)}, u32[]{:S(2)}) %collective-permute-start.39) | collective-permute-done | bytes 110624 | tf_op jit(solution)/shard_map/ppermute | solution.py:433
  362.7 2.8 collective-permute-start.42
  367.2 2.4 collective-permute-done.41
  369.5 5.4 collective-permute-start.43
  379.9 2.6 convolution_convert_fusion.3.part_ref
  382.8 2.6 add_convert_fusion
  387.1 16.6 %collective-permute-done.58 = bf16[768,768]{1,0:T(8,128)(2,1)S(1)} collective-permute-done((bf16[768,768]{1,0:T(8,128)(2,1)S(1)}, bf16[768,768]{1,0:T(8,128)(2,1)S(1)}, u32[]{:S(2)}, u32[]{:S(2)}) %collective-permute-start.58) | collective-permute-done | bytes 1179680 | tf_op jit(solution)/shard_map/ppermute | solution.py:433
  408.0 27.3 %collective-permute-done.47 = bf16[960,768]{1,0:T(8,128)(2,1)S(1)} collective-permute-done((bf16[960,768]{1,0:T(8,128)(2,1)S(1)}, bf16[960,768]{1,0:T(8,128)(2,1)S(1)}, u32[]{:S(2)}, u32[]{:S(2)}) %collective-permute-start.47) | collective-permute-done | bytes 1474592 | tf_op jit(solution)/shard_map/ppermute | solution.py:433
  439.8 2.0 copy.44
  441.8 2.0 copy.45
  443.8 2.5 maximum_convert_fusion.1
  450.8 2.5 collective-permute-start.62
  453.3 13.2 %collective-permute-done.30.far_ref = bf16[1024,768]{1,0:T(8,128)(2,1)} collective-permute-done((bf16[1024,768]{1,0:T(8,128)(2,1)}, bf16[1024,768]{1,0:T(8,128)(2,1)}, u32[]{:S(2)}, u32[]{:S(2)}) %collective-permute-start.30) | collective-permute-done | bytes 1572896 | tf_op jit(solution)/shard_map/ppermute | solution.py:433
  466.5 6.8 %final.1 = (bf16[1024,768]{1,0:T(8,128)(2,1)}, f32[1,768]{1,0:T(1,128)}, f32[1,768]{1,0:T(1,128)}, f32[1,768]{1,0:T(1,128)}) custom-call(bf16[1024,768]{1,0:T(8,128)(2,1)} %x_ref.3, f32[1,768]{1,0:T(1,128)} %broadcast_in_dim.85.embed_ref, f32[1,768]{1,0:T(1,128)} %broadcast_in_dim.89.gain_ref, bf16[1024,768]{1,0:T(8,128)(2,1)} %convolution_convert_fusion.3.part_ref, ...), custom_call_target="tpu_custom_call" | custom-call | tf_op jit(solution)/shard_map/final/pallas_call | solution.py:658
  476.4 2.7 collective-permute-start.50
  481.5 2.5 collective-permute-start.63
  484.0 2.6 collective-permute-done.49
  486.6 12.5 %collective-permute-done.50 = bf16[120,768]{1,0:T(8,128)(2,1)S(1)} collective-permute-done((bf16[120,768]{1,0:T(8,128)(2,1)S(1)}, bf16[120,768]{1,0:T(8,128)(2,1)S(1)}, u32[]{:S(2)}, u32[]{:S(2)}) %collective-permute-start.50) | collective-permute-done | bytes 184352 | tf_op jit(solution)/shard_map/ppermute | solution.py:433
  500.3 2.5 collective-permute-start.52
  502.7 8.9 %collective-permute-start.53 = (bf16[120,768]{1,0:T(8,128)(2,1)S(1)}, bf16[120,768]{1,0:T(8,128)(2,1)S(1)}, u32[]{:S(2)}, u32[]{:S(2)}) collective-permute-start(bf16[120,768]{1,0:T(8,128)(2,1)S(1)} %fusion.71), channel_id=1, source_target_pairs={{0,16},{4,20},{8,24},{12,28},{16,0},{20,4},{24,8},{28,12},{1,17},{... | collective-permute-start | bytes 552968 | tf_op jit(solution)/shard_map/ppermute | solution.py:433
  511.6 5.0 collective-permute-done.64
  519.0 2.0 collective-permute-done.33
  520.9 2.0 collective-permute-start.34
  525.0 2.7 collective-permute-start.36
  534.8 11.1 %collective-permute-done.55 = bf16[480,768]{1,0:T(8,128)(2,1)S(1)} collective-permute-done((bf16[480,768]{1,0:T(8,128)(2,1)}, bf16[480,768]{1,0:T(8,128)(2,1)S(1)}, u32[]{:S(2)}, u32[]{:S(2)}) %collective-permute-start.55) | collective-permute-done | bytes 737312 | tf_op jit(solution)/shard_map/ppermute | solution.py:433
  (302 shorter events, 107.9 us)
Async XLA Ops:
  5.3 48.3 %collective-permute-start.4 = (bf16[1024,768]{1,0:T(8,128)(2,1)}, bf16[1024,768]{1,0:T(8,128)(2,1)}, u32[]{:S(2)}, u32[]{:S(2)}) collective-permute-start(bf16[1024,768]{1,0:T(8,128)(2,1)} %add_convert_fusion.1), channel_id=1, source_target_pairs={{0,1},{1,0},{2,3},{3,2},{4,5},{5,4},{6,7},{7,6},{8,9},{9,8},{10,11... | collective-permute-start | bytes 4718600 | tf_op jit(solution)/shard_map/ppermute | solution.py:433
  5.8 37.9 %collective-permute-start.5 = (bf16[1024,768]{1,0:T(8,128)(2,1)}, bf16[1024,768]{1,0:T(8,128)(2,1)}, u32[]{:S(2)}, u32[]{:S(2)}) collective-permute-start(bf16[1024,768]{1,0:T(8,128)(2,1)} %add_convert_fusion.1), channel_id=1, source_target_pairs={{0,2},{1,3},{2,0},{3,1},{4,6},{5,7},{6,4},{7,5},{8,10},{9,11},{10,... | collective-permute-start | bytes 4718600 | tf_op jit(solution)/shard_map/ppermute | solution.py:433
  12.8 35.4 %collective-permute-start = (f32[1,1]{1,0:T(1,128)}, f32[1,1]{1,0:T(1,128)}, u32[]{:S(2)}, u32[]{:S(2)}) collective-permute-start(f32[1,1]{1,0:T(1,128)} %bitcast), channel_id=1, source_target_pairs={{0,4},{4,0},{8,12},{12,8},{16,20},{20,16},{24,28},{28,24},{1,5},{5... | collective-permute-start | bytes 20 | tf_op jit(solution)/shard_map/ppermute | solution.py:433
  43.6 20.8 %collective-permute-start.6 = (bf16[1024,768]{1,0:T(8,128)(2,1)}, bf16[1024,768]{1,0:T(8,128)(2,1)S(1)}, u32[]{:S(2)}, u32[]{:S(2)}) collective-permute-start(bf16[1024,768]{1,0:T(8,128)(2,1)} %collective-permute-done.5), channel_id=1, source_target_pairs={{0,1},{1,0},{2,3},{3,2},{4,5},{5,4},{6,7},{7,6},{8,9},{9,8},{10,11... | collective-permute-start | bytes 4718600 | tf_op jit(solution)/shard_map/ppermute | solution.py:433
  48.9 53.8 %collective-permute-start.1 = (f32[1,1]{1,0:T(1,128)}, f32[1,1]{1,0:T(1,128)}, u32[]{:S(2)}, u32[]{:S(2)}) collective-permute-start(f32[1,1]{1,0:T(1,128)} %add.214), channel_id=1, source_target_pairs={{0,8},{4,12},{8,0},{12,4},{16,24},{20,28},{24,16},{28,20},{1,9},{5... | collective-permute-start | bytes 20 | tf_op jit(solution)/shard_map/ppermute | solution.py:433
  52.1 11.0 %collective-permute-start.14 = (bf16[192,768]{1,0:T(8,128)(2,1)S(1)}, bf16[192,768]{1,0:T(8,128)(2,1)}, u32[]{:S(2)}, u32[]{:S(2)}) collective-permute-start(bf16[192,768]{1,0:T(8,128)(2,1)S(1)} %copy-done.19), channel_id=1, source_target_pairs={{0,2},{1,3},{2,0},{3,1},{4,6},{5,7},{6,4},{7,5},{8,10},{9,11},{10,... | collective-permute-start | bytes 884744 | tf_op jit(solution)/shard_map/ppermute | solution.py:433
  60.1 52.5 %collective-permute-start.13 = (bf16[192,768]{1,0:T(8,128)(2,1)S(1)}, bf16[192,768]{1,0:T(8,128)(2,1)}, u32[]{:S(2)}, u32[]{:S(2)}) collective-permute-start(bf16[192,768]{1,0:T(8,128)(2,1)S(1)} %copy-done.19), channel_id=1, source_target_pairs={{0,1},{1,0},{2,3},{3,2},{4,5},{5,4},{6,7},{7,6},{8,9},{9,8},{10,11... | collective-permute-start | bytes 884744 | tf_op jit(solution)/shard_map/ppermute | solution.py:433
  60.1 58.8 %collective-permute-start.17 = (bf16[768,768]{1,0:T(8,128)(2,1)}, bf16[768,768]{1,0:T(8,128)(2,1)}, u32[]{:S(2)}, u32[]{:S(2)}) collective-permute-start(bf16[768,768]{1,0:T(8,128)(2,1)} %e0.1), channel_id=1, source_target_pairs={{0,2},{1,3},{2,0},{3,1},{4,6},{5,7},{6,4},{7,5},{8,10},{9,11},{10,... | collective-permute-start | bytes 3538952 | tf_op jit(solution)/shard_map/ppermute | solution.py:433
  63.0 56.2 %collective-permute-start.20 = (bf16[768,768]{1,0:T(8,128)(2,1)}, bf16[768,768]{1,0:T(8,128)(2,1)}, u32[]{:S(2)}, u32[]{:S(2)}) collective-permute-start(bf16[768,768]{1,0:T(8,128)(2,1)} %r0.1), channel_id=1, source_target_pairs={{0,2},{1,3},{2,0},{3,1},{4,6},{5,7},{6,4},{7,5},{8,10},{9,11},{10,... | collective-permute-start | bytes 3538952 | tf_op jit(solution)/shard_map/ppermute | solution.py:433
  64.5 49.5 %collective-permute-start.15 = (bf16[192,768]{1,0:T(8,128)(2,1)}, bf16[192,768]{1,0:T(8,128)(2,1)}, u32[]{:S(2)}, u32[]{:S(2)}) collective-permute-start(bf16[192,768]{1,0:T(8,128)(2,1)} %collective-permute-done.14), channel_id=1, source_target_pairs={{0,1},{1,0},{2,3},{3,2},{4,5},{5,4},{6,7},{7,6},{8,9},{9,8},{10,11... | collective-permute-start | bytes 884744 | tf_op jit(solution)/shard_map/ppermute | solution.py:433
  107.1 5.5 collective-permute-start.3
  112.6 6.8 %collective-permute-start.8 = (bf16[64,1024]{1,0:T(8,128)(2,1)}, bf16[64,1024]{1,0:T(8,128)(2,1)S(1)}, u32[]{:S(2)}, u32[]{:S(2)}) collective-permute-start(bf16[64,1024]{1,0:T(8,128)(2,1)} %get-tuple-element.143), channel_id=1, source_target_pairs={{0,1},{1,0},{2,3},{3,2},{4,5},{5,4},{6,7},{7,6},{8,9},{9,8},{10,11... | collective-permute-start | bytes 393224 | tf_op jit(solution)/shard_map/ppermute | solution.py:433
  112.6 7.1 %collective-permute-start.10 = (bf16[64,1024]{1,0:T(8,128)(2,1)}, bf16[64,1024]{1,0:T(8,128)(2,1)S(1)}, u32[]{:S(2)}, u32[]{:S(2)}) collective-permute-start(bf16[64,1024]{1,0:T(8,128)(2,1)} %get-tuple-element.142), channel_id=1, source_target_pairs={{0,2},{1,3},{2,0},{3,1},{4,6},{5,7},{6,4},{7,5},{8,10},{9,11},{10,... | collective-permute-start | bytes 393224 | tf_op jit(solution)/shard_map/ppermute | solution.py:433
  114.0 7.0 %collective-permute-start.7 = (bf16[128,1024]{1,0:T(8,128)(2,1)S(1)}, bf16[128,1024]{1,0:T(8,128)(2,1)S(1)}, u32[]{:S(2)}, u32[]{:S(2)}) collective-permute-start(bf16[128,1024]{1,0:T(8,128)(2,1)S(1)} %get-tuple-element.126), channel_id=1, source_target_pairs={{0,1},{1,0},{2,3},{3,2},{4,5},{5,4},{6,7},{7,6},{8,9},{9,8},{10,11... | collective-permute-start | bytes 786440 | tf_op jit(solution)/shard_map/ppermute | solution.py:433
  118.9 25.5 %collective-permute-start.16 = (bf16[768,768]{1,0:T(8,128)(2,1)}, bf16[768,768]{1,0:T(8,128)(2,1)S(1)}, u32[]{:S(2)}, u32[]{:S(2)}) collective-permute-start(bf16[768,768]{1,0:T(8,128)(2,1)} %e0.1), channel_id=1, source_target_pairs={{0,1},{1,0},{2,3},{3,2},{4,5},{5,4},{6,7},{7,6},{8,9},{9,8},{10,11... | collective-permute-start | bytes 3538952 | tf_op jit(solution)/shard_map/ppermute | solution.py:433
  119.2 26.2 %collective-permute-start.19 = (bf16[768,768]{1,0:T(8,128)(2,1)}, bf16[768,768]{1,0:T(8,128)(2,1)S(1)}, u32[]{:S(2)}, u32[]{:S(2)}) collective-permute-start(bf16[768,768]{1,0:T(8,128)(2,1)} %r0.1), channel_id=1, source_target_pairs={{0,1},{1,0},{2,3},{3,2},{4,5},{5,4},{6,7},{7,6},{8,9},{9,8},{10,11... | collective-permute-start | bytes 3538952 | tf_op jit(solution)/shard_map/ppermute | solution.py:433
  119.4 27.0 %collective-permute-start.18 = (bf16[768,768]{1,0:T(8,128)(2,1)}, bf16[768,768]{1,0:T(8,128)(2,1)S(1)}, u32[]{:S(2)}, u32[]{:S(2)}) collective-permute-start(bf16[768,768]{1,0:T(8,128)(2,1)} %collective-permute-done.17.e2), channel_id=1, source_target_pairs={{0,1},{1,0},{2,3},{3,2},{4,5},{5,4},{6,7},{7,6},{8,9},{9,8},{10,11... | collective-permute-start | bytes 3538952 | tf_op jit(solution)/shard_map/ppermute | solution.py:433
  119.7 27.7 %collective-permute-start.21 = (bf16[768,768]{1,0:T(8,128)(2,1)}, bf16[768,768]{1,0:T(8,128)(2,1)S(1)}, u32[]{:S(2)}, u32[]{:S(2)}) collective-permute-start(bf16[768,768]{1,0:T(8,128)(2,1)} %collective-permute-done.20.r2), channel_id=1, source_target_pairs={{0,1},{1,0},{2,3},{3,2},{4,5},{5,4},{6,7},{7,6},{8,9},{9,8},{10,11... | collective-permute-start | bytes 3538952 | tf_op jit(solution)/shard_map/ppermute | solution.py:433
  121.0 8.6 %collective-permute-start.9 = (bf16[128,1024]{1,0:T(8,128)(2,1)S(1)}, bf16[128,1024]{1,0:T(8,128)(2,1)S(1)}, u32[]{:S(2)}, u32[]{:S(2)}) collective-permute-start(bf16[128,1024]{1,0:T(8,128)(2,1)S(1)} %get-tuple-element.127), channel_id=1, source_target_pairs={{0,2},{1,3},{2,0},{3,1},{4,6},{5,7},{6,4},{7,5},{8,10},{9,11},{10,... | collective-permute-start | bytes 786440 | tf_op jit(solution)/shard_map/ppermute | solution.py:433
  129.6 8.6 %collective-permute-start.11 = (bf16[128,1024]{1,0:T(8,128)(2,1)S(1)}, bf16[128,1024]{1,0:T(8,128)(2,1)S(1)}, u32[]{:S(2)}, u32[]{:S(2)}) collective-permute-start(bf16[128,1024]{1,0:T(8,128)(2,1)S(1)} %get-tuple-element.124), channel_id=1, source_target_pairs={{0,3},{1,2},{2,1},{3,0},{4,7},{5,6},{6,5},{7,4},{8,11},{9,10},{10,... | collective-permute-start | bytes 786440 | tf_op jit(solution)/shard_map/ppermute | solution.py:433
  138.2 5.5 %collective-permute-start.12 = (bf16[64,1024]{1,0:T(8,128)(2,1)S(1)}, bf16[64,1024]{1,0:T(8,128)(2,1)S(1)}, u32[]{:S(2)}, u32[]{:S(2)}) collective-permute-start(bf16[64,1024]{1,0:T(8,128)(2,1)S(1)} %copy-done.20), channel_id=1, source_target_pairs={{0,3},{1,2},{2,1},{3,0},{4,7},{5,6},{6,5},{7,4},{8,11},{9,10},{10,... | collective-permute-start | bytes 393224 | tf_op jit(solution)/shard_map/ppermute | solution.py:433
  221.5 8.8 %collective-permute-start.25 = (bf16[64,1024]{1,0:T(8,128)(2,1)S(1)}, bf16[64,1024]{1,0:T(8,128)(2,1)S(1)}, u32[]{:S(2)}, u32[]{:S(2)}) collective-permute-start(bf16[64,1024]{1,0:T(8,128)(2,1)S(1)} %get-tuple-element.103), channel_id=1, source_target_pairs={{0,3},{1,2},{2,1},{3,0},{4,7},{5,6},{6,5},{7,4},{8,11},{9,10},{10,... | collective-permute-start | bytes 393224 | tf_op jit(solution)/shard_map/ppermute | solution.py:433
  222.4 8.1 %collective-permute-start.26 = (bf16[64,1024]{1,0:T(8,128)(2,1)S(1)}, bf16[64,1024]{1,0:T(8,128)(2,1)S(1)}, u32[]{:S(2)}, u32[]{:S(2)}) collective-permute-start(bf16[64,1024]{1,0:T(8,128)(2,1)S(1)} %get-tuple-element.102), channel_id=1, source_target_pairs={{0,2},{1,3},{2,0},{3,1},{4,6},{5,7},{6,4},{7,5},{8,10},{9,11},{10,... | collective-permute-start | bytes 393224 | tf_op jit(solution)/shard_map/ppermute | solution.py:433
  223.3 7.2 %collective-permute-start.27 = (bf16[64,1024]{1,0:T(8,128)(2,1)S(1)}, bf16[64,1024]{1,0:T(8,128)(2,1)S(1)}, u32[]{:S(2)}, u32[]{:S(2)}) collective-permute-start(bf16[64,1024]{1,0:T(8,128)(2,1)S(1)} %get-tuple-element.101), channel_id=1, source_target_pairs={{0,1},{1,0},{2,3},{3,2},{4,5},{5,4},{6,7},{7,6},{8,9},{9,8},{10,11... | collective-permute-start | bytes 393224 | tf_op jit(solution)/shard_map/ppermute | solution.py:433
  223.4 34.4 %collective-permute-start.22 = (bf16[128,1024]{1,0:T(8,128)(2,1)S(1)}, bf16[128,1024]{1,0:T(8,128)(2,1)S(1)}, u32[]{:S(2)}, u32[]{:S(2)}) collective-permute-start(bf16[128,1024]{1,0:T(8,128)(2,1)S(1)} %bitcast.222), channel_id=1, source_target_pairs={{0,3},{1,2},{2,1},{3,0},{4,7},{5,6},{6,5},{7,4},{8,11},{9,10},{10,... | collective-permute-start | bytes 786440 | tf_op jit(solution)/shard_map/ppermute | solution.py:433
  224.5 33.4 %collective-permute-start.23 = (bf16[128,1024]{1,0:T(8,128)(2,1)S(1)}, bf16[128,1024]{1,0:T(8,128)(2,1)S(1)}, u32[]{:S(2)}, u32[]{:S(2)}) collective-permute-start(bf16[128,1024]{1,0:T(8,128)(2,1)S(1)} %bitcast.221), channel_id=1, source_target_pairs={{0,2},{1,3},{2,0},{3,1},{4,6},{5,7},{6,4},{7,5},{8,10},{9,11},{10,... | collective-permute-start | bytes 786440 | tf_op jit(solution)/shard_map/ppermute | solution.py:433
  230.3 27.7 %collective-permute-start.24 = (bf16[128,1024]{1,0:T(8,128)(2,1)S(1)}, bf16[128,1024]{1,0:T(8,128)(2,1)S(1)}, u32[]{:S(2)}, u32[]{:S(2)}) collective-permute-start(bf16[128,1024]{1,0:T(8,128)(2,1)S(1)} %bitcast.220), channel_id=1, source_target_pairs={{0,1},{1,0},{2,3},{3,2},{4,5},{5,4},{6,7},{7,6},{8,9},{9,8},{10,11... | collective-permute-start | bytes 786440 | tf_op jit(solution)/shard_map/ppermute | solution.py:433
  325.6 19.7 %collective-permute-start.37 = (bf16[384,576]{0,1:T(8,128)(2,1)S(1)}, bf16[384,576]{0,1:T(8,128)(2,1)S(1)}, u32[]{:S(2)}, u32[]{:S(2)}) collective-permute-start(bf16[384,576]{0,1:T(8,128)(2,1)S(1)} %bitcast.209), channel_id=1, source_target_pairs={{0,4},{4,0},{8,12},{12,8},{16,20},{20,16},{24,28},{28,24},{1,5},{5... | collective-permute-start | bytes 1327112 | tf_op jit(solution)/shard_map/ppermute | solution.py:433
  335.1 27.6 %collective-permute-start.57 = (bf16[768,768]{1,0:T(8,128)(2,1)}, bf16[768,768]{1,0:T(8,128)(2,1)}, u32[]{:S(2)}, u32[]{:S(2)}) collective-permute-start(bf16[768,768]{1,0:T(8,128)(2,1)} %fusion.35), channel_id=1, source_target_pairs={{0,1},{1,0},{2,3},{3,2},{4,5},{5,4},{6,7},{7,6},{8,9},{9,8},{10,11... | collective-permute-start | bytes 3538952 | tf_op jit(solution)/shard_map/ppermute | solution.py:433
  335.3 39.6 %collective-permute-start.46 = (bf16[960,768]{1,0:T(8,128)(2,1)}, bf16[960,768]{1,0:T(8,128)(2,1)}, u32[]{:S(2)}, u32[]{:S(2)}) collective-permute-start(bf16[960,768]{1,0:T(8,128)(2,1)} %pad_maximum_fusion.3), channel_id=1, source_target_pairs={{0,1},{1,0},{2,3},{3,2},{4,5},{5,4},{6,7},{7,6},{8,9},{9,8},{10,11... | collective-permute-start | bytes 4423688 | tf_op jit(solution)/shard_map/ppermute | solution.py:433
  348.8 33.9 %collective-permute-start.29 = (bf16[1024,768]{1,0:T(8,128)(2,1)S(1)}, bf16[1024,768]{1,0:T(8,128)(2,1)S(1)}, u32[]{:S(2)}, u32[]{:S(2)}) collective-permute-start(bf16[1024,768]{1,0:T(8,128)(2,1)S(1)} %convolution_convert_fusion), channel_id=1, source_target_pairs={{0,1},{1,0},{2,3},{3,2},{4,5},{5,4},{6,7},{7,6},{8,9},{9,8},{10,11... | collective-permute-start | bytes 4718600 | tf_op jit(solution)/shard_map/ppermute | solution.py:433
  348.9 12.4 %collective-permute-start.39 = (bf16[96,576]{1,0:T(8,128)(2,1)S(1)}, bf16[96,576]{1,0:T(8,128)(2,1)S(1)}, u32[]{:S(2)}, u32[]{:S(2)}) collective-permute-start(bf16[96,576]{1,0:T(8,128)(2,1)S(1)} %get-tuple-element.132), channel_id=1, source_target_pairs={{0,16},{4,20},{8,24},{12,28},{16,0},{20,4},{24,8},{28,12},{1,17},{... | collective-permute-start | bytes 331784 | tf_op jit(solution)/shard_map/ppermute | solution.py:433
  351.0 10.3 %collective-permute-start.40 = (bf16[96,576]{1,0:T(8,128)(2,1)S(1)}, bf16[96,576]{1,0:T(8,128)(2,1)S(1)}, u32[]{:S(2)}, u32[]{:S(2)}) collective-permute-start(bf16[96,576]{1,0:T(8,128)(2,1)S(1)} %get-tuple-element.131), channel_id=1, source_target_pairs={{0,24},{4,28},{8,16},{12,20},{16,8},{20,12},{24,0},{28,4},{1,25},{... | collective-permute-start | bytes 331784 | tf_op jit(solution)/shard_map/ppermute | solution.py:433
  361.3 24.1 %collective-permute-start.56 = (bf16[768,768]{1,0:T(8,128)(2,1)S(1)}, bf16[768,768]{1,0:T(8,128)(2,1)S(1)}, u32[]{:S(2)}, u32[]{:S(2)}) collective-permute-start(bf16[768,768]{1,0:T(8,128)(2,1)S(1)} %copy-done.36), channel_id=1, source_target_pairs={{0,1},{1,0},{2,3},{3,2},{4,5},{5,4},{6,7},{7,6},{8,9},{9,8},{10,11... | collective-permute-start | bytes 3538952 | tf_op jit(solution)/shard_map/ppermute | solution.py:433
  361.4 8.2 %collective-permute-start.41 = (bf16[96,576]{1,0:T(8,128)(2,1)S(1)}, bf16[96,576]{1,0:T(8,128)(2,1)S(1)}, u32[]{:S(2)}, u32[]{:S(2)}) collective-permute-start(bf16[96,576]{1,0:T(8,128)(2,1)S(1)} %fusion.82), channel_id=1, source_target_pairs={{0,24},{4,28},{8,16},{12,20},{16,8},{20,12},{24,0},{28,4},{1,25},{... | collective-permute-start | bytes 331784 | tf_op jit(solution)/shard_map/ppermute | solution.py:433
  362.7 15.1 %collective-permute-start.42 = (bf16[96,576]{1,0:T(8,128)(2,1)S(1)}, bf16[96,576]{1,0:T(8,128)(2,1)S(1)}, u32[]{:S(2)}, u32[]{:S(2)}) collective-permute-start(bf16[96,576]{1,0:T(8,128)(2,1)S(1)} %fusion.82), channel_id=1, source_target_pairs={{0,16},{4,20},{8,24},{12,28},{16,0},{20,4},{24,8},{28,12},{1,17},{... | collective-permute-start | bytes 331784 | tf_op jit(solution)/shard_map/ppermute | solution.py:433
  369.5 9.3 %collective-permute-start.43 = (bf16[96,576]{1,0:T(8,128)(2,1)S(1)}, bf16[96,576]{1,0:T(8,128)(2,1)S(1)}, u32[]{:S(2)}, u32[]{:S(2)}) collective-permute-start(bf16[96,576]{1,0:T(8,128)(2,1)S(1)} %fusion.82), channel_id=1, source_target_pairs={{0,8},{4,12},{8,0},{12,4},{16,24},{20,28},{24,16},{28,20},{1,9},{5... | collective-permute-start | bytes 331784 | tf_op jit(solution)/shard_map/ppermute | solution.py:433
  374.9 28.8 %collective-permute-start.58 = (bf16[768,768]{1,0:T(8,128)(2,1)S(1)}, bf16[768,768]{1,0:T(8,128)(2,1)S(1)}, u32[]{:S(2)}, u32[]{:S(2)}) collective-permute-start(bf16[768,768]{1,0:T(8,128)(2,1)S(1)} %add_convert_fusion.3), channel_id=1, source_target_pairs={{0,2},{1,3},{2,0},{3,1},{4,6},{5,7},{6,4},{7,5},{8,10},{9,11},{10,... | collective-permute-start | bytes 3538952 | tf_op jit(solution)/shard_map/ppermute | solution.py:433
  377.8 28.4 %collective-permute-start.45 = (bf16[960,768]{1,0:T(8,128)(2,1)S(1)}, bf16[960,768]{1,0:T(8,128)(2,1)S(1)}, u32[]{:S(2)}, u32[]{:S(2)}) collective-permute-start(bf16[960,768]{1,0:T(8,128)(2,1)S(1)} %copy-done.12), channel_id=1, source_target_pairs={{0,1},{1,0},{2,3},{3,2},{4,5},{5,4},{6,7},{7,6},{8,9},{9,8},{10,11... | collective-permute-start | bytes 4423688 | tf_op jit(solution)/shard_map/ppermute | solution.py:433
  378.9 56.5 %collective-permute-start.47 = (bf16[960,768]{1,0:T(8,128)(2,1)S(1)}, bf16[960,768]{1,0:T(8,128)(2,1)S(1)}, u32[]{:S(2)}, u32[]{:S(2)}) collective-permute-start(bf16[960,768]{1,0:T(8,128)(2,1)S(1)} %add_convert_fusion.2), channel_id=1, source_target_pairs={{0,2},{1,3},{2,0},{3,1},{4,6},{5,7},{6,4},{7,5},{8,10},{9,11},{10,... | collective-permute-start | bytes 4423688 | tf_op jit(solution)/shard_map/ppermute | solution.py:433
  382.7 68.1 %collective-permute-start.28 = (bf16[1024,768]{1,0:T(8,128)(2,1)}, bf16[1024,768]{1,0:T(8,128)(2,1)}, u32[]{:S(2)}, u32[]{:S(2)}) collective-permute-start(bf16[1024,768]{1,0:T(8,128)(2,1)} %convolution_convert_fusion.2), channel_id=1, source_target_pairs={{0,1},{1,0},{2,3},{3,2},{4,5},{5,4},{6,7},{7,6},{8,9},{9,8},{10,11... | collective-permute-start | bytes 4718600 | tf_op jit(solution)/shard_map/ppermute | solution.py:433
  385.4 53.2 %collective-permute-start.44 = (bf16[384,576]{1,0:T(8,128)(2,1)S(1)}, bf16[384,576]{1,0:T(8,128)(2,1)S(1)}, u32[]{:S(2)}, u32[]{:S(2)}) collective-permute-start(bf16[384,576]{1,0:T(8,128)(2,1)S(1)} %pad_maximum_fusion.7), channel_id=1, source_target_pairs={{0,4},{4,0},{8,12},{12,8},{16,20},{20,16},{24,28},{28,24},{1,5},{5... | collective-permute-start | bytes 1327112 | tf_op jit(solution)/shard_map/ppermute | solution.py:433
  403.7 62.8 %collective-permute-start.30 = (bf16[1024,768]{1,0:T(8,128)(2,1)}, bf16[1024,768]{1,0:T(8,128)(2,1)}, u32[]{:S(2)}, u32[]{:S(2)}) collective-permute-start(bf16[1024,768]{1,0:T(8,128)(2,1)} %add_convert_fusion), channel_id=1, source_target_pairs={{0,2},{1,3},{2,0},{3,1},{4,6},{5,7},{6,4},{7,5},{8,10},{9,11},{10,... | collective-permute-start | bytes 4718600 | tf_op jit(solution)/shard_map/ppermute | solution.py:433
  406.2 40.1 %collective-permute-start.59 = (bf16[384,768]{1,0:T(8,128)(2,1)}, bf16[384,768]{1,0:T(8,128)(2,1)}, u32[]{:S(2)}, u32[]{:S(2)}) collective-permute-start(bf16[384,768]{1,0:T(8,128)(2,1)} %fusion.67), channel_id=1, source_target_pairs={{0,4},{4,0},{8,12},{12,8},{16,20},{20,16},{24,28},{28,24},{1,5},{5... | collective-permute-start | bytes 1769480 | tf_op jit(solution)/shard_map/ppermute | solution.py:433
  436.9 37.3 %collective-permute-start.48 = (bf16[480,768]{1,0:T(8,128)(2,1)}, bf16[480,768]{1,0:T(8,128)(2,1)}, u32[]{:S(2)}, u32[]{:S(2)}) collective-permute-start(bf16[480,768]{1,0:T(8,128)(2,1)} %fusion.66), channel_id=1, source_target_pairs={{0,4},{4,0},{8,12},{12,8},{16,20},{20,16},{24,28},{28,24},{1,5},{5... | collective-permute-start | bytes 2211848 | tf_op jit(solution)/shard_map/ppermute | solution.py:433
  448.9 27.5 %collective-permute-start.60 = (bf16[96,768]{1,0:T(8,128)(2,1)S(1)}, bf16[96,768]{1,0:T(8,128)(2,1)S(1)}, u32[]{:S(2)}, u32[]{:S(2)}) collective-permute-start(bf16[96,768]{1,0:T(8,128)(2,1)S(1)} %get-tuple-element.115), channel_id=1, source_target_pairs={{0,8},{4,12},{8,0},{12,4},{16,24},{20,28},{24,16},{28,20},{1,9},{5... | collective-permute-start | bytes 442376 | tf_op jit(solution)/shard_map/ppermute | solution.py:433
  449.0 30.1 %collective-permute-start.61 = (bf16[96,768]{1,0:T(8,128)(2,1)S(1)}, bf16[96,768]{1,0:T(8,128)(2,1)S(1)}, u32[]{:S(2)}, u32[]{:S(2)}) collective-permute-start(bf16[96,768]{1,0:T(8,128)(2,1)S(1)} %get-tuple-element.117), channel_id=1, source_target_pairs={{0,16},{4,20},{8,24},{12,28},{16,0},{20,4},{24,8},{28,12},{1,17},{... | collective-permute-start | bytes 442376 | tf_op jit(solution)/shard_map/ppermute | solution.py:433
  450.8 29.6 %collective-permute-start.62 = (bf16[96,768]{1,0:T(8,128)(2,1)S(1)}, bf16[96,768]{1,0:T(8,128)(2,1)S(1)}, u32[]{:S(2)}, u32[]{:S(2)}) collective-permute-start(bf16[96,768]{1,0:T(8,128)(2,1)S(1)} %get-tuple-element.116), channel_id=1, source_target_pairs={{0,24},{4,28},{8,16},{12,20},{16,8},{20,12},{24,0},{28,4},{1,25},{... | collective-permute-start | bytes 442376 | tf_op jit(solution)/shard_map/ppermute | solution.py:433
  474.1 9.9 %collective-permute-start.31 = (f32[6,768]{1,0:T(8,128)S(1)}, f32[6,768]{1,0:T(8,128)S(1)}, u32[]{:S(2)}, u32[]{:S(2)}) collective-permute-start(f32[6,768]{1,0:T(8,128)S(1)} %stack.3), channel_id=1, source_target_pairs={{0,1},{1,0},{2,3},{3,2},{4,5},{5,4},{6,7},{7,6},{8,9},{9,8},{10,11... | collective-permute-start | bytes 55304 | tf_op jit(solution)/shard_map/ppermute | solution.py:433
  476.0 10.6 %collective-permute-start.49 = (bf16[120,768]{1,0:T(8,128)(2,1)S(1)}, bf16[120,768]{1,0:T(8,128)(2,1)S(1)}, u32[]{:S(2)}, u32[]{:S(2)}) collective-permute-start(bf16[120,768]{1,0:T(8,128)(2,1)S(1)} %get-tuple-element.110), channel_id=1, source_target_pairs={{0,8},{4,12},{8,0},{12,4},{16,24},{20,28},{24,16},{28,20},{1,9},{5... | collective-permute-start | bytes 552968 | tf_op jit(solution)/shard_map/ppermute | solution.py:433
  476.4 22.7 %collective-permute-start.50 = (bf16[120,768]{1,0:T(8,128)(2,1)S(1)}, bf16[120,768]{1,0:T(8,128)(2,1)S(1)}, u32[]{:S(2)}, u32[]{:S(2)}) collective-permute-start(bf16[120,768]{1,0:T(8,128)(2,1)S(1)} %get-tuple-element.112), channel_id=1, source_target_pairs={{0,16},{4,20},{8,24},{12,28},{16,0},{20,4},{24,8},{28,12},{1,17},{... | collective-permute-start | bytes 552968 | tf_op jit(solution)/shard_map/ppermute | solution.py:433
  479.0 21.1 %collective-permute-start.51 = (bf16[120,768]{1,0:T(8,128)(2,1)S(1)}, bf16[120,768]{1,0:T(8,128)(2,1)S(1)}, u32[]{:S(2)}, u32[]{:S(2)}) collective-permute-start(bf16[120,768]{1,0:T(8,128)(2,1)S(1)} %get-tuple-element.111), channel_id=1, source_target_pairs={{0,24},{4,28},{8,16},{12,20},{16,8},{20,12},{24,0},{28,4},{1,25},{... | collective-permute-start | bytes 552968 | tf_op jit(solution)/shard_map/ppermute | solution.py:433
  481.5 21.2 %collective-permute-start.63 = (bf16[96,768]{1,0:T(8,128)(2,1)S(1)}, bf16[96,768]{1,0:T(8,128)(2,1)S(1)}, u32[]{:S(2)}, u32[]{:S(2)}) collective-permute-start(bf16[96,768]{1,0:T(8,128)(2,1)S(1)} %fusion.74), channel_id=1, source_target_pairs={{0,24},{4,28},{8,16},{12,20},{16,8},{20,12},{24,0},{28,4},{1,25},{... | collective-permute-start | bytes 442376 | tf_op jit(solution)/shard_map/ppermute | solution.py:433
  484.0 32.7 %collective-permute-start.64 = (bf16[96,768]{1,0:T(8,128)(2,1)S(1)}, bf16[96,768]{1,0:T(8,128)(2,1)S(1)}, u32[]{:S(2)}, u32[]{:S(2)}) collective-permute-start(bf16[96,768]{1,0:T(8,128)(2,1)S(1)} %fusion.74), channel_id=1, source_target_pairs={{0,16},{4,20},{8,24},{12,28},{16,0},{20,4},{24,8},{28,12},{1,17},{... | collective-permute-start | bytes 442376 | tf_op jit(solution)/shard_map/ppermute | solution.py:433
  486.6 30.1 %collective-permute-start.65 = (bf16[96,768]{1,0:T(8,128)(2,1)S(1)}, bf16[96,768]{1,0:T(8,128)(2,1)S(1)}, u32[]{:S(2)}, u32[]{:S(2)}) collective-permute-start(bf16[96,768]{1,0:T(8,128)(2,1)S(1)} %fusion.74), channel_id=1, source_target_pairs={{0,8},{4,12},{8,0},{12,4},{16,24},{20,28},{24,16},{28,20},{1,9},{5... | collective-permute-start | bytes 442376 | tf_op jit(solution)/shard_map/ppermute | solution.py:433
  499.1 17.7 %collective-permute-start.32 = (f32[6,768]{1,0:T(8,128)S(1)}, f32[6,768]{1,0:T(8,128)S(1)}, u32[]{:S(2)}, u32[]{:S(2)}) collective-permute-start(f32[6,768]{1,0:T(8,128)S(1)} %add.232), channel_id=1, source_target_pairs={{0,2},{1,3},{2,0},{3,1},{4,6},{5,7},{6,4},{7,5},{8,10},{9,11},{10,... | collective-permute-start | bytes 55304 | tf_op jit(solution)/shard_map/ppermute | solution.py:433
  500.3 22.7 %collective-permute-start.52 = (bf16[120,768]{1,0:T(8,128)(2,1)S(1)}, bf16[120,768]{1,0:T(8,128)(2,1)S(1)}, u32[]{:S(2)}, u32[]{:S(2)}) collective-permute-start(bf16[120,768]{1,0:T(8,128)(2,1)S(1)} %fusion.71), channel_id=1, source_target_pairs={{0,24},{4,28},{8,16},{12,20},{16,8},{20,12},{24,0},{28,4},{1,25},{... | collective-permute-start | bytes 552968 | tf_op jit(solution)/shard_map/ppermute | solution.py:433
  502.7 22.3 %collective-permute-start.53 = (bf16[120,768]{1,0:T(8,128)(2,1)S(1)}, bf16[120,768]{1,0:T(8,128)(2,1)S(1)}, u32[]{:S(2)}, u32[]{:S(2)}) collective-permute-start(bf16[120,768]{1,0:T(8,128)(2,1)S(1)} %fusion.71), channel_id=1, source_target_pairs={{0,16},{4,20},{8,24},{12,28},{16,0},{20,4},{24,8},{28,12},{1,17},{... | collective-permute-start | bytes 552968 | tf_op jit(solution)/shard_map/ppermute | solution.py:433
  516.6 11.1 %collective-permute-start.54 = (bf16[120,768]{1,0:T(8,128)(2,1)S(1)}, bf16[120,768]{1,0:T(8,128)(2,1)S(1)}, u32[]{:S(2)}, u32[]{:S(2)}) collective-permute-start(bf16[120,768]{1,0:T(8,128)(2,1)S(1)} %fusion.71), channel_id=1, source_target_pairs={{0,8},{4,12},{8,0},{12,4},{16,24},{20,28},{24,16},{28,20},{1,9},{5... | collective-permute-start | bytes 552968 | tf_op jit(solution)/shard_map/ppermute | solution.py:433
  518.6 13.4 %collective-permute-start.66 = (bf16[384,768]{1,0:T(8,128)(2,1)S(1)}, bf16[384,768]{1,0:T(8,128)(2,1)}, u32[]{:S(2)}, u32[]{:S(2)}) collective-permute-start(bf16[384,768]{1,0:T(8,128)(2,1)S(1)} %pad_maximum_fusion.6), channel_id=1, source_target_pairs={{0,4},{4,0},{8,12},{12,8},{16,20},{20,16},{24,28},{28,24},{1,5},{5... | collective-permute-start | bytes 1769480 | tf_op jit(solution)/shard_map/ppermute | solution.py:433
  520.9 9.6 %collective-permute-start.34 = (f32[6,768]{1,0:T(8,128)S(1)}, f32[6,768]{1,0:T(8,128)S(1)}, u32[]{:S(2)}, u32[]{:S(2)}) collective-permute-start(f32[6,768]{1,0:T(8,128)S(1)} %add.234), channel_id=1, source_target_pairs={{0,8},{4,12},{8,0},{12,4},{16,24},{20,28},{24,16},{28,20},{1,9},{5... | collective-permute-start | bytes 55304 | tf_op jit(solution)/shard_map/ppermute | solution.py:433
  522.9 7.5 %collective-permute-start.35 = (f32[6,768]{1,0:T(8,128)S(1)}, f32[6,768]{1,0:T(8,128)S(1)}, u32[]{:S(2)}, u32[]{:S(2)}) collective-permute-start(f32[6,768]{1,0:T(8,128)S(1)} %add.234), channel_id=1, source_target_pairs={{0,16},{4,20},{8,24},{12,28},{16,0},{20,4},{24,8},{28,12},{1,17},{... | collective-permute-start | bytes 55304 | tf_op jit(solution)/shard_map/ppermute | solution.py:433
  525.0 5.6 %collective-permute-start.36 = (f32[6,768]{1,0:T(8,128)S(1)}, f32[6,768]{1,0:T(8,128)S(1)}, u32[]{:S(2)}, u32[]{:S(2)}) collective-permute-start(f32[6,768]{1,0:T(8,128)S(1)} %add.234), channel_id=1, source_target_pairs={{0,24},{4,28},{8,16},{12,20},{16,8},{20,12},{24,0},{28,4},{1,25},{... | collective-permute-start | bytes 55304 | tf_op jit(solution)/shard_map/ppermute | solution.py:433
  528.7 17.2 %collective-permute-start.55 = (bf16[480,768]{1,0:T(8,128)(2,1)}, bf16[480,768]{1,0:T(8,128)(2,1)S(1)}, u32[]{:S(2)}, u32[]{:S(2)}) collective-permute-start(bf16[480,768]{1,0:T(8,128)(2,1)} %pad_maximum_fusion.5), channel_id=1, source_target_pairs={{0,4},{4,0},{8,12},{12,8},{16,20},{20,16},{24,28},{28,24},{1,5},{5... | collective-permute-start | bytes 2211848 | tf_op jit(solution)/shard_map/ppermute | solution.py:433
  (53 other events, 403.3 us)

commit v6 on v5

--- a/solution.py
+++ b/solution.py
@@ -146,11 +146,15 @@
 
 
 def bwd_kernel(
-    last_ref, q_ref, k_ref, v_ref, g_ref, wide_ref, lse_ref, start_ref, bias_ref,
+    last_ref, slots_ref, q_ref, k_ref, v_ref, g0, g1, g2, g3, wide_ref, lse_ref, start_ref, bias_ref,
     out_ref, qn, kn, vn, gn, qx, gx, dq,
 ):
     qn[...] = q_ref[0].T
-    gn[...] = g_ref[0].T
+    for n, piece in enumerate((g0, g1, g2, g3)):
+        size = piece.shape[1]
+        place = pl.ds(pl.multiple_of(slots_ref[n] * size, size), size)
+        gx[0:HD, place] = piece[...]
+        gn[place, :] = piece[...].T
     ones = jnp.where(lax.broadcasted_iota(jnp.int32, (GLEN, HD), 1) < 3, 1.0, 0.0).astype(bf16)
     kn[:, :HD] = k_ref[0].T
     kn[:, HD:] = ones
@@ -159,16 +163,16 @@
     zeros = jnp.zeros((HD - 16, GLEN), bf16)
     row = lax.broadcasted_iota(jnp.int32, (16, GLEN), 0)
 
-    def extend(ref, head, tail):
-        ref[0:HD, :] = head
+    def extend(ref, tail):
         a, b, c = (jnp.broadcast_to(x.astype(f32), (16, GLEN)) for x in split3(-tail))
         ref[HD : HD + 16, :] = jnp.where(
             row == 0, a, jnp.where(row == 1, b, jnp.where(row == 2, c, 0.0))
         ).astype(bf16)
         ref[HD + 16 :, :] = zeros
 
-    extend(qx, q_ref[0], lse_ref[0])
-    extend(gx, g_ref[0], jnp.sum(g_ref[0].astype(f32) * wide_ref[0], 0, keepdims=True))
+    qx[0:HD, :] = q_ref[0]
+    extend(qx, lse_ref[0])
+    extend(gx, jnp.sum(gx[0:HD, :].astype(f32) * wide_ref[0], 0, keepdims=True))
     dq[...] = jnp.zeros_like(dq)
 
     def block(key_off, key_span, off, span, mask):
@@ -235,27 +239,30 @@
     out_ref[0] = (dq[...] * SCALE).astype(bf16)
 
 
-def attn_bwd(head, grads, bounds, qkv, adj, wide, lse, doc_start, key_bias):
+def attn_bwd(head, grads, bounds, slots, qkv, pieces, row, wide, lse, doc_start, key_bias):
     heads = qkv.shape[0] // 3
     specs = [
+        SMEM_SPEC,
         SMEM_SPEC,
         head_spec(head),
         head_spec(head + heads),
         head_spec(head + 2 * heads),
-        whole(1, HD, GLEN),
+    ]
+    specs += [pl.BlockSpec((HD, piece.shape[1]), lambda i: (row, 0)) for piece in pieces]
+    specs += [
         whole(1, HD, GLEN),
         whole(1, 1, GLEN),
         whole(1, PROMPT),
         whole(GLEN - PROMPT, 128),
     ]
-    args = [bounds, qkv, qkv, qkv, adj, wide, lse, doc_start, key_bias]
+    args = [bounds, slots, qkv, qkv, qkv, *pieces, wide, lse, doc_start, key_bias]
     kernel = bwd_kernel
     aliases = {}
     if grads is not None:
         specs.append(pl.BlockSpec(memory_space=pl.ANY))
         aliases = {len(args): 0}
         args.append(grads)
-        kernel = lambda *refs: bwd_kernel(*refs[:9], *refs[10:])
+        kernel = lambda *refs: bwd_kernel(*refs[:13], *refs[14:])
     return pl.pallas_call(
         kernel,
         grid=(1,),
@@ -308,11 +315,34 @@
     return (adj - first - norm * second) * rstd
 
 
+def join_rows(joined, *parts):
+    @pl.when(pl.program_id(0) == 0)
+    def _():
+        size = parts[0].shape[0]
+        for k, part in enumerate(parts):
+            joined[k * size : (k + 1) * size, :] = part[...]
+
+
+def packed_specs(rows):
+    once = pl.Buffered(1)
+    expand = pl.BlockSpec((D, D), lambda i: (0, 0), pipeline_mode=once)
+    reduce = pl.BlockSpec((D, D), lambda i: (1, 0), pipeline_mode=once)
+    size = rows - 2 * D
+    last = pl.BlockSpec((size, D), lambda i: (2 * D // size, 0), pipeline_mode=once)
+    return [expand] * 4 + [reduce] * 4 + [last] * 4
+
+
 def mid_fwd_kernel(
-    scale_ref, att_ref, x_ref, embed_ref, gain_ref, shift_ref, teacher_ref, cot_ref, valid_ref,
-    out_w, e0, e1, e2, e3, r0, r1, r2, r3,
-    layer_ref, norm_ref, act_ref, slope_ref, branch_ref, middle_ref, adj_ref, squares_ref,
+    scale_ref, a0, a1, a2, a3, b0, b1, b2, b3,
+    x_ref, embed_ref, gain_ref, shift_ref, teacher_ref, cot_ref, valid_ref,
+    e0, e1, e2, e3, r0, r1, r2, r3, w0, w1, w2, w3,
+    layer_ref, norm_ref, act_ref, slope_ref, branch_ref, middle_ref, adj_ref, att_ref, squares_ref, out_w,
 ):
+    join_rows(out_w, w0, w1, w2, w3)
+    place = 0
+    for piece in (a0, b0, a1, b1, a2, b2, a3, b3):
+        att_ref[place : place + piece.shape[0], :] = piece[...]
+        place += piece.shape[0]
     hidden = x_ref[...].astype(f32) + embed_ref[...]
     middle = hidden + dot(att_ref[...], out_w[...], 0, 0)
     middle_ref[...] = middle
@@ -342,9 +372,10 @@
 
 
 def mid_bwd_kernel(
-    branch_ref, slope_ref, middle_ref, adj_ref, gain_ref, out_w, e0, e1, e2, e3, r0, r1, r2, r3,
-    pre_ref, middle_adj_ref, attn_ref, att_ref, gain_out, shift_out,
+    branch_ref, slope_ref, middle_ref, adj_ref, gain_ref, e0, e1, e2, e3, r0, r1, r2, r3, w0, w1, w2, w3,
+    pre_ref, middle_adj_ref, attn_ref, att_ref, gain_out, shift_out, out_w,
 ):
+    join_rows(out_w, w0, w1, w2, w3)
     branch = branch_ref[...]
     second = None
     for k, (expand, reduce) in enumerate(((e0, r0), (e1, r1), (e2, r2), (e3, r3))):
@@ -384,48 +415,52 @@
     return pl.BlockSpec((height, BLOCK), lambda i: (0, i))
 
 
-def mid_fwd(scale, att, x, embed, gain, shift, teacher, cot, valid, out_w, expand, reduce):
+def mid_fwd(scale, att, x, embed, gain, shift, teacher, cot, valid, weights):
     rows = x.shape[0]
-    width = expand[0].shape[1]
+    width = D
     shape = jax.ShapeDtypeStruct
     return pl.pallas_call(
         mid_fwd_kernel,
         grid=(rows // BLOCK,),
         in_specs=[
-            pl.BlockSpec(memory_space=pltpu.SMEM), by_cols(D), by_rows(D), fixed((1, D)), fixed((1, D)),
-            fixed((1, D)), by_rows(D), by_rows(D), by_rows(1), fixed((D, D)),
-        ] + [fixed((D, width))] * 4 + [fixed((width, D))] * 4,
+            pl.BlockSpec(memory_space=pltpu.SMEM),
+        ] + [by_cols(piece.shape[0]) for piece in att] + [
+            by_rows(D), fixed((1, D)), fixed((1, D)),
+            fixed((1, D)), by_rows(D), by_rows(D), by_rows(1),
+        ] + packed_specs(weights[0].shape[0]),
         out_specs=[
             by_rows(D), by_rows(D), by_rows4(width), by_rows4(width), by_rows(D), by_rows(D), by_rows(D),
-            fixed((1, D)),
+            by_cols(D), fixed((1, D)),
         ],
         out_shape=[
             shape((rows, D), bf16), shape((rows, D), bf16), shape((4, rows, width), bf16),
             shape((4, rows, width), f32), shape((rows, D), bf16), shape((rows, D), f32),
-            shape((rows, D), f32), shape((1, D), f32),
+            shape((rows, D), f32), shape((D, rows), bf16), shape((1, D), f32),
         ],
         cost_estimate=pl.CostEstimate(flops=22_000_000_000, transcendentals=0, bytes_accessed=30_000_000),
+        scratch_shapes=[pltpu.VMEM((D, D), bf16)],
         name="mid_fwd",
-    )(scale, att, x, embed, gain, shift, teacher, cot, valid, out_w, *expand, *reduce)
-
-
-def mid_bwd(branch, slope, middle, adj, gain, out_w, expand, reduce):
+    )(scale, *att, x, embed, gain, shift, teacher, cot, valid, *weights, *weights, *weights)
+
+
+def mid_bwd(branch, slope, middle, adj, gain, weights):
     rows = branch.shape[0]
-    width = expand[0].shape[1]
+    width = D
     shape = jax.ShapeDtypeStruct
     return pl.pallas_call(
         mid_bwd_kernel,
         grid=(rows // BLOCK,),
-        in_specs=[by_rows(D), by_rows4(width), by_rows(D), by_rows(D), fixed((1, D)), fixed((D, D))]
-        + [fixed((D, width))] * 4 + [fixed((width, D))] * 4,
+        in_specs=[by_rows(D), by_rows4(width), by_rows(D), by_rows(D), fixed((1, D))]
+        + packed_specs(weights[0].shape[0]),
         out_specs=[by_rows4(width), by_rows(D), by_rows(D), by_cols(D), fixed((1, D)), fixed((1, D))],
         out_shape=[
             shape((4, rows, width), bf16), shape((rows, D), f32), shape((rows, D), bf16),
             shape((D, rows), bf16), shape((1, D), f32), shape((1, D), f32),
         ],
         cost_estimate=pl.CostEstimate(flops=22_000_000_000, transcendentals=0, bytes_accessed=30_000_000),
+        scratch_shapes=[pltpu.VMEM((D, D), bf16)],
         name="mid_bwd",
-    )(branch, slope, middle, adj, gain, out_w, *expand, *reduce)
+    )(branch, slope, middle, adj, gain, *weights, *weights, *weights)
 
 
 def swap(x, bit, axis="tensor"):
@@ -516,7 +551,6 @@
     valid = valid_mask[0]
     docs = prompt_docs[0]
     valid_total = sum_small(jnp.sum(valid).astype(f32).reshape(1, 1), "dp")[0, 0]
-    divisor = valid_total * D
     doc_start = jnp.zeros_like(docs)
     for v in range(3):
         doc_start = doc_start + jnp.where(docs > v, jnp.sum((docs == v).astype(jnp.int32)), 0)
@@ -530,22 +564,25 @@
 
     hidden_in = layer_input.astype(f32) + pass_embed
     first_affine = affine_norm(hidden_in, first_gain, first_shift)
-    first_blocks = gather4(first_affine.astype(bf16))
+    first_norm = first_affine.astype(bf16)
+    far = swap(first_norm, 2)
+    near = swap(first_norm, 1)
     in_matrix = project_in.reshape(D, 3 * width)
 
-    expand_weight, reduce_weight, project_out, _ = lax.optimization_barrier(
-        (expand_weight, reduce_weight, project_out, first_blocks[2])
-    )
-    out_blocks = gather4(project_out)
-    expand_blocks = gather4(expand_weight)
-    reduce_blocks = gather4(reduce_weight)
-    out_full = jnp.concatenate(out_blocks, 0)
-
-    qkv = jnp.zeros((3 * width, GLEN), bf16)
-    for k in range(4):
-        part = dot(in_matrix, first_blocks[k], 0, 1).astype(bf16)
-        part = jnp.concatenate([part[:width] * SCALE, part[width:]], 0)
-        qkv = lax.dynamic_update_slice(qkv, part, (0, slots[k] * rows))
+    def project(block):
+        part = dot(in_matrix, block, 0, 1).astype(bf16)
+        return jnp.concatenate([part[:width] * SCALE, part[width:]], 0)
+
+    qkv = lax.dynamic_update_slice(jnp.zeros((3 * width, GLEN), bf16), project(first_norm), (0, slots[0] * rows))
+    far, valid_total, qkv = lax.optimization_barrier((far, valid_total, qkv))
+    divisor = valid_total * D
+    first_blocks = [first_norm, near, far, swap(far, 1)]
+    packed = jnp.concatenate([expand_weight, reduce_weight, project_out], 0)
+    packed, _ = lax.optimization_barrier((packed, far))
+    weights = gather4(packed)
+
+    for k in range(1, 4):
+        qkv = lax.dynamic_update_slice(qkv, project(first_blocks[k]), (0, slots[k] * rows))
     qkv = qkv.reshape(3 * heads, HD, GLEN)
     saved = []
     for h in range(heads):
@@ -558,38 +595,38 @@
         got = {k: swap(cut(k), k) for k in (3, 2, 1)}
         got[0] = cut(0)
         moved.append(got)
-    att_own = jnp.concatenate([got[k] for k in range(4) for got in moved], 0)
-    layer_out, second_norm, acts, slope, branch_adj, middle, out_adj, squares = mid_fwd(
-        (2.0 / divisor).reshape(1, 1), att_own, layer_input, pass_embed[None], second_gain[None],
-        second_shift[None], teacher, out_cotangent, row_valid, out_full, expand_blocks, reduce_blocks,
+    att_pieces = [got[k] for got in moved for k in range(4)]
+    layer_out, second_norm, acts, slope, branch_adj, middle, out_adj, att_own, squares = mid_fwd(
+        (2.0 / divisor).reshape(1, 1), att_pieces, layer_input, pass_embed[None], second_gain[None],
+        second_shift[None], teacher, out_cotangent, row_valid, weights,
     )
     reduce_parts = [dot(acts[k], branch_adj, 0, 0).astype(bf16) for k in range(4)]
     branch_adj, *reduce_parts = lax.optimization_barrier((branch_adj, *reduce_parts))
     reduce_grad = sum_all(scatter4(reduce_parts), "dp")
     pre_adjs, middle_adj, attn_adj, att_adj, second_gain_part, second_shift_part = mid_bwd(
-        branch_adj, slope, middle, out_adj, second_gain[None], out_full, expand_blocks, reduce_blocks
+        branch_adj, slope, middle, out_adj, second_gain[None], weights
     )
     att_adj = att_adj.reshape(4, heads, HD, rows)
     adj_heads = []
     for first, last in ((0, 1), (1, heads)):
-        full = jnp.zeros(((last - first) * HD, GLEN), bf16)
+        pieces = [None] * 4
         for k in (3, 2, 1, 0):
             piece = att_adj[k, first:last].reshape((last - first) * HD, rows)
-            piece = swap(piece, k) if k else piece
-            full = lax.dynamic_update_slice(full, piece, (0, slots[k] * rows))
-        adj_heads += [full[h * HD : (h + 1) * HD][None] for h in range(last - first)]
+            pieces[k] = swap(piece, k) if k else piece
+        adj_heads += [(pieces, h) for h in range(last - first)]
 
     expand_parts = [dot(second_norm, pre_adjs[k], 0, 0).astype(bf16) for k in range(4)]
     out_parts = dot(att_own, attn_adj, 1, 0).astype(bf16)
     other_parts = [
         jnp.concatenate([expand_parts[k], out_parts[k * width : (k + 1) * width]], 0) for k in range(4)
     ]
-    adj_heads[0], *other_parts = lax.optimization_barrier((adj_heads[0], *other_parts))
+    own, *other_parts = lax.optimization_barrier((adj_heads[0][0][0], *other_parts))
+    adj_heads[0][0][0] = own
     other_grad = sum_all(scatter4(other_parts), "dp")
 
     proj_adj = None
     for h in range(heads):
-        proj_adj = attn_bwd(h, proj_adj, last_block, qkv, adj_heads[h], *saved[h][1:], doc_start, key_bias)
+        proj_adj = attn_bwd(h, proj_adj, last_block, jnp.stack(slots), qkv, *adj_heads[h], *saved[h][1:], doc_start, key_bias)
     proj_adj = proj_adj.reshape(3 * width, GLEN)
     pieces = [lax.dynamic_slice(proj_adj, (0, slots[k] * rows), (3 * width, rows)) for k in range(4)]
     first_parts = []

time: 557 us -> 562 us (level)
  waiting for transfers between devices: 151 us -> 164 us
  local copies, waits for them, and re-layouts: 40.1 us -> 28.7 us
    ppermute x67 -> x61, waiting for transfers between devices: 151 us -> 164 us  [swap(): return lax.ppermute(x, axis, [(i, i ^ bit) for i in range(size)])]
    unnamed x106 -> x87, local copies, waits for them, and re-layouts: 16.5 us -> 6.31 us
    ppermute x67 -> x61, starting transfers between devices: 92.5 us -> 87 us  [swap(): return lax.ppermute(x, axis, [(i, i ^ bit) for i in range(size)])]
  transfers between devices with their start and end apart: 67 -> 61, of which waited for: 22 -> 21; matrix products, arithmetic and copies ran while one was open for 14% -> 13% of each run, Pallas kernels for 12% -> 12%
where the time goes in v6:
time: 562 us; the launch traced here: 555 us
  Pallas kernels  167 us (30%)
  waiting for transfers between devices  164 us (29%)
  starting transfers between devices  87 us (15%)
  matrix products  56 us (10%)
  other arithmetic  45.8 us (8%)
  local copies, waits for them, and re-layouts  28.7 us (5%)
  between operations  6.66 us (1%)
    ppermute x61, waiting for transfers between devices, swap(): return lax.ppermute(x, axis, [(i, i ^ bit) for i in range(size)])  164 us
    ppermute x61, starting transfers between devices, swap(): return lax.ppermute(x, axis, [(i, i ^ bit) for i in range(size)])  87 us
    pallas_call x3, Pallas kernels, attn_bwd(): pl.pallas_call(kernel, grid=(1,), in_specs=specs, out_specs=pl.BlockSpec(...  79.1 us
    dot_general x21, matrix products, dot(): lax.dot_general(a, b, (((ca,), (cb,)), ((), ())), preferred_element_type=...  56 us
    pallas_call x3, Pallas kernels, attn_fwd(): pl.pallas_call(fwd_kernel, grid=(1,), in_specs=[head_spec(head), head_spe...  32.3 us
    pallas_call x1, Pallas kernels, mid_fwd(): pl.pallas_call(mid_fwd_kernel, grid=(rows // BLOCK,), in_specs=[pl.BlockS...  25.8 us
    pallas_call x1, Pallas kernels, mid_bwd(): pl.pallas_call(mid_bwd_kernel, grid=(rows // BLOCK,), in_specs=[by_rows(D...  23.3 us
  transfers between devices with their start and end apart: 61, of which 21 were waited for; matrix products, arithmetic and copies ran while one was open for 13% of the time, Pallas kernels for 12%

profile of v6, /device:TPU:0, one launch (start us, length us, event | category | flops | bytes accessed | tf_op | source)
XLA Modules:
  0.0 555.3 jit_solution(7599224999885099928)
XLA Ops:
  5.3 3.0 collective-permute-start
  8.9 3.2 fusion.109
  12.8 2.9 collective-permute-start.1
  15.6 2.5 fusion.50
  18.3 2.7 broadcast_in_dim.57
  24.4 2.9 collective-permute-start.2
  27.4 3.9 collective-permute-start.3
  34.0 2.7 collective-permute-done.4
  37.3 5.6 %collective-permute-done = bf16[1024,768]{1,0:T(8,128)(2,1)} collective-permute-done((bf16[1024,768]{1,0:T(8,128)(2,1)}, bf16[1024,768]{1,0:T(8,128)(2,1)}, u32[]{:S(2)}, u32[]{:S(2)}) %collective-permute-start) | collective-permute-done | bytes 1572896 | tf_op jit(solution)/shard_map/ppermute | solution.py:468
  46.9 2.5 fusion.51
  49.5 2.5 fusion.52
  54.6 2.5 fusion.53
  59.7 10.8 %attn_fwd.4 = (bf16[1,64,4096]{2,1,0:T(8,128)(2,1)}, f32[1,64,4096]{2,1,0:T(8,128)}, f32[1,1,4096]{2,1,0:T(1,128)}) custom-call(bf16[9,64,4096]{2,1,0:T(8,128)(2,1)} %bitcast.8.q_ref.k_ref.v_ref.refs_2_.refs_3_.refs_4_, bf16[9,64,4096]{2,1,0:T(8,128)(2,1)} %bitcast.8.q_ref.k_ref.v_ref.refs_2_.refs_3_.refs_4_, ...), custom_call_target="tpu_custom_call" | custom-call | flops 16999999488 | bytes 4000000 | tf_op jit(solution)/shard_map/attn_fwd/pallas_call | solution.py:117
  70.5 34.5 %collective-permute-done.14.e2.r2.w2 = bf16[1728,768]{1,0:T(8,128)(2,1)} collective-permute-done((bf16[1728,768]{1,0:T(8,128)(2,1)S(1)}, bf16[1728,768]{1,0:T(8,128)(2,1)}, u32[]{:S(2)}, u32[]{:S(2)}) %collective-permute-start.14) | collective-permute-done | bytes 2654240 | tf_op jit(solution)/shard_map/ppermute | solution.py:468
  105.0 10.6 %attn_fwd.5 = (bf16[1,64,4096]{2,1,0:T(8,128)(2,1)}, f32[1,64,4096]{2,1,0:T(8,128)}, f32[1,1,4096]{2,1,0:T(1,128)}) custom-call(bf16[9,64,4096]{2,1,0:T(8,128)(2,1)} %bitcast.8.q_ref.k_ref.v_ref.refs_2_.refs_3_.refs_4_, bf16[9,64,4096]{2,1,0:T(8,128)(2,1)} %bitcast.8.q_ref.k_ref.v_ref.refs_2_.refs_3_.refs_4_, ...), custom_call_target="tpu_custom_call" | custom-call | flops 16999999488 | bytes 4000000 | tf_op jit(solution)/shard_map/attn_fwd/pallas_call | solution.py:117
  119.8 10.8 %attn_fwd.3 = (bf16[1,64,4096]{2,1,0:T(8,128)(2,1)}, f32[1,64,4096]{2,1,0:T(8,128)}, f32[1,1,4096]{2,1,0:T(1,128)}) custom-call(bf16[9,64,4096]{2,1,0:T(8,128)(2,1)} %bitcast.8.q_ref.k_ref.v_ref.refs_2_.refs_3_.refs_4_, bf16[9,64,4096]{2,1,0:T(8,128)(2,1)} %bitcast.8.q_ref.k_ref.v_ref.refs_2_.refs_3_.refs_4_, ...), custom_call_target="tpu_custom_call" | custom-call | flops 16999999488 | bytes 4000000 | tf_op jit(solution)/shard_map/attn_fwd/pallas_call | solution.py:117
  130.7 2.3 fusion.78
  139.8 3.1 collective-permute-done.8.a2
  142.9 4.0 collective-permute-done.9.a3
  146.9 25.8 %mid_fwd.1 = (bf16[1024,768]{1,0:T(8,128)(2,1)}, bf16[1024,768]{1,0:T(8,128)(2,1)}, bf16[4,1024,768]{2,1,0:T(8,128)(2,1)}, f32[4,1024,768]{2,1,0:T(8,128)}, bf16...) custom-call(f32[1,1]{1,0:T(1,128)} %bitcast.4.scale_ref, ...), custom_call_target="tpu_custom_call" | custom-call | flops 22000001024 | bytes 30000000 | tf_op jit(solution)/shard_map/mid_fwd/pallas_call | solution.py:422
  172.7 4.5 fusion.35
  177.2 4.0 fusion.32
  181.2 2.5 fusion.29
  183.7 2.5 fusion.26
  186.2 23.3 %mid_bwd.1 = (bf16[4,1024,768]{2,1,0:T(8,128)(2,1)}, f32[1024,768]{1,0:T(8,128)}, bf16[1024,768]{1,0:T(8,128)(2,1)}, bf16[768,1024]{1,0:T(8,128)(2,1)}, f32[1,768]{1,0:T(1,128)}, /*index=5*/f32[1,768]{1,0:T(1,128)}) custom-call(bf16[1024,768]{1,0:T(8,128)(2,1)} %get-tuple-element.64.branch_ref, f32[4,1024,768]{2,1,0:T(8,128)} %get-tuple-element.65.slope_ref, ...), custom_call_target="tpu_custom_call" | custom-call | flops 22000001024 | bytes 30000000 | tf_op jit(solution)/shard_map/mid_bwd/pallas_call | solution.py:450
  209.5 3.0 fusion.47
  232.7 2.3 collective-permute-done.21.g3
  235.7 26.7 %attn_bwd.3.refs_13_ = bf16[3,3,64,4096]{3,2,1,0:T(8,128)(2,1)} custom-call(s32[8]{0:T(128)} %and_select_fusion.last_ref.refs_0_, s32[4]{0:T(128)} %pad_add_fusion.slots_ref.refs_1_, bf16[9,64,4096]{2,1,0:T(8,128)(2,1)} %bitcast.8.q_ref.k_ref.v_ref.refs_2_.refs_3_.refs_4_, bf16[9,64,4096]{2,1,0:T(8,128)(2,1)} %bitcast.8.q_ref.k_ref.v_ref.refs_2_.refs_3_.refs_4_, ...), custom_call_target="tpu_custom_call" | custom-call | flops 30000001024 | bytes 8000000 | tf_op jit(solution)/shard_map/attn_bwd/pallas_call | solution.py:266
  263.2 26.2 %attn_bwd.4.refs_13_ = bf16[3,3,64,4096]{3,2,1,0:T(8,128)(2,1)} custom-call(s32[8]{0:T(128)} %and_select_fusion.last_ref.refs_0_, s32[4]{0:T(128)} %pad_add_fusion.slots_ref.refs_1_, bf16[9,64,4096]{2,1,0:T(8,128)(2,1)} %bitcast.8.q_ref.k_ref.v_ref.refs_2_.refs_3_.refs_4_, ...), custom_call_target="tpu_custom_call", output_to_operand_aliasing={{}: (13, {})} | custom-call | flops 30000001024 | bytes 8000000 | tf_op jit(solution)/shard_map/attn_bwd/pallas_call | solution.py:266
  289.5 26.2 %attn_bwd.5 = bf16[3,3,64,4096]{3,2,1,0:T(8,128)(2,1)} custom-call(s32[8]{0:T(128)} %and_select_fusion.last_ref.refs_0_, s32[4]{0:T(128)} %pad_add_fusion.slots_ref.refs_1_, bf16[9,64,4096]{2,1,0:T(8,128)(2,1)} %bitcast.8.q_ref.k_ref.v_ref.refs_2_.refs_3_.refs_4_, ...), custom_call_target="tpu_custom_call", output_to_operand_aliasing={{}: (13, {})} | custom-call | flops 30000001024 | bytes 8000000 | tf_op jit(solution)/shard_map/attn_bwd/pallas_call | solution.py:266
  315.7 3.0 fusion.60
  318.9 2.5 fusion.66
  321.4 2.5 fusion.63
  323.9 3.7 add_add_fusion
  327.6 2.4 reshape.126
  330.9 8.9 %collective-permute-start.31 = (bf16[384,576]{0,1:T(8,128)(2,1)S(1)}, bf16[384,576]{0,1:T(8,128)(2,1)S(1)}, u32[]{:S(2)}, u32[]{:S(2)}) collective-permute-start(bf16[384,576]{0,1:T(8,128)(2,1)S(1)} %bitcast.199), channel_id=1, source_target_pairs={{0,4},{4,0},{8,12},{12,8},{16,20},{20,16},{24,28},{28,24},{1,5},{5... | collective-permute-start | bytes 1327112 | tf_op jit(solution)/shard_map/ppermute | solution.py:468
  341.7 3.9 convolution_convert_fusion
  345.6 5.3 collective-permute-done.31
  351.4 2.9 convolution_convert_fusion.1
  354.6 2.4 collective-permute-start.33
  358.9 2.6 convolution_convert_fusion.2
  361.5 5.4 collective-permute-done.33
  367.0 2.2 collective-permute-start.35
  372.8 2.4 collective-permute-done.35
  375.2 5.4 collective-permute-start.37
  384.5 2.6 convolution_convert_fusion.3.part_ref
  390.9 18.5 %collective-permute-done.52 = bf16[768,768]{1,0:T(8,128)(2,1)S(1)} collective-permute-done((bf16[768,768]{1,0:T(8,128)(2,1)S(1)}, bf16[768,768]{1,0:T(8,128)(2,1)S(1)}, u32[]{:S(2)}, u32[]{:S(2)}) %collective-permute-start.52) | collective-permute-done | bytes 1179680 | tf_op jit(solution)/shard_map/ppermute | solution.py:468
  412.9 28.0 %collective-permute-done.41 = bf16[960,768]{1,0:T(8,128)(2,1)S(1)} collective-permute-done((bf16[960,768]{1,0:T(8,128)(2,1)S(1)}, bf16[960,768]{1,0:T(8,128)(2,1)S(1)}, u32[]{:S(2)}, u32[]{:S(2)}) %collective-permute-start.41) | collective-permute-done | bytes 1474592 | tf_op jit(solution)/shard_map/ppermute | solution.py:468
  447.4 2.2 copy.45
  449.6 2.5 maximum_convert_fusion.1
  454.5 2.7 collective-permute-start.55
  458.9 13.1 %collective-permute-done.24.far_ref = bf16[1024,768]{1,0:T(8,128)(2,1)} collective-permute-done((bf16[1024,768]{1,0:T(8,128)(2,1)}, bf16[1024,768]{1,0:T(8,128)(2,1)}, u32[]{:S(2)}, u32[]{:S(2)}) %collective-permute-start.24) | collective-permute-done | bytes 1572896 | tf_op jit(solution)/shard_map/ppermute | solution.py:468
  472.0 6.7 %final.1 = (bf16[1024,768]{1,0:T(8,128)(2,1)}, f32[1,768]{1,0:T(1,128)}, f32[1,768]{1,0:T(1,128)}, f32[1,768]{1,0:T(1,128)}) custom-call(bf16[1024,768]{1,0:T(8,128)(2,1)} %x_ref.3, f32[1,768]{1,0:T(1,128)} %broadcast_in_dim.64.embed_ref, f32[1,768]{1,0:T(1,128)} %broadcast_in_dim.68.gain_ref, bf16[1024,768]{1,0:T(8,128)(2,1)} %convolution_convert_fusion.3.part_ref, ...), custom_call_target="tpu_custom_call" | custom-call | tf_op jit(solution)/shard_map/final/pallas_call | solution.py:695
  481.8 2.4 collective-permute-start.44
  486.9 2.2 collective-permute-start.57
  489.2 2.7 collective-permute-done.43
  491.9 12.6 %collective-permute-done.44 = bf16[120,768]{1,0:T(8,128)(2,1)S(1)} collective-permute-done((bf16[120,768]{1,0:T(8,128)(2,1)S(1)}, bf16[120,768]{1,0:T(8,128)(2,1)S(1)}, u32[]{:S(2)}, u32[]{:S(2)}) %collective-permute-start.44) | collective-permute-done | bytes 184352 | tf_op jit(solution)/shard_map/ppermute | solution.py:468
  504.9 2.2 collective-permute-start.46
  507.1 9.7 %collective-permute-start.47 = (bf16[120,768]{1,0:T(8,128)(2,1)S(1)}, bf16[120,768]{1,0:T(8,128)(2,1)S(1)}, u32[]{:S(2)}, u32[]{:S(2)}) collective-permute-start(bf16[120,768]{1,0:T(8,128)(2,1)S(1)} %fusion.74), channel_id=1, source_target_pairs={{0,16},{4,20},{8,24},{12,28},{16,0},{20,4},{24,8},{28,12},{1,17},{... | collective-permute-start | bytes 552968 | tf_op jit(solution)/shard_map/ppermute | solution.py:468
  516.8 5.0 collective-permute-done.58
  526.1 2.0 collective-permute-start.28
  528.4 2.0 collective-permute-done.47
  530.5 2.4 collective-permute-start.30
  540.3 11.0 %collective-permute-done.49 = bf16[480,768]{1,0:T(8,128)(2,1)S(1)} collective-permute-done((bf16[480,768]{1,0:T(8,128)(2,1)}, bf16[480,768]{1,0:T(8,128)(2,1)S(1)}, u32[]{:S(2)}, u32[]{:S(2)}) %collective-permute-start.49) | collective-permute-done | bytes 737312 | tf_op jit(solution)/shard_map/ppermute | solution.py:468
  (259 shorter events, 102.4 us)
Async XLA Ops:
  5.3 37.7 %collective-permute-start = (bf16[1024,768]{1,0:T(8,128)(2,1)}, bf16[1024,768]{1,0:T(8,128)(2,1)}, u32[]{:S(2)}, u32[]{:S(2)}) collective-permute-start(bf16[1024,768]{1,0:T(8,128)(2,1)} %add_convert_fusion.1), channel_id=1, source_target_pairs={{0,2},{1,3},{2,0},{3,1},{4,6},{5,7},{6,4},{7,5},{8,10},{9,11},{10,... | collective-permute-start | bytes 4718600 | tf_op jit(solution)/shard_map/ppermute | solution.py:468
  8.3 38.7 %collective-permute-start.5 = (bf16[1024,768]{1,0:T(8,128)(2,1)}, bf16[1024,768]{1,0:T(8,128)(2,1)}, u32[]{:S(2)}, u32[]{:S(2)}) collective-permute-start(bf16[1024,768]{1,0:T(8,128)(2,1)} %add_convert_fusion.1), channel_id=1, source_target_pairs={{0,1},{1,0},{2,3},{3,2},{4,5},{5,4},{6,7},{7,6},{8,9},{9,8},{10,11... | collective-permute-start | bytes 4718600 | tf_op jit(solution)/shard_map/ppermute | solution.py:468
  12.8 11.0 %collective-permute-start.1 = (f32[1,1]{1,0:T(1,128)}, f32[1,1]{1,0:T(1,128)}, u32[]{:S(2)}, u32[]{:S(2)}) collective-permute-start(f32[1,1]{1,0:T(1,128)} %bitcast), channel_id=1, source_target_pairs={{0,4},{4,0},{8,12},{12,8},{16,20},{20,16},{24,28},{28,24},{1,5},{5... | collective-permute-start | bytes 20 | tf_op jit(solution)/shard_map/ppermute | solution.py:468
  23.8 25.7 %copy-start.6 = (bf16[1728,768]{1,0:T(8,128)(2,1)}, bf16[1728,768]{1,0:T(8,128)(2,1)S(1)}, u32[]{:S(2)}) copy-start(bf16[1728,768]{1,0:T(8,128)(2,1)S(1)} %pad_maximum_fusion.e0.r0.w0) | copy-start | bytes 7962628
  24.4 8.3 %collective-permute-start.2 = (f32[1,1]{1,0:T(1,128)}, f32[1,1]{1,0:T(1,128)}, u32[]{:S(2)}, u32[]{:S(2)}) collective-permute-start(f32[1,1]{1,0:T(1,128)} %add.212), channel_id=1, source_target_pairs={{0,8},{4,12},{8,0},{12,4},{16,24},{20,28},{24,16},{28,20},{1,9},{5... | collective-permute-start | bytes 20 | tf_op jit(solution)/shard_map/ppermute | solution.py:468
  27.4 6.0 %collective-permute-start.3 = (f32[1,1]{1,0:T(1,128)}, f32[1,1]{1,0:T(1,128)}, u32[]{:S(2)}, u32[]{:S(2)}) collective-permute-start(f32[1,1]{1,0:T(1,128)} %add.212), channel_id=1, source_target_pairs={{0,16},{4,20},{8,24},{12,28},{16,0},{20,4},{24,8},{28,12},{1,17},{... | collective-permute-start | bytes 20 | tf_op jit(solution)/shard_map/ppermute | solution.py:468
  31.3 5.5 collective-permute-start.4
  43.0 11.6 %collective-permute-start.6 = (bf16[1024,768]{1,0:T(8,128)(2,1)}, bf16[1024,768]{1,0:T(8,128)(2,1)}, u32[]{:S(2)}, u32[]{:S(2)}) collective-permute-start(bf16[1024,768]{1,0:T(8,128)(2,1)} %collective-permute-done), channel_id=1, source_target_pairs={{0,1},{1,0},{2,3},{3,2},{4,5},{5,4},{6,7},{7,6},{8,9},{9,8},{10,11... | collective-permute-start | bytes 4718600 | tf_op jit(solution)/shard_map/ppermute | solution.py:468
  44.9 60.1 %collective-permute-start.14 = (bf16[1728,768]{1,0:T(8,128)(2,1)S(1)}, bf16[1728,768]{1,0:T(8,128)(2,1)}, u32[]{:S(2)}, u32[]{:S(2)}) collective-permute-start(bf16[1728,768]{1,0:T(8,128)(2,1)S(1)} %pad_maximum_fusion.e0.r0.w0), channel_id=1, source_target_pairs={{0,2},{1,3},{2,0},{3,1},{4,6},{5,7},{6,4},{7,5},{8,10},{9,11},{10,... | collective-permute-start | bytes 7962632 | tf_op jit(solution)/shard_map/ppermute | solution.py:468
  46.7 100.2 %collective-permute-start.13 = (bf16[1728,768]{1,0:T(8,128)(2,1)S(1)}, bf16[1728,768]{1,0:T(8,128)(2,1)}, u32[]{:S(2)}, u32[]{:S(2)}) collective-permute-start(bf16[1728,768]{1,0:T(8,128)(2,1)S(1)} %pad_maximum_fusion.e0.r0.w0), channel_id=1, source_target_pairs={{0,1},{1,0},{2,3},{3,2},{4,5},{5,4},{6,7},{7,6},{8,9},{9,8},{10,11... | collective-permute-start | bytes 7962632 | tf_op jit(solution)/shard_map/ppermute | solution.py:468
  105.0 41.9 %collective-permute-start.15 = (bf16[1728,768]{1,0:T(8,128)(2,1)}, bf16[1728,768]{1,0:T(8,128)(2,1)}, u32[]{:S(2)}, u32[]{:S(2)}) collective-permute-start(bf16[1728,768]{1,0:T(8,128)(2,1)} %collective-permute-done.14.e2.r2.w2), channel_id=1, source_target_pairs={{0,1},{1,0},{2,3},{3,2},{4,5},{5,4},{6,7},{7,6},{8,9},{9,8},{10,11... | collective-permute-start | bytes 7962632 | tf_op jit(solution)/shard_map/ppermute | solution.py:468
  117.6 15.4 %collective-permute-start.10 = (bf16[64,1024]{1,0:T(8,128)(2,1)}, bf16[64,1024]{1,0:T(8,128)(2,1)}, u32[]{:S(2)}, u32[]{:S(2)}) collective-permute-start(bf16[64,1024]{1,0:T(8,128)(2,1)} %get-tuple-element.146), channel_id=1, source_target_pairs={{0,1},{1,0},{2,3},{3,2},{4,5},{5,4},{6,7},{7,6},{8,9},{9,8},{10,11... | collective-permute-start | bytes 393224 | tf_op jit(solution)/shard_map/ppermute | solution.py:468
  118.1 15.3 %collective-permute-start.11 = (bf16[64,1024]{1,0:T(8,128)(2,1)}, bf16[64,1024]{1,0:T(8,128)(2,1)}, u32[]{:S(2)}, u32[]{:S(2)}) collective-permute-start(bf16[64,1024]{1,0:T(8,128)(2,1)} %get-tuple-element.145), channel_id=1, source_target_pairs={{0,2},{1,3},{2,0},{3,1},{4,6},{5,7},{6,4},{7,5},{8,10},{9,11},{10,... | collective-permute-start | bytes 393224 | tf_op jit(solution)/shard_map/ppermute | solution.py:468
  119.8 15.3 %collective-permute-start.12 = (bf16[64,1024]{1,0:T(8,128)(2,1)}, bf16[64,1024]{1,0:T(8,128)(2,1)}, u32[]{:S(2)}, u32[]{:S(2)}) collective-permute-start(bf16[64,1024]{1,0:T(8,128)(2,1)} %get-tuple-element.144), channel_id=1, source_target_pairs={{0,3},{1,2},{2,1},{3,0},{4,7},{5,6},{6,5},{7,4},{8,11},{9,10},{10,... | collective-permute-start | bytes 393224 | tf_op jit(solution)/shard_map/ppermute | solution.py:468
  133.0 6.8 %collective-permute-start.7 = (bf16[128,1024]{1,0:T(8,128)(2,1)}, bf16[128,1024]{1,0:T(8,128)(2,1)}, u32[]{:S(2)}, u32[]{:S(2)}) collective-permute-start(bf16[128,1024]{1,0:T(8,128)(2,1)} %get-tuple-element.129), channel_id=1, source_target_pairs={{0,1},{1,0},{2,3},{3,2},{4,5},{5,4},{6,7},{7,6},{8,9},{9,8},{10,11... | collective-permute-start | bytes 786440 | tf_op jit(solution)/shard_map/ppermute | solution.py:468
  133.4 9.5 %collective-permute-start.8 = (bf16[128,1024]{1,0:T(8,128)(2,1)}, bf16[128,1024]{1,0:T(8,128)(2,1)}, u32[]{:S(2)}, u32[]{:S(2)}) collective-permute-start(bf16[128,1024]{1,0:T(8,128)(2,1)} %get-tuple-element.130), channel_id=1, source_target_pairs={{0,2},{1,3},{2,0},{3,1},{4,6},{5,7},{6,4},{7,5},{8,10},{9,11},{10,... | collective-permute-start | bytes 786440 | tf_op jit(solution)/shard_map/ppermute | solution.py:468
  135.1 11.7 %collective-permute-start.9 = (bf16[128,1024]{1,0:T(8,128)(2,1)}, bf16[128,1024]{1,0:T(8,128)(2,1)}, u32[]{:S(2)}, u32[]{:S(2)}) collective-permute-start(bf16[128,1024]{1,0:T(8,128)(2,1)} %get-tuple-element.127), channel_id=1, source_target_pairs={{0,3},{1,2},{2,1},{3,0},{4,7},{5,6},{6,5},{7,4},{8,11},{9,10},{10,... | collective-permute-start | bytes 786440 | tf_op jit(solution)/shard_map/ppermute | solution.py:468
  186.2 23.3 %copy-start.37 = (bf16[1024,768]{1,0:T(8,128)(2,1)S(1)}, bf16[1024,768]{1,0:T(8,128)(2,1)}, u32[]{:S(2)}) copy-start(bf16[1024,768]{1,0:T(8,128)(2,1)} %get-tuple-element.73) | copy-start | bytes 4718596
  226.0 5.2 collective-permute-start.19
  226.6 6.1 %collective-permute-start.20 = (bf16[64,1024]{1,0:T(8,128)(2,1)S(1)}, bf16[64,1024]{1,0:T(8,128)(2,1)S(1)}, u32[]{:S(2)}, u32[]{:S(2)}) collective-permute-start(bf16[64,1024]{1,0:T(8,128)(2,1)S(1)} %get-tuple-element.106), channel_id=1, source_target_pairs={{0,2},{1,3},{2,0},{3,1},{4,6},{5,7},{6,4},{7,5},{8,10},{9,11},{10,... | collective-permute-start | bytes 393224 | tf_op jit(solution)/shard_map/ppermute | solution.py:468
  228.3 6.7 %collective-permute-start.21 = (bf16[64,1024]{1,0:T(8,128)(2,1)S(1)}, bf16[64,1024]{1,0:T(8,128)(2,1)S(1)}, u32[]{:S(2)}, u32[]{:S(2)}) collective-permute-start(bf16[64,1024]{1,0:T(8,128)(2,1)S(1)} %get-tuple-element.105), channel_id=1, source_target_pairs={{0,3},{1,2},{2,1},{3,0},{4,7},{5,6},{6,5},{7,4},{8,11},{9,10},{10,... | collective-permute-start | bytes 393224 | tf_op jit(solution)/shard_map/ppermute | solution.py:468
  229.1 33.2 %collective-permute-start.16 = (bf16[128,1024]{1,0:T(8,128)(2,1)S(1)}, bf16[128,1024]{1,0:T(8,128)(2,1)S(1)}, u32[]{:S(2)}, u32[]{:S(2)}) collective-permute-start(bf16[128,1024]{1,0:T(8,128)(2,1)S(1)} %bitcast.214), channel_id=1, source_target_pairs={{0,1},{1,0},{2,3},{3,2},{4,5},{5,4},{6,7},{7,6},{8,9},{9,8},{10,11... | collective-permute-start | bytes 786440 | tf_op jit(solution)/shard_map/ppermute | solution.py:468
  229.5 32.8 %collective-permute-start.17 = (bf16[128,1024]{1,0:T(8,128)(2,1)S(1)}, bf16[128,1024]{1,0:T(8,128)(2,1)S(1)}, u32[]{:S(2)}, u32[]{:S(2)}) collective-permute-start(bf16[128,1024]{1,0:T(8,128)(2,1)S(1)} %bitcast.213), channel_id=1, source_target_pairs={{0,2},{1,3},{2,0},{3,1},{4,6},{5,7},{6,4},{7,5},{8,10},{9,11},{10,... | collective-permute-start | bytes 786440 | tf_op jit(solution)/shard_map/ppermute | solution.py:468
  231.3 31.1 %collective-permute-start.18 = (bf16[128,1024]{1,0:T(8,128)(2,1)S(1)}, bf16[128,1024]{1,0:T(8,128)(2,1)S(1)}, u32[]{:S(2)}, u32[]{:S(2)}) collective-permute-start(bf16[128,1024]{1,0:T(8,128)(2,1)S(1)} %bitcast.212), channel_id=1, source_target_pairs={{0,3},{1,2},{2,1},{3,0},{4,7},{5,6},{6,5},{7,4},{8,11},{9,10},{10,... | collective-permute-start | bytes 786440 | tf_op jit(solution)/shard_map/ppermute | solution.py:468
  330.9 19.9 %collective-permute-start.31 = (bf16[384,576]{0,1:T(8,128)(2,1)S(1)}, bf16[384,576]{0,1:T(8,128)(2,1)S(1)}, u32[]{:S(2)}, u32[]{:S(2)}) collective-permute-start(bf16[384,576]{0,1:T(8,128)(2,1)S(1)} %bitcast.199), channel_id=1, source_target_pairs={{0,4},{4,0},{8,12},{12,8},{16,20},{20,16},{24,28},{28,24},{1,5},{5... | collective-permute-start | bytes 1327112 | tf_op jit(solution)/shard_map/ppermute | solution.py:468
  340.5 28.8 %collective-permute-start.51 = (bf16[768,768]{1,0:T(8,128)(2,1)}, bf16[768,768]{1,0:T(8,128)(2,1)}, u32[]{:S(2)}, u32[]{:S(2)}) collective-permute-start(bf16[768,768]{1,0:T(8,128)(2,1)} %fusion.35), channel_id=1, source_target_pairs={{0,1},{1,0},{2,3},{3,2},{4,5},{5,4},{6,7},{7,6},{8,9},{9,8},{10,11... | collective-permute-start | bytes 3538952 | tf_op jit(solution)/shard_map/ppermute | solution.py:468
  340.9 39.6 %collective-permute-start.40 = (bf16[960,768]{1,0:T(8,128)(2,1)}, bf16[960,768]{1,0:T(8,128)(2,1)}, u32[]{:S(2)}, u32[]{:S(2)}) collective-permute-start(bf16[960,768]{1,0:T(8,128)(2,1)} %pad_maximum_fusion.4), channel_id=1, source_target_pairs={{0,1},{1,0},{2,3},{3,2},{4,5},{5,4},{6,7},{7,6},{8,9},{9,8},{10,11... | collective-permute-start | bytes 4423688 | tf_op jit(solution)/shard_map/ppermute | solution.py:468
  351.4 5.6 %collective-permute-start.32 = (bf16[96,576]{1,0:T(8,128)(2,1)S(1)}, bf16[96,576]{1,0:T(8,128)(2,1)S(1)}, u32[]{:S(2)}, u32[]{:S(2)}) collective-permute-start(bf16[96,576]{1,0:T(8,128)(2,1)S(1)} %get-tuple-element.133), channel_id=1, source_target_pairs={{0,8},{4,12},{8,0},{12,4},{16,24},{20,28},{24,16},{28,20},{1,9},{5... | collective-permute-start | bytes 331784 | tf_op jit(solution)/shard_map/ppermute | solution.py:468
  354.4 32.9 %collective-permute-start.23 = (bf16[1024,768]{1,0:T(8,128)(2,1)S(1)}, bf16[1024,768]{1,0:T(8,128)(2,1)S(1)}, u32[]{:S(2)}, u32[]{:S(2)}) collective-permute-start(bf16[1024,768]{1,0:T(8,128)(2,1)S(1)} %copy-done.27), channel_id=1, source_target_pairs={{0,1},{1,0},{2,3},{3,2},{4,5},{5,4},{6,7},{7,6},{8,9},{9,8},{10,11... | collective-permute-start | bytes 4718600 | tf_op jit(solution)/shard_map/ppermute | solution.py:468
  354.6 12.4 %collective-permute-start.33 = (bf16[96,576]{1,0:T(8,128)(2,1)S(1)}, bf16[96,576]{1,0:T(8,128)(2,1)S(1)}, u32[]{:S(2)}, u32[]{:S(2)}) collective-permute-start(bf16[96,576]{1,0:T(8,128)(2,1)S(1)} %get-tuple-element.135), channel_id=1, source_target_pairs={{0,16},{4,20},{8,24},{12,28},{16,0},{20,4},{24,8},{28,12},{1,17},{... | collective-permute-start | bytes 331784 | tf_op jit(solution)/shard_map/ppermute | solution.py:468
  357.0 9.9 %collective-permute-start.34 = (bf16[96,576]{1,0:T(8,128)(2,1)S(1)}, bf16[96,576]{1,0:T(8,128)(2,1)S(1)}, u32[]{:S(2)}, u32[]{:S(2)}) collective-permute-start(bf16[96,576]{1,0:T(8,128)(2,1)S(1)} %get-tuple-element.134), channel_id=1, source_target_pairs={{0,24},{4,28},{8,16},{12,20},{16,8},{20,12},{24,0},{28,4},{1,25},{... | collective-permute-start | bytes 331784 | tf_op jit(solution)/shard_map/ppermute | solution.py:468
  366.9 22.2 %collective-permute-start.50 = (bf16[768,768]{1,0:T(8,128)(2,1)S(1)}, bf16[768,768]{1,0:T(8,128)(2,1)S(1)}, u32[]{:S(2)}, u32[]{:S(2)}) collective-permute-start(bf16[768,768]{1,0:T(8,128)(2,1)S(1)} %copy-done.28), channel_id=1, source_target_pairs={{0,1},{1,0},{2,3},{3,2},{4,5},{5,4},{6,7},{7,6},{8,9},{9,8},{10,11... | collective-permute-start | bytes 3538952 | tf_op jit(solution)/shard_map/ppermute | solution.py:468
  367.0 8.2 %collective-permute-start.35 = (bf16[96,576]{1,0:T(8,128)(2,1)S(1)}, bf16[96,576]{1,0:T(8,128)(2,1)S(1)}, u32[]{:S(2)}, u32[]{:S(2)}) collective-permute-start(bf16[96,576]{1,0:T(8,128)(2,1)S(1)} %fusion.84), channel_id=1, source_target_pairs={{0,24},{4,28},{8,16},{12,20},{16,8},{20,12},{24,0},{28,4},{1,25},{... | collective-permute-start | bytes 331784 | tf_op jit(solution)/shard_map/ppermute | solution.py:468
  369.2 13.3 %collective-permute-start.36 = (bf16[96,576]{1,0:T(8,128)(2,1)S(1)}, bf16[96,576]{1,0:T(8,128)(2,1)S(1)}, u32[]{:S(2)}, u32[]{:S(2)}) collective-permute-start(bf16[96,576]{1,0:T(8,128)(2,1)S(1)} %fusion.84), channel_id=1, source_target_pairs={{0,16},{4,20},{8,24},{12,28},{16,0},{20,4},{24,8},{28,12},{1,17},{... | collective-permute-start | bytes 331784 | tf_op jit(solution)/shard_map/ppermute | solution.py:468
  375.2 9.2 %collective-permute-start.37 = (bf16[96,576]{1,0:T(8,128)(2,1)S(1)}, bf16[96,576]{1,0:T(8,128)(2,1)S(1)}, u32[]{:S(2)}, u32[]{:S(2)}) collective-permute-start(bf16[96,576]{1,0:T(8,128)(2,1)S(1)} %fusion.84), channel_id=1, source_target_pairs={{0,8},{4,12},{8,0},{12,4},{16,24},{20,28},{24,16},{28,20},{1,9},{5... | collective-permute-start | bytes 331784 | tf_op jit(solution)/shard_map/ppermute | solution.py:468
  380.5 28.8 %collective-permute-start.52 = (bf16[768,768]{1,0:T(8,128)(2,1)S(1)}, bf16[768,768]{1,0:T(8,128)(2,1)S(1)}, u32[]{:S(2)}, u32[]{:S(2)}) collective-permute-start(bf16[768,768]{1,0:T(8,128)(2,1)S(1)} %add_convert_fusion.3), channel_id=1, source_target_pairs={{0,2},{1,3},{2,0},{3,1},{4,6},{5,7},{6,4},{7,5},{8,10},{9,11},{10,... | collective-permute-start | bytes 3538952 | tf_op jit(solution)/shard_map/ppermute | solution.py:468
  382.5 28.4 %collective-permute-start.39 = (bf16[960,768]{1,0:T(8,128)(2,1)S(1)}, bf16[960,768]{1,0:T(8,128)(2,1)S(1)}, u32[]{:S(2)}, u32[]{:S(2)}) collective-permute-start(bf16[960,768]{1,0:T(8,128)(2,1)S(1)} %copy-done.8), channel_id=1, source_target_pairs={{0,1},{1,0},{2,3},{3,2},{4,5},{5,4},{6,7},{7,6},{8,9},{9,8},{10,11... | collective-permute-start | bytes 4423688 | tf_op jit(solution)/shard_map/ppermute | solution.py:468
  384.4 56.6 %collective-permute-start.41 = (bf16[960,768]{1,0:T(8,128)(2,1)S(1)}, bf16[960,768]{1,0:T(8,128)(2,1)S(1)}, u32[]{:S(2)}, u32[]{:S(2)}) collective-permute-start(bf16[960,768]{1,0:T(8,128)(2,1)S(1)} %add_convert_fusion.2), channel_id=1, source_target_pairs={{0,2},{1,3},{2,0},{3,1},{4,6},{5,7},{6,4},{7,5},{8,10},{9,11},{10,... | collective-permute-start | bytes 4423688 | tf_op jit(solution)/shard_map/ppermute | solution.py:468
  387.3 69.9 %collective-permute-start.22 = (bf16[1024,768]{1,0:T(8,128)(2,1)}, bf16[1024,768]{1,0:T(8,128)(2,1)}, u32[]{:S(2)}, u32[]{:S(2)}) collective-permute-start(bf16[1024,768]{1,0:T(8,128)(2,1)} %convolution_convert_fusion.2), channel_id=1, source_target_pairs={{0,1},{1,0},{2,3},{3,2},{4,5},{5,4},{6,7},{7,6},{8,9},{9,8},{10,11... | collective-permute-start | bytes 4718600 | tf_op jit(solution)/shard_map/ppermute | solution.py:468
  389.1 55.1 %collective-permute-start.38 = (bf16[384,576]{1,0:T(8,128)(2,1)S(1)}, bf16[384,576]{1,0:T(8,128)(2,1)S(1)}, u32[]{:S(2)}, u32[]{:S(2)}) collective-permute-start(bf16[384,576]{1,0:T(8,128)(2,1)S(1)} %pad_maximum_fusion.8), channel_id=1, source_target_pairs={{0,4},{4,0},{8,12},{12,8},{16,20},{20,16},{24,28},{28,24},{1,5},{5... | collective-permute-start | bytes 1327112 | tf_op jit(solution)/shard_map/ppermute | solution.py:468
  409.4 62.7 %collective-permute-start.24 = (bf16[1024,768]{1,0:T(8,128)(2,1)}, bf16[1024,768]{1,0:T(8,128)(2,1)}, u32[]{:S(2)}, u32[]{:S(2)}) collective-permute-start(bf16[1024,768]{1,0:T(8,128)(2,1)} %add_convert_fusion), channel_id=1, source_target_pairs={{0,2},{1,3},{2,0},{3,1},{4,6},{5,7},{6,4},{7,5},{8,10},{9,11},{10,... | collective-permute-start | bytes 4718600 | tf_op jit(solution)/shard_map/ppermute | solution.py:468
  409.5 31.5 %copy-start.3 = (bf16[960,768]{1,0:T(8,128)(2,1)S(1)}, bf16[960,768]{1,0:T(8,128)(2,1)}, u32[]{:S(2)}) copy-start(bf16[960,768]{1,0:T(8,128)(2,1)} %pad_maximum_fusion.1) | copy-start | bytes 4423684
  410.9 41.2 %collective-permute-start.53 = (bf16[384,768]{1,0:T(8,128)(2,1)}, bf16[384,768]{1,0:T(8,128)(2,1)}, u32[]{:S(2)}, u32[]{:S(2)}) collective-permute-start(bf16[384,768]{1,0:T(8,128)(2,1)} %fusion.70), channel_id=1, source_target_pairs={{0,4},{4,0},{8,12},{12,8},{16,20},{20,16},{24,28},{28,24},{1,5},{5... | collective-permute-start | bytes 1769480 | tf_op jit(solution)/shard_map/ppermute | solution.py:468
  442.5 37.1 %collective-permute-start.42 = (bf16[480,768]{1,0:T(8,128)(2,1)}, bf16[480,768]{1,0:T(8,128)(2,1)}, u32[]{:S(2)}, u32[]{:S(2)}) collective-permute-start(bf16[480,768]{1,0:T(8,128)(2,1)} %fusion.69), channel_id=1, source_target_pairs={{0,4},{4,0},{8,12},{12,8},{16,20},{20,16},{24,28},{28,24},{1,5},{5... | collective-permute-start | bytes 2211848 | tf_op jit(solution)/shard_map/ppermute | solution.py:468
  454.4 27.3 %collective-permute-start.54 = (bf16[96,768]{1,0:T(8,128)(2,1)S(1)}, bf16[96,768]{1,0:T(8,128)(2,1)S(1)}, u32[]{:S(2)}, u32[]{:S(2)}) collective-permute-start(bf16[96,768]{1,0:T(8,128)(2,1)S(1)} %get-tuple-element.120), channel_id=1, source_target_pairs={{0,8},{4,12},{8,0},{12,4},{16,24},{20,28},{24,16},{28,20},{1,9},{5... | collective-permute-start | bytes 442376 | tf_op jit(solution)/shard_map/ppermute | solution.py:468
  454.5 29.7 %collective-permute-start.55 = (bf16[96,768]{1,0:T(8,128)(2,1)S(1)}, bf16[96,768]{1,0:T(8,128)(2,1)S(1)}, u32[]{:S(2)}, u32[]{:S(2)}) collective-permute-start(bf16[96,768]{1,0:T(8,128)(2,1)S(1)} %get-tuple-element.122), channel_id=1, source_target_pairs={{0,16},{4,20},{8,24},{12,28},{16,0},{20,4},{24,8},{28,12},{1,17},{... | collective-permute-start | bytes 442376 | tf_op jit(solution)/shard_map/ppermute | solution.py:468
  457.2 28.7 %collective-permute-start.56 = (bf16[96,768]{1,0:T(8,128)(2,1)S(1)}, bf16[96,768]{1,0:T(8,128)(2,1)S(1)}, u32[]{:S(2)}, u32[]{:S(2)}) collective-permute-start(bf16[96,768]{1,0:T(8,128)(2,1)S(1)} %get-tuple-element.121), channel_id=1, source_target_pairs={{0,24},{4,28},{8,16},{12,20},{16,8},{20,12},{24,0},{28,4},{1,25},{... | collective-permute-start | bytes 442376 | tf_op jit(solution)/shard_map/ppermute | solution.py:468
  479.5 9.6 %collective-permute-start.25 = (f32[6,768]{1,0:T(8,128)S(1)}, f32[6,768]{1,0:T(8,128)S(1)}, u32[]{:S(2)}, u32[]{:S(2)}) collective-permute-start(f32[6,768]{1,0:T(8,128)S(1)} %stack.33), channel_id=1, source_target_pairs={{0,1},{1,0},{2,3},{3,2},{4,5},{5,4},{6,7},{7,6},{8,9},{9,8},{10,11... | collective-permute-start | bytes 55304 | tf_op jit(solution)/shard_map/ppermute | solution.py:468
  481.4 10.4 %collective-permute-start.43 = (bf16[120,768]{1,0:T(8,128)(2,1)S(1)}, bf16[120,768]{1,0:T(8,128)(2,1)S(1)}, u32[]{:S(2)}, u32[]{:S(2)}) collective-permute-start(bf16[120,768]{1,0:T(8,128)(2,1)S(1)} %get-tuple-element.115), channel_id=1, source_target_pairs={{0,8},{4,12},{8,0},{12,4},{16,24},{20,28},{24,16},{28,20},{1,9},{5... | collective-permute-start | bytes 552968 | tf_op jit(solution)/shard_map/ppermute | solution.py:468
  481.8 22.7 %collective-permute-start.44 = (bf16[120,768]{1,0:T(8,128)(2,1)S(1)}, bf16[120,768]{1,0:T(8,128)(2,1)S(1)}, u32[]{:S(2)}, u32[]{:S(2)}) collective-permute-start(bf16[120,768]{1,0:T(8,128)(2,1)S(1)} %get-tuple-element.117), channel_id=1, source_target_pairs={{0,16},{4,20},{8,24},{12,28},{16,0},{20,4},{24,8},{28,12},{1,17},{... | collective-permute-start | bytes 552968 | tf_op jit(solution)/shard_map/ppermute | solution.py:468
  484.2 20.6 %collective-permute-start.45 = (bf16[120,768]{1,0:T(8,128)(2,1)S(1)}, bf16[120,768]{1,0:T(8,128)(2,1)S(1)}, u32[]{:S(2)}, u32[]{:S(2)}) collective-permute-start(bf16[120,768]{1,0:T(8,128)(2,1)S(1)} %get-tuple-element.116), channel_id=1, source_target_pairs={{0,24},{4,28},{8,16},{12,20},{16,8},{20,12},{24,0},{28,4},{1,25},{... | collective-permute-start | bytes 552968 | tf_op jit(solution)/shard_map/ppermute | solution.py:468
  486.9 20.2 %collective-permute-start.57 = (bf16[96,768]{1,0:T(8,128)(2,1)S(1)}, bf16[96,768]{1,0:T(8,128)(2,1)S(1)}, u32[]{:S(2)}, u32[]{:S(2)}) collective-permute-start(bf16[96,768]{1,0:T(8,128)(2,1)S(1)} %fusion.77), channel_id=1, source_target_pairs={{0,24},{4,28},{8,16},{12,20},{16,8},{20,12},{24,0},{28,4},{1,25},{... | collective-permute-start | bytes 442376 | tf_op jit(solution)/shard_map/ppermute | solution.py:468
  489.1 32.7 %collective-permute-start.58 = (bf16[96,768]{1,0:T(8,128)(2,1)S(1)}, bf16[96,768]{1,0:T(8,128)(2,1)S(1)}, u32[]{:S(2)}, u32[]{:S(2)}) collective-permute-start(bf16[96,768]{1,0:T(8,128)(2,1)S(1)} %fusion.77), channel_id=1, source_target_pairs={{0,16},{4,20},{8,24},{12,28},{16,0},{20,4},{24,8},{28,12},{1,17},{... | collective-permute-start | bytes 442376 | tf_op jit(solution)/shard_map/ppermute | solution.py:468
  491.9 30.0 %collective-permute-start.59 = (bf16[96,768]{1,0:T(8,128)(2,1)S(1)}, bf16[96,768]{1,0:T(8,128)(2,1)S(1)}, u32[]{:S(2)}, u32[]{:S(2)}) collective-permute-start(bf16[96,768]{1,0:T(8,128)(2,1)S(1)} %fusion.77), channel_id=1, source_target_pairs={{0,8},{4,12},{8,0},{12,4},{16,24},{20,28},{24,16},{28,20},{1,9},{5... | collective-permute-start | bytes 442376 | tf_op jit(solution)/shard_map/ppermute | solution.py:468
  504.5 17.4 %collective-permute-start.26 = (f32[6,768]{1,0:T(8,128)S(1)}, f32[6,768]{1,0:T(8,128)S(1)}, u32[]{:S(2)}, u32[]{:S(2)}) collective-permute-start(f32[6,768]{1,0:T(8,128)S(1)} %add.224), channel_id=1, source_target_pairs={{0,2},{1,3},{2,0},{3,1},{4,6},{5,7},{6,4},{7,5},{8,10},{9,11},{10,... | collective-permute-start | bytes 55304 | tf_op jit(solution)/shard_map/ppermute | solution.py:468
  504.9 23.2 %collective-permute-start.46 = (bf16[120,768]{1,0:T(8,128)(2,1)S(1)}, bf16[120,768]{1,0:T(8,128)(2,1)S(1)}, u32[]{:S(2)}, u32[]{:S(2)}) collective-permute-start(bf16[120,768]{1,0:T(8,128)(2,1)S(1)} %fusion.74), channel_id=1, source_target_pairs={{0,24},{4,28},{8,16},{12,20},{16,8},{20,12},{24,0},{28,4},{1,25},{... | collective-permute-start | bytes 552968 | tf_op jit(solution)/shard_map/ppermute | solution.py:468
  507.1 23.4 %collective-permute-start.47 = (bf16[120,768]{1,0:T(8,128)(2,1)S(1)}, bf16[120,768]{1,0:T(8,128)(2,1)S(1)}, u32[]{:S(2)}, u32[]{:S(2)}) collective-permute-start(bf16[120,768]{1,0:T(8,128)(2,1)S(1)} %fusion.74), channel_id=1, source_target_pairs={{0,16},{4,20},{8,24},{12,28},{16,0},{20,4},{24,8},{28,12},{1,17},{... | collective-permute-start | bytes 552968 | tf_op jit(solution)/shard_map/ppermute | solution.py:468
  521.8 11.1 %collective-permute-start.48 = (bf16[120,768]{1,0:T(8,128)(2,1)S(1)}, bf16[120,768]{1,0:T(8,128)(2,1)S(1)}, u32[]{:S(2)}, u32[]{:S(2)}) collective-permute-start(bf16[120,768]{1,0:T(8,128)(2,1)S(1)} %fusion.74), channel_id=1, source_target_pairs={{0,8},{4,12},{8,0},{12,4},{16,24},{20,28},{24,16},{28,20},{1,9},{5... | collective-permute-start | bytes 552968 | tf_op jit(solution)/shard_map/ppermute | solution.py:468
  521.9 4.2 collective-permute-start.27
  523.9 13.5 %collective-permute-start.60 = (bf16[384,768]{1,0:T(8,128)(2,1)S(1)}, bf16[384,768]{1,0:T(8,128)(2,1)}, u32[]{:S(2)}, u32[]{:S(2)}) collective-permute-start(bf16[384,768]{1,0:T(8,128)(2,1)S(1)} %pad_maximum_fusion.7), channel_id=1, source_target_pairs={{0,4},{4,0},{8,12},{12,8},{16,20},{20,16},{24,28},{28,24},{1,5},{5... | collective-permute-start | bytes 1769480 | tf_op jit(solution)/shard_map/ppermute | solution.py:468
  526.1 9.7 %collective-permute-start.28 = (f32[6,768]{1,0:T(8,128)S(1)}, f32[6,768]{1,0:T(8,128)S(1)}, u32[]{:S(2)}, u32[]{:S(2)}) collective-permute-start(f32[6,768]{1,0:T(8,128)S(1)} %add.226), channel_id=1, source_target_pairs={{0,8},{4,12},{8,0},{12,4},{16,24},{20,28},{24,16},{28,20},{1,9},{5... | collective-permute-start | bytes 55304 | tf_op jit(solution)/shard_map/ppermute | solution.py:468
  528.1 7.6 %collective-permute-start.29 = (f32[6,768]{1,0:T(8,128)S(1)}, f32[6,768]{1,0:T(8,128)S(1)}, u32[]{:S(2)}, u32[]{:S(2)}) collective-permute-start(f32[6,768]{1,0:T(8,128)S(1)} %add.226), channel_id=1, source_target_pairs={{0,16},{4,20},{8,24},{12,28},{16,0},{20,4},{24,8},{28,12},{1,17},{... | collective-permute-start | bytes 55304 | tf_op jit(solution)/shard_map/ppermute | solution.py:468
  530.5 5.6 %collective-permute-start.30 = (f32[6,768]{1,0:T(8,128)S(1)}, f32[6,768]{1,0:T(8,128)S(1)}, u32[]{:S(2)}, u32[]{:S(2)}) collective-permute-start(f32[6,768]{1,0:T(8,128)S(1)} %add.226), channel_id=1, source_target_pairs={{0,24},{4,28},{8,16},{12,20},{16,8},{20,12},{24,0},{28,4},{1,25},{... | collective-permute-start | bytes 55304 | tf_op jit(solution)/shard_map/ppermute | solution.py:468
  533.9 17.3 %collective-permute-start.49 = (bf16[480,768]{1,0:T(8,128)(2,1)}, bf16[480,768]{1,0:T(8,128)(2,1)S(1)}, u32[]{:S(2)}, u32[]{:S(2)}) collective-permute-start(bf16[480,768]{1,0:T(8,128)(2,1)} %pad_maximum_fusion.6), channel_id=1, source_target_pairs={{0,4},{4,0},{8,12},{12,8},{16,20},{20,16},{24,28},{28,24},{1,5},{5... | collective-permute-start | bytes 2211848 | tf_op jit(solution)/shard_map/ppermute | solution.py:468
  (40 other events, 208.6 us)

commit v7 on v6

--- a/solution.py
+++ b/solution.py
@@ -628,20 +628,23 @@
     for h in range(heads):
         proj_adj = attn_bwd(h, proj_adj, last_block, jnp.stack(slots), qkv, *adj_heads[h], *saved[h][1:], doc_start, key_bias)
     proj_adj = proj_adj.reshape(3 * width, GLEN)
-    pieces = [lax.dynamic_slice(proj_adj, (0, slots[k] * rows), (3 * width, rows)) for k in range(4)]
-    first_parts = []
-    for k in range(4):
-        first_parts.append(dot(pieces[k], in_matrix, 0, 1).astype(bf16))
-    near3 = swap(first_parts[3], 1)
-    near1 = swap(first_parts[1], 1)
-    across = (first_parts[2].astype(f32) + near3.astype(f32)).astype(bf16)
+    spare = -(3 * width) % (16 * lax.axis_size("dp"))
+
+    def part(k):
+        piece = lax.dynamic_slice(proj_adj, (0, slots[k] * rows), (3 * width, rows))
+        return dot(in_matrix, piece, 1, 0).astype(bf16)
+
+    near3 = swap(part(3), 1)
+    across = (part(2).astype(f32) + near3.astype(f32)).astype(bf16)
     far = swap(across, 2)
-    in_proj_grad = dot(first_blocks[0], pieces[0], 0, 1)
-    for k in range(1, 4):
-        in_proj_grad = in_proj_grad + dot(first_blocks[k], pieces[k], 0, 1)
-    in_proj_grad = sum_all(in_proj_grad, "dp")
+    order = (1, 0, 3, 2)
+    part1, part0, gained = tail(
+        jnp.stack([slots[k] for k in order]), proj_adj, in_matrix, [first_blocks[k] for k in order], spare
+    )
+    near1 = swap(part1, 1)
+    in_proj_grad = sum_all(gained, "dp")[: 3 * width]
     input_gradient, embed_part, first_gain_part, first_shift_part = final(
-        layer_input, pass_embed[None], first_gain[None], first_parts[0], near1, far, middle_adj
+        layer_input, pass_embed[None], first_gain[None], part0, near1, far, middle_adj
     )
     small = jnp.stack(
         [
@@ -661,7 +664,7 @@
         small[0],
         small[1],
         small[2],
-        in_proj_grad.reshape(D, 3, width),
+        in_proj_grad.reshape(3, width, D).transpose(2, 0, 1),
         other_grad[D:],
         small[3],
         small[4],
@@ -670,11 +673,45 @@
     )
 
 
+def tail_kernel(slots_ref, grads, weight, x0, x1, x2, x3, fa, fb, sum_ref):
+    step = pl.program_id(0)
+    width = grads.shape[0]
+    for k, x in enumerate((x0, x1, x2, x3)):
+
+        @pl.when(step == k)
+        def _():
+            gained = dot_f32(grads[...], x[...])
+            if k == 0:
+                sum_ref[:width, :] = gained
+                sum_ref[width:, :] = jnp.zeros((sum_ref.shape[0] - width, D), f32)
+            else:
+                sum_ref[:width, :] += gained
+            if k < 2:
+                (fa, fb)[k][...] = dot_f32(weight[...], grads[...]).astype(bf16)
+
+
+def tail(slots, grads, weight, blocks, spare):
+    width, rows = grads.shape[0], blocks[0].shape[0]
+    once = lambda *shape: pl.BlockSpec(shape, lambda i, s: (0, 0), pipeline_mode=pl.Buffered(1))
+    return pl.pallas_call(
+        tail_kernel,
+        grid_spec=pltpu.PrefetchScalarGridSpec(
+            num_scalar_prefetch=1,
+            grid=(4,),
+            in_specs=[pl.BlockSpec((width, rows), lambda i, s: (0, s[i])), once(D, width)] + [once(rows, D)] * 4,
+            out_specs=[once(D, rows), once(D, rows), once(width + spare, D)],
+        ),
+        out_shape=[jax.ShapeDtypeStruct((D, rows), bf16)] * 2 + [jax.ShapeDtypeStruct((width + spare, D), f32)],
+        cost_estimate=pl.CostEstimate(flops=14_000_000_000, transcendentals=0, bytes_accessed=12_000_000),
+        name="tail",
+    )(slots, grads, weight, *blocks)
+
+
 def final_kernel(
     x_ref, embed_ref, gain_ref, part_ref, near_ref, far_ref, adj_ref, out_ref, embed_out, gain_out, shift_out
 ):
     norm, rstd = row_norm(x_ref[...].astype(f32) + embed_ref[...])
-    first = part_ref[...].astype(f32) + near_ref[...].astype(f32) + far_ref[...].astype(f32)
+    first = (part_ref[...].astype(f32) + near_ref[...].astype(f32) + far_ref[...].astype(f32)).T
     input_adj = adj_ref[...] + norm_pull(norm, rstd, first * gain_ref[...])
     out_ref[...] = input_adj.astype(bf16)
 
@@ -695,7 +732,7 @@
     return pl.pallas_call(
         final_kernel,
         grid=(rows // BLOCK,),
-        in_specs=[by_rows(D), fixed((1, D)), fixed((1, D))] + [by_rows(D)] * 4,
+        in_specs=[by_rows(D), fixed((1, D)), fixed((1, D))] + [by_cols(D)] * 3 + [by_rows(D)],
         out_specs=[by_rows(D)] + [fixed((1, D))] * 3,
         out_shape=[jax.ShapeDtypeStruct((rows, D), bf16), line, line, line],
         name="final",

time: 562 us -> 567 us (level)
  matrix products: 56 us -> 39.5 us
  waiting for transfers between devices: 164 us -> 179 us
  Pallas kernels: 167 us -> 181 us
  starting transfers between devices: 87 us -> 81.3 us
    dot_general x21 -> x15, matrix products: 56 us -> 39.5 us  [dot(): lax.dot_general(a, b, (((ca,), (cb,)), ((), ())), preferred_element_type=...]
    ppermute x61, waiting for transfers between devices: 164 us -> 179 us  [swap(): return lax.ppermute(x, axis, [(i, i ^ bit) for i in range(size)])]
    pallas_call x0 -> x1, Pallas kernels: none -> 13.7 us  [tail(): pl.pallas_call(tail_kernel, grid_spec=pltpu.PrefetchScalarGridSpec(num_sc...]
  transfers between devices with their start and end apart: 61 -> 61, of which waited for: 21 -> 22; matrix products, arithmetic and copies ran while one was open for 13% -> 12% of each run, Pallas kernels for 12% -> 12%
where the time goes in v7:
time: 567 us; the launch traced here: 560 us
  Pallas kernels  181 us (32%)
  waiting for transfers between devices  179 us (32%)
  starting transfers between devices  81.3 us (14%)
  other arithmetic  48 us (8%)
  matrix products  39.5 us (7%)
  local copies, waits for them, and re-layouts  24.6 us (4%)
  between operations  6.61 us (1%)
    ppermute x61, waiting for transfers between devices, swap(): return lax.ppermute(x, axis, [(i, i ^ bit) for i in range(size)])  179 us
    ppermute x61, starting transfers between devices, swap(): return lax.ppermute(x, axis, [(i, i ^ bit) for i in range(size)])  81.3 us
    pallas_call x3, Pallas kernels, attn_bwd(): pl.pallas_call(kernel, grid=(1,), in_specs=specs, out_specs=pl.BlockSpec(...  78.9 us
    dot_general x15, matrix products, dot(): lax.dot_general(a, b, (((ca,), (cb,)), ((), ())), preferred_element_type=...  39.5 us
    pallas_call x3, Pallas kernels, attn_fwd(): pl.pallas_call(fwd_kernel, grid=(1,), in_specs=[head_spec(head), head_spe...  32.5 us
    pallas_call x1, Pallas kernels, mid_fwd(): pl.pallas_call(mid_fwd_kernel, grid=(rows // BLOCK,), in_specs=[pl.BlockS...  25.6 us
    pallas_call x1, Pallas kernels, mid_bwd(): pl.pallas_call(mid_bwd_kernel, grid=(rows // BLOCK,), in_specs=[by_rows(D...  23.5 us
    pallas_call x1, Pallas kernels, tail(): pl.pallas_call(tail_kernel, grid_spec=pltpu.PrefetchScalarGridSpec(num_sc...  13.7 us
  transfers between devices with their start and end apart: 61, of which 22 were waited for; matrix products, arithmetic and copies ran while one was open for 12% of the time, Pallas kernels for 12%

profile of v7, /device:TPU:0, one launch (start us, length us, event | category | flops | bytes accessed | tf_op | source)
XLA Modules:
  0.0 560.0 jit_solution(296714255313765536)
XLA Ops:
  5.2 3.0 collective-permute-start
  8.9 3.2 fusion.93
  12.7 2.9 collective-permute-start.1
  15.6 2.5 fusion.52
  18.8 2.7 broadcast_in_dim.57
  24.9 2.9 collective-permute-start.2
  27.8 3.9 collective-permute-start.3
  34.4 2.7 collective-permute-done.4
  37.8 5.1 collective-permute-done.x3
  46.9 2.5 fusion.53
  49.5 2.5 fusion.54
  54.5 2.5 fusion.55
  59.7 11.1 %attn_fwd.4 = (bf16[1,64,4096]{2,1,0:T(8,128)(2,1)}, f32[1,64,4096]{2,1,0:T(8,128)}, f32[1,1,4096]{2,1,0:T(1,128)}) custom-call(bf16[9,64,4096]{2,1,0:T(8,128)(2,1)} %bitcast.8.q_ref.k_ref.v_ref.refs_2_.refs_3_.refs_4_, bf16[9,64,4096]{2,1,0:T(8,128)(2,1)} %bitcast.8.q_ref.k_ref.v_ref.refs_2_.refs_3_.refs_4_, ...), custom_call_target="tpu_custom_call" | custom-call | flops 16999999488 | bytes 4000000 | tf_op jit(solution)/shard_map/attn_fwd/pallas_call | solution.py:117
  70.8 34.3 %collective-permute-done.14.e2.r2.w2 = bf16[1728,768]{1,0:T(8,128)(2,1)} collective-permute-done((bf16[1728,768]{1,0:T(8,128)(2,1)S(1)}, bf16[1728,768]{1,0:T(8,128)(2,1)}, u32[]{:S(2)}, u32[]{:S(2)}) %collective-permute-start.14) | collective-permute-done | bytes 2654240 | tf_op jit(solution)/shard_map/ppermute | solution.py:468
  105.0 10.6 %attn_fwd.5 = (bf16[1,64,4096]{2,1,0:T(8,128)(2,1)}, f32[1,64,4096]{2,1,0:T(8,128)}, f32[1,1,4096]{2,1,0:T(1,128)}) custom-call(bf16[9,64,4096]{2,1,0:T(8,128)(2,1)} %bitcast.8.q_ref.k_ref.v_ref.refs_2_.refs_3_.refs_4_, bf16[9,64,4096]{2,1,0:T(8,128)(2,1)} %bitcast.8.q_ref.k_ref.v_ref.refs_2_.refs_3_.refs_4_, ...), custom_call_target="tpu_custom_call" | custom-call | flops 16999999488 | bytes 4000000 | tf_op jit(solution)/shard_map/attn_fwd/pallas_call | solution.py:117
  115.7 2.0 dynamic-slice_bitcast_fusion
  119.9 10.8 %attn_fwd.3 = (bf16[1,64,4096]{2,1,0:T(8,128)(2,1)}, f32[1,64,4096]{2,1,0:T(8,128)}, f32[1,1,4096]{2,1,0:T(1,128)}) custom-call(bf16[9,64,4096]{2,1,0:T(8,128)(2,1)} %bitcast.8.q_ref.k_ref.v_ref.refs_2_.refs_3_.refs_4_, bf16[9,64,4096]{2,1,0:T(8,128)(2,1)} %bitcast.8.q_ref.k_ref.v_ref.refs_2_.refs_3_.refs_4_, ...), custom_call_target="tpu_custom_call" | custom-call | flops 16999999488 | bytes 4000000 | tf_op jit(solution)/shard_map/attn_fwd/pallas_call | solution.py:117
  130.7 2.3 fusion.68
  142.9 4.0 collective-permute-done.9.a3
  146.9 25.6 %mid_fwd.1 = (bf16[1024,768]{1,0:T(8,128)(2,1)}, bf16[1024,768]{1,0:T(8,128)(2,1)}, bf16[4,1024,768]{2,1,0:T(8,128)(2,1)}, f32[4,1024,768]{2,1,0:T(8,128)}, bf16...) custom-call(f32[1,1]{1,0:T(1,128)} %bitcast.4.scale_ref, ...), custom_call_target="tpu_custom_call" | custom-call | flops 22000001024 | bytes 30000000 | tf_op jit(solution)/shard_map/mid_fwd/pallas_call | solution.py:422
  172.6 4.5 fusion.36
  177.1 4.0 fusion.33
  181.1 2.5 fusion.30
  183.6 2.5 fusion.27
  186.1 23.5 %mid_bwd.1 = (bf16[4,1024,768]{2,1,0:T(8,128)(2,1)}, f32[1024,768]{1,0:T(8,128)}, bf16[1024,768]{1,0:T(8,128)(2,1)}, bf16[768,1024]{1,0:T(8,128)(2,1)}, f32[1,768]{1,0:T(1,128)}, /*index=5*/f32[1,768]{1,0:T(1,128)}) custom-call(bf16[1024,768]{1,0:T(8,128)(2,1)} %get-tuple-element.67.branch_ref, f32[4,1024,768]{2,1,0:T(8,128)} %get-tuple-element.68.slope_ref, ...), custom_call_target="tpu_custom_call" | custom-call | flops 22000001024 | bytes 30000000 | tf_op jit(solution)/shard_map/mid_bwd/pallas_call | solution.py:450
  209.6 3.0 fusion.48
  231.6 2.3 collective-permute-done.21.g3
  234.5 26.4 %attn_bwd.3.refs_13_ = bf16[3,3,64,4096]{3,2,1,0:T(8,128)(2,1)} custom-call(s32[8]{0:T(128)} %and_select_fusion.last_ref.refs_0_, s32[4]{0:T(128)} %pad_add_fusion.1.slots_ref.refs_1_, bf16[9,64,4096]{2,1,0:T(8,128)(2,1)} %bitcast.8.q_ref.k_ref.v_ref.refs_2_.refs_3_.refs_4_, bf16[9,64,4096]{2,1,0:T(8,128)(2,1)} %bitcast.8.q_ref.k_ref.v_ref.refs_2_.refs_3_.refs_4_, ...), custom_call_target="tpu_custom_call" | custom-call | flops 30000001024 | bytes 8000000 | tf_op jit(solution)/shard_map/attn_bwd/pallas_call | solution.py:266
  261.8 26.2 %attn_bwd.4.refs_13_ = bf16[3,3,64,4096]{3,2,1,0:T(8,128)(2,1)} custom-call(s32[8]{0:T(128)} %and_select_fusion.last_ref.refs_0_, s32[4]{0:T(128)} %pad_add_fusion.1.slots_ref.refs_1_, bf16[9,64,4096]{2,1,0:T(8,128)(2,1)} %bitcast.8.q_ref.k_ref.v_ref.refs_2_.refs_3_.refs_4_, ...), custom_call_target="tpu_custom_call", output_to_operand_aliasing={{}: (13, {})} | custom-call | flops 30000001024 | bytes 8000000 | tf_op jit(solution)/shard_map/attn_bwd/pallas_call | solution.py:266
  288.1 26.2 %attn_bwd.5 = bf16[3,3,64,4096]{3,2,1,0:T(8,128)(2,1)} custom-call(s32[8]{0:T(128)} %and_select_fusion.last_ref.refs_0_, s32[4]{0:T(128)} %pad_add_fusion.1.slots_ref.refs_1_, bf16[9,64,4096]{2,1,0:T(8,128)(2,1)} %bitcast.8.q_ref.k_ref.v_ref.refs_2_.refs_3_.refs_4_, ...), custom_call_target="tpu_custom_call", output_to_operand_aliasing={{}: (13, {})} | custom-call | flops 30000001024 | bytes 8000000 | tf_op jit(solution)/shard_map/attn_bwd/pallas_call | solution.py:266
  314.3 13.7 %tail.1 = (bf16[768,1024]{1,0:T(8,128)(2,1)}, bf16[768,1024]{1,0:T(8,128)(2,1)}, f32[640,768]{1,0:T(8,128)}) custom-call(s32[4]{0:T(128)} %pad_add_fusion.slots_ref, bf16[576,4096]{1,0:T(8,128)(2,1)} %bitcast.208, bf16[768,576]{1,0:T(8,128)(2,1)} %copy.36.weight, bf16[1024,768]{1,0:T(8,128)(2,1)} %collective-permute-done.5.x0, ...), custom_call_target="tpu_custom_call" | custom-call | flops 14000000000 | bytes 12000000 | tf_op jit(solution)/shard_map/tail/pallas_call | solution.py:696
  329.3 8.9 %collective-permute-start.31 = (bf16[320,768]{1,0:T(8,128)(2,1)S(1)}, bf16[320,768]{1,0:T(8,128)(2,1)}, u32[]{:S(2)}, u32[]{:S(2)}) collective-permute-start(bf16[320,768]{1,0:T(8,128)(2,1)S(1)} %fusion.61), channel_id=1, source_target_pairs={{0,4},{4,0},{8,12},{12,8},{16,20},{20,16},{24,28},{28,24},{1,5},{5... | collective-permute-start | bytes 1474568 | tf_op jit(solution)/shard_map/ppermute | solution.py:468
  338.8 11.6 %collective-permute-done.31 = bf16[320,768]{1,0:T(8,128)(2,1)} collective-permute-done((bf16[320,768]{1,0:T(8,128)(2,1)S(1)}, bf16[320,768]{1,0:T(8,128)(2,1)}, u32[]{:S(2)}, u32[]{:S(2)}) %collective-permute-start.31) | collective-permute-done | bytes 491552 | tf_op jit(solution)/shard_map/ppermute | solution.py:468
  352.6 2.7 collective-permute-start.33
  357.0 3.1 collective-permute-done.32
  360.0 5.3 collective-permute-done.33
  366.3 2.2 collective-permute-start.35
  370.8 3.9 fusion.51
  374.7 4.7 collective-permute-done.36
  381.2 2.6 add_convert_fusion.2
  383.9 2.0 collective-permute-start.52
  385.9 2.8 add_convert_fusion.1
  388.7 4.6 collective-permute-done.38
  396.7 3.3 fusion
  400.6 12.4 %collective-permute-done.52 = bf16[768,768]{1,0:T(8,128)(2,1)} collective-permute-done((bf16[768,768]{1,0:T(8,128)(2,1)}, bf16[768,768]{1,0:T(8,128)(2,1)}, u32[]{:S(2)}, u32[]{:S(2)}) %collective-permute-start.52) | collective-permute-done | bytes 1179680 | tf_op jit(solution)/shard_map/ppermute | solution.py:468
  413.0 2.3 convert_add_fusion.2
  417.4 27.2 %collective-permute-done.41 = bf16[960,768]{1,0:T(8,128)(2,1)} collective-permute-done((bf16[960,768]{1,0:T(8,128)(2,1)}, bf16[960,768]{1,0:T(8,128)(2,1)}, u32[]{:S(2)}, u32[]{:S(2)}) %collective-permute-start.41) | collective-permute-done | bytes 1474592 | tf_op jit(solution)/shard_map/ppermute | solution.py:468
  444.6 2.5 convert_add_fusion.1
  452.2 2.4 collective-permute-start.55
  456.6 20.8 %collective-permute-done.24.far_ref = bf16[768,1024]{1,0:T(8,128)(2,1)} collective-permute-done((bf16[768,1024]{1,0:T(8,128)(2,1)S(1)}, bf16[768,1024]{1,0:T(8,128)(2,1)}, u32[]{:S(2)}, u32[]{:S(2)}) %collective-permute-start.24) | collective-permute-done | bytes 1572896 | tf_op jit(solution)/shard_map/ppermute | solution.py:468
  477.4 6.9 %final.1 = (bf16[1024,768]{1,0:T(8,128)(2,1)}, f32[1,768]{1,0:T(1,128)}, f32[1,768]{1,0:T(1,128)}, f32[1,768]{1,0:T(1,128)}) custom-call(bf16[1024,768]{1,0:T(8,128)(2,1)} %x_ref.3, f32[1,768]{1,0:T(1,128)} %broadcast_in_dim.64.embed_ref, f32[1,768]{1,0:T(1,128)} %broadcast_in_dim.68.gain_ref, bf16[768,1024]{1,0:T(8,128)(2,1)} %get-tuple-element.83.part_ref, ...), custom_call_target="tpu_custom_call" | custom-call | tf_op jit(solution)/shard_map/final/pallas_call | solution.py:732
  487.1 2.7 collective-permute-start.44
  492.5 2.2 collective-permute-start.57
  494.7 2.8 collective-permute-done.43
  497.5 12.3 %collective-permute-done.44 = bf16[120,768]{1,0:T(8,128)(2,1)S(1)} collective-permute-done((bf16[120,768]{1,0:T(8,128)(2,1)S(1)}, bf16[120,768]{1,0:T(8,128)(2,1)S(1)}, u32[]{:S(2)}, u32[]{:S(2)}) %collective-permute-start.44) | collective-permute-done | bytes 184352 | tf_op jit(solution)/shard_map/ppermute | solution.py:468
  511.7 2.2 collective-permute-start.46
  513.9 8.2 %collective-permute-start.47 = (bf16[120,768]{1,0:T(8,128)(2,1)S(1)}, bf16[120,768]{1,0:T(8,128)(2,1)S(1)}, u32[]{:S(2)}, u32[]{:S(2)}) collective-permute-start(bf16[120,768]{1,0:T(8,128)(2,1)S(1)} %fusion.64), channel_id=1, source_target_pairs={{0,16},{4,20},{8,24},{12,28},{16,0},{20,4},{24,8},{28,12},{1,17},{... | collective-permute-start | bytes 552968 | tf_op jit(solution)/shard_map/ppermute | solution.py:468
  522.1 5.0 collective-permute-done.58
  529.4 2.0 collective-permute-done.27
  531.4 2.0 collective-permute-start.28
  533.8 2.3 collective-permute-done.47
  536.0 2.2 collective-permute-start.30
  538.7 2.9 collective-permute-done.30
  545.8 10.1 %collective-permute-done.49 = bf16[480,768]{1,0:T(8,128)(2,1)S(1)} collective-permute-done((bf16[480,768]{1,0:T(8,128)(2,1)S(1)}, bf16[480,768]{1,0:T(8,128)(2,1)S(1)}, u32[]{:S(2)}, u32[]{:S(2)}) %collective-permute-start.49) | collective-permute-done | bytes 737312 | tf_op jit(solution)/shard_map/ppermute | solution.py:468
  (241 shorter events, 92.2 us)
Async XLA Ops:
  5.2 37.7 %collective-permute-start = (bf16[1024,768]{1,0:T(8,128)(2,1)}, bf16[1024,768]{1,0:T(8,128)(2,1)}, u32[]{:S(2)}, u32[]{:S(2)}) collective-permute-start(bf16[1024,768]{1,0:T(8,128)(2,1)} %add_convert_fusion.x1), channel_id=1, source_target_pairs={{0,2},{1,3},{2,0},{3,1},{4,6},{5,7},{6,4},{7,5},{8,10},{9,11},{10,... | collective-permute-start | bytes 4718600 | tf_op jit(solution)/shard_map/ppermute | solution.py:468
  8.2 38.7 %collective-permute-start.5 = (bf16[1024,768]{1,0:T(8,128)(2,1)}, bf16[1024,768]{1,0:T(8,128)(2,1)}, u32[]{:S(2)}, u32[]{:S(2)}) collective-permute-start(bf16[1024,768]{1,0:T(8,128)(2,1)} %add_convert_fusion.x1), channel_id=1, source_target_pairs={{0,1},{1,0},{2,3},{3,2},{4,5},{5,4},{6,7},{7,6},{8,9},{9,8},{10,11... | collective-permute-start | bytes 4718600 | tf_op jit(solution)/shard_map/ppermute | solution.py:468
  12.7 11.5 %collective-permute-start.1 = (f32[1,1]{1,0:T(1,128)}, f32[1,1]{1,0:T(1,128)}, u32[]{:S(2)}, u32[]{:S(2)}) collective-permute-start(f32[1,1]{1,0:T(1,128)} %bitcast), channel_id=1, source_target_pairs={{0,4},{4,0},{8,12},{12,8},{16,20},{20,16},{24,28},{28,24},{1,5},{5... | collective-permute-start | bytes 20 | tf_op jit(solution)/shard_map/ppermute | solution.py:468
  24.2 25.3 %copy-start.3 = (bf16[1728,768]{1,0:T(8,128)(2,1)}, bf16[1728,768]{1,0:T(8,128)(2,1)S(1)}, u32[]{:S(2)}) copy-start(bf16[1728,768]{1,0:T(8,128)(2,1)S(1)} %pad_maximum_fusion.e0.r0.w0) | copy-start | bytes 7962628
  24.9 8.3 %collective-permute-start.2 = (f32[1,1]{1,0:T(1,128)}, f32[1,1]{1,0:T(1,128)}, u32[]{:S(2)}, u32[]{:S(2)}) collective-permute-start(f32[1,1]{1,0:T(1,128)} %add.201), channel_id=1, source_target_pairs={{0,8},{4,12},{8,0},{12,4},{16,24},{20,28},{24,16},{28,20},{1,9},{5... | collective-permute-start | bytes 20 | tf_op jit(solution)/shard_map/ppermute | solution.py:468
  27.8 6.0 %collective-permute-start.3 = (f32[1,1]{1,0:T(1,128)}, f32[1,1]{1,0:T(1,128)}, u32[]{:S(2)}, u32[]{:S(2)}) collective-permute-start(f32[1,1]{1,0:T(1,128)} %add.201), channel_id=1, source_target_pairs={{0,16},{4,20},{8,24},{12,28},{16,0},{20,4},{24,8},{28,12},{1,17},{... | collective-permute-start | bytes 20 | tf_op jit(solution)/shard_map/ppermute | solution.py:468
  31.7 5.5 collective-permute-start.4
  42.9 11.6 %collective-permute-start.6 = (bf16[1024,768]{1,0:T(8,128)(2,1)}, bf16[1024,768]{1,0:T(8,128)(2,1)}, u32[]{:S(2)}, u32[]{:S(2)}) collective-permute-start(bf16[1024,768]{1,0:T(8,128)(2,1)} %collective-permute-done.x3), channel_id=1, source_target_pairs={{0,1},{1,0},{2,3},{3,2},{4,5},{5,4},{6,7},{7,6},{8,9},{9,8},{10,11... | collective-permute-start | bytes 4718600 | tf_op jit(solution)/shard_map/ppermute | solution.py:468
  44.9 60.1 %collective-permute-start.14 = (bf16[1728,768]{1,0:T(8,128)(2,1)S(1)}, bf16[1728,768]{1,0:T(8,128)(2,1)}, u32[]{:S(2)}, u32[]{:S(2)}) collective-permute-start(bf16[1728,768]{1,0:T(8,128)(2,1)S(1)} %pad_maximum_fusion.e0.r0.w0), channel_id=1, source_target_pairs={{0,2},{1,3},{2,0},{3,1},{4,6},{5,7},{6,4},{7,5},{8,10},{9,11},{10,... | collective-permute-start | bytes 7962632 | tf_op jit(solution)/shard_map/ppermute | solution.py:468
  46.7 100.2 %collective-permute-start.13 = (bf16[1728,768]{1,0:T(8,128)(2,1)S(1)}, bf16[1728,768]{1,0:T(8,128)(2,1)}, u32[]{:S(2)}, u32[]{:S(2)}) collective-permute-start(bf16[1728,768]{1,0:T(8,128)(2,1)S(1)} %pad_maximum_fusion.e0.r0.w0), channel_id=1, source_target_pairs={{0,1},{1,0},{2,3},{3,2},{4,5},{5,4},{6,7},{7,6},{8,9},{9,8},{10,11... | collective-permute-start | bytes 7962632 | tf_op jit(solution)/shard_map/ppermute | solution.py:468
  105.0 41.9 %collective-permute-start.15 = (bf16[1728,768]{1,0:T(8,128)(2,1)}, bf16[1728,768]{1,0:T(8,128)(2,1)}, u32[]{:S(2)}, u32[]{:S(2)}) collective-permute-start(bf16[1728,768]{1,0:T(8,128)(2,1)} %collective-permute-done.14.e2.r2.w2), channel_id=1, source_target_pairs={{0,1},{1,0},{2,3},{3,2},{4,5},{5,4},{6,7},{7,6},{8,9},{9,8},{10,11... | collective-permute-start | bytes 7962632 | tf_op jit(solution)/shard_map/ppermute | solution.py:468
  117.6 15.3 %collective-permute-start.10 = (bf16[64,1024]{1,0:T(8,128)(2,1)}, bf16[64,1024]{1,0:T(8,128)(2,1)}, u32[]{:S(2)}, u32[]{:S(2)}) collective-permute-start(bf16[64,1024]{1,0:T(8,128)(2,1)} %get-tuple-element.152), channel_id=1, source_target_pairs={{0,1},{1,0},{2,3},{3,2},{4,5},{5,4},{6,7},{7,6},{8,9},{9,8},{10,11... | collective-permute-start | bytes 393224 | tf_op jit(solution)/shard_map/ppermute | solution.py:468
  118.1 15.3 %collective-permute-start.11 = (bf16[64,1024]{1,0:T(8,128)(2,1)}, bf16[64,1024]{1,0:T(8,128)(2,1)}, u32[]{:S(2)}, u32[]{:S(2)}) collective-permute-start(bf16[64,1024]{1,0:T(8,128)(2,1)} %get-tuple-element.151), channel_id=1, source_target_pairs={{0,2},{1,3},{2,0},{3,1},{4,6},{5,7},{6,4},{7,5},{8,10},{9,11},{10,... | collective-permute-start | bytes 393224 | tf_op jit(solution)/shard_map/ppermute | solution.py:468
  119.9 15.3 %collective-permute-start.12 = (bf16[64,1024]{1,0:T(8,128)(2,1)}, bf16[64,1024]{1,0:T(8,128)(2,1)}, u32[]{:S(2)}, u32[]{:S(2)}) collective-permute-start(bf16[64,1024]{1,0:T(8,128)(2,1)} %get-tuple-element.150), channel_id=1, source_target_pairs={{0,3},{1,2},{2,1},{3,0},{4,7},{5,6},{6,5},{7,4},{8,11},{9,10},{10,... | collective-permute-start | bytes 393224 | tf_op jit(solution)/shard_map/ppermute | solution.py:468
  133.0 8.2 %collective-permute-start.7 = (bf16[128,1024]{1,0:T(8,128)(2,1)}, bf16[128,1024]{1,0:T(8,128)(2,1)}, u32[]{:S(2)}, u32[]{:S(2)}) collective-permute-start(bf16[128,1024]{1,0:T(8,128)(2,1)} %get-tuple-element.135), channel_id=1, source_target_pairs={{0,1},{1,0},{2,3},{3,2},{4,5},{5,4},{6,7},{7,6},{8,9},{9,8},{10,11... | collective-permute-start | bytes 786440 | tf_op jit(solution)/shard_map/ppermute | solution.py:468
  133.4 9.5 %collective-permute-start.8 = (bf16[128,1024]{1,0:T(8,128)(2,1)}, bf16[128,1024]{1,0:T(8,128)(2,1)}, u32[]{:S(2)}, u32[]{:S(2)}) collective-permute-start(bf16[128,1024]{1,0:T(8,128)(2,1)} %get-tuple-element.136), channel_id=1, source_target_pairs={{0,2},{1,3},{2,0},{3,1},{4,6},{5,7},{6,4},{7,5},{8,10},{9,11},{10,... | collective-permute-start | bytes 786440 | tf_op jit(solution)/shard_map/ppermute | solution.py:468
  135.2 11.7 %collective-permute-start.9 = (bf16[128,1024]{1,0:T(8,128)(2,1)}, bf16[128,1024]{1,0:T(8,128)(2,1)}, u32[]{:S(2)}, u32[]{:S(2)}) collective-permute-start(bf16[128,1024]{1,0:T(8,128)(2,1)} %get-tuple-element.133), channel_id=1, source_target_pairs={{0,3},{1,2},{2,1},{3,0},{4,7},{5,6},{6,5},{7,4},{8,11},{9,10},{10,... | collective-permute-start | bytes 786440 | tf_op jit(solution)/shard_map/ppermute | solution.py:468
  224.9 5.2 collective-permute-start.19
  225.5 6.1 %collective-permute-start.20 = (bf16[64,1024]{1,0:T(8,128)(2,1)S(1)}, bf16[64,1024]{1,0:T(8,128)(2,1)S(1)}, u32[]{:S(2)}, u32[]{:S(2)}) collective-permute-start(bf16[64,1024]{1,0:T(8,128)(2,1)S(1)} %get-tuple-element.112), channel_id=1, source_target_pairs={{0,2},{1,3},{2,0},{3,1},{4,6},{5,7},{6,4},{7,5},{8,10},{9,11},{10,... | collective-permute-start | bytes 393224 | tf_op jit(solution)/shard_map/ppermute | solution.py:468
  227.2 6.7 %collective-permute-start.21 = (bf16[64,1024]{1,0:T(8,128)(2,1)S(1)}, bf16[64,1024]{1,0:T(8,128)(2,1)S(1)}, u32[]{:S(2)}, u32[]{:S(2)}) collective-permute-start(bf16[64,1024]{1,0:T(8,128)(2,1)S(1)} %get-tuple-element.111), channel_id=1, source_target_pairs={{0,3},{1,2},{2,1},{3,0},{4,7},{5,6},{6,5},{7,4},{8,11},{9,10},{10,... | collective-permute-start | bytes 393224 | tf_op jit(solution)/shard_map/ppermute | solution.py:468
  228.0 33.0 %collective-permute-start.16 = (bf16[128,1024]{1,0:T(8,128)(2,1)S(1)}, bf16[128,1024]{1,0:T(8,128)(2,1)S(1)}, u32[]{:S(2)}, u32[]{:S(2)}) collective-permute-start(bf16[128,1024]{1,0:T(8,128)(2,1)S(1)} %bitcast.203), channel_id=1, source_target_pairs={{0,1},{1,0},{2,3},{3,2},{4,5},{5,4},{6,7},{7,6},{8,9},{9,8},{10,11... | collective-permute-start | bytes 786440 | tf_op jit(solution)/shard_map/ppermute | solution.py:468
  228.4 32.6 %collective-permute-start.17 = (bf16[128,1024]{1,0:T(8,128)(2,1)S(1)}, bf16[128,1024]{1,0:T(8,128)(2,1)S(1)}, u32[]{:S(2)}, u32[]{:S(2)}) collective-permute-start(bf16[128,1024]{1,0:T(8,128)(2,1)S(1)} %bitcast.202), channel_id=1, source_target_pairs={{0,2},{1,3},{2,0},{3,1},{4,6},{5,7},{6,4},{7,5},{8,10},{9,11},{10,... | collective-permute-start | bytes 786440 | tf_op jit(solution)/shard_map/ppermute | solution.py:468
  230.1 30.9 %collective-permute-start.18 = (bf16[128,1024]{1,0:T(8,128)(2,1)S(1)}, bf16[128,1024]{1,0:T(8,128)(2,1)S(1)}, u32[]{:S(2)}, u32[]{:S(2)}) collective-permute-start(bf16[128,1024]{1,0:T(8,128)(2,1)S(1)} %bitcast.201), channel_id=1, source_target_pairs={{0,3},{1,2},{2,1},{3,0},{4,7},{5,6},{6,5},{7,4},{8,11},{9,10},{10,... | collective-permute-start | bytes 786440 | tf_op jit(solution)/shard_map/ppermute | solution.py:468
  329.3 21.1 %collective-permute-start.31 = (bf16[320,768]{1,0:T(8,128)(2,1)S(1)}, bf16[320,768]{1,0:T(8,128)(2,1)}, u32[]{:S(2)}, u32[]{:S(2)}) collective-permute-start(bf16[320,768]{1,0:T(8,128)(2,1)S(1)} %fusion.61), channel_id=1, source_target_pairs={{0,4},{4,0},{8,12},{12,8},{16,20},{20,16},{24,28},{28,24},{1,5},{5... | collective-permute-start | bytes 1474568 | tf_op jit(solution)/shard_map/ppermute | solution.py:468
  338.3 32.5 %copy-start.11 = (bf16[768,3,192]{0,2,1:T(8,128)(2,1)S(1)}, bf16[768,3,192]{0,2,1:T(8,128)(2,1)}, u32[]{:S(2)}) copy-start(bf16[768,3,192]{0,2,1:T(8,128)(2,1)} %param.22) | copy-start | bytes 2654212
  338.3 41.7 %collective-permute-start.51 = (bf16[768,768]{1,0:T(8,128)(2,1)}, bf16[768,768]{1,0:T(8,128)(2,1)}, u32[]{:S(2)}, u32[]{:S(2)}) collective-permute-start(bf16[768,768]{1,0:T(8,128)(2,1)} %fusion.36), channel_id=1, source_target_pairs={{0,1},{1,0},{2,3},{3,2},{4,5},{5,4},{6,7},{7,6},{8,9},{9,8},{10,11... | collective-permute-start | bytes 3538952 | tf_op jit(solution)/shard_map/ppermute | solution.py:468
  338.6 45.2 %collective-permute-start.40 = (bf16[960,768]{1,0:T(8,128)(2,1)}, bf16[960,768]{1,0:T(8,128)(2,1)}, u32[]{:S(2)}, u32[]{:S(2)}) collective-permute-start(bf16[960,768]{1,0:T(8,128)(2,1)} %pad_maximum_fusion.4), channel_id=1, source_target_pairs={{0,1},{1,0},{2,3},{3,2},{4,5},{5,4},{6,7},{7,6},{8,9},{9,8},{10,11... | collective-permute-start | bytes 4423688 | tf_op jit(solution)/shard_map/ppermute | solution.py:468
  352.6 7.4 %collective-permute-start.32 = (bf16[80,768]{1,0:T(8,128)(2,1)}, bf16[80,768]{1,0:T(8,128)(2,1)S(1)}, u32[]{:S(2)}, u32[]{:S(2)}) collective-permute-start(bf16[80,768]{1,0:T(8,128)(2,1)} %get-tuple-element.139), channel_id=1, source_target_pairs={{0,8},{4,12},{8,0},{12,4},{16,24},{20,28},{24,16},{28,20},{1,9},{5... | collective-permute-start | bytes 368648 | tf_op jit(solution)/shard_map/ppermute | solution.py:468
  352.6 12.7 %collective-permute-start.33 = (bf16[80,768]{1,0:T(8,128)(2,1)}, bf16[80,768]{1,0:T(8,128)(2,1)}, u32[]{:S(2)}, u32[]{:S(2)}) collective-permute-start(bf16[80,768]{1,0:T(8,128)(2,1)} %get-tuple-element.141), channel_id=1, source_target_pairs={{0,16},{4,20},{8,24},{12,28},{16,0},{20,4},{24,8},{28,12},{1,17},{... | collective-permute-start | bytes 368648 | tf_op jit(solution)/shard_map/ppermute | solution.py:468
  355.3 10.0 %collective-permute-start.34 = (bf16[80,768]{1,0:T(8,128)(2,1)}, bf16[80,768]{1,0:T(8,128)(2,1)}, u32[]{:S(2)}, u32[]{:S(2)}) collective-permute-start(bf16[80,768]{1,0:T(8,128)(2,1)} %get-tuple-element.140), channel_id=1, source_target_pairs={{0,24},{4,28},{8,16},{12,20},{16,8},{20,12},{24,0},{28,4},{1,25},{... | collective-permute-start | bytes 368648 | tf_op jit(solution)/shard_map/ppermute | solution.py:468
  366.3 8.3 %collective-permute-start.35 = (bf16[80,768]{1,0:T(8,128)(2,1)S(1)}, bf16[80,768]{1,0:T(8,128)(2,1)S(1)}, u32[]{:S(2)}, u32[]{:S(2)}) collective-permute-start(bf16[80,768]{1,0:T(8,128)(2,1)S(1)} %fusion.74), channel_id=1, source_target_pairs={{0,24},{4,28},{8,16},{12,20},{16,8},{20,12},{24,0},{28,4},{1,25},{... | collective-permute-start | bytes 368648 | tf_op jit(solution)/shard_map/ppermute | solution.py:468
  368.5 10.8 %collective-permute-start.36 = (bf16[80,768]{1,0:T(8,128)(2,1)S(1)}, bf16[80,768]{1,0:T(8,128)(2,1)S(1)}, u32[]{:S(2)}, u32[]{:S(2)}) collective-permute-start(bf16[80,768]{1,0:T(8,128)(2,1)S(1)} %fusion.74), channel_id=1, source_target_pairs={{0,16},{4,20},{8,24},{12,28},{16,0},{20,4},{24,8},{28,12},{1,17},{... | collective-permute-start | bytes 368648 | tf_op jit(solution)/shard_map/ppermute | solution.py:468
  370.2 9.2 %collective-permute-start.37 = (bf16[80,768]{1,0:T(8,128)(2,1)S(1)}, bf16[80,768]{1,0:T(8,128)(2,1)S(1)}, u32[]{:S(2)}, u32[]{:S(2)}) collective-permute-start(bf16[80,768]{1,0:T(8,128)(2,1)S(1)} %fusion.74), channel_id=1, source_target_pairs={{0,8},{4,12},{8,0},{12,4},{16,24},{20,28},{24,16},{28,20},{1,9},{5... | collective-permute-start | bytes 368648 | tf_op jit(solution)/shard_map/ppermute | solution.py:468
  374.7 25.4 %collective-permute-start.50 = (bf16[768,768]{1,0:T(8,128)(2,1)}, bf16[768,768]{1,0:T(8,128)(2,1)}, u32[]{:S(2)}, u32[]{:S(2)}) collective-permute-start(bf16[768,768]{1,0:T(8,128)(2,1)} %fusion.30), channel_id=1, source_target_pairs={{0,1},{1,0},{2,3},{3,2},{4,5},{5,4},{6,7},{7,6},{8,9},{9,8},{10,11... | collective-permute-start | bytes 3538952 | tf_op jit(solution)/shard_map/ppermute | solution.py:468
  379.4 36.9 %collective-permute-start.39 = (bf16[960,768]{1,0:T(8,128)(2,1)}, bf16[960,768]{1,0:T(8,128)(2,1)S(1)}, u32[]{:S(2)}, u32[]{:S(2)}) collective-permute-start(bf16[960,768]{1,0:T(8,128)(2,1)} %pad_maximum_fusion.2), channel_id=1, source_target_pairs={{0,1},{1,0},{2,3},{3,2},{4,5},{5,4},{6,7},{7,6},{8,9},{9,8},{10,11... | collective-permute-start | bytes 4423688 | tf_op jit(solution)/shard_map/ppermute | solution.py:468
  379.4 17.2 %collective-permute-start.23 = (bf16[768,1024]{1,0:T(8,128)(2,1)}, bf16[768,1024]{1,0:T(8,128)(2,1)}, u32[]{:S(2)}, u32[]{:S(2)}) collective-permute-start(bf16[768,1024]{1,0:T(8,128)(2,1)} %fusion.51), channel_id=1, source_target_pairs={{0,1},{1,0},{2,3},{3,2},{4,5},{5,4},{6,7},{7,6},{8,9},{9,8},{10,11... | collective-permute-start | bytes 4718600 | tf_op jit(solution)/shard_map/ppermute | solution.py:468
  380.0 13.3 %collective-permute-start.38 = (bf16[320,768]{1,0:T(8,128)(2,1)S(1)}, bf16[320,768]{1,0:T(8,128)(2,1)}, u32[]{:S(2)}, u32[]{:S(2)}) collective-permute-start(bf16[320,768]{1,0:T(8,128)(2,1)S(1)} %pad_maximum_fusion.9), channel_id=1, source_target_pairs={{0,4},{4,0},{8,12},{12,8},{16,20},{20,16},{24,28},{28,24},{1,5},{5... | collective-permute-start | bytes 1474568 | tf_op jit(solution)/shard_map/ppermute | solution.py:468
  383.9 29.2 %collective-permute-start.52 = (bf16[768,768]{1,0:T(8,128)(2,1)}, bf16[768,768]{1,0:T(8,128)(2,1)}, u32[]{:S(2)}, u32[]{:S(2)}) collective-permute-start(bf16[768,768]{1,0:T(8,128)(2,1)} %add_convert_fusion.2), channel_id=1, source_target_pairs={{0,2},{1,3},{2,0},{3,1},{4,6},{5,7},{6,4},{7,5},{8,10},{9,11},{10,... | collective-permute-start | bytes 3538952 | tf_op jit(solution)/shard_map/ppermute | solution.py:468
  393.3 51.3 %collective-permute-start.41 = (bf16[960,768]{1,0:T(8,128)(2,1)}, bf16[960,768]{1,0:T(8,128)(2,1)}, u32[]{:S(2)}, u32[]{:S(2)}) collective-permute-start(bf16[960,768]{1,0:T(8,128)(2,1)} %add_convert_fusion.1), channel_id=1, source_target_pairs={{0,2},{1,3},{2,0},{3,1},{4,6},{5,7},{6,4},{7,5},{8,10},{9,11},{10,... | collective-permute-start | bytes 4423688 | tf_op jit(solution)/shard_map/ppermute | solution.py:468
  396.6 58.0 %collective-permute-start.22 = (bf16[768,1024]{1,0:T(8,128)(2,1)}, bf16[768,1024]{1,0:T(8,128)(2,1)}, u32[]{:S(2)}, u32[]{:S(2)}) collective-permute-start(bf16[768,1024]{1,0:T(8,128)(2,1)} %get-tuple-element.84), channel_id=1, source_target_pairs={{0,1},{1,0},{2,3},{3,2},{4,5},{5,4},{6,7},{7,6},{8,9},{9,8},{10,11... | collective-permute-start | bytes 4718600 | tf_op jit(solution)/shard_map/ppermute | solution.py:468
  400.0 77.4 %collective-permute-start.24 = (bf16[768,1024]{1,0:T(8,128)(2,1)S(1)}, bf16[768,1024]{1,0:T(8,128)(2,1)}, u32[]{:S(2)}, u32[]{:S(2)}) collective-permute-start(bf16[768,1024]{1,0:T(8,128)(2,1)S(1)} %fusion), channel_id=1, source_target_pairs={{0,2},{1,3},{2,0},{3,1},{4,6},{5,7},{6,4},{7,5},{8,10},{9,11},{10,... | collective-permute-start | bytes 4718600 | tf_op jit(solution)/shard_map/ppermute | solution.py:468
  413.0 31.6 %copy-start.1 = (bf16[960,768]{1,0:T(8,128)(2,1)S(1)}, bf16[960,768]{1,0:T(8,128)(2,1)}, u32[]{:S(2)}) copy-start(bf16[960,768]{1,0:T(8,128)(2,1)} %pad_maximum_fusion.1) | copy-start | bytes 4423684
  415.4 34.9 %collective-permute-start.53 = (bf16[384,768]{1,0:T(8,128)(2,1)S(1)}, bf16[384,768]{1,0:T(8,128)(2,1)S(1)}, u32[]{:S(2)}, u32[]{:S(2)}) collective-permute-start(bf16[384,768]{1,0:T(8,128)(2,1)S(1)} %fusion.60), channel_id=1, source_target_pairs={{0,4},{4,0},{8,12},{12,8},{16,20},{20,16},{24,28},{28,24},{1,5},{5... | collective-permute-start | bytes 1769480 | tf_op jit(solution)/shard_map/ppermute | solution.py:468
  448.1 37.5 %collective-permute-start.42 = (bf16[480,768]{1,0:T(8,128)(2,1)}, bf16[480,768]{1,0:T(8,128)(2,1)}, u32[]{:S(2)}, u32[]{:S(2)}) collective-permute-start(bf16[480,768]{1,0:T(8,128)(2,1)} %fusion.59), channel_id=1, source_target_pairs={{0,4},{4,0},{8,12},{12,8},{16,20},{20,16},{24,28},{28,24},{1,5},{5... | collective-permute-start | bytes 2211848 | tf_op jit(solution)/shard_map/ppermute | solution.py:468
  452.2 34.9 %collective-permute-start.54 = (bf16[96,768]{1,0:T(8,128)(2,1)}, bf16[96,768]{1,0:T(8,128)(2,1)S(1)}, u32[]{:S(2)}, u32[]{:S(2)}) collective-permute-start(bf16[96,768]{1,0:T(8,128)(2,1)} %get-tuple-element.126), channel_id=1, source_target_pairs={{0,8},{4,12},{8,0},{12,4},{16,24},{20,28},{24,16},{28,20},{1,9},{5... | collective-permute-start | bytes 442376 | tf_op jit(solution)/shard_map/ppermute | solution.py:468
  452.2 37.6 %collective-permute-start.55 = (bf16[96,768]{1,0:T(8,128)(2,1)}, bf16[96,768]{1,0:T(8,128)(2,1)S(1)}, u32[]{:S(2)}, u32[]{:S(2)}) collective-permute-start(bf16[96,768]{1,0:T(8,128)(2,1)} %get-tuple-element.128), channel_id=1, source_target_pairs={{0,16},{4,20},{8,24},{12,28},{16,0},{20,4},{24,8},{28,12},{1,17},{... | collective-permute-start | bytes 442376 | tf_op jit(solution)/shard_map/ppermute | solution.py:468
  454.6 36.8 %collective-permute-start.56 = (bf16[96,768]{1,0:T(8,128)(2,1)S(1)}, bf16[96,768]{1,0:T(8,128)(2,1)S(1)}, u32[]{:S(2)}, u32[]{:S(2)}) collective-permute-start(bf16[96,768]{1,0:T(8,128)(2,1)S(1)} %get-tuple-element.127), channel_id=1, source_target_pairs={{0,24},{4,28},{8,16},{12,20},{16,8},{20,12},{24,0},{28,4},{1,25},{... | collective-permute-start | bytes 442376 | tf_op jit(solution)/shard_map/ppermute | solution.py:468
  485.6 9.1 %collective-permute-start.25 = (f32[6,768]{1,0:T(8,128)}, f32[6,768]{1,0:T(8,128)S(1)}, u32[]{:S(2)}, u32[]{:S(2)}) collective-permute-start(f32[6,768]{1,0:T(8,128)} %stack.20), channel_id=1, source_target_pairs={{0,1},{1,0},{2,3},{3,2},{4,5},{5,4},{6,7},{7,6},{8,9},{9,8},{10,11... | collective-permute-start | bytes 55304 | tf_op jit(solution)/shard_map/ppermute | solution.py:468
  487.0 10.5 %collective-permute-start.43 = (bf16[120,768]{1,0:T(8,128)(2,1)S(1)}, bf16[120,768]{1,0:T(8,128)(2,1)S(1)}, u32[]{:S(2)}, u32[]{:S(2)}) collective-permute-start(bf16[120,768]{1,0:T(8,128)(2,1)S(1)} %get-tuple-element.121), channel_id=1, source_target_pairs={{0,8},{4,12},{8,0},{12,4},{16,24},{20,28},{24,16},{28,20},{1,9},{5... | collective-permute-start | bytes 552968 | tf_op jit(solution)/shard_map/ppermute | solution.py:468
  487.1 22.8 %collective-permute-start.44 = (bf16[120,768]{1,0:T(8,128)(2,1)S(1)}, bf16[120,768]{1,0:T(8,128)(2,1)S(1)}, u32[]{:S(2)}, u32[]{:S(2)}) collective-permute-start(bf16[120,768]{1,0:T(8,128)(2,1)S(1)} %get-tuple-element.123), channel_id=1, source_target_pairs={{0,16},{4,20},{8,24},{12,28},{16,0},{20,4},{24,8},{28,12},{1,17},{... | collective-permute-start | bytes 552968 | tf_op jit(solution)/shard_map/ppermute | solution.py:468
  489.7 21.8 %collective-permute-start.45 = (bf16[120,768]{1,0:T(8,128)(2,1)S(1)}, bf16[120,768]{1,0:T(8,128)(2,1)S(1)}, u32[]{:S(2)}, u32[]{:S(2)}) collective-permute-start(bf16[120,768]{1,0:T(8,128)(2,1)S(1)} %get-tuple-element.122), channel_id=1, source_target_pairs={{0,24},{4,28},{8,16},{12,20},{16,8},{20,12},{24,0},{28,4},{1,25},{... | collective-permute-start | bytes 552968 | tf_op jit(solution)/shard_map/ppermute | solution.py:468
  492.5 21.4 %collective-permute-start.57 = (bf16[96,768]{1,0:T(8,128)(2,1)S(1)}, bf16[96,768]{1,0:T(8,128)(2,1)S(1)}, u32[]{:S(2)}, u32[]{:S(2)}) collective-permute-start(bf16[96,768]{1,0:T(8,128)(2,1)S(1)} %fusion.67), channel_id=1, source_target_pairs={{0,24},{4,28},{8,16},{12,20},{16,8},{20,12},{24,0},{28,4},{1,25},{... | collective-permute-start | bytes 442376 | tf_op jit(solution)/shard_map/ppermute | solution.py:468
  494.7 32.4 %collective-permute-start.58 = (bf16[96,768]{1,0:T(8,128)(2,1)S(1)}, bf16[96,768]{1,0:T(8,128)(2,1)S(1)}, u32[]{:S(2)}, u32[]{:S(2)}) collective-permute-start(bf16[96,768]{1,0:T(8,128)(2,1)S(1)} %fusion.67), channel_id=1, source_target_pairs={{0,16},{4,20},{8,24},{12,28},{16,0},{20,4},{24,8},{28,12},{1,17},{... | collective-permute-start | bytes 442376 | tf_op jit(solution)/shard_map/ppermute | solution.py:468
  497.5 29.6 %collective-permute-start.59 = (bf16[96,768]{1,0:T(8,128)(2,1)S(1)}, bf16[96,768]{1,0:T(8,128)(2,1)S(1)}, u32[]{:S(2)}, u32[]{:S(2)}) collective-permute-start(bf16[96,768]{1,0:T(8,128)(2,1)S(1)} %fusion.67), channel_id=1, source_target_pairs={{0,8},{4,12},{8,0},{12,4},{16,24},{20,28},{24,16},{28,20},{1,9},{5... | collective-permute-start | bytes 442376 | tf_op jit(solution)/shard_map/ppermute | solution.py:468
  509.8 17.4 %collective-permute-start.26 = (f32[6,768]{1,0:T(8,128)S(1)}, f32[6,768]{1,0:T(8,128)S(1)}, u32[]{:S(2)}, u32[]{:S(2)}) collective-permute-start(f32[6,768]{1,0:T(8,128)S(1)} %add.213), channel_id=1, source_target_pairs={{0,2},{1,3},{2,0},{3,1},{4,6},{5,7},{6,4},{7,5},{8,10},{9,11},{10,... | collective-permute-start | bytes 55304 | tf_op jit(solution)/shard_map/ppermute | solution.py:468
  511.7 21.7 %collective-permute-start.46 = (bf16[120,768]{1,0:T(8,128)(2,1)S(1)}, bf16[120,768]{1,0:T(8,128)(2,1)S(1)}, u32[]{:S(2)}, u32[]{:S(2)}) collective-permute-start(bf16[120,768]{1,0:T(8,128)(2,1)S(1)} %fusion.64), channel_id=1, source_target_pairs={{0,24},{4,28},{8,16},{12,20},{16,8},{20,12},{24,0},{28,4},{1,25},{... | collective-permute-start | bytes 552968 | tf_op jit(solution)/shard_map/ppermute | solution.py:468
  513.9 22.1 %collective-permute-start.47 = (bf16[120,768]{1,0:T(8,128)(2,1)S(1)}, bf16[120,768]{1,0:T(8,128)(2,1)S(1)}, u32[]{:S(2)}, u32[]{:S(2)}) collective-permute-start(bf16[120,768]{1,0:T(8,128)(2,1)S(1)} %fusion.64), channel_id=1, source_target_pairs={{0,16},{4,20},{8,24},{12,28},{16,0},{20,4},{24,8},{28,12},{1,17},{... | collective-permute-start | bytes 552968 | tf_op jit(solution)/shard_map/ppermute | solution.py:468
  527.1 11.2 %collective-permute-start.48 = (bf16[120,768]{1,0:T(8,128)(2,1)S(1)}, bf16[120,768]{1,0:T(8,128)(2,1)S(1)}, u32[]{:S(2)}, u32[]{:S(2)}) collective-permute-start(bf16[120,768]{1,0:T(8,128)(2,1)S(1)} %fusion.64), channel_id=1, source_target_pairs={{0,8},{4,12},{8,0},{12,4},{16,24},{20,28},{24,16},{28,20},{1,9},{5... | collective-permute-start | bytes 552968 | tf_op jit(solution)/shard_map/ppermute | solution.py:468
  527.2 4.2 collective-permute-start.27
  527.6 15.3 %collective-permute-start.60 = (bf16[384,768]{1,0:T(8,128)(2,1)S(1)}, bf16[384,768]{1,0:T(8,128)(2,1)}, u32[]{:S(2)}, u32[]{:S(2)}) collective-permute-start(bf16[384,768]{1,0:T(8,128)(2,1)S(1)} %pad_maximum_fusion.8), channel_id=1, source_target_pairs={{0,4},{4,0},{8,12},{12,8},{16,20},{20,16},{24,28},{28,24},{1,5},{5... | collective-permute-start | bytes 1769480 | tf_op jit(solution)/shard_map/ppermute | solution.py:468
  531.4 7.3 %collective-permute-start.28 = (f32[6,768]{1,0:T(8,128)S(1)}, f32[6,768]{1,0:T(8,128)S(1)}, u32[]{:S(2)}, u32[]{:S(2)}) collective-permute-start(f32[6,768]{1,0:T(8,128)S(1)} %add.215), channel_id=1, source_target_pairs={{0,8},{4,12},{8,0},{12,4},{16,24},{20,28},{24,16},{28,20},{1,9},{5... | collective-permute-start | bytes 55304 | tf_op jit(solution)/shard_map/ppermute | solution.py:468
  533.4 5.3 collective-permute-start.29
  536.0 5.6 %collective-permute-start.30 = (f32[6,768]{1,0:T(8,128)S(1)}, f32[6,768]{1,0:T(8,128)S(1)}, u32[]{:S(2)}, u32[]{:S(2)}) collective-permute-start(f32[6,768]{1,0:T(8,128)S(1)} %add.215), channel_id=1, source_target_pairs={{0,24},{4,28},{8,16},{12,20},{16,8},{20,12},{24,0},{28,4},{1,25},{... | collective-permute-start | bytes 55304 | tf_op jit(solution)/shard_map/ppermute | solution.py:468
  538.4 17.5 %collective-permute-start.49 = (bf16[480,768]{1,0:T(8,128)(2,1)S(1)}, bf16[480,768]{1,0:T(8,128)(2,1)S(1)}, u32[]{:S(2)}, u32[]{:S(2)}) collective-permute-start(bf16[480,768]{1,0:T(8,128)(2,1)S(1)} %pad_maximum_fusion.7), channel_id=1, source_target_pairs={{0,4},{4,0},{8,12},{12,8},{16,20},{20,16},{24,28},{28,24},{1,5},{5... | collective-permute-start | bytes 2211848 | tf_op jit(solution)/shard_map/ppermute | solution.py:468
  (36 other events, 174.1 us)
